TPU v7x, 32 devices: a whole 2x2x4 slice. The times are simulated.
32 devices in a mesh: seq: 8 (over z, core), state: 4 (over y, x).
Axes of the slice: x: 2, y: 2, z: 4, core: 2. Of those that a mesh axis runs over, the one named last changes fastest.
Arguments:
- tokens: bfloat16 [16384, 1024], P(('seq', 'state')), may hold values from -6 to 6
- lengths: int32 [8], P('seq'), may hold values from 1024 to 2048, as said below
- grad_out: bfloat16 [16384, 1024], P(('seq', 'state')), may hold values from -6 to 6
- norm_gain: float32 [1024], replicated, may hold values from 0.5 to 1.5
- in_weight: bfloat16 [1024, 4096], replicated, may hold values from -0.1875 to 0.1875
- conv_weight: float32 [4, 2048], replicated, may hold values from -2 to 2
- conv_bias: float32 [2048], replicated, may hold values from -0.5 to 0.5
- xproj_weight: bfloat16 [2048, 96], replicated, may hold values from -0.125 to 0.125
- dtproj_weight: bfloat16 [2048, 64], replicated, may hold values from -0.75 to 0.75
- dt_bias: float32 [2048], replicated, may hold values from -5 to -2
- a_log: float32 [16, 2048], P('state'), may hold values from -3 to 2.5
- d_skip: float32 [2048], replicated, may hold values from 0.5 to 1.5
- out_weight: bfloat16 [2048, 1024], replicated, may hold values from -0.25 to 0.25
Outputs:
- output: bfloat16 [16384, 1024], P(('seq', 'state'))
- grad_tokens: float32 [16384, 1024], P(('seq', 'state'))
- grad_norm_gain: float32 [1024], replicated
- grad_in_weight: float32 [1024, 4096], P('seq')
- grad_conv_weight: float32 [4, 2048], replicated
- grad_conv_bias: float32 [2048], replicated
- grad_xproj_weight: float32 [2048, 96], P('seq')
- grad_dtproj_weight: float32 [2048, 64], P('seq')
- grad_dt_bias: float32 [2048], replicated
- grad_a_log: float32 [16, 2048], P('state')
- grad_d_skip: float32 [2048], replicated
- grad_out_weight: float32 [2048, 1024], P('seq')
- dt_mean: float32 [2048], replicated
- dt_spread: float32 [2048], replicated
Inputs may be any that keep to these rules, and one draw needn't show every extreme that they name: `lengths`: each slot of 2048 rows holds one sequence from its first row on, padding after it; in every draw one slot is full and one holds exactly half of 2048 tokens.
All inputs are finite; a program needn't handle non-finite values.
Results may differ from a plain program's by a relative error of at most 0.0034.
The roundings to bfloat16 on the way count: a program that leaves them out, or rounds other values in their place, can miss the bound.
Values may be sent and summed in bfloat16 or wider, within the bound.
No kernel may reach another device: no remote copies, remote signals or barrier semaphores. Data moves between devices by JAX's collectives and lax.ppermute only.
A program may use at most 832 MiB of HBM per device.

v0:
```python
import jax
import jax.numpy as jnp
from jax import lax
from jax.sharding import PartitionSpec as P

EPSILON = 1e-05


def shifted(value, axis, steps):
    count = lax.axis_size(axis)
    leading, last = (max(0, -steps), min(count, count - steps))
    return lax.ppermute(value, axis, [(source, source + steps) for source in range(leading, last)])


def combine(earlier, later_pair):
    return (earlier[0] * later_pair[0], later_pair[0] * earlier[1] + later_pair[1])


def chain(factor_in, source_in, block_span, reverse):
    count = factor_in.shape[0]
    total_rows = factor_in.shape[1]
    rest = factor_in.shape[2:]
    blocks = total_rows // block_span
    block_shape = (count, blocks, block_span) + rest
    factor_in = factor_in.reshape(block_shape)
    source_in = source_in.reshape(block_shape)
    running = jnp.zeros((count, blocks) + rest, jnp.float32)
    product = jnp.ones((count, blocks) + rest, jnp.float32)
    running_list = [None] * block_span
    product_list = [None] * block_span
    moments = range(block_span - 1, -1, -1) if reverse else range(block_span)
    for moment in moments:
        running = factor_in[:, :, moment] * running + source_in[:, :, moment]
        product = product * factor_in[:, :, moment]
        running_list[moment] = running
        product_list[moment] = product
    local_part = jnp.stack(running_list, axis=2)
    cum_factor = jnp.stack(product_list, axis=2)
    link_values = lax.associative_scan(combine, (product, running), reverse=reverse, axis=1)[1]
    zero_block = jnp.zeros_like(link_values[:, :1])
    if reverse:
        entering = jnp.concatenate([link_values[:, 1:], zero_block], axis=1)
    else:
        entering = jnp.concatenate([zero_block, link_values[:, :-1]], axis=1)
    combined = local_part + cum_factor * entering[:, :, None]
    return combined.reshape((count, total_rows) + rest)


def convolve(inner_part, position, conv_part, bias_part):
    tap_count = conv_part.shape[0]
    channel_count = inner_part.shape[1]
    conv_pre = bias_part + conv_part[tap_count - 1] * inner_part
    for shift_rows in range(1, tap_count):
        moved_rows = jnp.concatenate(
            [jnp.zeros((shift_rows, channel_count), inner_part.dtype), inner_part[:-shift_rows]],
            axis=0,
        )
        moved_rows = jnp.where(
            (position >= shift_rows)[:, None], moved_rows, jnp.zeros_like(moved_rows)
        )
        conv_pre = conv_pre + conv_part[tap_count - 1 - shift_rows] * moved_rows
    return conv_pre


def prepare(
    inner_all, position, conv_weight, conv_bias, xproj_weight, dtproj_weight, dt_bias, rank_width
):
    conv_pre = convolve(inner_all, position, conv_weight, conv_bias)
    mixed = jax.nn.silu(conv_pre)
    mixed_low = mixed.astype(jnp.bfloat16)
    projected = jnp.dot(mixed_low, xproj_weight, preferred_element_type=jnp.float32)
    rank_low = projected[:, :rank_width].astype(jnp.bfloat16)
    raised = (
        lax.dot_general(
            rank_low, dtproj_weight, (((1,), (1,)), ((), ())), preferred_element_type=jnp.float32
        )
        + dt_bias
    )
    step_size = jax.nn.softplus(raised)
    return (conv_pre, mixed, mixed_low, projected, rank_low, raised, step_size)


def scan_backward(
    grad_y_in, b_cols, c_cols, decay_in, mixed, step_size, factor, states, block_span
):
    source = c_cols[:, :, None] * grad_y_in[None]
    next_factor = jnp.concatenate([factor[:, 1:], jnp.zeros_like(factor[:, :1])], axis=1)
    grad_states = chain(next_factor, source, block_span, True)
    previous = jnp.concatenate([jnp.zeros_like(states[:, :1]), states[:, :-1]], axis=1)
    through_decay = grad_states * previous * factor
    grad_step = jnp.sum(
        through_decay * decay_in[:, None, :] + grad_states * b_cols[:, :, None] * mixed[None],
        axis=0,
    )
    grad_rate = jnp.sum(through_decay * step_size[None], axis=1)
    grad_mixed_scan = jnp.sum(grad_states * b_cols[:, :, None], axis=0) * step_size
    grad_b = jnp.sum(grad_states * (step_size * mixed)[None], axis=2).T
    grad_c = jnp.sum(states * grad_y_in[None], axis=2).T
    return (grad_step, grad_rate, grad_mixed_scan, grad_b, grad_c)


def body(
    tokens,
    lengths,
    grad_out,
    norm_gain,
    in_weight,
    conv_weight,
    conv_bias,
    xproj_weight,
    dtproj_weight,
    dt_bias,
    a_log,
    d_skip,
    out_weight,
):
    block_span = 16
    tok_rows = tokens.shape[0]
    inner_width = out_weight.shape[0]
    local_states = a_log.shape[0]
    rank_width = dtproj_weight.shape[1]
    pair_states = xproj_weight.shape[1] - rank_width
    all_states = pair_states // 2
    tap_count = conv_weight.shape[0]
    state_count = lax.axis_size("state")
    group_rows = tok_rows * state_count
    member = lax.axis_index("state")
    offset = member * tok_rows
    first_state = member * local_states
    slot_rows = group_rows // lengths.shape[0]
    position = jnp.arange(group_rows, dtype=jnp.int32) % slot_rows
    alive_rows = (
        (jnp.arange(slot_rows, dtype=jnp.int32)[None, :] < lengths[:, None])
        .reshape(group_rows)
        .astype(jnp.float32)
    )
    alive_own = lax.dynamic_slice_in_dim(alive_rows, offset, tok_rows)
    not_start = (position != 0).astype(jnp.float32)

    def own_rows(values):
        return lax.dynamic_slice_in_dim(values, offset, tok_rows)

    inputs = tokens.astype(jnp.float32)
    inv_scale = lax.rsqrt(jnp.mean(inputs * inputs, axis=1, keepdims=True) + EPSILON)
    normed = inputs * inv_scale
    normed_low = (normed * norm_gain).astype(jnp.bfloat16)
    joined = jnp.dot(normed_low, in_weight, preferred_element_type=jnp.float32)
    inner_low = joined[:, :inner_width].astype(jnp.bfloat16)
    gate_in = joined[:, inner_width:]
    inner_all = lax.all_gather(inner_low, "state", axis=0, tiled=True)
    gate_act = jax.nn.silu(gate_in)
    stat_count = jnp.sum(alive_own)
    decay_rate = -jnp.exp(a_log)

    def scan_inputs():
        conv_pre, mixed, mixed_low, projected, rank_low, raised, step_size = prepare(
            inner_all,
            position,
            conv_weight,
            conv_bias,
            xproj_weight,
            dtproj_weight,
            dt_bias,
            rank_width,
        )
        b_local = lax.dynamic_slice_in_dim(projected, rank_width + first_state, local_states, 1).T
        c_local = lax.dynamic_slice_in_dim(
            projected, rank_width + all_states + first_state, local_states, 1
        ).T
        factor = jnp.exp(decay_rate[:, None, :] * step_size[None]) * not_start[None, :, None]
        drive_term = b_local[:, :, None] * (step_size * mixed)[None]
        states = chain(factor, drive_term, block_span, False)
        return (
            conv_pre,
            mixed,
            mixed_low,
            rank_low,
            raised,
            step_size,
            b_local,
            c_local,
            factor,
            states,
        )

    kept_values = scan_inputs()
    mixed_fwd, step_fwd, c_fwd, states_fwd = (
        kept_values[1],
        kept_values[5],
        kept_values[7],
        kept_values[9],
    )
    partial_y = jnp.sum(c_fwd[:, :, None] * states_fwd, axis=0)
    summed_y = lax.psum_scatter(partial_y, "state", scatter_dimension=0, tiled=True)
    mixed_own = own_rows(mixed_fwd)
    full_y = summed_y + d_skip * mixed_own
    step_own = own_rows(step_fwd)
    weighted = alive_own[:, None] * step_own
    stat_first = jnp.sum(weighted, axis=0)
    stat_second = jnp.sum(weighted * step_own, axis=0)
    gated_low = (full_y * gate_act).astype(jnp.bfloat16)
    branch = jnp.dot(gated_low, out_weight, preferred_element_type=jnp.float32)
    output = (inputs + alive_own[:, None] * branch).astype(jnp.bfloat16)
    stat_totals = lax.psum((stat_first, stat_second, stat_count), ("seq", "state"))
    cotangent = grad_out.astype(jnp.float32)
    masked_low = (cotangent * alive_own[:, None]).astype(jnp.bfloat16)
    grad_out_w = lax.dot_general(
        gated_low, masked_low, (((0,), (0,)), ((), ())), preferred_element_type=jnp.float32
    )
    grad_gated = lax.dot_general(
        masked_low, out_weight, (((1,), (1,)), ((), ())), preferred_element_type=jnp.float32
    )
    grad_y = grad_gated * gate_act
    gate_sigmoid = jax.nn.sigmoid(gate_in)
    grad_gate_in = grad_gated * full_y * gate_sigmoid * (1.0 + gate_in * (1.0 - gate_sigmoid))
    grad_skip = jnp.sum(grad_y * mixed_own, axis=0)
    grad_y_all = lax.all_gather(grad_y.astype(jnp.bfloat16), "state", axis=0, tiled=True)
    conv_pre, mixed, mixed_low, rank_low, raised, step_size, b_local, c_local, factor, states = (
        scan_inputs()
    )
    grad_step, grad_rate, grad_mixed_scan, grad_b, grad_c = scan_backward(
        grad_y_all.astype(jnp.float32),
        b_local,
        c_local,
        decay_rate,
        mixed,
        step_size,
        factor,
        states,
        block_span,
    )
    grad_bc = jnp.zeros((group_rows, pair_states), jnp.float32)
    grad_bc = lax.dynamic_update_slice_in_dim(grad_bc, grad_b, first_state, 1)
    grad_bc = lax.dynamic_update_slice_in_dim(grad_bc, grad_c, all_states + first_state, 1)
    own_mixed, own_step, own_bc = (
        lax.psum_scatter(grad_mixed_scan, "state", scatter_dimension=0, tiled=True),
        lax.psum_scatter(grad_step, "state", scatter_dimension=0, tiled=True),
        lax.psum_scatter(grad_bc, "state", scatter_dimension=0, tiled=True),
    )
    grad_raised = own_step * jax.nn.sigmoid(own_rows(raised))
    grad_dt_bias = jnp.sum(grad_raised, axis=0)
    raised_low = grad_raised.astype(jnp.bfloat16)
    grad_dtproj = lax.dot_general(
        raised_low, own_rows(rank_low), (((0,), (0,)), ((), ())), preferred_element_type=jnp.float32
    )
    grad_rank = jnp.dot(raised_low, dtproj_weight, preferred_element_type=jnp.float32)
    grad_proj_low = jnp.concatenate([grad_rank, own_bc], axis=1).astype(jnp.bfloat16)
    grad_xproj = lax.dot_general(
        own_rows(mixed_low),
        grad_proj_low,
        (((0,), (0,)), ((), ())),
        preferred_element_type=jnp.float32,
    )
    grad_mixed = (
        own_mixed
        + grad_y * d_skip
        + lax.dot_general(
            grad_proj_low,
            xproj_weight,
            (((1,), (1,)), ((), ())),
            preferred_element_type=jnp.float32,
        )
    )
    pre_own = own_rows(conv_pre)
    pre_sigmoid = jax.nn.sigmoid(pre_own)
    grad_pre = grad_mixed * pre_sigmoid * (1.0 + pre_own * (1.0 - pre_sigmoid))
    ahead_rows = shifted(grad_pre[: tap_count - 1], "state", -1)
    grad_ext = jnp.concatenate([grad_pre, ahead_rows], axis=0)
    pos_ext = (offset + jnp.arange(tok_rows + tap_count - 1, dtype=jnp.int32)) % slot_rows
    own_pos = lax.dynamic_slice_in_dim(position, offset, tok_rows)
    inner_ext = lax.dynamic_slice_in_dim(
        jnp.concatenate(
            [jnp.zeros((tap_count - 1, inner_width), inner_all.dtype), inner_all], axis=0
        ),
        offset,
        tok_rows + tap_count - 1,
    )
    grad_inner = conv_weight[tap_count - 1] * grad_pre
    conv_rows = [None] * tap_count
    conv_rows[tap_count - 1] = jnp.sum(
        grad_pre * inner_ext[tap_count - 1 : tap_count - 1 + tok_rows], axis=0
    )
    for shift_rows in range(1, tap_count):
        later_rows = grad_ext[shift_rows : shift_rows + tok_rows]
        later_rows = jnp.where(
            (pos_ext[shift_rows : shift_rows + tok_rows] >= shift_rows)[:, None],
            later_rows,
            jnp.zeros_like(later_rows),
        )
        grad_inner = grad_inner + conv_weight[tap_count - 1 - shift_rows] * later_rows
        earlier_rows = inner_ext[tap_count - 1 - shift_rows : tap_count - 1 - shift_rows + tok_rows]
        earlier_rows = jnp.where(
            (own_pos >= shift_rows)[:, None], earlier_rows, jnp.zeros_like(earlier_rows)
        )
        conv_rows[tap_count - 1 - shift_rows] = jnp.sum(grad_pre * earlier_rows, axis=0)
    grad_conv = jnp.stack(conv_rows, axis=0)
    grad_conv_bias = jnp.sum(grad_pre, axis=0)
    rate_term = grad_rate * decay_rate
    grad_joined_low = jnp.concatenate([grad_inner, grad_gate_in], axis=1).astype(jnp.bfloat16)
    grad_in_w = lax.dot_general(
        normed_low, grad_joined_low, (((0,), (0,)), ((), ())), preferred_element_type=jnp.float32
    )
    grad_normed = lax.dot_general(
        grad_joined_low, in_weight, (((1,), (1,)), ((), ())), preferred_element_type=jnp.float32
    )
    grad_gain = jnp.sum(grad_normed * normed, axis=0)
    scaled = grad_normed * norm_gain
    grad_tokens = cotangent + inv_scale * (
        scaled - normed * jnp.mean(scaled * normed, axis=1, keepdims=True)
    )
    large_shards = (
        lax.psum_scatter(grad_in_w, "seq", scatter_dimension=0, tiled=True),
        lax.psum_scatter(grad_out_w, "seq", scatter_dimension=0, tiled=True),
        lax.psum_scatter(grad_xproj, "seq", scatter_dimension=0, tiled=True),
        lax.psum_scatter(grad_dtproj, "seq", scatter_dimension=0, tiled=True),
    )
    large_grads = lax.psum(
        (large_shards[0], large_shards[1], large_shards[2], large_shards[3]), "state"
    )
    small_grads = lax.psum(
        (grad_gain, grad_conv, grad_conv_bias, grad_dt_bias, grad_skip), ("seq", "state")
    )
    total_first, total_second, total_count = stat_totals
    grad_a_log = lax.psum(rate_term, "seq")
    dt_mean = total_first / total_count
    dt_spread = jnp.sqrt(total_second / total_count - dt_mean * dt_mean + 1e-06)
    return (
        output,
        grad_tokens,
        small_grads[0],
        large_grads[0],
        small_grads[1],
        small_grads[2],
        large_grads[2],
        large_grads[3],
        small_grads[3],
        grad_a_log,
        small_grads[4],
        large_grads[1],
        dt_mean,
        dt_spread,
    )


def solution(mesh):
    placed = (
        P(("seq", "state"), None),
        P("seq"),
        P(("seq", "state"), None),
        P(),
        P(),
        P(),
        P(),
        P(),
        P(),
        P(),
        P("state", None),
        P(),
        P(),
    )
    return jax.shard_map(
        body,
        mesh=mesh,
        in_specs=placed,
        out_specs=(
            P(("seq", "state"), None),
            P(("seq", "state"), None),
            P(),
            P("seq", None),
            P(),
            P(),
            P("seq", None),
            P("seq", None),
            P(),
            P("state", None),
            P(),
            P("seq", None),
            P(),
            P(),
        ),
        check_vma=False,
    )
```

profile of v0, /device:TPU:0, one launch (start us, length us, event | category | flops | bytes accessed | tf_op | source)
XLA Modules:
  0.0 2986.5 jit_solution(17790475323709192883)
XLA Ops:
  23.2 88.4 %all-gather.3.cloned.1.call-done = bf16[2048,2048]{1,0:T(8,128)(2,1)} async-done(((bf16[512,2048]{1,0:T(8,128)(2,1)}), bf16[2048,2048]{1,0:T(8,128)(2,1)}) %all-gather.3.cloned.1.call-update) | async-done | bytes 8388624 | tf_op jit(solution)/shard_map/all_gather | solution.py:150
  111.6 30.6 %fusion.175 = (bf16[2048,2048]{1,0:T(8,128)(2,1)}, f32[2048,2048]{1,0:T(8,128)S(1)}, f32[2048,2048]{1,0:T(8,128)}) fusion(bf16[2045,2048]{1,0:T(8,128)(2,1)} %bitcast.472, pred[2048]{0:T(1024)(128)(4,1)S(1)} %get-tuple-element.205, f32[2048]{0:T(1024)S(1)} %bitcast.509, bf16[2046,2048]{1,0:T(8,128)(2,1)} %bitcast.473, ...), kind=kLoop, calls=%fused_computation.422 | loop fusion | flops 83886080 | bytes 75520000 | tf_op jit(solution)/shard_map/convert_element_type | solution.py:70
  154.4 18.5 compare_select_fusion
  173.0 26.0 exponential_multiply_fusion
  199.1 44.6 %slice.1014 = f32[4,2047,2048]{2,1,0:T(8,128)} slice(f32[4,2048,2048]{2,1,0:T(8,128)} %exponential_multiply_fusion), slice={[0:4], [1:2048], [0:2048]} | slice | bytes 134152192 | tf_op jit(solution)/shard_map/slice | solution.py:87
  256.4 46.3 %concatenate.91 = f32[4,2048,2048]{2,1,0:T(8,128)} pad(f32[4,2047,2048]{2,1,0:T(8,128)} %slice.1014, f32[]{:T(128)} %constant.39.clone.1), padding=0_0x0_1x0_0 | pad | bytes 134184960 | tf_op jit(solution)/shard_map/concatenate | solution.py:87
  302.6 183.2 %fusion.176 = (f32[4,128,1,2048]{3,2,1,0:T(1,128)}, f32[4,128,1,2048]{3,2,1,0:T(1,128)}, f32[4,128,1,2048]{3,2,1,0:T(1,128)}, f32[4,128,1,2048]{3,2,1,0:T(1,128)...) fusion(f32[4,128,16,2048]{3,2,1,0:T(8,128)} %bitcast.42), kind=kLoop, calls=%fused_computation.423 | loop fusion | bytes 134217728 | tf_op jit(solution)/shard_map/slice | solution.py:33
  487.8 46.1 %fusion.55 = f32[4,128,2048]{2,1,0:T(8,128)} fusion(f32[4,128,1,2048]{3,2,1,0:T(1,128)S(1)} %get-tuple-element.108, f32[4,128,1,2048]{3,2,1,0:T(1,128)} %get-tuple-element.93, f32[4,128,1,2048]{3,2,1,0:T(1,128)} %get-tuple-element.94, f32[4,128,1,2048]{3,2,1,0:T(1,128)} %get-tuple-element.95, f32[4,128,1,2048]{3,2,1,0:T(1,128)} %get-tuple-element.96, ...), kind=kLoop, calls=%fused_computation.86 | loop fusion | flops 15728640 | bytes 71303168 | tf_op jit(solution)/shard_map/mul | solution.py:34
  561.7 17.9 copy.75
  579.7 26.0 exponential_multiply_fusion.1
  605.7 24.3 fusion.86
  704.3 45.6 %multiply_dynamic-update-slice_fusion = (f32[4,128,16,2048]{3,1,0,2:T(8,128)}, f32[4,128,1,2048]{3,1,0,2:T(8,128)}, f32[4,128,1,2048]{3,1,0,2:T(8,128)}, f32[4,1...) fusion(f32[4,128,1,2048]{3,2,1,0:T(1,128)} %get-tuple-element.1, ...), kind=kLoop, calls=%fused_computation.148 | loop fusion | flops 15728639 | bytes 96468992
  764.1 27.5 broadcast_multiply_fusion
  791.6 52.1 %bitcast_add_fusion = f32[4,128,2048]{2,1,0:T(8,128)} fusion(f32[4,128,16,2048]{3,1,0,2:T(8,128)} %broadcast_multiply_fusion, f32[4,128,1,2048]{3,2,1,0:T(1,128)S(1)} %copy-done.3, f32[4,128,1,2048]{3,2,1,0:T(1,128)} %get-tuple-element.93, f32[4,128,1,2048]{3,2,1,0:T(1,128)} %get-tuple-element.94, f32[4,128,1,2048]{3,2,1,0:T(1,128)} %get-tuple-element.95, ...), kind=kLoop, calls=%fused_computation.87 | loop fusion | flops 33554432 | bytes 138412032 | tf_op jit(solution)/shard_map/add | solution.py:33
  976.8 58.3 %add_dynamic-update-slice_fusion = (f32[4,128,16,2048]{3,1,0,2:T(8,128)}, f32[4,128,1,2048]{3,1,0,2:T(8,128)}, f32[4,128,1,2048]{3,1,0,2:T(8,128)}, f32[4,128,1,...) fusion(f32[4,128,16,2048]{3,1,0,2:T(8,128)} %broadcast_multiply, ...), kind=kLoop, calls=%fused_computation.149 | loop fusion | flops 33554432 | bytes 167772160
  1094.3 33.2 %slice.939 = f32[4,127,2048]{2,1,0:T(8,128)} reverse(f32[4,127,2048]{2,1,0:T(8,128)} %slice_add_fusion.4), dimensions={1} | reverse | bytes 8323072 | tf_op jit(solution)/shard_map/slice | solution.py:42
  1280.3 108.1 %multiply_reduce_fusion.2 = (f32[4,128,16]{1,0,2:T(4,128)}, f32[128,16,2048]{2,0,1:T(8,128)}, f32[4,128,16,2048]{3,1,0,2:T(8,128)}, f32[4,128,16,2048]{3,1,0,2:T(8,128)}) fusion(f32[128,16,2048]{2,0,1:T(8,128)} %copy.77, f32[4,128,16]{1,0,2:T(4,128)S(1)} %copy-done.75, f32[4,128,16,2048]{3,1,0,2:T(8,128)} %get-tuple-element.146, ...), kind=kLoop, calls=%fused_computation.8 | loop fusion | flops 113238016 | bytes 306249728 | tf_op jit(solution)/shard_map/reduce_sum | solution.py:97
  1388.4 43.1 %bitcast_add_fusion.3 = f32[4,128,2048]{2,1,0:T(8,128)} fusion(f32[4,128,16,2048]{3,1,0,2:T(8,128)} %get-tuple-element.142, f32[4,128,16,2048]{3,1,0,2:T(8,128)} %exponential_multiply_fusion.1), kind=kLoop, calls=%fused_computation.93 | loop fusion | flops 33554432 | bytes 138412032 | tf_op jit(solution)/shard_map/add | solution.py:33
  1796.3 86.4 %multiply_reduce_fusion.1 = (f32[4,128,16]{1,0,2:T(4,128)S(1)}, f32[128,16,2048]{2,0,1:T(8,128)}, f32[4,128,16,2048]{3,1,0,2:T(8,128)}) fusion(f32[128,16,2048]{2,0,1:T(8,128)} %copy.95, f32[4,128,16]{1,0,2:T(4,128)S(1)} %copy-done.52, f32[4,128,16,2048]{3,1,0,2:T(8,128)} %get-tuple-element.110, f32[4,128,16,2048]{3,1,0,2:T(8,128)} %get-tuple-element.109, ...), kind=kLoop, calls=%fused_computation.7 | loop fusion | flops 96460800 | bytes 239140864 | tf_op jit(solution)/shard_map/reduce_sum | solution.py:98
  1882.8 56.6 %copy.100 = f32[4,128,16,2048]{3,2,1,0:T(8,128)} copy(f32[4,128,16,2048]{3,1,0,2:T(8,128)} %get-tuple-element.63) | data formatting | bytes 134217728 | tf_op jit(solution)/shard_map/add | solution.py:45
  1939.4 56.8 %copy.99 = f32[4,128,16,2048]{3,2,1,0:T(8,128)} copy(f32[4,128,16,2048]{3,1,0,2:T(8,128)} %get-tuple-element.47) | data formatting | bytes 134217728 | tf_op jit(solution)/shard_map/add | solution.py:45
  1996.2 63.6 %multiply_reduce_fusion = (f32[4,2048]{1,0:T(4,128)}, f32[2048,2048]{1,0:T(8,128)}) fusion(f32[2048,2048]{1,0:T(8,128)} %get-tuple-element.143, f32[4,2047,2048]{2,1,0:T(8,128)} %bitcast.467, f32[4,128,16,2048]{3,2,1,0:T(8,128)} %copy.99, f32[2048]{0:T(1024)S(1)} %copy-done.78, f32[4,2048]{1,0:T(4,128)S(1)} %copy-done.45, f32[2048,2048]{1,0:T(8,128)} %copy-done.1, ...), kind=kLoop, calls=%fused_computation.6 | loop fusion | flops 180346880 | bytes 184623104 | tf_op jit(solution)/shard_map/reduce_sum | solution.py:95
  2061.7 17.8 copy.78
  2112.9 100.6 %reduce-scatter.13.cloned.1.call-done = f32[512,2048]{1,0:T(8,128)} async-done(((f32[2048,2048]{1,0:T(8,128)}), f32[512,2048]{1,0:T(8,128)}) %reduce-scatter.13.cloned.1.call-update) | async-done | bytes 4194320 | tf_op jit(solution)/shard_map/reduce_scatter | solution.py:237
  2219.6 21.3 reduce-scatter.15.cloned.1.call-done
  2245.5 152.4 %reduce-scatter.9.cloned.1.call-done = f32[512,2048]{1,0:T(8,128)} async-done(((f32[2048,2048]{1,0:T(8,128)}), f32[512,2048]{1,0:T(8,128)}) %reduce-scatter.9.cloned.1.call-update) | async-done | bytes 4194320 | tf_op jit(solution)/shard_map/reduce_scatter | solution.py:194
  2413.8 141.1 %reduce-scatter.11.cloned.1.call-done = f32[512,2048]{1,0:T(8,128)} async-done(((f32[2048,2048]{1,0:T(8,128)}), f32[512,2048]{1,0:T(8,128)}) %reduce-scatter.11.cloned.1.call-update) | async-done | bytes 4194320 | tf_op jit(solution)/shard_map/reduce_scatter | solution.py:236
  2592.1 29.3 reduce-scatter.19.cloned.1.call-done
  2621.4 90.5 %reduce-scatter.23.cloned.1.call-done = f32[256,1024]{1,0:T(8,128)} async-done(((f32[2048,1024]{1,0:T(8,128)}), f32[256,1024]{1,0:T(8,128)}) %reduce-scatter.23.cloned.1.call-update) | async-done | bytes 1048592 | tf_op jit(solution)/shard_map/reduce_scatter | solution.py:313
  2711.9 168.9 %reduce-scatter.17.cloned.1.call-done = f32[128,4096]{1,0:T(8,128)} async-done(((f32[1024,4096]{1,0:T(8,128)}), f32[128,4096]{1,0:T(8,128)}) %reduce-scatter.17.cloned.1.call-update) | async-done | bytes 2097168 | tf_op jit(solution)/shard_map/reduce_scatter | solution.py:312
  2880.8 27.1 psum.98
  2925.8 40.1 %all-reduce.42 = (f32[1024]{0:T(1024)}, f32[4,2048]{1,0:T(4,128)}, f32[2048]{0:T(1024)}, f32[2048]{0:T(1024)}, f32[2048]{0:T(1024)}, /*index=5*/f32[2048]{0:T(1024)S(1)}, f32[]{:T(128)}, f32[2048]{0:T(1024)S(1)}) all-reduce(f32[1024]{0:T(1024)} %get-tuple-element.27, ...), channel_id=1, replica_groups=mesh['seq'=8,'state'=4] {'seq','state'}, use_global_device_ids=true, to_apply=%region_12.13 | all-reduce | flops 19457 | bytes 155656 | tf_op jit(solution)/shard_map/psum | solution.py:320
  (476 shorter events, 997.9 us)
Async XLA Ops:
  7.2 135.1 %copy-start = (bf16[2048,96]{0,1:T(8,128)(2,1)S(1)}, bf16[2048,96]{0,1:T(8,128)(2,1)}, u32[]{:S(2)}) copy-start(bf16[2048,96]{0,1:T(8,128)(2,1)} %param.20) | copy-start | bytes 1179652
  7.2 104.4 %all-gather.3.cloned.1.call-start = ((), (), s32[]{:S(2)}) async-start(), calls=%async_computation.8 | async-start | bytes 10485760 | tf_op jit(solution)/shard_map/all_gather | solution.py:150
  19.5 92.1 %copy-start.91 = (f32[2048]{0:T(1024)S(1)}, f32[2048]{0:T(1024)}, u32[]{:S(2)}) copy-start(f32[2048]{0:T(1024)} %param.19) | copy-start | bytes 24580
  21.1 728.8 %all-gather.5.cloned.1.call-start = ((), (), s32[]{:S(2)}) async-start(), calls=%async_computation.10 | async-start | bytes 10485760 | tf_op jit(solution)/shard_map/all_gather | solution.py:217
  22.4 221.3 %copy-start.93 = (f32[512]{0:T(512)}, f32[512]{0:T(512)S(1)}, u32[]{:S(2)}) copy-start(f32[512]{0:T(512)S(1)} %fusion.165) | copy-start | bytes 6148
  22.4 150.6 %copy-start.77 = (f32[2048]{0:T(1024)}, f32[2048]{0:T(1024)S(1)}, u32[]{:S(2)}) copy-start(f32[2048]{0:T(1024)S(1)} %compare_convert_fusion) | copy-start | bytes 24580
  23.1 119.1 %copy-start.79 = (f32[1,2048]{1,0:T(1,128)}, f32[1,2048]{1,0:T(1,128)S(1)}, u32[]{:S(2)}) copy-start(f32[1,2048]{1,0:T(1,128)S(1)} %get-tuple-element.191) | copy-start | bytes 24580
  23.1 119.1 %copy-start.81 = (f32[1,2048]{1,0:T(1,128)}, f32[1,2048]{1,0:T(1,128)S(1)}, u32[]{:S(2)}) copy-start(f32[1,2048]{1,0:T(1,128)S(1)} %get-tuple-element.192) | copy-start | bytes 24580
  23.1 119.1 %copy-start.83 = (f32[1,2048]{1,0:T(1,128)}, f32[1,2048]{1,0:T(1,128)S(1)}, u32[]{:S(2)}) copy-start(f32[1,2048]{1,0:T(1,128)S(1)} %get-tuple-element.193) | copy-start | bytes 24580
  23.1 119.1 %copy-start.85 = (f32[1,2048]{1,0:T(1,128)}, f32[1,2048]{1,0:T(1,128)S(1)}, u32[]{:S(2)}) copy-start(f32[1,2048]{1,0:T(1,128)S(1)} %get-tuple-element.194) | copy-start | bytes 24580
  23.2 149.8 %copy-start.43 = (f32[4,2048]{1,0:T(4,128)}, f32[4,2048]{1,0:T(4,128)S(1)}, u32[]{:S(2)}) copy-start(f32[4,2048]{1,0:T(4,128)S(1)} %exponential_negate_fusion) | copy-start | bytes 98308
  256.1 1957.4 %reduce-scatter.13.cloned.1.call-start = ((), (), s32[]{:S(2)}) async-start(), calls=%async_computation.12 | async-start | bytes 20971520 | tf_op jit(solution)/shard_map/reduce_scatter | solution.py:237
  680.0 84.1 %copy-start.51 = (f32[4,128,16]{1,0,2:T(4,128)}, f32[4,128,16]{1,0,2:T(4,128)S(1)}, u32[]{:S(2)}) copy-start(f32[4,128,16]{1,0,2:T(4,128)S(1)} %copy.74) | copy-start | bytes 98308
  976.8 58.3 %copy-start.70 = (f32[4,1,2048]{2,1,0:T(1,128)S(1)}, f32[4,1,2048]{2,1,0:T(1,128)}, u32[]{:S(2)}) copy-start(f32[4,1,2048]{2,1,0:T(1,128)} %get-tuple-element.179) | copy-start | bytes 98308
  976.8 58.3 %copy-start.71 = (f32[4,1,2048]{2,1,0:T(1,128)S(1)}, f32[4,1,2048]{2,1,0:T(1,128)}, u32[]{:S(2)}) copy-start(f32[4,1,2048]{2,1,0:T(1,128)} %get-tuple-element.180) | copy-start | bytes 98308
  976.8 58.5 %copy-start.55 = (f32[4,2,2048]{2,1,0:T(2,128)S(1)}, f32[4,2,2048]{2,1,0:T(2,128)}, u32[]{:S(2)}) copy-start(f32[4,2,2048]{2,1,0:T(2,128)} %pad_add_fusion) | copy-start | bytes 196612
  976.8 58.8 %copy-start.46 = (f32[4,3,2048]{2,1,0:T(4,128)S(1)}, f32[4,3,2048]{2,1,0:T(4,128)}, u32[]{:S(2)}) copy-start(f32[4,3,2048]{2,1,0:T(4,128)} %slice.911) | copy-start | bytes 294916
  976.8 58.8 %copy-start.47 = (f32[4,3,2048]{2,1,0:T(4,128)S(1)}, f32[4,3,2048]{2,1,0:T(4,128)}, u32[]{:S(2)}) copy-start(f32[4,3,2048]{2,1,0:T(4,128)} %slice.928) | copy-start | bytes 294916
  976.8 58.9 %copy-start.67 = (f32[4,1,2048]{2,1,0:T(1,128)S(1)}, f32[4,1,2048]{2,1,0:T(1,128)}, u32[]{:S(2)}) copy-start(f32[4,1,2048]{2,1,0:T(1,128)} %slice.1051) | copy-start | bytes 98308
  976.8 59.7 %copy-start.35 = (f32[4,7,2048]{2,1,0:T(8,128)S(1)}, f32[4,7,2048]{2,1,0:T(8,128)}, u32[]{:S(2)}) copy-start(f32[4,7,2048]{2,1,0:T(8,128)} %slice.905) | copy-start | bytes 688132
  976.8 59.7 %copy-start.36 = (f32[4,7,2048]{2,1,0:T(8,128)S(1)}, f32[4,7,2048]{2,1,0:T(8,128)}, u32[]{:S(2)}) copy-start(f32[4,7,2048]{2,1,0:T(8,128)} %slice.930) | copy-start | bytes 688132
  2059.8 181.0 %reduce-scatter.15.cloned.1.call-start = ((), (), s32[]{:S(2)}) async-start(), calls=%async_computation.13 | async-start | bytes 327680 | tf_op jit(solution)/shard_map/reduce_scatter | solution.py:238
  2061.7 336.2 %reduce-scatter.9.cloned.1.call-start = ((), (), s32[]{:S(2)}) async-start(), calls=%async_computation.9 | async-start | bytes 20971520 | tf_op jit(solution)/shard_map/reduce_scatter | solution.py:194
  2079.6 475.4 %reduce-scatter.11.cloned.1.call-start = ((), (), s32[]{:S(2)}) async-start(), calls=%async_computation.11 | async-start | bytes 20971520 | tf_op jit(solution)/shard_map/reduce_scatter | solution.py:236
  2111.7 480.4 %reduce-scatter.21.cloned.1.call-start = ((), (), s32[]{:S(2)}) async-start(), calls=%async_computation.16 | async-start | bytes 589824 | tf_op jit(solution)/shard_map/reduce_scatter | solution.py:315
  2112.9 128.8 %copy-start.34 = (bf16[2048,64]{0,1:T(8,128)(2,1)S(1)}, bf16[2048,64]{0,1:T(8,128)(2,1)}, u32[]{:S(2)}) copy-start(bf16[2048,64]{0,1:T(8,128)(2,1)} %param.21) | copy-start | bytes 786436
  2218.2 179.7 %copy-start.92 = (f32[2048]{0:T(1024)S(1)}, f32[2048]{0:T(1024)}, u32[]{:S(2)}) copy-start(f32[2048]{0:T(1024)} %param.24) | copy-start | bytes 24580
  2219.5 401.9 %reduce-scatter.19.cloned.1.call-start = ((), (), s32[]{:S(2)}) async-start(), calls=%async_computation.15 | async-start | bytes 884736 | tf_op jit(solution)/shard_map/reduce_scatter | solution.py:314
  2245.4 466.4 %reduce-scatter.23.cloned.1.call-start = ((), (), s32[]{:S(2)}) async-start(), calls=%async_computation.17 | async-start | bytes 9437184 | tf_op jit(solution)/shard_map/reduce_scatter | solution.py:313
  2413.7 467.1 %reduce-scatter.17.cloned.1.call-start = ((), (), s32[]{:S(2)}) async-start(), calls=%async_computation.14 | async-start | bytes 18874368 | tf_op jit(solution)/shard_map/reduce_scatter | solution.py:312
  2566.8 6.1 collective-permute-start
  2587.1 387.2 %all-reduce.41.cloned.1.call-start = ((), (), s32[]{:S(2)}) async-start(), calls=%async_computation.18 | async-start | bytes 6619136 | tf_op jit(solution)/shard_map/psum | solution.py:317
  (75 other events, 820.5 us)
Sparse Core Ops, SparseCore 0:
  21.3 90.2 all-gather.2
  256.3 87.6 all-gather.4
  2060.0 153.5 reduce-scatter.12
  2216.7 24.0 reduce-scatter.14
  2244.1 153.7 reduce-scatter.8
  2401.1 153.7 reduce-scatter.10
  2557.9 30.9 reduce-scatter.20
  2591.7 29.6 reduce-scatter.18
  2623.8 88.0 reduce-scatter.22
  2714.2 166.5 reduce-scatter.16
  2884.6 89.6 all-reduce.40
where the time goes:
time: 3000 us; the launch traced here: 2990 us
  other arithmetic  1060 us (35%)
  local copies, waits for them, and re-layouts  948 us (32%)
  waiting for transfers between devices  800 us (27%)
  matrix products  94.1 us (3%)
  blocking collectives  67.2 us (2%)
    unnamed x25, other arithmetic  370 us
    slice x84, local copies, waits for them, and re-layouts, chain(): lax.associative_scan(combine, (product, running), reverse=reverse, axis=1)  305 us
    slice x1, local copies, waits for them, and re-layouts, chain(): running = factor_in[:, :, moment] * running + source_in[:, :, moment]  183 us
    reduce_scatter x1, waiting for transfers between devices, body(): lax.psum_scatter(grad_in_w, 'seq', scatter_dimension=0, tiled=True)  169 us
    reduce_scatter x1, waiting for transfers between devices, body(): lax.psum_scatter(partial_y, 'state', scatter_dimension=0, tiled=True)  152 us
    reduce_scatter x1, waiting for transfers between devices, body(): lax.psum_scatter(grad_mixed_scan, 'state', scatter_dimension=0, tiled=True)  141 us
    add x2, local copies, waits for them, and re-layouts, chain(): combined = local_part + cum_factor * entering[:, :, None]  113 us
    reduce_sum x1, other arithmetic, scan_backward(): grad_b = jnp.sum(grad_states * (step_size * mixed)[None], axis=2).T  108 us
  transfers between devices with their start and end apart: 12, of which 10 were waited for; matrix products, arithmetic and copies ran while one was open for 21% of the time, Pallas kernels for 0%

commit v1 on v0

v1 whole, which is shorter than its diff:
```python
import functools

import jax
import jax.numpy as jnp
from jax import lax
from jax.experimental import pallas as pl
from jax.experimental.pallas import tpu as pltpu
from jax.sharding import PartitionSpec as P

EPSILON = 1e-05
LOG2E = 1.4426950408889634
LN2 = 0.6931471805599453
F32 = jnp.float32
BF16 = jnp.bfloat16


def swapped(value, distance):
    count = lax.axis_size("state")
    return lax.ppermute(value, "state", [(i, i ^ distance) for i in range(count)])


def shifted(value, axis, steps):
    count = lax.axis_size(axis)
    leading, last = (max(0, -steps), min(count, count - steps))
    return lax.ppermute(value, axis, [(source, source + steps) for source in range(leading, last)])


def rotated(value, axis, steps):
    count = lax.axis_size(axis)
    return lax.ppermute(value, axis, [(i, (i + steps) % count) for i in range(count)])


def gathered(value):
    count = lax.axis_size("state")
    return [value] + [swapped(value, d) for d in range(1, count)]


def column_exchange(value):
    count = lax.axis_size("state")
    me = lax.axis_index("state")
    width = value.shape[1] // count
    pieces = []
    for d in range(count):
        part = lax.dynamic_slice_in_dim(value, (me ^ d) * width, width, 1)
        pieces.append(part if d == 0 else swapped(part, d))
    return pieces


def row_reduce(value):
    count = lax.axis_size("state")
    me = lax.axis_index("state")
    height = value.shape[0] // count
    total = None
    for d in range(count):
        part = lax.dynamic_slice_in_dim(value, (me ^ d) * height, height, 0)
        part = part if d == 0 else swapped(part, d)
        total = part if total is None else total + part
    return total


def seq_rows_reduce(value, send_type):
    count = lax.axis_size("seq")
    me = lax.axis_index("seq")
    height = value.shape[0] // count
    total = lax.dynamic_slice_in_dim(value, me * height, height, 0)
    for r in range(1, count):
        part = lax.dynamic_slice_in_dim(value, lax.rem(me + r, count) * height, height, 0)
        total = total + rotated(part.astype(send_type), "seq", r).astype(F32)
    return total


def seq_sum(value):
    count = lax.axis_size("seq")
    total = value
    for r in range(1, count):
        total = total + rotated(value, "seq", r)
    return total


def channel_rows_reduce(value, send_type):
    seqs = lax.axis_size("seq")
    states = lax.axis_size("state")
    seq = lax.axis_index("seq")
    height = value.shape[0] // seqs
    total = None
    for r in range(seqs):
        pairs = []
        for s in range(seqs):
            for t in range(states):
                chunk = t * seqs + (r + s) % seqs
                pairs.append((s * states + t, (chunk // states) * states + chunk % states))
        part = lax.dynamic_slice_in_dim(value, lax.rem(seq + r, seqs) * height, height, 0)
        got = lax.ppermute(part.astype(send_type), ("seq", "state"), pairs).astype(F32)
        total = got if total is None else total + got
    return total


def placed_rows(value):
    count = lax.axis_size("state")
    me = lax.axis_index("state")
    out = jnp.zeros((count * value.shape[0],) + value.shape[1:], value.dtype)
    for d, piece in enumerate(gathered(value)):
        out = lax.dynamic_update_slice_in_dim(out, piece, (me ^ d) * value.shape[0], 0)
    return out


def placed_columns(value):
    count = lax.axis_size("state")
    me = lax.axis_index("state")
    out = jnp.zeros((value.shape[0], count * value.shape[1]), value.dtype)
    for d, piece in enumerate(gathered(value)):
        out = lax.dynamic_update_slice_in_dim(out, piece, (me ^ d) * value.shape[1], 1)
    return out


def fill_lanes(out_ref, cols_ref, rows):
    groups = 8
    states = cols_ref.shape[0]
    lanes = min(128, rows)

    def step(i, unused):
        tiles = []
        for u in range(groups):
            first = (i * groups + u) * 8
            base = pl.multiple_of((first // lanes) * lanes, lanes)
            tile = cols_ref[:, pl.ds(base, lanes)]
            tiles.append(pltpu.roll(tile, lax.rem(lanes - (first - base), lanes), axis=1))
        for u in range(groups):
            for r in range(8):
                out_ref[(i * groups + u) * 8 + r] = jnp.broadcast_to(
                    tiles[u][:, r : r + 1], (states, 128)
                )
        return 0

    lax.fori_loop(0, rows // (8 * groups), step, 0)


def sums_to_rows(values, sublane):
    step = 1
    while len(values) > 1:
        low = (sublane & step) == 0
        values = [
            jnp.where(low, a, b) + pltpu.roll(jnp.where(low, b, a), step, axis=0)
            for a, b in zip(values[::2], values[1::2])
        ]
        step *= 2
    return values[0]


def spread(ref, row, count):
    return jnp.broadcast_to(ref[pl.ds(row, 1), :], (count, ref.shape[1]))


def widened(value, times):
    return jnp.concatenate([value] * times, axis=1)


def ends_kernel(cols, rate, step, drive, grad_y, state_out, grad_out, lanes):
    rows, width = step.shape
    states = rate.shape[0]
    reps = width // 128

    @pl.when(pl.program_id(0) == 0)
    def _():
        fill_lanes(lanes, cols, rows)

    rates = rate[...]
    groups = rows // 8

    def body(i, carry):
        state, grad = carry
        for r in range(8):
            p = i * 8 + r
            factor = jnp.exp2(rates * spread(step, p, states))
            b_wide = widened(lanes[p, 0:states], reps)
            state = factor * state + spread(drive, p, states) * b_wide
        for r in range(7, -1, -1):
            p = (groups - 1 - i) * 8 + r
            factor = jnp.exp2(rates * spread(step, p, states))
            c_wide = widened(lanes[p, states : 2 * states], reps)
            grad = factor * (grad + spread(grad_y, p, states) * c_wide)
        return state, grad

    zero = jnp.zeros((states, width), F32)
    state, grad = lax.fori_loop(0, groups, body, (zero, zero))
    state_out[...] = state
    grad_out[...] = grad


def scan_kernel(
    cols, rate, step, drive, grad_y, state_in, grad_in,
    y_out, decay_out, source_out, rate_out, b_out, c_out, lanes, held
):
    rows, width = step.shape
    states = rate.shape[0]
    half = states // 2
    reps = width // 128

    @pl.when(pl.program_id(0) == 0)
    def _():
        fill_lanes(lanes, cols, rows)
        b_out[...] = jnp.zeros_like(b_out)
        c_out[...] = jnp.zeros_like(c_out)

    rates = rate[...]
    groups = rows // 8
    sublane = lax.broadcasted_iota(jnp.int32, (8, width), 0)
    held[0] = state_in[...]

    def forward(i, state):
        parts = []
        for r in range(8):
            p = i * 8 + r
            factor = jnp.exp2(rates * spread(step, p, states))
            b_wide = widened(lanes[p, 0:states], reps)
            c_wide = widened(lanes[p, states : 2 * states], reps)
            state = factor * state + spread(drive, p, states) * b_wide
            held[p + 1] = state
            seen = state * c_wide
            parts.append(seen[:half] + seen[half:])
        y_out[pl.ds(pl.multiple_of(i * 8, 8), 8), :] = sums_to_rows(parts, sublane)
        return state

    lax.fori_loop(0, groups, forward, state_in[...])

    def over_tiles(value):
        total = value[:, 0:128]
        for t in range(1, reps):
            total = total + value[:, 128 * t : 128 * t + 128]
        return total

    def backward(k, carry):
        grad_next, rate_sum = carry
        i = groups - 1 - k
        decay_parts = [None] * 8
        source_parts = [None] * 8
        here = held[i * 8 + 8]
        for r in range(7, -1, -1):
            p = i * 8 + r
            step_wide = spread(step, p, states)
            y_wide = spread(grad_y, p, states)
            factor = jnp.exp2(rates * step_wide)
            b_wide = widened(lanes[p, 0:states], reps)
            c_wide = widened(lanes[p, states : 2 * states], reps)
            grad = grad_next + y_wide * c_wide
            before = held[p]
            grad_next = factor * grad
            c_out[p] += over_tiles(here * y_wide)
            b_out[p] += over_tiles(grad * spread(drive, p, states))
            through = grad_next * before
            decay = through * rates
            rate_sum = rate_sum + through * step_wide
            source = grad * b_wide
            decay_parts[r] = decay[:half] + decay[half:]
            source_parts[r] = source[:half] + source[half:]
            here = before
        row = pl.ds(pl.multiple_of(i * 8, 8), 8)
        decay_out[row, :] = sums_to_rows(decay_parts, sublane)
        source_out[row, :] = sums_to_rows(source_parts, sublane)
        return grad_next, rate_sum

    zero = jnp.zeros((states, width), F32)
    unused, rate_sum = lax.fori_loop(0, groups, backward, (grad_in[...], zero))
    rate_out[...] = rate_sum


def block_width(channels):
    return min(512, channels)


def local_ends(cols, rate, step, drive, grad_y):
    rows, channels = step.shape
    states = rate.shape[0]
    width = block_width(channels)
    by_rows = pl.BlockSpec((rows, width), lambda q: (0, q))
    by_state = pl.BlockSpec((states, width), lambda q: (0, q))
    return pl.pallas_call(
        ends_kernel,
        grid=(channels // width,),
        in_specs=[pl.BlockSpec(cols.shape, lambda q: (0, 0)), by_state, by_rows, by_rows, by_rows],
        out_specs=[by_state, by_state],
        out_shape=[jax.ShapeDtypeStruct((states, channels), F32)] * 2,
        scratch_shapes=[pltpu.VMEM((rows, 2 * states, 128), F32)],
        compiler_params=pltpu.CompilerParams(vmem_limit_bytes=60 << 20),
        name="ends",
    )(cols, rate, step, drive, grad_y)


def full_scan(cols, rate, step, drive, grad_y, state_in, grad_in):
    rows, channels = step.shape
    states = rate.shape[0]
    width = block_width(channels)
    by_rows = pl.BlockSpec((rows, width), lambda q: (0, q))
    by_state = pl.BlockSpec((states, width), lambda q: (0, q))
    kept = pl.BlockSpec((rows, states, 128), lambda q: (0, 0, 0))
    return pl.pallas_call(
        scan_kernel,
        grid=(channels // width,),
        in_specs=[
            pl.BlockSpec(cols.shape, lambda q: (0, 0)),
            by_state,
            by_rows,
            by_rows,
            by_rows,
            by_state,
            by_state,
        ],
        out_specs=[by_rows, by_rows, by_rows, by_state, kept, kept],
        out_shape=[jax.ShapeDtypeStruct((rows, channels), F32)] * 3
        + [jax.ShapeDtypeStruct((states, channels), F32)]
        + [jax.ShapeDtypeStruct((rows, states, 128), F32)] * 2,
        scratch_shapes=[
            pltpu.VMEM((rows, 2 * states, 128), F32),
            pltpu.VMEM((rows + 1, states, width), F32),
        ],
        compiler_params=pltpu.CompilerParams(vmem_limit_bytes=63 << 20),
        name="scan",
    )(cols, rate, step, drive, grad_y, state_in, grad_in)


def dot(a, b, dims):
    return lax.dot_general(a, b, ((dims[0], dims[1]), ((), ())), preferred_element_type=F32)


def body(
    tokens,
    lengths,
    grad_out,
    norm_gain,
    in_weight,
    conv_weight,
    conv_bias,
    xproj_weight,
    dtproj_weight,
    dt_bias,
    a_log,
    d_skip,
    out_weight,
):
    rows, width = tokens.shape
    channels = out_weight.shape[0]
    rank = dtproj_weight.shape[1]
    states = (xproj_weight.shape[1] - rank) // 2
    taps = conv_weight.shape[0]
    group = lax.axis_size("state")
    member = lax.axis_index("state")
    position = member * rows + jnp.arange(rows, dtype=jnp.int32)
    alive = (position < lengths[0]).astype(F32)[:, None]

    cotangent = grad_out.astype(F32)
    masked_low = (cotangent * alive).astype(BF16)
    masked_all = gathered(masked_low)
    a_full = placed_rows(a_log)
    inputs = tokens.astype(F32)
    inv_scale = lax.rsqrt(jnp.mean(inputs * inputs, axis=1, keepdims=True) + EPSILON)
    normed = inputs * inv_scale
    normed_low = (normed * norm_gain).astype(BF16)
    normed_all = gathered(normed_low)
    inner = jnp.dot(normed_low, in_weight[:, :channels], preferred_element_type=F32).astype(BF16)
    inner_before = shifted(inner[rows - (taps - 1) :], "state", 1)
    inner_ext = jnp.concatenate([inner_before, inner], axis=0)
    gate_in = jnp.dot(normed_low, in_weight[:, channels:], preferred_element_type=F32)
    gate_sigmoid = jax.nn.sigmoid(gate_in)
    gate_act = gate_in * gate_sigmoid
    grad_gated = dot(masked_low, out_weight, ((1,), (1,)))
    grad_y = grad_gated * gate_act
    grad_y_low = grad_y.astype(BF16)

    conv_pre = conv_bias + conv_weight[taps - 1] * inner
    for s in range(1, taps):
        conv_pre = conv_pre + conv_weight[taps - 1 - s] * inner_ext[taps - 1 - s : taps - 1 - s + rows]
    mixed = jax.nn.silu(conv_pre)
    mixed_low = mixed.astype(BF16)
    projected = jnp.dot(mixed_low, xproj_weight, preferred_element_type=F32)
    rank_low = projected[:, :rank].astype(BF16)
    raised = dot(rank_low, dtproj_weight, ((1,), (1,))) + dt_bias
    step = jax.nn.softplus(raised)
    drive = step * mixed
    cols = projected[:, rank:].T
    rate = -jnp.exp(a_full)
    rate2 = rate * LOG2E

    state_end, grad_end = local_ends(cols, rate2, step, drive, grad_y_low.astype(F32))
    step_sum = jnp.sum(step, axis=0, keepdims=True)
    packed = jnp.concatenate(
        [state_end, grad_end, jnp.broadcast_to(step_sum, (8, channels))], axis=0
    )
    pieces = jnp.stack(gathered(packed))
    state_in = jnp.zeros((states, channels), F32)
    grad_in = jnp.zeros((states, channels), F32)
    for k in range(group):
        one = lax.dynamic_index_in_dim(pieces, member ^ k, 0, keepdims=False)
        passed = one[:states] + jnp.exp2(rate2 * one[2 * states : 2 * states + 1]) * state_in
        state_in = jnp.where(k < member, passed, state_in)
    for k in range(group - 1, -1, -1):
        one = lax.dynamic_index_in_dim(pieces, member ^ k, 0, keepdims=False)
        passed = (
            one[states : 2 * states] + jnp.exp2(rate2 * one[2 * states : 2 * states + 1]) * grad_in
        )
        grad_in = jnp.where(k > member, passed, grad_in)

    summed_y, decay_sum, source_sum, rate_sum, grad_b, grad_c = full_scan(
        cols, rate2, step, drive, grad_y_low.astype(F32), state_in, grad_in
    )

    full_y = summed_y + d_skip * mixed
    gated_low = (full_y * gate_act).astype(BF16)
    branch = jnp.dot(gated_low, out_weight, preferred_element_type=F32)
    output = (inputs + alive * branch).astype(BF16)
    grad_gate_low = (
        grad_gated * full_y * gate_sigmoid * (1.0 + gate_in * (1.0 - gate_sigmoid))
    ).astype(BF16)
    gated_all = column_exchange(gated_low)
    gate_all = column_exchange(grad_gate_low)
    out_part = sum(dot(g, m, ((0,), (0,))) for g, m in zip(gated_all, masked_all))
    gate_part = sum(dot(n, g, ((0,), (0,))) for n, g in zip(normed_all, gate_all))
    grad_out_w = placed_rows(channel_rows_reduce(out_part, BF16))
    gate_w = seq_rows_reduce(gate_part, BF16)

    weighted = alive * step
    grad_step = LN2 * decay_sum + mixed * source_sum
    grad_raised = grad_step * jax.nn.sigmoid(raised)
    raised_low = grad_raised.astype(BF16)
    grad_dtproj = dot(raised_low, rank_low, ((0,), (0,)))
    grad_rank = jnp.dot(raised_low, dtproj_weight, preferred_element_type=F32)
    grad_proj_low = jnp.concatenate(
        [grad_rank, jnp.sum(grad_b, axis=2), jnp.sum(grad_c, axis=2)], axis=1
    ).astype(BF16)
    grad_xproj = dot(mixed_low, grad_proj_low, ((0,), (0,)))
    grad_mixed = (
        step * source_sum + grad_y * d_skip + dot(grad_proj_low, xproj_weight, ((1,), (1,)))
    )
    pre_sigmoid = jax.nn.sigmoid(conv_pre)
    grad_pre = grad_mixed * pre_sigmoid * (1.0 + conv_pre * (1.0 - pre_sigmoid))
    grad_ahead = shifted(grad_pre[: taps - 1], "state", -1)
    grad_ext = jnp.concatenate([grad_pre, grad_ahead], axis=0)
    grad_inner = conv_weight[taps - 1] * grad_pre
    for s in range(1, taps):
        grad_inner = grad_inner + conv_weight[taps - 1 - s] * grad_ext[s : s + rows]
    grad_inner_low = grad_inner.astype(BF16)
    inner_all = column_exchange(grad_inner_low)
    inner_part = sum(dot(n, g, ((0,), (0,))) for n, g in zip(normed_all, inner_all))
    inner_w = seq_rows_reduce(inner_part, BF16)
    grad_in_w = jnp.concatenate([placed_columns(inner_w), placed_columns(gate_w)], axis=1)

    narrow = jnp.concatenate([grad_xproj, grad_dtproj], axis=1)
    narrow = placed_rows(channel_rows_reduce(row_reduce(narrow), F32))
    proj_width = xproj_weight.shape[1]

    vectors = [jnp.sum(grad_pre * inner_ext[k : k + rows].astype(F32), axis=0) for k in range(taps)]
    vectors += [
        jnp.sum(grad_pre, axis=0),
        jnp.sum(grad_raised, axis=0),
        jnp.sum(grad_y * mixed, axis=0),
        jnp.sum(weighted, axis=0),
        jnp.sum(weighted * step, axis=0),
    ]
    small = jnp.concatenate([jnp.stack(vectors), rate_sum * rate], axis=0)
    small = row_reduce(small.reshape(small.shape[0], group, -1).transpose(1, 0, 2).reshape(group * small.shape[0], -1))
    small = placed_columns(seq_sum(small))

    grad_normed = dot(grad_inner_low, in_weight[:, :channels], ((1,), (1,))) + dot(
        grad_gate_low, in_weight[:, channels:], ((1,), (1,))
    )
    grad_gain = jnp.sum(grad_normed * normed, axis=0)
    grad_gain = sum(gathered(seq_sum(grad_gain)))
    scaled = grad_normed * norm_gain
    grad_tokens = cotangent + inv_scale * (
        scaled - normed * jnp.mean(scaled * normed, axis=1, keepdims=True)
    )
    live = seq_sum(lengths[0].astype(F32))
    dt_mean = small[taps + 3] / live
    dt_spread = jnp.sqrt(small[taps + 4] / live - dt_mean * dt_mean + 1e-06)
    grad_a_log = lax.dynamic_slice_in_dim(
        small[taps + 5 :], member * a_log.shape[0], a_log.shape[0], 0
    )
    return (
        output,
        grad_tokens,
        grad_gain,
        grad_in_w,
        small[:taps],
        small[taps],
        narrow[:, :proj_width],
        narrow[:, proj_width:],
        small[taps + 1],
        grad_a_log,
        small[taps + 2],
        grad_out_w,
        dt_mean,
        dt_spread,
    )


def solution(mesh):
    rows = P(("seq", "state"), None)
    return jax.shard_map(
        body,
        mesh=mesh,
        in_specs=(rows, P("seq"), rows) + (P(),) * 7 + (P("state", None), P(), P()),
        out_specs=(rows, rows, P(), P("seq", None), P(), P(), P("seq", None), P("seq", None), P())
        + (P("state", None), P(), P("seq", None), P(), P()),
        check_vma=False,
    )
```

time: 3000 us -> 680 us (0.23)
  other arithmetic: 1060 us -> 46.3 us
  local copies, waits for them, and re-layouts: 948 us -> 38.8 us
  waiting for transfers between devices: 800 us -> 210 us
  starting transfers between devices: 2.92 us -> 196 us
  Pallas kernels: 0 us -> 107 us
  blocking collectives: 67.2 us -> 0 us
    reduce_scatter x8 -> x0, waiting for transfers between devices: 704 us -> none  [the longest x1 169 us: body(): lax.psum_scatter(grad_in_w, 'seq', scatter_dimension=0, tiled=True)]
    slice x93 -> x7, local copies, waits for them, and re-layouts: 580 us -> 1.96 us  [the longest x1 0.65 us: body(): narrow[:, :proj_width]]
    unnamed x25 -> x2, other arithmetic: 370 us -> 0.01 us
    reduce_sum x6 -> x4, other arithmetic: 267 us -> 26.3 us  [the longest x1 12.2 us: body(): jnp.sum(grad_raised, axis=0)]
    ppermute x0 -> x96, waiting for transfers between devices: none -> 207 us  [the longest x45 146 us: swapped(): lax.ppermute(value, 'state', [(i, i ^ distance) for i in range(count)])]
    mul x17 -> x4, other arithmetic: 198 us -> 3.58 us  [the longest x1 2.82 us: body(): drive = step * mixed]
    ppermute x0 -> x96, starting transfers between devices: none -> 190 us  [the longest x35 71.4 us: rotated(): lax.ppermute(value, axis, [(i, (i + steps) % count) for i in range(count)])]
    add x30 -> x7, other arithmetic: 136 us -> 4.25 us  [the longest x2 2.57 us: seq_rows_reduce(): total = total + rotated(part.astype(send_type), 'seq', r).astype(F32)]
  transfers between devices with their start and end apart: 12 -> 98, of which waited for: 10 -> 21; matrix products, arithmetic and copies ran while one was open for 21% -> 12% of each run, Pallas kernels for 0% -> 0%
where the time goes in v1:
time: 680 us; the launch traced here: 676 us
  waiting for transfers between devices  210 us (31%)
  starting transfers between devices  196 us (29%)
  Pallas kernels  107 us (16%)
  matrix products  70.4 us (10%)
  other arithmetic  46.3 us (7%)
  local copies, waits for them, and re-layouts  38.8 us (6%)
  between operations  7.46 us (1%)
    ppermute x45, waiting for transfers between devices, swapped(): lax.ppermute(value, 'state', [(i, i ^ distance) for i in range(count)])  146 us
    pallas_call x1, Pallas kernels, full_scan(): pl.pallas_call(scan_kernel, grid=(channels // width,), in_specs=[pl.Block...  75.6 us
    ppermute x35, starting transfers between devices, rotated(): lax.ppermute(value, axis, [(i, (i + steps) % count) for i in range(count)])  71.4 us
    ppermute x45, starting transfers between devices, swapped(): lax.ppermute(value, 'state', [(i, i ^ distance) for i in range(count)])  69.4 us
    dot_general x19, matrix products, dot(): lax.dot_general(a, b, ((dims[0], dims[1]), ((), ())), preferred_element_t...  55.6 us
    ppermute x16, waiting for transfers between devices, channel_rows_reduce(): lax.ppermute(part.astype(send_type), ('seq', 'state'), pairs).astype(F32)  54.5 us
    ppermute x16, starting transfers between devices, channel_rows_reduce(): lax.ppermute(part.astype(send_type), ('seq', 'state'), pairs).astype(F32)  49.1 us
    pallas_call x1, Pallas kernels, local_ends(): pl.pallas_call(ends_kernel, grid=(channels // width,), in_specs=[pl.Block...  31.1 us
  transfers between devices with their start and end apart: 98, of which 21 were waited for; matrix products, arithmetic and copies ran while one was open for 12% of the time, Pallas kernels for 0%

profile of v1, /device:TPU:0, one launch (start us, length us, event | category | flops | bytes accessed | tf_op | source)
XLA Modules:
  0.0 675.6 jit_solution(9946038398239955591)
XLA Ops:
  9.0 4.9 fusion.32
  24.0 14.6 %multiply_reduce_fusion.1 = (f32[2048]{0:T(1024)}, f32[512,2048]{1,0:T(8,128)S(1)}, f32[512,2048]{1,0:T(8,128)}, f32[512,2048]{1,0:T(8,128)}) fusion(f32[512,2048]{1,0:T(8,128)} %fusion.22, bf16[512,2048]{1,0:T(8,128)(2,1)} %copy-done.21, bf16[3,2048]{1,0:T(4,128)(2,1)S(1)} %collective-permute-done, f32[2048]{0:T(1024)S(1)} %bitcast.154, ...), kind=kOutput, calls=%fused_computation.32 | convolution fusion | flops 2183133184 | bytes 24178688 | tf_op jit(solution)/shard_map/dot_general | solution.py:322
  39.7 5.4 fusion.8
  49.4 31.1 %ends.1 = (f32[16,2048]{1,0:T(8,128)}, f32[16,2048]{1,0:T(8,128)}) custom-call(f32[32,512]{1,0:T(8,128)} %slice_bitcast_fusion.cols, f32[16,2048]{1,0:T(8,128)} %fusion.86.rate, f32[512,2048]{1,0:T(8,128)} %copy-done.2, f32[512,2048]{1,0:T(8,128)} %mul.485.drive, f32[512,2048]{1,0:T(8,128)} %get-tuple-element.51.grad_y), custom_call_target="tpu_custom_call" | custom-call | tf_op jit(solution)/shard_map/ends/pallas_call | solution.py:277
  107.0 75.6 %scan.1 = (f32[512,2048]{1,0:T(8,128)}, f32[512,2048]{1,0:T(8,128)}, f32[512,2048]{1,0:T(8,128)}, f32[16,2048]{1,0:T(8,128)}, f32[512,16,128]{2,1,0:T(8,128)}, /*index=5*/f32[512,16,128]{2,1,0:T(8,128)}) custom-call(f32[32,512]{1,0:T(8,128)} %slice_bitcast_fusion.cols, f32[16,2048]{1,0:T(8,128)} %fusion.86.rate, f32[512,2048]{1,0:T(8,128)} %copy-done.2, ...), custom_call_target="tpu_custom_call" | custom-call | tf_op jit(solution)/shard_map/scan/pallas_call | solution.py:296
  182.7 12.2 %fusion.100 = (f32[2048]{0:T(1024)}, bf16[512,2048]{1,0:T(8,128)(2,1)S(1)}, bf16[512,2048]{1,0:T(8,128)(2,1)S(1)}, bf16[512,2048]{1,0:T(8,128)(2,1)S(1)}) fusion(f32[512,2048]{1,0:T(8,128)} %get-tuple-element.118, f32[2048]{0:T(1024)S(1)} %copy-done.71, f32[512,2048]{1,0:T(8,128)} %copy-done.1, f32[512,2048]{1,0:T(8,128)} %get-tuple-element.25, ...), kind=kLoop, calls=%fused_computation.239 | loop fusion | flops 26212352 | bytes 35676160 | tf_op jit(solution)/shard_map/reduce_sum | solution.py:453
  224.8 10.7 %add_multiply_fusion = f32[512,2048]{1,0:T(8,128)S(1)} fusion(f32[512,2048]{1,0:T(8,128)S(1)} %copy-done.3, f32[512,2048]{1,0:T(8,128)} %get-tuple-element.25, bf16[2048,96]{0,1:T(8,128)(2,1)S(1)} %copy-done, f32[2048]{0:T(1024)S(1)} %copy-done.73, bf16[512,2048]{1,0:T(8,128)(2,1)} %copy-done.21, bf16[3,2048]{1,0:T(4,128)(2,1)S(1)} %copy-done.69, ...), kind=kOutput, calls=%fused_computation.34 | convolution fusion | flops 241467392 | bytes 23621632 | tf_op jit(solution)/shard_map/dot_general | solution.py:322
  241.4 6.1 fusion.5
  247.5 4.5 concatenate.58
  258.7 6.6 fusion.42
  293.2 24.2 %collective-permute-done.15 = f32[1024]{0:T(1024)S(1)} collective-permute-done((f32[1024]{0:T(1024)S(1)}, f32[1024]{0:T(1024)S(1)}, u32[]{:S(2)}, u32[]{:S(2)}) %collective-permute-start.15) | collective-permute-done | bytes 4128 | tf_op jit(solution)/shard_map/ppermute | solution.py:19
  321.5 6.5 collective-permute-done.57
  335.7 6.0 collective-permute-start.64
  347.0 10.4 %collective-permute-start.77 = (bf16[512,1024]{1,0:T(8,128)(2,1)S(1)}, bf16[512,1024]{1,0:T(8,128)(2,1)S(1)}, u32[]{:S(2)}, u32[]{:S(2)}) collective-permute-start(bf16[512,1024]{1,0:T(8,128)(2,1)S(1)} %copy-done.18), channel_id=1, source_target_pairs={{0,2},{1,3},{2,0},{3,1},{4,6},{5,7},{6,4},{7,5},{8,10},{9,11},{10,... | collective-permute-start | bytes 3145736 | tf_op jit(solution)/shard_map/ppermute | solution.py:19
  367.9 12.4 %collective-permute-done.68 = f32[64,160]{0,1:T(8,128)S(1)} collective-permute-done((f32[64,160]{0,1:T(8,128)S(1)}, f32[64,160]{0,1:T(8,128)S(1)}, u32[]{:S(2)}, u32[]{:S(2)}) %collective-permute-start.68) | collective-permute-done | bytes 40992 | tf_op jit(solution)/shard_map/ppermute | solution.py:93
  380.3 18.1 %collective-permute-done.69 = f32[64,160]{0,1:T(8,128)S(1)} collective-permute-done((f32[64,160]{0,1:T(8,128)S(1)}, f32[64,160]{0,1:T(8,128)S(1)}, u32[]{:S(2)}, u32[]{:S(2)}) %collective-permute-start.69) | collective-permute-done | bytes 40992 | tf_op jit(solution)/shard_map/ppermute | solution.py:93
  404.9 5.6 collective-permute-start.18
  411.2 13.0 %collective-permute-done.76 = bf16[512,512]{1,0:T(8,128)(2,1)S(1)} collective-permute-done((bf16[512,512]{1,0:T(8,128)(2,1)S(1)}, bf16[512,512]{1,0:T(8,128)(2,1)S(1)}, u32[]{:S(2)}, u32[]{:S(2)}) %collective-permute-start.76) | collective-permute-done | bytes 524320 | tf_op jit(solution)/shard_map/ppermute | solution.py:19
  427.5 17.9 %collective-permute-done.78 = bf16[512,512]{1,0:T(8,128)(2,1)S(1)} collective-permute-done((bf16[512,512]{1,0:T(8,128)(2,1)S(1)}, bf16[512,512]{1,0:T(8,128)(2,1)S(1)}, u32[]{:S(2)}, u32[]{:S(2)}) %collective-permute-start.78) | collective-permute-done | bytes 524320 | tf_op jit(solution)/shard_map/ppermute | solution.py:19
  449.7 7.4 %collective-permute-done.19 = bf16[512,512]{1,0:T(8,128)(2,1)S(1)} collective-permute-done((bf16[512,512]{1,0:T(8,128)(2,1)S(1)}, bf16[512,512]{1,0:T(8,128)(2,1)S(1)}, u32[]{:S(2)}, u32[]{:S(2)}) %collective-permute-start.19) | collective-permute-done | bytes 524320 | tf_op jit(solution)/shard_map/ppermute | solution.py:19
  459.9 31.0 %collective-permute-done.34 = bf16[512,512]{1,0:T(8,128)(2,1)S(1)} collective-permute-done((bf16[512,512]{1,0:T(8,128)(2,1)S(1)}, bf16[512,512]{1,0:T(8,128)(2,1)S(1)}, u32[]{:S(2)}, u32[]{:S(2)}) %collective-permute-start.34) | collective-permute-done | bytes 524320 | tf_op jit(solution)/shard_map/ppermute | solution.py:19
  493.0 24.7 %collective-permute-done.21 = bf16[512,512]{1,0:T(8,128)(2,1)S(1)} collective-permute-done((bf16[512,512]{1,0:T(8,128)(2,1)S(1)}, bf16[512,512]{1,0:T(8,128)(2,1)S(1)}, u32[]{:S(2)}, u32[]{:S(2)}) %collective-permute-start.21) | collective-permute-done | bytes 524320 | tf_op jit(solution)/shard_map/ppermute | solution.py:19
  523.7 9.4 %collective-permute-done.23 = bf16[512,512]{1,0:T(8,128)(2,1)S(1)} collective-permute-done((bf16[512,512]{1,0:T(8,128)(2,1)S(1)}, bf16[512,512]{1,0:T(8,128)(2,1)S(1)}, u32[]{:S(2)}, u32[]{:S(2)}) %collective-permute-start.23) | collective-permute-done | bytes 524320 | tf_op jit(solution)/shard_map/ppermute | solution.py:19
  534.9 5.9 collective-permute-start.81
  547.2 15.9 %collective-permute-start.26 = (bf16[128,512]{0,1:T(8,128)(2,1)S(1)}, bf16[128,512]{0,1:T(8,128)(2,1)S(1)}, u32[]{:S(2)}, u32[]{:S(2)}) collective-permute-start(bf16[128,512]{0,1:T(8,128)(2,1)S(1)} %get-tuple-element.63), channel_id=1, source_target_pairs={{0,12},{4,16},{8,20},{12,24},{16,28},{20,0},{24,4},{28,8},{1,13},{... | collective-permute-start | bytes 393224 | tf_op jit(solution)/shard_map/ppermute | solution.py:30
  563.3 5.6 collective-permute-start.28
  572.8 5.5 collective-permute-start.38
  601.9 6.9 %collective-permute-start.85 = (bf16[64,1024]{1,0:T(8,128)(2,1)S(1)}, bf16[64,1024]{1,0:T(8,128)(2,1)S(1)}, u32[]{:S(2)}, u32[]{:S(2)}) collective-permute-start(bf16[64,1024]{1,0:T(8,128)(2,1)S(1)} %copy-done.43), channel_id=1, source_target_pairs={{0,5},{1,13},{2,21},{3,29},{4,6},{5,14},{6,22},{7,30},{8,7},{9,15}... | collective-permute-start | bytes 393224 | tf_op jit(solution)/shard_map/ppermute | solution.py:93
  610.8 7.3 %collective-permute-start.87 = (bf16[64,1024]{1,0:T(8,128)(2,1)S(1)}, bf16[64,1024]{1,0:T(8,128)(2,1)S(1)}, u32[]{:S(2)}, u32[]{:S(2)}) collective-permute-start(bf16[64,1024]{1,0:T(8,128)(2,1)S(1)} %copy-done.39), channel_id=1, source_target_pairs={{0,7},{1,15},{2,23},{3,31},{4,0},{5,8},{6,16},{7,24},{8,1},{9,9},{... | collective-permute-start | bytes 393224 | tf_op jit(solution)/shard_map/ppermute | solution.py:93
  620.8 6.3 collective-permute-done.84
  627.1 14.9 %collective-permute-done.85 = bf16[64,1024]{1,0:T(8,128)(2,1)S(1)} collective-permute-done((bf16[64,1024]{1,0:T(8,128)(2,1)S(1)}, bf16[64,1024]{1,0:T(8,128)(2,1)S(1)}, u32[]{:S(2)}, u32[]{:S(2)}) %collective-permute-start.85) | collective-permute-done | bytes 131104 | tf_op jit(solution)/shard_map/ppermute | solution.py:93
  660.9 7.8 %collective-permute-done.46 = f32[128,512]{0,1:T(8,128)} collective-permute-done((f32[128,512]{0,1:T(8,128)S(1)}, f32[128,512]{0,1:T(8,128)}, u32[]{:S(2)}, u32[]{:S(2)}) %collective-permute-start.46) | collective-permute-done | bytes 262176 | tf_op jit(solution)/shard_map/ppermute | solution.py:19
  (444 shorter events, 233.7 us)
Async XLA Ops:
  0.7 48.0 %collective-permute-start.1 = (f32[4,2048]{1,0:T(4,128)}, f32[4,2048]{1,0:T(4,128)S(1)}, u32[]{:S(2)}, u32[]{:S(2)}) collective-permute-start(f32[4,2048]{1,0:T(4,128)} %param.23), channel_id=1, source_target_pairs={{0,1},{1,0},{2,3},{3,2},{4,5},{5,4},{6,7},{7,6},{8,9},{9,8},{10,11... | collective-permute-start | bytes 98312 | tf_op jit(solution)/shard_map/ppermute | solution.py:19
  3.7 45.0 %collective-permute-start.2 = (f32[4,2048]{1,0:T(4,128)}, f32[4,2048]{1,0:T(4,128)S(1)}, u32[]{:S(2)}, u32[]{:S(2)}) collective-permute-start(f32[4,2048]{1,0:T(4,128)} %param.23), channel_id=1, source_target_pairs={{0,2},{1,3},{2,0},{3,1},{4,6},{5,7},{6,4},{7,5},{8,10},{9,11},{10,... | collective-permute-start | bytes 98312 | tf_op jit(solution)/shard_map/ppermute | solution.py:19
  5.2 43.5 %collective-permute-start.3 = (f32[4,2048]{1,0:T(4,128)}, f32[4,2048]{1,0:T(4,128)S(1)}, u32[]{:S(2)}, u32[]{:S(2)}) collective-permute-start(f32[4,2048]{1,0:T(4,128)} %param.23), channel_id=1, source_target_pairs={{0,3},{1,2},{2,1},{3,0},{4,7},{5,6},{6,5},{7,4},{8,11},{9,10},{10,... | collective-permute-start | bytes 98312 | tf_op jit(solution)/shard_map/ppermute | solution.py:19
  81.6 24.3 %collective-permute-start.4 = (f32[40,2048]{1,0:T(8,128)S(1)}, f32[40,2048]{1,0:T(8,128)S(1)}, u32[]{:S(2)}, u32[]{:S(2)}) collective-permute-start(f32[40,2048]{1,0:T(8,128)S(1)} %get-tuple-element.104), channel_id=1, source_target_pairs={{0,1},{1,0},{2,3},{3,2},{4,5},{5,4},{6,7},{7,6},{8,9},{9,8},{10,11... | collective-permute-start | bytes 983048 | tf_op jit(solution)/shard_map/ppermute | solution.py:19
  285.9 124.6 %collective-permute-start.75 = (bf16[512,1024]{1,0:T(8,128)(2,1)S(1)}, bf16[512,1024]{1,0:T(8,128)(2,1)S(1)}, u32[]{:S(2)}, u32[]{:S(2)}) collective-permute-start(bf16[512,1024]{1,0:T(8,128)(2,1)S(1)} %copy-done.18), channel_id=1, source_target_pairs={{0,1},{1,0},{2,3},{3,2},{4,5},{5,4},{6,7},{7,6},{8,9},{9,8},{10,11... | collective-permute-start | bytes 3145736 | tf_op jit(solution)/shard_map/ppermute | solution.py:19
  287.8 41.0 %collective-permute-start.60 = (f32[512,160]{0,1:T(8,128)S(1)}, f32[512,160]{0,1:T(8,128)S(1)}, u32[]{:S(2)}, u32[]{:S(2)}) collective-permute-start(f32[512,160]{0,1:T(8,128)S(1)} %copy-done.33), channel_id=1, source_target_pairs={{0,1},{1,0},{2,3},{3,2},{4,5},{5,4},{6,7},{7,6},{8,9},{9,8},{10,11... | collective-permute-start | bytes 983048 | tf_op jit(solution)/shard_map/ppermute | solution.py:19
  289.6 27.8 %collective-permute-start.15 = (f32[1024]{0:T(1024)S(1)}, f32[1024]{0:T(1024)S(1)}, u32[]{:S(2)}, u32[]{:S(2)}) collective-permute-start(f32[1024]{0:T(1024)S(1)} %add_add_fusion.7), channel_id=1, source_target_pairs={{0,1},{1,0},{2,3},{3,2},{4,5},{5,4},{6,7},{7,6},{8,9},{9,8},{10,11... | collective-permute-start | bytes 12296 | tf_op jit(solution)/shard_map/ppermute | solution.py:19
  289.9 28.5 %collective-permute-start.16 = (f32[1024]{0:T(1024)S(1)}, f32[1024]{0:T(1024)S(1)}, u32[]{:S(2)}, u32[]{:S(2)}) collective-permute-start(f32[1024]{0:T(1024)S(1)} %add_add_fusion.7), channel_id=1, source_target_pairs={{0,2},{1,3},{2,0},{3,1},{4,6},{5,7},{6,4},{7,5},{8,10},{9,11},{10,... | collective-permute-start | bytes 12296 | tf_op jit(solution)/shard_map/ppermute | solution.py:19
  290.9 29.8 %collective-permute-start.17 = (f32[1024]{0:T(1024)S(1)}, f32[1024]{0:T(1024)S(1)}, u32[]{:S(2)}, u32[]{:S(2)}) collective-permute-start(f32[1024]{0:T(1024)S(1)} %add_add_fusion.7), channel_id=1, source_target_pairs={{0,3},{1,2},{2,1},{3,0},{4,7},{5,6},{6,5},{7,4},{8,11},{9,10},{10,... | collective-permute-start | bytes 12296 | tf_op jit(solution)/shard_map/ppermute | solution.py:19
  347.0 79.7 %collective-permute-start.77 = (bf16[512,1024]{1,0:T(8,128)(2,1)S(1)}, bf16[512,1024]{1,0:T(8,128)(2,1)S(1)}, u32[]{:S(2)}, u32[]{:S(2)}) collective-permute-start(bf16[512,1024]{1,0:T(8,128)(2,1)S(1)} %copy-done.18), channel_id=1, source_target_pairs={{0,2},{1,3},{2,0},{3,1},{4,6},{5,7},{6,4},{7,5},{8,10},{9,11},{10,... | collective-permute-start | bytes 3145736 | tf_op jit(solution)/shard_map/ppermute | solution.py:19
  357.4 47.5 %collective-permute-start.74 = (bf16[512,512]{1,0:T(8,128)(2,1)S(1)}, bf16[512,512]{1,0:T(8,128)(2,1)S(1)}, u32[]{:S(2)}, u32[]{:S(2)}) collective-permute-start(bf16[512,512]{1,0:T(8,128)(2,1)S(1)} %copy-done.30), channel_id=1, source_target_pairs={{0,1},{1,0},{2,3},{3,2},{4,5},{5,4},{6,7},{7,6},{8,9},{9,8},{10,11... | collective-permute-start | bytes 1572872 | tf_op jit(solution)/shard_map/ppermute | solution.py:19
  363.7 34.6 %collective-permute-start.69 = (f32[64,160]{0,1:T(8,128)S(1)}, f32[64,160]{0,1:T(8,128)S(1)}, u32[]{:S(2)}, u32[]{:S(2)}) collective-permute-start(f32[64,160]{0,1:T(8,128)S(1)} %get-tuple-element.97), channel_id=1, source_target_pairs={{0,6},{1,14},{2,22},{3,30},{4,7},{5,15},{6,23},{7,31},{8,0},{9,8},... | collective-permute-start | bytes 122888 | tf_op jit(solution)/shard_map/ppermute | solution.py:93
  380.3 68.5 %collective-permute-start.79 = (bf16[512,1024]{1,0:T(8,128)(2,1)S(1)}, bf16[512,1024]{1,0:T(8,128)(2,1)S(1)}, u32[]{:S(2)}, u32[]{:S(2)}) collective-permute-start(bf16[512,1024]{1,0:T(8,128)(2,1)S(1)} %copy-done.18), channel_id=1, source_target_pairs={{0,3},{1,2},{2,1},{3,0},{4,7},{5,6},{6,5},{7,4},{8,11},{9,10},{10,... | collective-permute-start | bytes 3145736 | tf_op jit(solution)/shard_map/ppermute | solution.py:19
  404.9 52.2 %collective-permute-start.18 = (bf16[512,1024]{1,0:T(8,128)(2,1)S(1)}, bf16[512,1024]{1,0:T(8,128)(2,1)S(1)}, u32[]{:S(2)}, u32[]{:S(2)}) collective-permute-start(bf16[512,1024]{1,0:T(8,128)(2,1)S(1)} %copy-done.5), channel_id=1, source_target_pairs={{0,1},{1,0},{2,3},{3,2},{4,5},{5,4},{6,7},{7,6},{8,9},{9,8},{10,11... | collective-permute-start | bytes 3145736 | tf_op jit(solution)/shard_map/ppermute | solution.py:19
  410.5 34.9 %collective-permute-start.78 = (bf16[512,512]{1,0:T(8,128)(2,1)S(1)}, bf16[512,512]{1,0:T(8,128)(2,1)S(1)}, u32[]{:S(2)}, u32[]{:S(2)}) collective-permute-start(bf16[512,512]{1,0:T(8,128)(2,1)S(1)} %copy-done.28), channel_id=1, source_target_pairs={{0,3},{1,2},{2,1},{3,0},{4,7},{5,6},{6,5},{7,4},{8,11},{9,10},{10,... | collective-permute-start | bytes 1572872 | tf_op jit(solution)/shard_map/ppermute | solution.py:19
  424.3 94.1 %collective-permute-start.20 = (bf16[512,1024]{1,0:T(8,128)(2,1)S(1)}, bf16[512,1024]{1,0:T(8,128)(2,1)S(1)}, u32[]{:S(2)}, u32[]{:S(2)}) collective-permute-start(bf16[512,1024]{1,0:T(8,128)(2,1)S(1)} %copy-done.5), channel_id=1, source_target_pairs={{0,2},{1,3},{2,0},{3,1},{4,6},{5,7},{6,4},{7,5},{8,10},{9,11},{10,... | collective-permute-start | bytes 3145736 | tf_op jit(solution)/shard_map/ppermute | solution.py:19
  426.8 30.3 %collective-permute-start.19 = (bf16[512,512]{1,0:T(8,128)(2,1)S(1)}, bf16[512,512]{1,0:T(8,128)(2,1)S(1)}, u32[]{:S(2)}, u32[]{:S(2)}) collective-permute-start(bf16[512,512]{1,0:T(8,128)(2,1)S(1)} %get-tuple-element.65), channel_id=1, source_target_pairs={{0,1},{1,0},{2,3},{3,2},{4,5},{5,4},{6,7},{7,6},{8,9},{9,8},{10,11... | collective-permute-start | bytes 1572872 | tf_op jit(solution)/shard_map/ppermute | solution.py:19
  445.4 88.0 %collective-permute-start.22 = (bf16[512,1024]{1,0:T(8,128)(2,1)S(1)}, bf16[512,1024]{1,0:T(8,128)(2,1)S(1)}, u32[]{:S(2)}, u32[]{:S(2)}) collective-permute-start(bf16[512,1024]{1,0:T(8,128)(2,1)S(1)} %copy-done.5), channel_id=1, source_target_pairs={{0,3},{1,2},{2,1},{3,0},{4,7},{5,6},{6,5},{7,4},{8,11},{9,10},{10,... | collective-permute-start | bytes 3145736 | tf_op jit(solution)/shard_map/ppermute | solution.py:19
  448.8 42.0 %collective-permute-start.34 = (bf16[512,512]{1,0:T(8,128)(2,1)S(1)}, bf16[512,512]{1,0:T(8,128)(2,1)S(1)}, u32[]{:S(2)}, u32[]{:S(2)}) collective-permute-start(bf16[512,512]{1,0:T(8,128)(2,1)S(1)} %copy-done.27), channel_id=1, source_target_pairs={{0,1},{1,0},{2,3},{3,2},{4,5},{5,4},{6,7},{7,6},{8,9},{9,8},{10,11... | collective-permute-start | bytes 1572872 | tf_op jit(solution)/shard_map/ppermute | solution.py:19
  457.1 64.6 %collective-permute-start.35 = (bf16[512,512]{1,0:T(8,128)(2,1)S(1)}, bf16[512,512]{1,0:T(8,128)(2,1)S(1)}, u32[]{:S(2)}, u32[]{:S(2)}) collective-permute-start(bf16[512,512]{1,0:T(8,128)(2,1)S(1)} %copy-done.26), channel_id=1, source_target_pairs={{0,2},{1,3},{2,0},{3,1},{4,6},{5,7},{6,4},{7,5},{8,10},{9,11},{10,... | collective-permute-start | bytes 1572872 | tf_op jit(solution)/shard_map/ppermute | solution.py:19
  457.1 60.6 %collective-permute-start.21 = (bf16[512,512]{1,0:T(8,128)(2,1)S(1)}, bf16[512,512]{1,0:T(8,128)(2,1)S(1)}, u32[]{:S(2)}, u32[]{:S(2)}) collective-permute-start(bf16[512,512]{1,0:T(8,128)(2,1)S(1)} %get-tuple-element.67), channel_id=1, source_target_pairs={{0,2},{1,3},{2,0},{3,1},{4,6},{5,7},{6,4},{7,5},{8,10},{9,11},{10,... | collective-permute-start | bytes 1572872 | tf_op jit(solution)/shard_map/ppermute | solution.py:19
  490.8 44.1 %collective-permute-start.36 = (bf16[512,512]{1,0:T(8,128)(2,1)S(1)}, bf16[512,512]{1,0:T(8,128)(2,1)S(1)}, u32[]{:S(2)}, u32[]{:S(2)}) collective-permute-start(bf16[512,512]{1,0:T(8,128)(2,1)S(1)} %copy-done.25), channel_id=1, source_target_pairs={{0,3},{1,2},{2,1},{3,0},{4,7},{5,6},{6,5},{7,4},{8,11},{9,10},{10,... | collective-permute-start | bytes 1572872 | tf_op jit(solution)/shard_map/ppermute | solution.py:19
  534.9 28.1 %collective-permute-start.81 = (bf16[64,1024]{1,0:T(8,128)(2,1)S(1)}, bf16[64,1024]{1,0:T(8,128)(2,1)S(1)}, u32[]{:S(2)}, u32[]{:S(2)}) collective-permute-start(bf16[64,1024]{1,0:T(8,128)(2,1)S(1)} %get-tuple-element.94), channel_id=1, source_target_pairs={{0,1},{1,9},{2,17},{3,25},{4,2},{5,10},{6,18},{7,26},{8,3},{9,11},... | collective-permute-start | bytes 393224 | tf_op jit(solution)/shard_map/ppermute | solution.py:93
  544.2 24.8 %collective-permute-start.24 = (bf16[128,512]{0,1:T(8,128)(2,1)S(1)}, bf16[128,512]{0,1:T(8,128)(2,1)S(1)}, u32[]{:S(2)}, u32[]{:S(2)}) collective-permute-start(bf16[128,512]{0,1:T(8,128)(2,1)S(1)} %get-tuple-element.58), channel_id=1, source_target_pairs={{0,4},{4,8},{8,12},{12,16},{16,20},{20,24},{24,28},{28,0},{1,5},{5... | collective-permute-start | bytes 393224 | tf_op jit(solution)/shard_map/ppermute | solution.py:30
  545.8 26.6 %collective-permute-start.25 = (bf16[128,512]{0,1:T(8,128)(2,1)S(1)}, bf16[128,512]{0,1:T(8,128)(2,1)S(1)}, u32[]{:S(2)}, u32[]{:S(2)}) collective-permute-start(bf16[128,512]{0,1:T(8,128)(2,1)S(1)} %get-tuple-element.64), channel_id=1, source_target_pairs={{0,8},{4,12},{8,16},{12,20},{16,24},{20,28},{24,0},{28,4},{1,9},{5... | collective-permute-start | bytes 393224 | tf_op jit(solution)/shard_map/ppermute | solution.py:30
  547.2 25.3 %collective-permute-start.26 = (bf16[128,512]{0,1:T(8,128)(2,1)S(1)}, bf16[128,512]{0,1:T(8,128)(2,1)S(1)}, u32[]{:S(2)}, u32[]{:S(2)}) collective-permute-start(bf16[128,512]{0,1:T(8,128)(2,1)S(1)} %get-tuple-element.63), channel_id=1, source_target_pairs={{0,12},{4,16},{8,20},{12,24},{16,28},{20,0},{24,4},{28,8},{1,13},{... | collective-permute-start | bytes 393224 | tf_op jit(solution)/shard_map/ppermute | solution.py:30
  600.7 26.4 %collective-permute-start.84 = (bf16[64,1024]{1,0:T(8,128)(2,1)S(1)}, bf16[64,1024]{1,0:T(8,128)(2,1)S(1)}, u32[]{:S(2)}, u32[]{:S(2)}) collective-permute-start(bf16[64,1024]{1,0:T(8,128)(2,1)S(1)} %copy-done.44), channel_id=1, source_target_pairs={{0,4},{1,12},{2,20},{3,28},{4,5},{5,13},{6,21},{7,29},{8,6},{9,14}... | collective-permute-start | bytes 393224 | tf_op jit(solution)/shard_map/ppermute | solution.py:93
  601.9 40.0 %collective-permute-start.85 = (bf16[64,1024]{1,0:T(8,128)(2,1)S(1)}, bf16[64,1024]{1,0:T(8,128)(2,1)S(1)}, u32[]{:S(2)}, u32[]{:S(2)}) collective-permute-start(bf16[64,1024]{1,0:T(8,128)(2,1)S(1)} %copy-done.43), channel_id=1, source_target_pairs={{0,5},{1,13},{2,21},{3,29},{4,6},{5,14},{6,22},{7,30},{8,7},{9,15}... | collective-permute-start | bytes 393224 | tf_op jit(solution)/shard_map/ppermute | solution.py:93
  608.8 33.1 %collective-permute-start.86 = (bf16[64,1024]{1,0:T(8,128)(2,1)S(1)}, bf16[64,1024]{1,0:T(8,128)(2,1)S(1)}, u32[]{:S(2)}, u32[]{:S(2)}) collective-permute-start(bf16[64,1024]{1,0:T(8,128)(2,1)S(1)} %copy-done.40), channel_id=1, source_target_pairs={{0,6},{1,14},{2,22},{3,30},{4,7},{5,15},{6,23},{7,31},{8,0},{9,8},... | collective-permute-start | bytes 393224 | tf_op jit(solution)/shard_map/ppermute | solution.py:93
  610.8 35.4 %collective-permute-start.87 = (bf16[64,1024]{1,0:T(8,128)(2,1)S(1)}, bf16[64,1024]{1,0:T(8,128)(2,1)S(1)}, u32[]{:S(2)}, u32[]{:S(2)}) collective-permute-start(bf16[64,1024]{1,0:T(8,128)(2,1)S(1)} %copy-done.39), channel_id=1, source_target_pairs={{0,7},{1,15},{2,23},{3,31},{4,0},{5,8},{6,16},{7,24},{8,1},{9,9},{... | collective-permute-start | bytes 393224 | tf_op jit(solution)/shard_map/ppermute | solution.py:93
  619.4 31.5 %collective-permute-start.31 = (f32[128,512]{0,1:T(8,128)S(1)}, f32[128,512]{0,1:T(8,128)S(1)}, u32[]{:S(2)}, u32[]{:S(2)}) collective-permute-start(f32[128,512]{0,1:T(8,128)S(1)} %convert_add_fusion.4), channel_id=1, source_target_pairs={{0,1},{1,0},{2,3},{3,2},{4,5},{5,4},{6,7},{7,6},{8,9},{9,8},{10,11... | collective-permute-start | bytes 786440 | tf_op jit(solution)/shard_map/ppermute | solution.py:19
  627.1 25.6 %collective-permute-start.32 = (f32[128,512]{0,1:T(8,128)S(1)}, f32[128,512]{0,1:T(8,128)}, u32[]{:S(2)}, u32[]{:S(2)}) collective-permute-start(f32[128,512]{0,1:T(8,128)S(1)} %convert_add_fusion.4), channel_id=1, source_target_pairs={{0,2},{1,3},{2,0},{3,1},{4,6},{5,7},{6,4},{7,5},{8,10},{9,11},{10,... | collective-permute-start | bytes 786440 | tf_op jit(solution)/shard_map/ppermute | solution.py:19
  (147 other events, 3180.8 us)

commit v2 on v1

v2 whole, which is shorter than its diff:
```python
import functools

import jax
import jax.numpy as jnp
from jax import lax
from jax.experimental import pallas as pl
from jax.experimental.pallas import tpu as pltpu
from jax.sharding import PartitionSpec as P

EPSILON = 1e-05
LOG2E = 1.4426950408889634
LN2 = 0.6931471805599453
F32 = jnp.float32
BF16 = jnp.bfloat16


def swapped(value, distance):
    count = lax.axis_size("state")
    return lax.ppermute(value, "state", [(i, i ^ distance) for i in range(count)])


def shifted(value, axis, steps):
    count = lax.axis_size(axis)
    leading, last = (max(0, -steps), min(count, count - steps))
    return lax.ppermute(value, axis, [(source, source + steps) for source in range(leading, last)])


def rotated(value, axis, steps):
    count = lax.axis_size(axis)
    return lax.ppermute(value, axis, [(i, (i + steps) % count) for i in range(count)])


def gathered(value):
    count = lax.axis_size("state")
    return [value] + [swapped(value, d) for d in range(1, count)]


def half_of(value, axis, bit):
    return lax.dynamic_index_in_dim(value, bit, axis, keepdims=True)


def halved(value, axis, index_bit, name, distance, send_type):
    mine = half_of(value, axis, index_bit)
    other = half_of(value, axis, 1 - index_bit).astype(send_type)
    count = lax.axis_size(name)
    got = lax.ppermute(other, name, [(i, i ^ distance) for i in range(count)])
    return mine + got.astype(F32)


def seq_scatter(value, send_type):
    seqs = lax.axis_size("seq")
    seq = lax.axis_index("seq")
    bits = seqs.bit_length() - 1
    value = value.reshape((2,) * bits + value.shape[1:])
    for k in range(bits):
        axis = bits - 1 - k
        value = halved(value, axis, (seq >> k) & 1, "seq", 1 << k, F32 if k == 0 else send_type)
    return value.reshape(value.shape[bits:])


def total_scatter(value):
    seqs = lax.axis_size("seq")
    states = lax.axis_size("state")
    seq = lax.axis_index("seq")
    state = lax.axis_index("state")
    seq_bits = seqs.bit_length() - 1
    state_bits = states.bit_length() - 1
    bits = seq_bits + state_bits
    value = value.reshape((2,) * bits + value.shape[1:])
    for name, index, k in (
        [("seq", seq, 0)]
        + [("state", state, k) for k in range(state_bits)]
        + [("seq", seq, k) for k in range(1, seq_bits)]
    ):
        axis = (seq_bits if name == "seq" else bits) - 1 - k
        value = halved(value, axis, (index >> k) & 1, name, 1 << k, F32)
    return value.reshape(value.shape[bits:])


def total_sum(value):
    for name in ("seq", "state"):
        count = lax.axis_size(name)
        for k in range(count.bit_length() - 1):
            value = value + lax.ppermute(value, name, [(i, i ^ (1 << k)) for i in range(count)])
    return value


def to_owner(value):
    seqs = lax.axis_size("seq")
    states = lax.axis_size("state")
    pairs = [(s * states + t, t * seqs + s) for s in range(seqs) for t in range(states)]
    return lax.ppermute(value, ("seq", "state"), pairs)


def placed(pieces, axis):
    me = lax.axis_index("state")
    size = pieces[0].shape[axis]
    shape = list(pieces[0].shape)
    shape[axis] = size * len(pieces)
    out = jnp.zeros(shape, pieces[0].dtype)
    for d, piece in enumerate(pieces):
        out = lax.dynamic_update_slice_in_dim(out, piece, (me ^ d) * size, axis)
    return out


def fill_lanes(out_ref, cols_ref, rows):
    groups = 8
    states = cols_ref.shape[0]
    lanes = min(128, rows)

    def step(i, unused):
        tiles = []
        for u in range(groups):
            first = (i * groups + u) * 8
            base = pl.multiple_of((first // lanes) * lanes, lanes)
            tile = cols_ref[:, pl.ds(base, lanes)]
            tiles.append(pltpu.roll(tile, lax.rem(lanes - (first - base), lanes), axis=1))
        for u in range(groups):
            for r in range(8):
                out_ref[(i * groups + u) * 8 + r] = jnp.broadcast_to(
                    tiles[u][:, r : r + 1], (states, 128)
                )
        return 0

    lax.fori_loop(0, rows // (8 * groups), step, 0)


def sums_to_rows(values, sublane):
    step = 1
    while len(values) > 1:
        low = (sublane & step) == 0
        values = [
            jnp.where(low, a, b) + pltpu.roll(jnp.where(low, b, a), step, axis=0)
            for a, b in zip(values[::2], values[1::2])
        ]
        step *= 2
    return values[0]


def spread(ref, row, count):
    return jnp.broadcast_to(ref[pl.ds(row, 1), :], (count, ref.shape[1]))


def widened(value, times):
    return jnp.concatenate([value] * times, axis=1)


def conv_window(window, weight, bias, rows):
    taps = weight.shape[0]
    total = bias + weight[taps - 1 : taps] * window[8:]
    for s in range(1, taps):
        total = total + weight[taps - 1 - s : taps - s] * window[8 - s : 8 - s + rows]
    return total


def logistic(value):
    return 1.0 / (1.0 + jnp.exp(-value))


def by_eight(value):
    total = value[0:8]
    for k in range(8, value.shape[0], 8):
        total = total + value[k : k + 8]
    return total


def widen_rows(ext, before, inner):
    rows = inner.shape[0]
    ext[0:8] = before[...].astype(F32)

    def move(i, unused):
        at = pl.multiple_of(i * 32, 32)
        ext[pl.ds(at + 8, 32), :] = inner[pl.ds(at, 32), :].astype(F32)
        return 0

    lax.fori_loop(0, rows // 32, move, 0)


def front_kernel(inner, before, conv_w, conv_b, xproj, mixed_out, proj_out, ext, low):
    rows = inner.shape[0]

    @pl.when(pl.program_id(0) == 0)
    def _():
        proj_out[...] = jnp.zeros_like(proj_out)

    widen_rows(ext, before, inner)
    weight = conv_w[...]
    bias = conv_b[...]

    def chunk(i, unused):
        at = pl.multiple_of(i * 32, 32)
        pre = conv_window(ext[pl.ds(at, 40), :], weight, bias, 32)
        mixed = pre * logistic(pre)
        mixed_out[pl.ds(at, 32), :] = mixed
        low[pl.ds(at, 32), :] = mixed.astype(BF16)
        return 0

    lax.fori_loop(0, rows // 32, chunk, 0)
    proj_out[...] += jnp.dot(low[...], xproj[...], preferred_element_type=F32)


def ends_kernel(
    live, proj, dtproj, dt_b, mixed, gate, grad_gated, rate,
    step_out, gy_out, sig_out, stat_out, state_out, grad_out, cols_out, lanes, drive, rank_low,
):
    rows, width = mixed.shape
    states = rate.shape[0]
    rank = dtproj.shape[1]
    reps = width // 128

    @pl.when(pl.program_id(0) == 0)
    def _():
        cols_out[...] = jnp.transpose(proj[...])[rank : rank + 2 * states]
        rank_low[...] = proj[:, :rank].astype(BF16)
        fill_lanes(lanes, cols_out, rows)

    bias = dt_b[...]
    count = min(64, rows)
    zero8 = jnp.zeros((8, width), F32)

    def prepare(i, sums):
        at = pl.ds(pl.multiple_of(i * count, count), count)
        raised = bias + dot(rank_low[at, :], dtproj[...], ((1,), (1,)))
        small = jnp.exp(-jnp.abs(raised))
        step = jnp.maximum(raised, 0.0) + jnp.log1p(small)
        inverse = 1.0 / (1.0 + small)
        step_out[at, :] = step
        sig_out[at, :] = jnp.where(raised >= 0.0, inverse, small * inverse)
        drive[at, :] = step * mixed[at, :]
        value = gate[at, :]
        grad_y = grad_gated[at, :] * (value * logistic(value))
        gy_out[at, :] = grad_y.astype(BF16).astype(F32)
        row = i * count + lax.broadcasted_iota(jnp.int32, (count, width), 0)
        seen = jnp.where(row < live[0], step, 0.0)
        return sums[0] + by_eight(step), sums[1] + by_eight(seen), sums[2] + by_eight(seen * step)

    sums = lax.fori_loop(0, rows // count, prepare, (zero8, zero8, zero8))
    stat_out[...] = zero8
    for k in range(3):
        stat_out[k : k + 1, :] = jnp.sum(sums[k], axis=0, keepdims=True)

    rates = rate[...]
    groups = rows // 8

    def body(i, carry):
        state, grad = carry
        for r in range(8):
            p = i * 8 + r
            factor = jnp.exp2(rates * spread(step_out, p, states))
            b_wide = widened(lanes[p, 0:states], reps)
            state = factor * state + spread(drive, p, states) * b_wide
        for r in range(7, -1, -1):
            p = (groups - 1 - i) * 8 + r
            factor = jnp.exp2(rates * spread(step_out, p, states))
            c_wide = widened(lanes[p, states : 2 * states], reps)
            grad = factor * (grad + spread(gy_out, p, states) * c_wide)
        return state, grad

    zero = jnp.zeros((states, width), F32)
    state, grad = lax.fori_loop(0, groups, body, (zero, zero))
    state_out[...] = state
    grad_out[...] = grad


def scan_kernel(
    order, cols, proj, rate, step, mixed, grad_y, sig, gate, grad_gated, state_in, grad_in, skip, dtproj,
    *rest,
):
    (
        gated_out, gate_out, send_out, mix_out, rate_out, vec_out, dtproj_out, rank_out, bc_out,
        lanes, held, b_sum, c_sum, drive, y_sum, decay_sum, source_sum, raised_low, rank_low,
    ) = rest[-19:]
    rows, width = step.shape
    states = rate.shape[0]
    rank = dtproj.shape[1]
    half = states // 2
    reps = width // 128
    block = pl.program_id(0)

    @pl.when(block == 0)
    def _():
        fill_lanes(lanes, cols, rows)
        rank_low[...] = proj[:, :rank].astype(BF16)
        b_sum[...] = jnp.zeros_like(b_sum)
        c_sum[...] = jnp.zeros_like(c_sum)
        rank_out[...] = jnp.zeros_like(rank_out)

    rates = rate[...]
    groups = rows // 8
    sublane = lax.broadcasted_iota(jnp.int32, (8, width), 0)
    held[0] = state_in[...]

    def forward(i, state):
        parts = []
        row = pl.ds(pl.multiple_of(i * 8, 8), 8)
        drive[row, :] = step[row, :] * mixed[row, :]
        for r in range(8):
            p = i * 8 + r
            factor = jnp.exp2(rates * spread(step, p, states))
            b_wide = widened(lanes[p, 0:states], reps)
            c_wide = widened(lanes[p, states : 2 * states], reps)
            state = factor * state + spread(drive, p, states) * b_wide
            held[p + 1] = state
            seen = state * c_wide
            parts.append(seen[:half] + seen[half:])
        y_sum[row, :] = sums_to_rows(parts, sublane)
        return state

    lax.fori_loop(0, groups, forward, state_in[...])

    def over_tiles(value):
        total = value[:, 0:128]
        for t in range(1, reps):
            total = total + value[:, 128 * t : 128 * t + 128]
        return total

    def backward(k, carry):
        grad_next, rate_sum = carry
        i = groups - 1 - k
        decay_parts = [None] * 8
        source_parts = [None] * 8
        here = held[i * 8 + 8]
        for r in range(7, -1, -1):
            p = i * 8 + r
            step_wide = spread(step, p, states)
            y_wide = spread(grad_y, p, states)
            factor = jnp.exp2(rates * step_wide)
            b_wide = widened(lanes[p, 0:states], reps)
            c_wide = widened(lanes[p, states : 2 * states], reps)
            grad = grad_next + y_wide * c_wide
            before = held[p]
            grad_next = factor * grad
            c_sum[p] += over_tiles(here * y_wide)
            b_sum[p] += over_tiles(grad * spread(drive, p, states))
            through = grad_next * before
            decay = through * rates
            rate_sum = rate_sum + through * step_wide
            source = grad * b_wide
            decay_parts[r] = decay[:half] + decay[half:]
            source_parts[r] = source[:half] + source[half:]
            here = before
        row = pl.ds(pl.multiple_of(i * 8, 8), 8)
        decay_sum[row, :] = sums_to_rows(decay_parts, sublane)
        source_sum[row, :] = sums_to_rows(source_parts, sublane)
        return grad_next, rate_sum

    zero = jnp.zeros((states, width), F32)
    unused, rate_sum = lax.fori_loop(0, groups, backward, (grad_in[...], zero))
    rate_out[...] = rate_sum * (rates * LN2)

    gain = skip[...]
    count = min(32, rows)
    zero8 = jnp.zeros((8, width), F32)

    def finish(i, sums):
        at = pl.ds(pl.multiple_of(i * count, count), count)
        value = gate[at, :]
        mix = mixed[at, :]
        upstream = grad_gated[at, :]
        full_y = y_sum[at, :] + gain * mix
        squash = logistic(value)
        act = value * squash
        gated = (full_y * act).astype(BF16)
        grad_gate = (upstream * full_y * squash * (1.0 + value * (1.0 - squash))).astype(BF16)
        gated_out[at, :] = gated
        gate_out[at, :] = grad_gate
        send_out[0, at, 0:width] = gated
        send_out[0, at, width : 2 * width] = grad_gate
        grad_full = upstream * act
        source = source_sum[at, :]
        grad_raised = (LN2 * decay_sum[at, :] + mix * source) * sig[at, :]
        raised = grad_raised.astype(BF16)
        raised_low[at, :] = raised
        mix_out[at, :] = step[at, :] * source + grad_full * gain
        rank_out[at, :] += jnp.dot(raised, dtproj[...], preferred_element_type=F32)
        return sums[0] + by_eight(grad_raised), sums[1] + by_eight(grad_full * mix)

    sums = lax.fori_loop(0, rows // count, finish, (zero8, zero8))
    vec_out[...] = zero8
    for k in range(2):
        vec_out[k : k + 1, :] = jnp.sum(sums[k], axis=0, keepdims=True)
    dtproj_out[...] = dot(raised_low[...], rank_low[...], ((0,), (0,)))

    @pl.when(block == pl.num_programs(0) - 1)
    def _():
        lane = lax.broadcasted_iota(jnp.int32, (states, 128), 1)

        def tile(j, unused):
            def gather(i, carry):
                b_tile, c_tile = carry
                for r in range(16):
                    p = j * 128 + i * 16 + r
                    here = lane == i * 16 + r
                    b_tile = jnp.where(here, jnp.sum(b_sum[p], axis=1, keepdims=True), b_tile)
                    c_tile = jnp.where(here, jnp.sum(c_sum[p], axis=1, keepdims=True), c_tile)
                return b_tile, c_tile

            zero_tile = jnp.zeros((states, 128), F32)
            b_tile, c_tile = lax.fori_loop(0, 8, gather, (zero_tile, zero_tile))
            at = pl.ds(pl.multiple_of(j * 128, 128), 128)
            bc_out[0:states, at] = b_tile
            bc_out[states : 2 * states, at] = c_tile
            return 0

        lax.fori_loop(0, rows // 128, tile, 0)


def back_kernel(
    order, proj_grad, xproj, mix_grad, inner, before, ahead, conv_w, conv_b,
    inner_out, send_out, vec_out, xproj_out, ext, pre_ext, low,
):
    rows, width = mix_grad.shape
    taps = conv_w.shape[0]
    widen_rows(ext, before, inner)
    weight = conv_w[...]
    bias = conv_b[...]
    pre_ext[rows : rows + 8, :] = ahead[...]
    zero8 = jnp.zeros((8, width), F32)

    def chunk(i, sums):
        at = pl.multiple_of(i * 32, 32)
        window = ext[pl.ds(at, 40), :]
        pre = conv_window(window, weight, bias, 32)
        squash = logistic(pre)
        low[pl.ds(at, 32), :] = (pre * squash).astype(BF16)
        grad_mixed = mix_grad[pl.ds(at, 32), :] + dot(
            proj_grad[pl.ds(at, 32), :], xproj[...], ((1,), (1,))
        )
        grad_pre = grad_mixed * squash * (1.0 + pre * (1.0 - squash))
        pre_ext[pl.ds(at, 32), :] = grad_pre
        added = [sums[taps] + by_eight(grad_pre)]
        for k in range(taps - 1, -1, -1):
            shift = taps - 1 - k
            added.insert(0, sums[k] + by_eight(grad_pre * window[8 - shift : 40 - shift]))
        return tuple(added)

    sums = lax.fori_loop(0, rows // 32, chunk, (zero8,) * (taps + 1))
    vec_out[...] = zero8
    for k in range(taps + 1):
        vec_out[k : k + 1, :] = jnp.sum(sums[k], axis=0, keepdims=True)

    def spread_back(i, unused):
        at = pl.multiple_of(i * 32, 32)
        window = pre_ext[pl.ds(at, 40), :]
        total = weight[taps - 1 : taps] * window[0:32]
        for s in range(1, taps):
            total = total + weight[taps - 1 - s : taps - s] * window[s : s + 32]
        rounded = total.astype(BF16)
        inner_out[pl.ds(at, 32), :] = rounded
        send_out[0, pl.ds(at, 32), :] = rounded
        return 0

    lax.fori_loop(0, rows // 32, spread_back, 0)
    xproj_out[...] = dot(low[...], proj_grad[...], ((0,), (0,)))


def struct(*shape, dtype=F32):
    return jax.ShapeDtypeStruct(shape, dtype)


def whole(shape):
    return pl.BlockSpec(shape, lambda *unused: (0,) * len(shape))


LIMIT = pltpu.CompilerParams(vmem_limit_bytes=63 << 20)


def front(inner, before, conv_weight, conv_bias, xproj, width):
    rows, channels = inner.shape

    def part(height):
        return pl.BlockSpec((height, width), lambda q: (0, q))

    return pl.pallas_call(
        front_kernel,
        grid=(channels // width,),
        in_specs=[
            part(rows), part(8), part(conv_weight.shape[0]), part(1),
            pl.BlockSpec((width, xproj.shape[1]), lambda q: (q, 0)),
        ],
        out_specs=[part(rows), whole((rows, xproj.shape[1]))],
        out_shape=[struct(rows, channels), struct(rows, xproj.shape[1])],
        scratch_shapes=[pltpu.VMEM((rows + 8, width), F32), pltpu.VMEM((rows, width), BF16)],
        compiler_params=LIMIT,
        name="front",
    )(inner, before, conv_weight, conv_bias, xproj)


def local_ends(live, proj, dtproj, dt_bias, mixed, gate, grad_gated, rate, width):
    rows, channels = mixed.shape
    states = rate.shape[0]
    rank = dtproj.shape[1]

    def part(height):
        return pl.BlockSpec((height, width), lambda q: (0, q))

    return pl.pallas_call(
        ends_kernel,
        grid=(channels // width,),
        in_specs=[
            pl.BlockSpec(memory_space=pltpu.SMEM), whole(proj.shape),
            pl.BlockSpec((width, rank), lambda q: (q, 0)), part(1),
            part(rows), part(rows), part(rows), part(states),
        ],
        out_specs=[part(rows)] * 3 + [part(8), part(states), part(states), whole((2 * states, rows))],
        out_shape=[struct(rows, channels)] * 3
        + [struct(8, channels), struct(states, channels), struct(states, channels), struct(2 * states, rows)],
        scratch_shapes=[
            pltpu.VMEM((rows, 2 * states, 128), F32),
            pltpu.VMEM((rows, width), F32),
            pltpu.VMEM((rows, rank), BF16),
        ],
        compiler_params=LIMIT,
        name="ends",
    )(live, proj, dtproj, dt_bias, mixed, gate, grad_gated, rate)


def full_scan(
    order, cols, proj, rate, step, mixed, grad_y, sig, gate, grad_gated, state_in, grad_in, skip, dtproj,
    earlier,
):
    rows, channels = step.shape
    states = rate.shape[0]
    rank = dtproj.shape[1]
    width = channels // lax.axis_size("state")
    blocks = order.shape[0]

    def part(height):
        return pl.BlockSpec((height, width), lambda q, order: (0, order[q]))

    tall = pl.BlockSpec((width, rank), lambda q, order: (order[q], 0))
    rows_f32 = part(rows)
    in_specs = [
        whole(cols.shape), whole(proj.shape), part(states), rows_f32, rows_f32, rows_f32, rows_f32,
        rows_f32, rows_f32, part(states), part(states), part(1), tall,
    ]
    out_specs = [
        part(rows), part(rows), pl.BlockSpec((1, rows, 2 * width), lambda q, order: (q, 0, 0)),
        part(rows), part(states), part(8), tall, whole((rows, rank)), whole((2 * states, rows)),
    ]
    out_shape = [
        struct(rows, channels, dtype=BF16), struct(rows, channels, dtype=BF16),
        struct(blocks, rows, 2 * width, dtype=BF16), struct(rows, channels), struct(states, channels),
        struct(8, channels), struct(channels, rank), struct(rows, rank), struct(2 * states, rows),
    ]
    args = [
        order, cols, proj, rate, step, mixed, grad_y, sig, gate, grad_gated, state_in, grad_in, skip, dtproj,
    ]
    aliases = {}
    for out, value in earlier:
        aliases[len(args)] = out
        args.append(value)
        in_specs.append(pl.BlockSpec(memory_space=pl.ANY))
    block = pltpu.VMEM((rows, width), F32)
    return pl.pallas_call(
        scan_kernel,
        grid_spec=pltpu.PrefetchScalarGridSpec(
            num_scalar_prefetch=1,
            grid=(blocks,),
            in_specs=in_specs,
            out_specs=out_specs,
            scratch_shapes=[
                pltpu.VMEM((rows, 2 * states, 128), F32),
                pltpu.VMEM((rows + 1, states, width), F32),
                pltpu.VMEM((rows, states, 128), F32),
                pltpu.VMEM((rows, states, 128), F32),
                block, block, block, block,
                pltpu.VMEM((rows, width), BF16),
                pltpu.VMEM((rows, rank), BF16),
            ],
        ),
        out_shape=out_shape,
        input_output_aliases=aliases,
        compiler_params=LIMIT,
        name="scan",
    )(*args)


def back(order, proj_grad, xproj, mix_grad, inner, before, ahead, conv_weight, conv_bias):
    rows, channels = mix_grad.shape
    width = channels // lax.axis_size("state")
    blocks = order.shape[0]

    def part(height):
        return pl.BlockSpec((height, width), lambda q, order: (0, order[q]))

    tall = pl.BlockSpec((width, xproj.shape[1]), lambda q, order: (order[q], 0))
    return pl.pallas_call(
        back_kernel,
        grid_spec=pltpu.PrefetchScalarGridSpec(
            num_scalar_prefetch=1,
            grid=(blocks,),
            in_specs=[
                whole(proj_grad.shape), tall, part(rows), part(rows), part(8), part(8),
                part(conv_weight.shape[0]), part(1),
            ],
            out_specs=[
                part(rows), pl.BlockSpec((1, rows, width), lambda q, order: (q, 0, 0)), part(8), tall,
            ],
            scratch_shapes=[
                pltpu.VMEM((rows + 8, width), F32),
                pltpu.VMEM((rows + 8, width), F32),
                pltpu.VMEM((rows, width), BF16),
            ],
        ),
        out_shape=[
            struct(rows, channels, dtype=BF16), struct(blocks, rows, width, dtype=BF16),
            struct(8, channels), struct(channels, xproj.shape[1]),
        ],
        compiler_params=LIMIT,
        name="back",
    )(order, proj_grad, xproj, mix_grad, inner, before, ahead, conv_weight, conv_bias)


def dot(a, b, dims):
    return lax.dot_general(a, b, (dims, ((), ())), preferred_element_type=F32)


def body(
    tokens,
    lengths,
    grad_out,
    norm_gain,
    in_weight,
    conv_weight,
    conv_bias,
    xproj_weight,
    dtproj_weight,
    dt_bias,
    a_log,
    d_skip,
    out_weight,
):
    rows, features = tokens.shape
    channels = out_weight.shape[0]
    rank = dtproj_weight.shape[1]
    proj_width = xproj_weight.shape[1]
    states = (proj_width - rank) // 2
    taps = conv_weight.shape[0]
    group = lax.axis_size("state")
    seqs = lax.axis_size("seq")
    member = lax.axis_index("state")
    width = channels // group
    live_rows = jnp.clip(lengths - member * rows, 0, rows)
    alive = (jnp.arange(rows, dtype=jnp.int32) < live_rows[0]).astype(F32)[:, None]
    conv_row = conv_bias[None]
    xproj = jnp.pad(xproj_weight, ((0, 0), (0, 128 - proj_width)))

    a_full = lax.all_gather(a_log, "state", axis=0, tiled=True)
    rate2 = -jnp.exp(a_full) * LOG2E
    cotangent = grad_out.astype(F32)
    masked_low = (cotangent * alive).astype(BF16)
    masked_all = lax.all_gather(masked_low, "state", axis=0, tiled=True)
    inputs = tokens.astype(F32)
    inv_scale = lax.rsqrt(jnp.mean(inputs * inputs, axis=1, keepdims=True) + EPSILON)
    normed = inputs * inv_scale
    normed_low = (normed * norm_gain).astype(BF16)
    normed_all = lax.all_gather(normed_low, "state", axis=0, tiled=True)
    inner = jnp.dot(normed_low, in_weight[:, :channels], preferred_element_type=F32).astype(BF16)
    before = shifted(inner[rows - 8 :], "state", 1)
    gate_in = jnp.dot(normed_low, in_weight[:, channels:], preferred_element_type=F32)
    grad_gated = dot(masked_low, out_weight, ((1,), (1,)))
    mixed, proj = front(inner, before, conv_weight, conv_row, xproj, width)
    step, grad_y, sig, stats, state_end, grad_end, cols = local_ends(
        live_rows, proj, dtproj_weight, dt_bias[None], mixed, gate_in, grad_gated, rate2, width
    )

    sums_row = stats[0:8]
    pieces = [jnp.concatenate([state_end, sums_row], axis=0)]
    for d in range(1, group):
        chosen = jnp.where(member < (member ^ d), state_end, grad_end)
        pieces.append(swapped(jnp.concatenate([chosen, sums_row], axis=0), d))
    pieces = jnp.stack(pieces)
    state_in = jnp.zeros((states, channels), F32)
    grad_in = jnp.zeros((states, channels), F32)
    for k in range(group - 1):
        one = lax.dynamic_index_in_dim(pieces, member ^ k, 0, keepdims=False)
        passed = one[:states] + jnp.exp2(rate2 * one[states : states + 1]) * state_in
        state_in = jnp.where(k < member, passed, state_in)
    for k in range(group - 1, 0, -1):
        one = lax.dynamic_index_in_dim(pieces, member ^ k, 0, keepdims=False)
        passed = one[:states] + jnp.exp2(rate2 * one[states : states + 1]) * grad_in
        grad_in = jnp.where(k > member, passed, grad_in)

    first = list(range(1, group // 2 + 1))
    second = list(range(group // 2 + 1, group)) + [0]
    call = (cols, proj, rate2, step, mixed, grad_y, sig, gate_in, grad_gated, state_in, grad_in)
    call += (d_skip[None], dtproj_weight)
    one = full_scan(jnp.stack([member ^ d for d in first]), *call, [])
    gates = {d: swapped(one[2][q], d) for q, d in enumerate(first)}
    shared = [(k, one[k]) for k in (0, 1, 3, 4, 5, 6)]
    two = full_scan(jnp.stack([member ^ d for d in second]), *call, shared)
    gates.update({d: swapped(two[2][q], d) if d else two[2][q] for q, d in enumerate(second)})
    gated_low, grad_gate_low, _, mix_grad, grad_a, scan_sums, grad_dtproj, _, _ = two
    grad_rank = one[7] + two[7]
    grad_bc = (one[8] + two[8]).T

    grad_proj = jnp.concatenate(
        [grad_rank, grad_bc, jnp.zeros((rows, 128 - proj_width), F32)], axis=1
    ).astype(BF16)
    window = jnp.concatenate([before, inner[:8]], axis=0).astype(F32)
    head_pre = conv_window(window, conv_weight, conv_row, 8)
    head_squash = jax.nn.sigmoid(head_pre)
    head_mixed = mix_grad[:8] + dot(grad_proj[:8], xproj, ((1,), (1,)))
    head_grad = head_mixed * head_squash * (1.0 + head_pre * (1.0 - head_squash))
    ahead = shifted(head_grad, "state", -1)
    order = jnp.stack([member ^ d for d in range(group)])
    grad_inner_low, inner_sends, conv_sums, grad_xproj = back(
        order, grad_proj, xproj, mix_grad, inner, before, ahead, conv_weight, conv_row
    )
    inners = {d: swapped(inner_sends[d], d) if d else inner_sends[0] for d in range(group)}

    branch = jnp.dot(gated_low, out_weight, preferred_element_type=F32)
    output = (inputs + alive * branch).astype(BF16)

    def rows_of(values, d):
        return lax.dynamic_slice_in_dim(values, (member ^ d) * rows, rows, 0)

    out_part = sum(dot(gates[d][:, :width], rows_of(masked_all, d), ((0,), (0,))) for d in range(group))
    gate_part = sum(dot(rows_of(normed_all, d), gates[d][:, width:], ((0,), (0,))) for d in range(group))
    early = jnp.concatenate([out_part.reshape(seqs, -1), gate_part.reshape(seqs, -1)], axis=1)
    early = seq_scatter(early, BF16)
    half = early.shape[0] // 2
    early_out = to_owner(early[:half].reshape(width // seqs, features))
    grad_out_w = placed(gathered(early_out), 0)
    gate_w = early[half:].reshape(features // seqs, width)

    inner_part = sum(dot(rows_of(normed_all, d), inners[d], ((0,), (0,))) for d in range(group))
    inner_w = seq_scatter(inner_part.reshape(seqs, -1), BF16).reshape(features // seqs, width)
    grad_in_w = jnp.concatenate([placed(gathered(inner_w), 1), placed(gathered(gate_w), 1)], axis=1)

    narrow = jnp.concatenate([grad_xproj[:, :proj_width], grad_dtproj], axis=1)
    narrow = total_scatter(narrow.reshape(seqs * group, -1)).reshape(-1, proj_width + rank)
    narrow = placed(gathered(narrow), 0)

    small = total_sum(jnp.concatenate([grad_a, scan_sums, stats], axis=0))
    dtb, skip_sum = small[states], small[states + 1]
    sum_one, sum_two = small[states + 9], small[states + 10]

    grad_normed = dot(grad_inner_low, in_weight[:, :channels], ((1,), (1,))) + dot(
        grad_gate_low, in_weight[:, channels:], ((1,), (1,))
    )
    gain_part = jnp.sum(grad_normed * normed, axis=0)
    scaled = grad_normed * norm_gain
    grad_tokens = cotangent + inv_scale * (
        scaled - normed * jnp.mean(scaled * normed, axis=1, keepdims=True)
    )
    live_part = jnp.broadcast_to(live_rows.astype(F32), (channels - features,))
    late = jnp.concatenate([conv_sums[: taps + 1], jnp.concatenate([gain_part, live_part])[None]], axis=0)
    late = total_sum(late)
    live_count = late[taps + 1, features]
    dt_mean = sum_one / live_count
    dt_spread = jnp.sqrt(sum_two / live_count - dt_mean * dt_mean + 1e-06)
    grad_a_log = lax.dynamic_slice_in_dim(small, member * a_log.shape[0], a_log.shape[0], 0)
    return (
        output,
        grad_tokens,
        late[taps + 1, :features],
        grad_in_w,
        late[:taps],
        late[taps],
        narrow[:, :proj_width],
        narrow[:, proj_width:],
        dtb,
        grad_a_log,
        skip_sum,
        grad_out_w,
        dt_mean,
        dt_spread,
    )


def solution(mesh):
    rows = P(("seq", "state"), None)
    return jax.shard_map(
        body,
        mesh=mesh,
        in_specs=(rows, P("seq"), rows) + (P(),) * 7 + (P("state", None), P(), P()),
        out_specs=(rows, rows, P(), P("seq", None), P(), P(), P("seq", None), P("seq", None), P())
        + (P("state", None), P(), P("seq", None), P(), P()),
        check_vma=False,
    )
```

time: 680 us -> 509 us (0.75)
  waiting for transfers between devices: 210 us -> 81.7 us
  starting transfers between devices: 196 us -> 75.9 us
  Pallas kernels: 107 us -> 180 us
  other arithmetic: 46.3 us -> 26.6 us
  local copies, waits for them, and re-layouts: 38.8 us -> 56.3 us
  matrix products: 70.4 us -> 55.6 us
  blocking collectives: 0 us -> 9.33 us
  between operations: 7.46 us -> 16.1 us
    ppermute x45 -> x21, waiting for transfers between devices: 146 us -> 22.4 us  [swapped(): lax.ppermute(value, 'state', [(i, i ^ distance) for i in range(count)])]
    ppermute x51 -> x22, starting transfers between devices: 120 us -> 27 us  [the longest x11 15 us: halved(): got = lax.ppermute(other, name, [(i, i ^ distance) for i in range(count)])]
    pallas_call x1 -> x4, Pallas kernels: 75.6 us -> 136 us  [the longest x2 108 us: full_scan(): pl.pallas_call(scan_kernel, grid_spec=pltpu.PrefetchScalarGridSpec(num_sc...]
    ppermute x45 -> x21, starting transfers between devices: 69.4 us -> 42.7 us  [swapped(): lax.ppermute(value, 'state', [(i, i ^ distance) for i in range(count)])]
    reduce_sum x4 -> x0, other arithmetic: 26.3 us -> none  [the longest x1 12.2 us: body(): jnp.sum(grad_raised, axis=0)]
    dot_general x21 -> x16, matrix products: 57.8 us -> 40.3 us  [dot(): return lax.dot_general(a, b, (dims, ((), ())), preferred_element_type=F32)]
    pallas_call x1, Pallas kernels: 31.1 us -> 44 us  [local_ends(): pl.pallas_call(ends_kernel, grid=(channels // width,), in_specs=[pl.Block...]
    unnamed x162 -> x97, local copies, waits for them, and re-layouts: 3.28 us -> 13.4 us
  transfers between devices with their start and end apart: 98 -> 47, of which waited for: 21 -> 12; matrix products, arithmetic and copies ran while one was open for 12% -> 26% of each run, Pallas kernels for 0% -> 36%
where the time goes in v2:
time: 509 us; the launch traced here: 502 us
  Pallas kernels  180 us (35%)
  waiting for transfers between devices  81.7 us (16%)
  starting transfers between devices  75.9 us (15%)
  local copies, waits for them, and re-layouts  56.3 us (11%)
  matrix products  55.6 us (11%)
  other arithmetic  26.6 us (5%)
  between operations  16.1 us (3%)
  blocking collectives  9.33 us (2%)
    pallas_call x2, Pallas kernels, full_scan(): pl.pallas_call(scan_kernel, grid_spec=pltpu.PrefetchScalarGridSpec(num_sc...  108 us
    pallas_call x1, Pallas kernels, local_ends(): pl.pallas_call(ends_kernel, grid=(channels // width,), in_specs=[pl.Block...  44 us
    ppermute x21, starting transfers between devices, swapped(): lax.ppermute(value, 'state', [(i, i ^ distance) for i in range(count)])  42.7 us
    dot_general x16, matrix products, dot(): return lax.dot_general(a, b, (dims, ((), ())), preferred_element_type=F32)  40.3 us
    ppermute x11, waiting for transfers between devices, halved(): got = lax.ppermute(other, name, [(i, i ^ distance) for i in range(count)])  35.4 us
    ppermute x10, waiting for transfers between devices, total_sum(): lax.ppermute(value, name, [(i, i ^ 1 << k) for i in range(count)])  23.8 us
    ppermute x21, waiting for transfers between devices, swapped(): lax.ppermute(value, 'state', [(i, i ^ distance) for i in range(count)])  22.4 us
    pallas_call x1, Pallas kernels, back(): pl.pallas_call(back_kernel, grid_spec=pltpu.PrefetchScalarGridSpec(num_sc...  20.1 us
  transfers between devices with their start and end apart: 47, of which 12 were waited for; matrix products, arithmetic and copies ran while one was open for 26% of the time, Pallas kernels for 36%

profile of v2, /device:TPU:0, one launch (start us, length us, event | category | flops | bytes accessed | tf_op | source)
XLA Modules:
  0.0 501.8 jit_solution(16565619582068207486)
XLA Ops:
  11.7 4.9 fusion.12.inner
  18.0 4.8 collective-permute-start
  22.9 7.1 %fusion.2.gate = f32[512,2048]{1,0:T(8,128)} fusion(bf16[512,1024]{1,0:T(8,128)(2,1)} %copy-done.10, bf16[1024,4096]{1,0:T(8,128)(2,1)} %param.17), kind=kOutput, calls=%fused_computation.2 | convolution fusion | flops 2147483648 | bytes 9437184 | tf_op jit(solution)/shard_map/dot_general | solution.py:661
  30.0 4.3 fusion.100.grad_gated
  34.3 9.3 %all-gather = f32[4,4,2048]{2,1,0:T(4,128)S(1)} all-gather(f32[1,4,2048]{2,1,0:T(4,128)S(1)} %bitcast.110), channel_id=1, replica_groups=mesh['seq'=8,'state'=4] {'state'}, dimensions={0}, use_global_device_ids=true | all-gather | bytes 163840 | tf_op jit(solution)/shard_map/all_gather | solution.py:649
  49.7 8.5 %front.1 = (f32[512,2048]{1,0:T(8,128)}, f32[512,128]{1,0:T(8,128)}) custom-call(bf16[512,2048]{1,0:T(8,128)(2,1)} %copy-done.5, bf16[8,2048]{1,0:T(8,128)(2,1)} %copy-done.28, f32[4,2048]{1,0:T(4,128)} %conv_w.3, f32[1,2048]{1,0:T(1,128)} %bitcast.114, bf16[2048,128]{1,0:T(8,128)(2,1)} %pad.5.xproj), custom_call_target="tpu_custom_call" | custom-call | tf_op jit(solution)/shard_map/front/pallas_call | solution.py:474
  58.2 44.0 %ends.1 = (f32[512,2048]{1,0:T(8,128)}, f32[512,2048]{1,0:T(8,128)}, f32[512,2048]{1,0:T(8,128)}, f32[8,2048]{1,0:T(8,128)}, f32[16,2048]{1,0:T(8,128)}, /*index=5*/f32[16,2048]{1,0:T(8,128)}, f32[32,512]{1,0:T(8,128)}) custom-call(s32[1]{0:T(128)} %min.6.live, f32[512,128]{1,0:T(8,128)} %get-tuple-element.45.proj, bf16[2048,64]{1,0:T(8,128)(2,1)} %copy.62.dtproj, ...), custom_call_target="tpu_custom_call" | custom-call | tf_op jit(solution)/shard_map/ends/pallas_call | solution.py:497
  107.9 9.3 %collective-permute-done.3 = f32[24,2048]{1,0:T(8,128)S(1)} collective-permute-done((f32[24,2048]{1,0:T(8,128)S(1)}, f32[24,2048]{1,0:T(8,128)S(1)}, u32[]{:S(2)}, u32[]{:S(2)}) %collective-permute-start.3) | collective-permute-done | bytes 196640 | tf_op jit(solution)/shard_map/ppermute | solution.py:19
  117.2 6.5 %collective-permute-done.1 = f32[24,2048]{1,0:T(8,128)S(1)} collective-permute-done((f32[24,2048]{1,0:T(8,128)S(1)}, f32[24,2048]{1,0:T(8,128)S(1)}, u32[]{:S(2)}, u32[]{:S(2)}) %collective-permute-start.1) | collective-permute-done | bytes 196640 | tf_op jit(solution)/shard_map/ppermute | solution.py:19
  124.7 53.7 %scan.2 = (bf16[512,2048]{1,0:T(8,128)(2,1)}, bf16[512,2048]{1,0:T(8,128)(2,1)}, bf16[2,512,1024]{2,1,0:T(8,128)(2,1)}, f32[512,2048]{1,0:T(8,128)}, f32[16,2048...) custom-call(s32[2]{0:T(128)} %get-tuple-element.112.order, ...), custom_call_target="tpu_custom_call" | custom-call | tf_op jit(solution)/shard_map/scan/pallas_call | solution.py:555
  178.4 53.9 %scan.3 = (bf16[512,2048]{1,0:T(8,128)(2,1)}, bf16[512,2048]{1,0:T(8,128)(2,1)}, bf16[2,512,1024]{2,1,0:T(8,128)(2,1)}, f32[512,2048]{1,0:T(8,128)}, f32[16,2048...) custom-call(s32[2]{0:T(128)} %get-tuple-element.111.order, ...), custom_call_target="tpu_custom_call", output_to_operand_aliasing={{0}: (14, {}), {1}: (15, {}), {3}: (16, {}), {4}: (17, {}),... | custom-call | tf_op jit(solution)/shard_map/scan/pallas_call | solution.py:555
  241.4 6.1 %fusion = f32[512,1024]{1,0:T(8,128)} fusion(bf16[512,2048]{1,0:T(8,128)(2,1)S(1)} %copy-done.18, bf16[1024,4096]{1,0:T(8,128)(2,1)} %param.17), kind=kOutput, calls=%fused_computation | convolution fusion | flops 2147483648 | bytes 8388608 | tf_op jit(solution)/shard_map/dot_general | solution.py:616
  249.1 3.4 collective-permute-start.21
  253.1 20.1 %back.1 = (bf16[512,2048]{1,0:T(8,128)(2,1)}, bf16[4,512,512]{2,1,0:T(8,128)(2,1)}, f32[8,2048]{1,0:T(8,128)}, f32[2048,128]{1,0:T(8,128)}) custom-call(s32[4]{0:T(128)} %pad_add_fusion.2.order, bf16[512,128]{1,0:T(8,128)(2,1)} %copy-done.25, bf16[2048,128]{1,0:T(8,128)(2,1)} %pad.5.xproj, f32[512,2048]{1,0:T(8,128)} %get-tuple-element.65.mix_grad, ...), custom_call_target="tpu_custom_call" | custom-call | tf_op jit(solution)/shard_map/back/pallas_call | solution.py:588
  273.3 8.4 %fusion.20 = (f32[1024]{0:T(1024)S(1)}, f32[512]{0:T(512)}, f32[512,1024]{1,0:T(8,128)}) fusion(bf16[512,1024]{1,0:T(8,128)(2,1)} %param.13, f32[512]{0:T(512)S(1)} %copy-done.38, f32[1024]{0:T(1024)S(1)} %copy-done.40, f32[512,1024]{1,0:T(8,128)} %fusion, bf16[512,2048]{1,0:T(8,128)(2,1)} %get-tuple-element.66, bf16[1024,4096]{1,0:T(8,128)(2,1)} %param.17), kind=kOutput, calls=%fused_computation.23 | convolution fusion | flops 2151676416 | bytes 11546624 | tf_op jit(solution)/shard_map/dot_general | solution.py:616
  285.5 3.2 slice_bitcast_fusion.2
  294.6 3.3 fusion.22
  300.8 3.3 collective-permute-done.7
  311.6 5.2 %collective-permute-done.38 = f32[32,2048]{1,0:T(8,128)S(1)} collective-permute-done((f32[32,2048]{1,0:T(8,128)S(1)}, f32[32,2048]{1,0:T(8,128)S(1)}, u32[]{:S(2)}, u32[]{:S(2)}) %collective-permute-start.38) | collective-permute-done | bytes 262176 | tf_op jit(solution)/shard_map/ppermute | solution.py:84
  327.4 15.3 %collective-permute-done.40 = f32[32,2048]{1,0:T(8,128)S(1)} collective-permute-done((f32[32,2048]{1,0:T(8,128)S(1)}, f32[32,2048]{1,0:T(8,128)S(1)}, u32[]{:S(2)}, u32[]{:S(2)}) %collective-permute-start.40) | collective-permute-done | bytes 262176 | tf_op jit(solution)/shard_map/ppermute | solution.py:84
  349.4 3.0 collective-permute-start.32
  354.9 2.9 concatenate.50
  357.9 4.6 copy_dynamic-update-slice_fusion.1
  380.2 3.3 reshape_reshape.12
  386.5 3.0 copy_dynamic-update-slice_fusion
  393.2 12.5 %collective-permute-done.14 = bf16[2,1,1,65536]{3,2,1,0:T(2,128)(2,1)S(1)} collective-permute-done((bf16[2,1,1,65536]{3,2,1,0:T(2,128)(2,1)S(1)}, bf16[2,1,1,65536]{3,2,1,0:T(2,128)(2,1)S(1)}, u32[]{:S(2)}, u32[]{:S(2)}) %collective-permute-start.14) | collective-permute-done | bytes 262176 | tf_op jit(solution)/shard_map/ppermute | solution.py:46
  415.7 11.3 %collective-permute-done.15 = bf16[1,1,1,65536]{3,2,1,0:T(2,128)(2,1)S(1)} collective-permute-done((bf16[1,1,1,65536]{3,2,1,0:T(2,128)(2,1)S(1)}, bf16[1,1,1,65536]{3,2,1,0:T(2,128)(2,1)S(1)}, u32[]{:S(2)}, u32[]{:S(2)}) %collective-permute-start.15) | collective-permute-done | bytes 131104 | tf_op jit(solution)/shard_map/ppermute | solution.py:46
  431.4 3.4 collective-permute-start.24
  445.2 11.4 %collective-permute-done.24 = bf16[1,1,1,131072]{3,0,2,1:T(2,128)(2,1)S(1)} collective-permute-done((bf16[1,1,1,131072]{3,0,2,1:T(2,128)(2,1)S(1)}, bf16[1,1,1,131072]{3,0,2,1:T(2,128)(2,1)S(1)}, u32[]{:S(2)}, u32[]{:S(2)}) %collective-permute-start.24) | collective-permute-done | bytes 262176 | tf_op jit(solution)/shard_map/ppermute | solution.py:46
  466.2 7.1 %collective-permute-start.42 = (f32[64,1024]{1,0:T(8,128)S(1)}, f32[64,1024]{1,0:T(8,128)S(1)}, u32[]{:S(2)}, u32[]{:S(2)}) collective-permute-start(f32[64,1024]{1,0:T(8,128)S(1)} %collective-permute-done.41), channel_id=1, source_target_pairs={{0,1},{1,0},{2,3},{3,2},{4,5},{5,4},{6,7},{7,6},{8,9},{9,8},{10,11... | collective-permute-start | bytes 786440 | tf_op jit(solution)/shard_map/ppermute | solution.py:19
  473.4 10.0 %collective-permute-start.43 = (f32[64,1024]{1,0:T(8,128)S(1)}, f32[64,1024]{1,0:T(8,128)S(1)}, u32[]{:S(2)}, u32[]{:S(2)}) collective-permute-start(f32[64,1024]{1,0:T(8,128)S(1)} %collective-permute-done.41), channel_id=1, source_target_pairs={{0,2},{1,3},{2,0},{3,1},{4,6},{5,7},{6,4},{7,5},{8,10},{9,11},{10,... | collective-permute-start | bytes 786440 | tf_op jit(solution)/shard_map/ppermute | solution.py:19
  487.7 5.1 %collective-permute-done.43 = f32[64,1024]{1,0:T(8,128)S(1)} collective-permute-done((f32[64,1024]{1,0:T(8,128)S(1)}, f32[64,1024]{1,0:T(8,128)S(1)}, u32[]{:S(2)}, u32[]{:S(2)}) %collective-permute-start.43) | collective-permute-done | bytes 262176 | tf_op jit(solution)/shard_map/ppermute | solution.py:19
  (296 shorter events, 133.1 us)
Async XLA Ops:
  7.2 337.4 %all-gather.6.cloned.1.call-start = ((), (), s32[]{:S(2)}) async-start(), calls=%async_computation.1 | async-start | bytes 5242880 | tf_op jit(solution)/shard_map/all_gather | solution.py:653
  10.5 352.0 %all-gather.4.cloned.1.call-start = ((), (), s32[]{:S(2)}) async-start(), calls=%async_computation | async-start | bytes 5242880 | tf_op jit(solution)/shard_map/all_gather | solution.py:658
  18.0 31.1 %collective-permute-start = (bf16[8,2048]{1,0:T(8,128)(2,1)S(1)}, bf16[8,2048]{1,0:T(8,128)(2,1)S(1)}, u32[]{:S(2)}, u32[]{:S(2)}) collective-permute-start(bf16[8,2048]{1,0:T(8,128)(2,1)S(1)} %get-tuple-element.88), channel_id=1, source_target_pairs={{0,1},{1,2},{2,3},{4,5},{5,6},{6,7},{8,9},{9,10},{10,11},{12,13},{... | collective-permute-start | bytes 98312 | tf_op jit(solution)/shard_map/ppermute | solution.py:25
  105.8 17.9 %collective-permute-start.1 = (f32[24,2048]{1,0:T(8,128)S(1)}, f32[24,2048]{1,0:T(8,128)S(1)}, u32[]{:S(2)}, u32[]{:S(2)}) collective-permute-start(f32[24,2048]{1,0:T(8,128)S(1)} %get-tuple-element.103), channel_id=1, source_target_pairs={{0,1},{1,0},{2,3},{3,2},{4,5},{5,4},{6,7},{7,6},{8,9},{9,8},{10,11... | collective-permute-start | bytes 589832 | tf_op jit(solution)/shard_map/ppermute | solution.py:19
  106.5 17.2 %collective-permute-start.2 = (f32[24,2048]{1,0:T(8,128)S(1)}, f32[24,2048]{1,0:T(8,128)S(1)}, u32[]{:S(2)}, u32[]{:S(2)}) collective-permute-start(f32[24,2048]{1,0:T(8,128)S(1)} %get-tuple-element.104), channel_id=1, source_target_pairs={{0,2},{1,3},{2,0},{3,1},{4,6},{5,7},{6,4},{7,5},{8,10},{9,11},{10,... | collective-permute-start | bytes 589832 | tf_op jit(solution)/shard_map/ppermute | solution.py:19
  236.1 54.8 %collective-permute-start.36 = (f32[32,2048]{1,0:T(8,128)}, f32[32,2048]{1,0:T(8,128)}, u32[]{:S(2)}, u32[]{:S(2)}) collective-permute-start(f32[32,2048]{1,0:T(8,128)} %constant_dynamic-update-slice_fusion.12), channel_id=1, source_target_pairs={{0,4},{4,0},{8,12},{12,8},{16,20},{20,16},{24,28},{28,24},{1,5},{5... | collective-permute-start | bytes 786440 | tf_op jit(solution)/shard_map/ppermute | solution.py:84
  249.1 104.1 %collective-permute-start.21 = (bf16[512,1024]{1,0:T(8,128)(2,1)}, bf16[512,1024]{1,0:T(8,128)(2,1)}, u32[]{:S(2)}, u32[]{:S(2)}) collective-permute-start(bf16[512,1024]{1,0:T(8,128)(2,1)} %get-tuple-element.83), channel_id=1, source_target_pairs={{0,3},{1,2},{2,1},{3,0},{4,7},{5,6},{6,5},{7,4},{8,11},{9,10},{10,... | collective-permute-start | bytes 3145736 | tf_op jit(solution)/shard_map/ppermute | solution.py:19
  288.7 58.0 %collective-permute-start.20 = (bf16[512,1024]{1,0:T(8,128)(2,1)}, bf16[512,1024]{1,0:T(8,128)(2,1)S(1)}, u32[]{:S(2)}, u32[]{:S(2)}) collective-permute-start(bf16[512,1024]{1,0:T(8,128)(2,1)} %get-tuple-element.86), channel_id=1, source_target_pairs={{0,2},{1,3},{2,0},{3,1},{4,6},{5,7},{6,4},{7,5},{8,10},{9,11},{10,... | collective-permute-start | bytes 3145736 | tf_op jit(solution)/shard_map/ppermute | solution.py:19
  292.0 13.2 %collective-permute-start.37 = (f32[32,2048]{1,0:T(8,128)S(1)}, f32[32,2048]{1,0:T(8,128)S(1)}, u32[]{:S(2)}, u32[]{:S(2)}) collective-permute-start(f32[32,2048]{1,0:T(8,128)S(1)} %add.358), channel_id=1, source_target_pairs={{0,8},{4,12},{8,0},{12,4},{16,24},{20,28},{24,16},{28,20},{1,9},{5... | collective-permute-start | bytes 786440 | tf_op jit(solution)/shard_map/ppermute | solution.py:84
  293.4 13.6 %collective-permute-start.29 = (f32[2,2,1,2,1,10240]{5,4,3,2,1,0:T(1,128)S(1)}, f32[2,2,1,2,1,10240]{5,4,3,2,1,0:T(1,128)S(1)}, u32[]{:S(2)}, u32[]{:S(2)}) collective-permute-start(f32[2,2,1,2,1,10240]{5,4,3,2,1,0:T(1,128)S(1)} %constant_dynamic-slice_fusion.4), channel_id=1, source_target_pairs={{0,1},{1,0},{2,3},{3,2},{4,5},{5,4},{6,7},{7,6},{8,9},{9,8},{10,11... | collective-permute-start | bytes 983048 | tf_op jit(solution)/shard_map/ppermute | solution.py:46
  321.4 28.0 %collective-permute-start.19 = (bf16[512,1024]{1,0:T(8,128)(2,1)}, bf16[512,1024]{1,0:T(8,128)(2,1)S(1)}, u32[]{:S(2)}, u32[]{:S(2)}) collective-permute-start(bf16[512,1024]{1,0:T(8,128)(2,1)} %get-tuple-element.85), channel_id=1, source_target_pairs={{0,1},{1,0},{2,3},{3,2},{4,5},{5,4},{6,7},{7,6},{8,9},{9,8},{10,11... | collective-permute-start | bytes 3145736 | tf_op jit(solution)/shard_map/ppermute | solution.py:19
  325.2 49.3 %collective-permute-start.11 = (bf16[512,512]{1,0:T(8,128)(2,1)}, bf16[512,512]{1,0:T(8,128)(2,1)}, u32[]{:S(2)}, u32[]{:S(2)}) collective-permute-start(bf16[512,512]{1,0:T(8,128)(2,1)} %get-tuple-element.81), channel_id=1, source_target_pairs={{0,2},{1,3},{2,0},{3,1},{4,6},{5,7},{6,4},{7,5},{8,10},{9,11},{10,... | collective-permute-start | bytes 1572872 | tf_op jit(solution)/shard_map/ppermute | solution.py:19
  325.7 17.1 %collective-permute-start.40 = (f32[32,2048]{1,0:T(8,128)S(1)}, f32[32,2048]{1,0:T(8,128)S(1)}, u32[]{:S(2)}, u32[]{:S(2)}) collective-permute-start(f32[32,2048]{1,0:T(8,128)S(1)} %add.361), channel_id=1, source_target_pairs={{0,2},{1,3},{2,0},{3,1},{4,6},{5,7},{6,4},{7,5},{8,10},{9,11},{10,... | collective-permute-start | bytes 786440 | tf_op jit(solution)/shard_map/ppermute | solution.py:84
  342.8 33.8 %collective-permute-start.10 = (bf16[512,512]{1,0:T(8,128)(2,1)}, bf16[512,512]{1,0:T(8,128)(2,1)}, u32[]{:S(2)}, u32[]{:S(2)}) collective-permute-start(bf16[512,512]{1,0:T(8,128)(2,1)} %get-tuple-element.82), channel_id=1, source_target_pairs={{0,1},{1,0},{2,3},{3,2},{4,5},{5,4},{6,7},{7,6},{8,9},{9,8},{10,11... | collective-permute-start | bytes 1572872 | tf_op jit(solution)/shard_map/ppermute | solution.py:19
  346.8 31.6 %collective-permute-start.12 = (bf16[512,512]{1,0:T(8,128)(2,1)}, bf16[512,512]{1,0:T(8,128)(2,1)}, u32[]{:S(2)}, u32[]{:S(2)}) collective-permute-start(bf16[512,512]{1,0:T(8,128)(2,1)} %get-tuple-element.80), channel_id=1, source_target_pairs={{0,3},{1,2},{2,1},{3,0},{4,7},{5,6},{6,5},{7,4},{8,11},{9,10},{10,... | collective-permute-start | bytes 1572872 | tf_op jit(solution)/shard_map/ppermute | solution.py:19
  349.4 61.8 %collective-permute-start.32 = (f32[1,1,1,1,1,10240]{5,4,3,2,1,0:T(1,128)S(1)}, f32[1,1,1,1,1,10240]{5,4,3,2,1,0:T(1,128)}, u32[]{:S(2)}, u32[]{:S(2)}) collective-permute-start(f32[1,1,1,1,1,10240]{5,4,3,2,1,0:T(1,128)S(1)} %constant_dynamic-slice_fusion.1), channel_id=1, source_target_pairs={{0,16},{4,20},{8,24},{12,28},{16,0},{20,4},{24,8},{28,12},{1,17},{... | collective-permute-start | bytes 122888 | tf_op jit(solution)/shard_map/ppermute | solution.py:46
  391.3 14.4 %collective-permute-start.14 = (bf16[2,1,1,65536]{3,2,1,0:T(2,128)(2,1)S(1)}, bf16[2,1,1,65536]{3,2,1,0:T(2,128)(2,1)S(1)}, u32[]{:S(2)}, u32[]{:S(2)}) collective-permute-start(bf16[2,1,1,65536]{3,2,1,0:T(2,128)(2,1)S(1)} %dynamic-slice_convert_fusion.2), channel_id=1, source_target_pairs={{0,8},{4,12},{8,0},{12,4},{16,24},{20,28},{24,16},{28,20},{1,9},{5... | collective-permute-start | bytes 786440 | tf_op jit(solution)/shard_map/ppermute | solution.py:46
  392.9 13.4 %collective-permute-start.22 = (f32[2,2,1,131072]{3,0,2,1:T(2,128)S(1)}, f32[2,2,1,131072]{3,0,2,1:T(2,128)S(1)}, u32[]{:S(2)}, u32[]{:S(2)}) collective-permute-start(f32[2,2,1,131072]{3,0,2,1:T(2,128)S(1)} %constant_dynamic-slice_fusion.6), channel_id=1, source_target_pairs={{0,4},{4,0},{8,12},{12,8},{16,20},{20,16},{24,28},{28,24},{1,5},{5... | collective-permute-start | bytes 6291464 | tf_op jit(solution)/shard_map/ppermute | solution.py:46
  408.6 20.7 %collective-permute-start.23 = (bf16[2,1,1,131072]{3,0,2,1:T(2,128)(2,1)}, bf16[2,1,1,131072]{3,0,2,1:T(2,128)(2,1)}, u32[]{:S(2)}, u32[]{:S(2)}) collective-permute-start(bf16[2,1,1,131072]{3,0,2,1:T(2,128)(2,1)} %dynamic-slice_convert_fusion), channel_id=1, source_target_pairs={{0,8},{4,12},{8,0},{12,4},{16,24},{20,28},{24,16},{28,20},{1,9},{5... | collective-permute-start | bytes 1572872 | tf_op jit(solution)/shard_map/ppermute | solution.py:46
  410.3 16.7 %collective-permute-start.15 = (bf16[1,1,1,65536]{3,2,1,0:T(2,128)(2,1)S(1)}, bf16[1,1,1,65536]{3,2,1,0:T(2,128)(2,1)S(1)}, u32[]{:S(2)}, u32[]{:S(2)}) collective-permute-start(bf16[1,1,1,65536]{3,2,1,0:T(2,128)(2,1)S(1)} %dynamic-slice_convert_fusion.3), channel_id=1, source_target_pairs={{0,16},{4,20},{8,24},{12,28},{16,0},{20,4},{24,8},{28,12},{1,17},{... | collective-permute-start | bytes 393224 | tf_op jit(solution)/shard_map/ppermute | solution.py:46
  412.1 24.3 %collective-permute-start.33 = (f32[64,160]{1,0:T(8,128)S(1)}, f32[64,160]{1,0:T(8,128)}, u32[]{:S(2)}, u32[]{:S(2)}) collective-permute-start(f32[64,160]{1,0:T(8,128)S(1)} %reshape_reshape.15), channel_id=1, source_target_pairs={{0,1},{1,0},{2,3},{3,2},{4,5},{5,4},{6,7},{7,6},{8,9},{9,8},{10,11... | collective-permute-start | bytes 122888 | tf_op jit(solution)/shard_map/ppermute | solution.py:19
  413.6 24.7 %collective-permute-start.34 = (f32[64,160]{1,0:T(8,128)S(1)}, f32[64,160]{1,0:T(8,128)}, u32[]{:S(2)}, u32[]{:S(2)}) collective-permute-start(f32[64,160]{1,0:T(8,128)S(1)} %reshape_reshape.15), channel_id=1, source_target_pairs={{0,2},{1,3},{2,0},{3,1},{4,6},{5,7},{6,4},{7,5},{8,10},{9,11},{10,... | collective-permute-start | bytes 122888 | tf_op jit(solution)/shard_map/ppermute | solution.py:19
  414.4 25.4 %collective-permute-start.35 = (f32[64,160]{1,0:T(8,128)S(1)}, f32[64,160]{1,0:T(8,128)S(1)}, u32[]{:S(2)}, u32[]{:S(2)}) collective-permute-start(f32[64,160]{1,0:T(8,128)S(1)} %reshape_reshape.15), channel_id=1, source_target_pairs={{0,3},{1,2},{2,1},{3,0},{4,7},{5,6},{6,5},{7,4},{8,11},{9,10},{10,... | collective-permute-start | bytes 122888 | tf_op jit(solution)/shard_map/ppermute | solution.py:19
  427.8 16.4 %collective-permute-start.16 = (f32[128,512]{1,0:T(8,128)S(1)}, f32[128,512]{1,0:T(8,128)}, u32[]{:S(2)}, u32[]{:S(2)}) collective-permute-start(f32[128,512]{1,0:T(8,128)S(1)} %reshape_reshape.13), channel_id=1, source_target_pairs={{0,1},{1,0},{2,3},{3,2},{4,5},{5,4},{6,7},{7,6},{8,9},{9,8},{10,11... | collective-permute-start | bytes 786440 | tf_op jit(solution)/shard_map/ppermute | solution.py:19
  431.4 25.2 %collective-permute-start.24 = (bf16[1,1,1,131072]{3,0,2,1:T(2,128)(2,1)S(1)}, bf16[1,1,1,131072]{3,0,2,1:T(2,128)(2,1)S(1)}, u32[]{:S(2)}, u32[]{:S(2)}) collective-permute-start(bf16[1,1,1,131072]{3,0,2,1:T(2,128)(2,1)S(1)} %dynamic-slice_convert_fusion.1), channel_id=1, source_target_pairs={{0,16},{4,20},{8,24},{12,28},{16,0},{20,4},{24,8},{28,12},{1,17},{... | collective-permute-start | bytes 786440 | tf_op jit(solution)/shard_map/ppermute | solution.py:46
  442.0 19.3 %collective-permute-start.17 = (f32[128,512]{1,0:T(8,128)S(1)}, f32[128,512]{1,0:T(8,128)}, u32[]{:S(2)}, u32[]{:S(2)}) collective-permute-start(f32[128,512]{1,0:T(8,128)S(1)} %reshape_reshape.13), channel_id=1, source_target_pairs={{0,2},{1,3},{2,0},{3,1},{4,6},{5,7},{6,4},{7,5},{8,10},{9,11},{10,... | collective-permute-start | bytes 786440 | tf_op jit(solution)/shard_map/ppermute | solution.py:19
  442.8 22.2 %collective-permute-start.18 = (f32[128,512]{1,0:T(8,128)S(1)}, f32[128,512]{1,0:T(8,128)}, u32[]{:S(2)}, u32[]{:S(2)}) collective-permute-start(f32[128,512]{1,0:T(8,128)S(1)} %reshape_reshape.13), channel_id=1, source_target_pairs={{0,3},{1,2},{2,1},{3,0},{4,7},{5,6},{6,5},{7,4},{8,11},{9,10},{10,... | collective-permute-start | bytes 786440 | tf_op jit(solution)/shard_map/ppermute | solution.py:19
  459.5 23.9 %collective-permute-start.25 = (f32[128,512]{1,0:T(8,128)S(1)}, f32[128,512]{1,0:T(8,128)S(1)}, u32[]{:S(2)}, u32[]{:S(2)}) collective-permute-start(f32[128,512]{1,0:T(8,128)S(1)} %reshape.89), channel_id=1, source_target_pairs={{0,1},{1,0},{2,3},{3,2},{4,5},{5,4},{6,7},{7,6},{8,9},{9,8},{10,11... | collective-permute-start | bytes 786440 | tf_op jit(solution)/shard_map/ppermute | solution.py:19
  462.3 21.1 %collective-permute-start.26 = (f32[128,512]{1,0:T(8,128)S(1)}, f32[128,512]{1,0:T(8,128)S(1)}, u32[]{:S(2)}, u32[]{:S(2)}) collective-permute-start(f32[128,512]{1,0:T(8,128)S(1)} %reshape.89), channel_id=1, source_target_pairs={{0,2},{1,3},{2,0},{3,1},{4,6},{5,7},{6,4},{7,5},{8,10},{9,11},{10,... | collective-permute-start | bytes 786440 | tf_op jit(solution)/shard_map/ppermute | solution.py:19
  466.0 17.5 %collective-permute-start.27 = (f32[128,512]{1,0:T(8,128)S(1)}, f32[128,512]{1,0:T(8,128)S(1)}, u32[]{:S(2)}, u32[]{:S(2)}) collective-permute-start(f32[128,512]{1,0:T(8,128)S(1)} %reshape.89), channel_id=1, source_target_pairs={{0,3},{1,2},{2,1},{3,0},{4,7},{5,6},{6,5},{7,4},{8,11},{9,10},{10,... | collective-permute-start | bytes 786440 | tf_op jit(solution)/shard_map/ppermute | solution.py:19
  466.2 21.5 %collective-permute-start.42 = (f32[64,1024]{1,0:T(8,128)S(1)}, f32[64,1024]{1,0:T(8,128)S(1)}, u32[]{:S(2)}, u32[]{:S(2)}) collective-permute-start(f32[64,1024]{1,0:T(8,128)S(1)} %collective-permute-done.41), channel_id=1, source_target_pairs={{0,1},{1,0},{2,3},{3,2},{4,5},{5,4},{6,7},{7,6},{8,9},{9,8},{10,11... | collective-permute-start | bytes 786440 | tf_op jit(solution)/shard_map/ppermute | solution.py:19
  473.4 19.5 %collective-permute-start.43 = (f32[64,1024]{1,0:T(8,128)S(1)}, f32[64,1024]{1,0:T(8,128)S(1)}, u32[]{:S(2)}, u32[]{:S(2)}) collective-permute-start(f32[64,1024]{1,0:T(8,128)S(1)} %collective-permute-done.41), channel_id=1, source_target_pairs={{0,2},{1,3},{2,0},{3,1},{4,6},{5,7},{6,4},{7,5},{8,10},{9,11},{10,... | collective-permute-start | bytes 786440 | tf_op jit(solution)/shard_map/ppermute | solution.py:19
  (61 other events, 690.5 us)
Sparse Core Ops, SparseCore 0:
  10.6 55.6 all-gather.5
  68.8 61.3 all-gather.3

commit v3 on v2

--- a/solution.py
+++ b/solution.py
@@ -35,54 +35,50 @@
     return [value] + [swapped(value, d) for d in range(1, count)]
 
 
-def half_of(value, axis, bit):
-    return lax.dynamic_index_in_dim(value, bit, axis, keepdims=True)
-
-
-def halved(value, axis, index_bit, name, distance, send_type):
-    mine = half_of(value, axis, index_bit)
-    other = half_of(value, axis, 1 - index_bit).astype(send_type)
-    count = lax.axis_size(name)
-    got = lax.ppermute(other, name, [(i, i ^ distance) for i in range(count)])
-    return mine + got.astype(F32)
-
-
-def seq_scatter(value, send_type):
+def two_words(value):
+    high = lax.reduce_precision(value, 8, 7)
+    return jnp.concatenate([high.astype(BF16), (value - high).astype(BF16)], axis=0)
+
+
+def one_word(value):
+    count = value.shape[0] // 2
+    return value[:count].astype(F32) + value[count:].astype(F32)
+
+
+def seq_exchange(value, distance):
+    count = lax.axis_size("seq")
+    return lax.ppermute(value, "seq", [(i, i ^ distance) for i in range(count)])
+
+
+def seq_scatter(mine, other, extra=0, hold=None, behind=None):
     seqs = lax.axis_size("seq")
     seq = lax.axis_index("seq")
-    bits = seqs.bit_length() - 1
-    value = value.reshape((2,) * bits + value.shape[1:])
-    for k in range(bits):
-        axis = bits - 1 - k
-        value = halved(value, axis, (seq >> k) & 1, "seq", 1 << k, F32 if k == 0 else send_type)
-    return value.reshape(value.shape[bits:])
-
-
-def total_scatter(value):
-    seqs = lax.axis_size("seq")
-    states = lax.axis_size("state")
-    seq = lax.axis_index("seq")
-    state = lax.axis_index("state")
-    seq_bits = seqs.bit_length() - 1
-    state_bits = states.bit_length() - 1
-    bits = seq_bits + state_bits
-    value = value.reshape((2,) * bits + value.shape[1:])
-    for name, index, k in (
-        [("seq", seq, 0)]
-        + [("state", state, k) for k in range(state_bits)]
-        + [("seq", seq, k) for k in range(1, seq_bits)]
-    ):
-        axis = (seq_bits if name == "seq" else bits) - 1 - k
-        value = halved(value, axis, (index >> k) & 1, name, 1 << k, F32)
-    return value.reshape(value.shape[bits:])
-
-
-def total_sum(value):
-    for name in ("seq", "state"):
-        count = lax.axis_size(name)
-        for k in range(count.bit_length() - 1):
-            value = value + lax.ppermute(value, name, [(i, i ^ (1 << k)) for i in range(count)])
-    return value
+    width = mine.shape[1]
+    total = mine + seq_exchange(other, 1)
+    if behind is not None:
+        total, behind = lax.optimization_barrier((total, behind))
+    chips = seqs // 2
+    high = (total.shape[0] - extra) // chips
+    total, sums = total[: chips * high], total[chips * high :]
+    k = 1
+    while chips > 1:
+        chips //= 2
+        total = total.reshape(chips, 2, high, width)
+        bit = (seq >> k) & 1
+        kept = lax.dynamic_index_in_dim(total, bit, 1, keepdims=False)
+        away = lax.dynamic_index_in_dim(total, 1 - bit, 1, keepdims=False).astype(BF16)
+        away = away.reshape(chips * high, width)
+        if extra:
+            away = jnp.concatenate([away, two_words(sums)], axis=0)
+        got = seq_exchange(away, 1 << k)
+        total = kept + got[: chips * high].astype(F32).reshape(kept.shape)
+        if extra:
+            sums = sums + one_word(got[chips * high :])
+        k += 1
+    total = total.reshape(high, width)
+    if hold is not None:
+        total, hold = lax.optimization_barrier((total, hold))
+    return total, sums, hold, behind
 
 
 def to_owner(value):
@@ -92,14 +88,15 @@
     return lax.ppermute(value, ("seq", "state"), pairs)
 
 
-def placed(pieces, axis):
+def placed(pieces, axis, out=None, start=0):
     me = lax.axis_index("state")
     size = pieces[0].shape[axis]
-    shape = list(pieces[0].shape)
-    shape[axis] = size * len(pieces)
-    out = jnp.zeros(shape, pieces[0].dtype)
+    if out is None:
+        shape = list(pieces[0].shape)
+        shape[axis] = size * len(pieces)
+        out = jnp.zeros(shape, pieces[0].dtype)
     for d, piece in enumerate(pieces):
-        out = lax.dynamic_update_slice_in_dim(out, piece, (me ^ d) * size, axis)
+        out = lax.dynamic_update_slice_in_dim(out, piece, start + (me ^ d) * size, axis)
     return out
 
 
@@ -263,13 +260,15 @@
 
 
 def scan_kernel(
-    order, cols, proj, rate, step, mixed, grad_y, sig, gate, grad_gated, state_in, grad_in, skip, dtproj,
+    skipped, order, cols, proj, rate, step, mixed, grad_y, sig, gate, grad_gated, state_in, grad_in, skip, dtproj,
     *rest,
 ):
+    rest = rest[skipped:]
+    gated_out, gate_out, mix_out, rate_out, vec_out, dtproj_out, rank_out, bc_out = rest[:8]
+    sends = rest[8:-10]
     (
-        gated_out, gate_out, send_out, mix_out, rate_out, vec_out, dtproj_out, rank_out, bc_out,
-        lanes, held, b_sum, c_sum, drive, y_sum, decay_sum, source_sum, raised_low, rank_low,
-    ) = rest[-19:]
+        lanes, held, b_sum, c_sum, drive, y_sum, decay_sum, source_sum, raised_low, rank_low
+    ) = rest[-10:]
     rows, width = step.shape
     states = rate.shape[0]
     rank = dtproj.shape[1]
@@ -364,8 +363,13 @@
         grad_gate = (upstream * full_y * squash * (1.0 + value * (1.0 - squash))).astype(BF16)
         gated_out[at, :] = gated
         gate_out[at, :] = grad_gate
-        send_out[0, at, 0:width] = gated
-        send_out[0, at, width : 2 * width] = grad_gate
+        for d, send in enumerate(sends):
+
+            @pl.when(block == d)
+            def _(send=send):
+                send[at, 0:width] = gated
+                send[at, width : 2 * width] = grad_gate
+
         grad_full = upstream * act
         source = source_sum[at, :]
         grad_raised = (LN2 * decay_sum[at, :] + mix * source) * sig[at, :]
@@ -406,11 +410,14 @@
 
 
 def back_kernel(
-    order, proj_grad, xproj, mix_grad, inner, before, ahead, conv_w, conv_b,
-    inner_out, send_out, vec_out, xproj_out, ext, pre_ext, low,
+    order, proj_grad, xproj, mix_grad, inner, before, ahead, conv_w, conv_b, rate_sums, scan_sums, step_sums,
+    dtproj_grad, inner_out, thin_out, *rest,
 ):
+    sends, (ext, pre_ext, low) = rest[:-3], rest[-3:]
     rows, width = mix_grad.shape
     taps = conv_w.shape[0]
+    states = rate_sums.shape[0]
+    block = pl.program_id(0)
     widen_rows(ext, before, inner)
     weight = conv_w[...]
     bias = conv_b[...]
@@ -435,9 +442,35 @@
         return tuple(added)
 
     sums = lax.fori_loop(0, rows // 32, chunk, (zero8,) * (taps + 1))
-    vec_out[...] = zero8
-    for k in range(taps + 1):
-        vec_out[k : k + 1, :] = jnp.sum(sums[k], axis=0, keepdims=True)
+
+    summed = jnp.concatenate(
+        [rate_sums[...], scan_sums[0:2, :], step_sums[1:3, :]]
+        + [jnp.sum(v, axis=0, keepdims=True) for v in sums]
+        + [jnp.zeros((32 - states - 5 - taps, width), F32)],
+        axis=0,
+    )
+    high = summed.astype(BF16)
+    words = jnp.concatenate([high, (summed - high.astype(F32)).astype(BF16)], axis=0)
+
+    xproj_grad = dot(low[...], proj_grad[...], ((0,), (0,)))
+    xproj_grad = xproj_grad.astype(BF16)
+    step_grad = dtproj_grad[...].astype(BF16)
+    group, entries, thin, _ = thin_out.shape
+    seqs = width // thin
+    side = seqs // (entries - seqs)
+    me = order[group - 1]
+    for c in range(seqs):
+        chunk_index = order[block] * seqs + c
+        place = lax.rem(chunk_index, group) ^ me
+        thin_out[place, chunk_index // group] = xproj_grad[c * thin : (c + 1) * thin]
+    for c in range(0, seqs, side * group):
+        for t in range(group):
+            parts = [
+                step_grad[(c + k * group + t) * thin : (c + k * group + t + 1) * thin] for k in range(side)
+            ]
+            parts += [jnp.zeros_like(parts[0])] * (2 - side)
+            at = (order[block] * seqs + c) // (group * side)
+            thin_out[t ^ me, seqs + at] = jnp.concatenate(parts, axis=1)
 
     def spread_back(i, unused):
         at = pl.multiple_of(i * 32, 32)
@@ -447,11 +480,185 @@
             total = total + weight[taps - 1 - s : taps - s] * window[s : s + 32]
         rounded = total.astype(BF16)
         inner_out[pl.ds(at, 32), :] = rounded
-        send_out[0, pl.ds(at, 32), :] = rounded
+        for d, send in enumerate(sends):
+
+            @pl.when(block == d)
+            def _(send=send):
+                send[pl.ds(at, 32), :] = rounded
+
         return 0
 
     lax.fori_loop(0, rows // 32, spread_back, 0)
-    xproj_out[...] = dot(low[...], proj_grad[...], ((0,), (0,)))
+    for d, send in enumerate(sends):
+
+        @pl.when(block == d)
+        def _(send=send):
+            send[rows : rows + 64, :] = words
+
+
+def put_chunks(targets, total, core, step, entry, high, first_row, fold):
+    width = targets[0].shape[1]
+    rows = high // fold
+    each = total.shape[0] // rows
+    for c in range(each):
+        first = pl.multiple_of((step * each + c) // 2 * entry, 8) + first_row
+        for parity in range(2):
+
+            @pl.when(lax.rem(core + c, 2) == parity)
+            def _(parity=parity, first=first, c=c):
+                for f in range(fold):
+                    targets[parity][pl.ds(first + f * rows, rows), :] = total[
+                        c * rows : (c + 1) * rows, f * width : (f + 1) * width
+                    ]
+
+
+def summed_products(lefts, rights):
+    total = None
+    for left, right in zip(lefts, rights):
+        part = dot(left, right, ((0,), (0,)))
+        total = part if total is None else total + part
+    return total
+
+
+def wide_kernel(high, at, *refs):
+    count = (len(refs) - 2) // 4
+    outs, gates, masked, normed = (refs[k * count : (k + 1) * count] for k in range(4))
+    targets = refs[-2:]
+    width = targets[0].shape[1]
+    total = summed_products([r[...] for r in outs], [r[...] for r in masked])
+    fold = masked[0].shape[1] // width
+    step = pl.program_id(0)
+    put_chunks(targets, total, at[0], step, 2 * high, high, 0, fold)
+    total = summed_products([r[...] for r in normed], [r[...] for r in gates])
+    put_chunks(targets, total, at[0], step, 2 * high, high, high, 1)
+
+
+def inner_kernel(total_chunks, at, *refs):
+    count = (len(refs) - 4) // 3
+    normed, inners, thins = (refs[k * count : (k + 1) * count] for k in range(3))
+    gain, live = refs[3 * count : 3 * count + 2]
+    targets = refs[-2:]
+    core = at[0]
+    rows = normed[0].shape[0]
+    width = inners[0].shape[1]
+    entries, thin, _ = thins[0].shape
+    columns = 256
+    seqs = total_chunks
+    side = seqs // (entries - seqs)
+    chips = seqs // 2
+    extra = 48 if gain.shape[0] <= 8 else 0
+    entry = (targets[0].shape[0] - extra) // chips
+    packed = thin * columns // width
+    high = entry - packed
+    step = pl.program_id(0)
+    total = summed_products([r[...] for r in normed], [r[0:rows, :] for r in inners])
+    each = total.shape[0] // high
+    for c in range(each):
+        first = pl.multiple_of((step * each + c) // 2 * entry, 8)
+        for parity in range(2):
+
+            @pl.when(lax.rem(core + c, 2) == parity)
+            def _(parity=parity, first=first, c=c):
+                targets[parity][pl.ds(first, high), :] = total[c * high : (c + 1) * high]
+
+    @pl.when(step == 0)
+    def _():
+        for i in range(seqs):
+            value = thins[0][i].astype(F32)
+            near = thins[0][seqs + i // side].astype(F32)
+            for r in thins[1:]:
+                value = value + r[i].astype(F32)
+                near = near + r[seqs + i // side].astype(F32)
+            at_lane = (i % side) * 64
+            near = near[:, at_lane : at_lane + 64]
+            value = jnp.concatenate([value, near, jnp.zeros_like(near)], axis=1)
+            first = i // 2 * entry + high
+            for parity in range(2):
+
+                @pl.when(lax.rem(core + i, 2) == parity)
+                def _(parity=parity, first=first, value=value):
+                    if columns >= width:
+                        for f in range(columns // width):
+                            targets[parity][first + f * thin : first + (f + 1) * thin, :] = value[
+                                :, f * width : (f + 1) * width
+                            ]
+                    else:
+                        for f in range(width // columns):
+                            targets[parity][
+                                first : first + packed, f * columns : (f + 1) * columns
+                            ] = value[f * packed : (f + 1) * packed]
+
+        sums = None
+        for r in inners:
+            words = r[rows : rows + 64, :]
+            value = words[0:32].astype(F32) + words[32:64].astype(F32)
+            sums = value if sums is None else sums + value
+        tail = jnp.concatenate(
+            [sums, gain[...], jnp.full((extra - 32 - gain.shape[0], width), live[0], F32)], axis=0
+        )
+        for target in targets:
+            target[chips * entry : chips * entry + extra, :] = tail
+
+
+def assemble_kernel(
+    at, *refs
+):
+    in_out, out_out, xproj_out, dtproj_out, conv_out, bias_out, dtb_out, skip_out, mean_out, spread_out = refs[-13:-3]
+    a_out, gain_out, narrow = refs[-3:]
+    count = (len(refs) - 13) // 2
+    wides, lasts = refs[:count], refs[count : 2 * count]
+    high = in_out.shape[0]
+    channels = in_out.shape[1] // 2
+    width = wides[0].shape[1]
+    fold = out_out.shape[1] // width
+    strip = high // fold
+    thin, columns = narrow.shape[0] // count, narrow.shape[1]
+    packed = thin * columns // width
+    taps = conv_out.shape[0]
+    mine = a_out.shape[0]
+    states = mine * count
+    rest = None
+    first = high + packed
+    for d in range(count):
+        them = at[d + 1]
+        piece = lasts[d]
+        lanes = pl.ds(pl.multiple_of(them * width, 128), width)
+        in_out[:, lanes] = piece[0:high, :]
+        in_out[:, pl.ds(pl.multiple_of(channels + them * width, 128), width)] = wides[d][high : 2 * high, :]
+        for f in range(fold):
+            rows = pl.ds(pl.multiple_of(them * strip, 8), strip)
+            out_out[rows, f * width : (f + 1) * width] = wides[d][f * strip : (f + 1) * strip, :]
+        if columns >= width:
+            for f in range(columns // width):
+                rows = pl.ds(pl.multiple_of(them * thin, 8), thin)
+                narrow[rows, f * width : (f + 1) * width] = piece[high + f * thin : high + (f + 1) * thin, :]
+        else:
+            for f in range(width // columns):
+                rows = pl.ds(pl.multiple_of(them * thin + f * packed, 8), packed)
+                narrow[rows, :] = piece[high : high + packed, f * columns : (f + 1) * columns]
+        for k in range(count):
+
+            @pl.when(at[1] == k)
+            def _(k=k, lanes=lanes, piece=piece):
+                a_out[:, lanes] = piece[first + k * mine : first + (k + 1) * mine, :]
+
+        after = first + states
+        dtb_out[:, lanes] = piece[after : after + 1, :]
+        skip_out[:, lanes] = piece[after + 1 : after + 2, :]
+        mean_out[:, lanes] = piece[after + 2 : after + 3, :]
+        spread_out[:, lanes] = piece[after + 3 : after + 4, :]
+        conv_out[:, lanes] = piece[after + 4 : after + 4 + taps, :]
+        bias_out[:, lanes] = piece[after + 4 + taps : after + 5 + taps, :]
+        tail = piece[first + 32 : first + 48, :]
+        rest = tail if rest is None else rest + tail
+    xproj_out[...] = narrow[:, 0 : xproj_out.shape[1]]
+    dtproj_out[...] = narrow[:, 128 : 128 + dtproj_out.shape[1]]
+    gain_out[...] = rest[0:fold]
+    live = rest[fold : fold + 1, 0:1]
+    mean = mean_out[...] / live
+    spread = spread_out[...] / live - mean * mean + 1e-06
+    mean_out[...] = mean
+    spread_out[...] = jnp.sqrt(spread)
 
 
 def struct(*shape, dtype=F32):
@@ -482,6 +689,7 @@
         out_shape=[struct(rows, channels), struct(rows, xproj.shape[1])],
         scratch_shapes=[pltpu.VMEM((rows + 8, width), F32), pltpu.VMEM((rows, width), BF16)],
         compiler_params=LIMIT,
+        cost_estimate=cost(8),
         name="front",
     )(inner, before, conv_weight, conv_bias, xproj)
 
@@ -511,6 +719,7 @@
             pltpu.VMEM((rows, rank), BF16),
         ],
         compiler_params=LIMIT,
+        cost_estimate=cost(40),
         name="ends",
     )(live, proj, dtproj, dt_bias, mixed, gate, grad_gated, rate)
 
@@ -535,14 +744,14 @@
         rows_f32, rows_f32, part(states), part(states), part(1), tall,
     ]
     out_specs = [
-        part(rows), part(rows), pl.BlockSpec((1, rows, 2 * width), lambda q, order: (q, 0, 0)),
-        part(rows), part(states), part(8), tall, whole((rows, rank)), whole((2 * states, rows)),
-    ]
+        part(rows), part(rows), part(rows), part(states), part(8), tall, whole((rows, rank)),
+        whole((2 * states, rows)),
+    ] + [whole((rows, 2 * width))] * blocks
     out_shape = [
         struct(rows, channels, dtype=BF16), struct(rows, channels, dtype=BF16),
-        struct(blocks, rows, 2 * width, dtype=BF16), struct(rows, channels), struct(states, channels),
+        struct(rows, channels), struct(states, channels),
         struct(8, channels), struct(channels, rank), struct(rows, rank), struct(2 * states, rows),
-    ]
+    ] + [struct(rows, 2 * width, dtype=BF16)] * blocks
     args = [
         order, cols, proj, rate, step, mixed, grad_y, sig, gate, grad_gated, state_in, grad_in, skip, dtproj,
     ]
@@ -553,7 +762,7 @@
         in_specs.append(pl.BlockSpec(memory_space=pl.ANY))
     block = pltpu.VMEM((rows, width), F32)
     return pl.pallas_call(
-        scan_kernel,
+        functools.partial(scan_kernel, len(earlier)),
         grid_spec=pltpu.PrefetchScalarGridSpec(
             num_scalar_prefetch=1,
             grid=(blocks,),
@@ -572,31 +781,40 @@
         out_shape=out_shape,
         input_output_aliases=aliases,
         compiler_params=LIMIT,
+        cost_estimate=cost(50),
         name="scan",
     )(*args)
 
 
-def back(order, proj_grad, xproj, mix_grad, inner, before, ahead, conv_weight, conv_bias):
+def back(
+    order, proj_grad, xproj, mix_grad, inner, before, ahead, conv_weight, conv_bias, rate_sums, scan_sums,
+    step_sums, dtproj_grad,
+):
     rows, channels = mix_grad.shape
-    width = channels // lax.axis_size("state")
     blocks = order.shape[0]
+    seqs = lax.axis_size("seq")
+    width = channels // blocks
+    thin = width // seqs
+    side = min(2, seqs // blocks)
+    rank = dtproj_grad.shape[1]
 
     def part(height):
         return pl.BlockSpec((height, width), lambda q, order: (0, order[q]))
 
-    tall = pl.BlockSpec((width, xproj.shape[1]), lambda q, order: (order[q], 0))
+    def tall(columns):
+        return pl.BlockSpec((width, columns), lambda q, order: (order[q], 0))
+
     return pl.pallas_call(
         back_kernel,
         grid_spec=pltpu.PrefetchScalarGridSpec(
             num_scalar_prefetch=1,
             grid=(blocks,),
             in_specs=[
-                whole(proj_grad.shape), tall, part(rows), part(rows), part(8), part(8),
-                part(conv_weight.shape[0]), part(1),
+                whole(proj_grad.shape), tall(xproj.shape[1]), part(rows), part(rows), part(8), part(8),
+                part(conv_weight.shape[0]), part(1), part(rate_sums.shape[0]), part(8), part(8), tall(rank),
             ],
-            out_specs=[
-                part(rows), pl.BlockSpec((1, rows, width), lambda q, order: (q, 0, 0)), part(8), tall,
-            ],
+            out_specs=[part(rows), whole((blocks, seqs + seqs // side, thin, 128))]
+            + [whole((rows + 64, width))] * blocks,
             scratch_shapes=[
                 pltpu.VMEM((rows + 8, width), F32),
                 pltpu.VMEM((rows + 8, width), F32),
@@ -604,12 +822,112 @@
             ],
         ),
         out_shape=[
-            struct(rows, channels, dtype=BF16), struct(blocks, rows, width, dtype=BF16),
-            struct(8, channels), struct(channels, xproj.shape[1]),
-        ],
+            struct(rows, channels, dtype=BF16), struct(blocks, seqs + seqs // side, thin, 128, dtype=BF16),
+        ] + [struct(rows + 64, width, dtype=BF16)] * blocks,
         compiler_params=LIMIT,
+        cost_estimate=cost(18),
         name="back",
-    )(order, proj_grad, xproj, mix_grad, inner, before, ahead, conv_weight, conv_bias)
+    )(
+        order, proj_grad, xproj, mix_grad, inner, before, ahead, conv_weight, conv_bias, rate_sums,
+        scan_sums, step_sums, dtproj_grad,
+    )
+
+
+def cost(micros):
+    return pl.CostEstimate(flops=int(micros), transcendentals=0, bytes_accessed=1024)
+
+
+def places():
+    me = lax.axis_index("state")
+    core = lax.axis_index("seq") % 2
+    return jnp.stack([core] + [me ^ d for d in range(lax.axis_size("state"))]).astype(jnp.int32)
+
+
+def wide_grads(gates, masked, normed, seqs):
+    count = len(gates)
+    rows = gates[0].shape[0]
+    width = gates[0].shape[1] // 2
+    features = masked.shape[1]
+    steps = max(1, width // 256)
+    high = features // seqs
+    chips = seqs // 2
+    fixed = pl.BlockSpec((rows, width), lambda i, at: (0, 1))
+    part = pl.BlockSpec((rows, width // steps), lambda i, at: (0, i))
+
+    def wholly(d):
+        return pl.BlockSpec((rows, features), lambda i, at: (at[d + 1], 0))
+
+    def partly(d):
+        return pl.BlockSpec((rows, features // steps), lambda i, at: (at[d + 1], i))
+
+    return pl.pallas_call(
+        functools.partial(wide_kernel, high),
+        grid_spec=pltpu.PrefetchScalarGridSpec(
+            num_scalar_prefetch=1,
+            grid=(steps,),
+            in_specs=[part] * count + [fixed] * count
+            + [wholly(d) for d in range(count)] + [partly(d) for d in range(count)],
+            out_specs=[whole((chips * 2 * high, width))] * 2,
+        ),
+        out_shape=[struct(chips * 2 * high, width)] * 2,
+        compiler_params=LIMIT,
+        cost_estimate=cost(10),
+        name="wide",
+    )(places(), *gates, *gates, *([masked] * count), *([normed] * count))
+
+
+SUM_ROWS = 48
+
+
+def inner_grads(normed, inners, thins, gain, live, seqs):
+    count = len(inners)
+    width = inners[0].shape[1]
+    features = normed.shape[1]
+    rows = normed.shape[0] // count
+    steps = max(1, width // 256)
+    chips = seqs // 2
+    entry = features // seqs + thins[0].shape[1] * 256 // width
+
+    def partly(d):
+        return pl.BlockSpec((rows, features // steps), lambda i, at: (at[d + 1], i))
+
+    shape = (chips * entry + SUM_ROWS, width)
+    return pl.pallas_call(
+        functools.partial(inner_kernel, seqs),
+        grid_spec=pltpu.PrefetchScalarGridSpec(
+            num_scalar_prefetch=1,
+            grid=(steps,),
+            in_specs=[partly(d) for d in range(count)]
+            + [whole(inners[0].shape)] * count + [whole(thins[0].shape)] * count
+            + [whole(gain.shape), pl.BlockSpec(memory_space=pltpu.SMEM)],
+            out_specs=[whole(shape)] * 2,
+        ),
+        out_shape=[struct(*shape)] * 2,
+        compiler_params=LIMIT,
+        cost_estimate=cost(5),
+        name="inner",
+    )(places(), *([normed] * count), *inners, *thins, gain, live)
+
+
+def assemble(wides, lasts, features, channels, seqs, taps, states, proj_width, rank):
+    width = wides[0].shape[1]
+    count = len(wides)
+    rows = channels // seqs
+    shapes = [
+        (features // seqs, 2 * channels), (rows, features), (rows, proj_width), (rows, rank), (taps, channels),
+        (1, channels), (1, channels), (1, channels), (1, channels), (1, channels),
+        (states // count, channels), (features // width, width),
+    ]
+    return pl.pallas_call(
+        assemble_kernel,
+        in_specs=[pl.BlockSpec(memory_space=pltpu.SMEM)] + [pl.BlockSpec(memory_space=pltpu.VMEM)] * 2 * count,
+        out_specs=[pl.BlockSpec(memory_space=pltpu.VMEM)] * len(shapes),
+        out_shape=[struct(*shape) for shape in shapes],
+        scratch_shapes=[pltpu.VMEM((rows, 256), F32)],
+        compiler_params=LIMIT,
+        cost_estimate=cost(4),
+        name="assemble",
+    )(places(), *wides, *lasts)
 
 
 def dot(a, b, dims):
@@ -646,7 +964,7 @@
     conv_row = conv_bias[None]
     xproj = jnp.pad(xproj_weight, ((0, 0), (0, 128 - proj_width)))
 
-    a_full = lax.all_gather(a_log, "state", axis=0, tiled=True)
+    a_full = placed(gathered(a_log), 0)
     rate2 = -jnp.exp(a_full) * LOG2E
     cotangent = grad_out.astype(F32)
     masked_low = (cotangent * alive).astype(BF16)
@@ -655,7 +973,6 @@
     inv_scale = lax.rsqrt(jnp.mean(inputs * inputs, axis=1, keepdims=True) + EPSILON)
     normed = inputs * inv_scale
     normed_low = (normed * norm_gain).astype(BF16)
-    normed_all = lax.all_gather(normed_low, "state", axis=0, tiled=True)
     inner = jnp.dot(normed_low, in_weight[:, :channels], preferred_element_type=F32).astype(BF16)
     before = shifted(inner[rows - 8 :], "state", 1)
     gate_in = jnp.dot(normed_low, in_weight[:, channels:], preferred_element_type=F32)
@@ -682,18 +999,22 @@
         passed = one[:states] + jnp.exp2(rate2 * one[states : states + 1]) * grad_in
         grad_in = jnp.where(k > member, passed, grad_in)
 
+    normed_late, state_in = lax.optimization_barrier((normed_low, state_in))
+    normed_all = lax.all_gather(normed_late, "state", axis=0, tiled=True)
+
     first = list(range(1, group // 2 + 1))
     second = list(range(group // 2 + 1, group)) + [0]
     call = (cols, proj, rate2, step, mixed, grad_y, sig, gate_in, grad_gated, state_in, grad_in)
     call += (d_skip[None], dtproj_weight)
     one = full_scan(jnp.stack([member ^ d for d in first]), *call, [])
-    gates = {d: swapped(one[2][q], d) for q, d in enumerate(first)}
-    shared = [(k, one[k]) for k in (0, 1, 3, 4, 5, 6)]
+    gates = {d: swapped(one[8 + q], d) for q, d in enumerate(first)}
+    shared = [(k, one[k]) for k in (0, 1, 2, 3, 4, 5)]
     two = full_scan(jnp.stack([member ^ d for d in second]), *call, shared)
-    gates.update({d: swapped(two[2][q], d) if d else two[2][q] for q, d in enumerate(second)})
-    gated_low, grad_gate_low, _, mix_grad, grad_a, scan_sums, grad_dtproj, _, _ = two
-    grad_rank = one[7] + two[7]
-    grad_bc = (one[8] + two[8]).T
+    gated_low, grad_gate_low, mix_grad, grad_a, scan_sums, grad_dtproj = two[:6]
+    first_gates = [gates[d] for d in first]
+    *first_gates, grad_rank = lax.optimization_barrier((*first_gates, one[6] + two[6]))
+    gates.update(dict(zip(first, first_gates)))
+    grad_bc = (one[7] + two[7]).T
 
     grad_proj = jnp.concatenate(
         [grad_rank, grad_bc, jnp.zeros((rows, 128 - proj_width), F32)], axis=1
@@ -704,69 +1025,67 @@
     head_mixed = mix_grad[:8] + dot(grad_proj[:8], xproj, ((1,), (1,)))
     head_grad = head_mixed * head_squash * (1.0 + head_pre * (1.0 - head_squash))
     ahead = shifted(head_grad, "state", -1)
-    order = jnp.stack([member ^ d for d in range(group)])
-    grad_inner_low, inner_sends, conv_sums, grad_xproj = back(
-        order, grad_proj, xproj, mix_grad, inner, before, ahead, conv_weight, conv_row
+    late_sends = [two[8 + q] for q in range(len(second))]
+    ahead, *late_sends = lax.optimization_barrier((ahead, *late_sends))
+    gates.update({d: swapped(v, d) if d else v for d, v in zip(second, late_sends)})
+    order = jnp.stack([member ^ d for d in range(1, group)] + [member])
+    grad_inner_low, thin_sends, *inner_sends = back(
+        order, grad_proj, xproj, mix_grad, inner, before, ahead, conv_weight, conv_row, grad_a, scan_sums,
+        stats, grad_dtproj,
     )
-    inners = {d: swapped(inner_sends[d], d) if d else inner_sends[0] for d in range(group)}
-
-    branch = jnp.dot(gated_low, out_weight, preferred_element_type=F32)
+    *last_gates, inner_sends = lax.optimization_barrier((*[gates[d] for d in second], inner_sends))
+    gates.update(dict(zip(second, last_gates)))
+    inner_pieces = [inner_sends[-1]] + [swapped(v, d + 1) for d, v in enumerate(inner_sends[:-1])]
+    thin_pieces = [thin_sends[0]] + [swapped(thin_sends[d], d) for d in range(1, group)]
+    fold = features // width
+    high = features // seqs
+    thin = width // seqs
+    thin_rows = thin * 256 // width
+
+    wide = wide_grads([gates[d] for d in range(group)], masked_all, normed_all, seqs)
+    wide, _, (inner_pieces, thin_pieces), gated_late = seq_scatter(
+        *wide, hold=(inner_pieces, thin_pieces), behind=gated_low
+    )
+    branch = jnp.dot(gated_late, out_weight, preferred_element_type=F32)
     output = (inputs + alive * branch).astype(BF16)
-
-    def rows_of(values, d):
-        return lax.dynamic_slice_in_dim(values, (member ^ d) * rows, rows, 0)
-
-    out_part = sum(dot(gates[d][:, :width], rows_of(masked_all, d), ((0,), (0,))) for d in range(group))
-    gate_part = sum(dot(rows_of(normed_all, d), gates[d][:, width:], ((0,), (0,))) for d in range(group))
-    early = jnp.concatenate([out_part.reshape(seqs, -1), gate_part.reshape(seqs, -1)], axis=1)
-    early = seq_scatter(early, BF16)
-    half = early.shape[0] // 2
-    early_out = to_owner(early[:half].reshape(width // seqs, features))
-    grad_out_w = placed(gathered(early_out), 0)
-    gate_w = early[half:].reshape(features // seqs, width)
-
-    inner_part = sum(dot(rows_of(normed_all, d), inners[d], ((0,), (0,))) for d in range(group))
-    inner_w = seq_scatter(inner_part.reshape(seqs, -1), BF16).reshape(features // seqs, width)
-    grad_in_w = jnp.concatenate([placed(gathered(inner_w), 1), placed(gathered(gate_w), 1)], axis=1)
-
-    narrow = jnp.concatenate([grad_xproj[:, :proj_width], grad_dtproj], axis=1)
-    narrow = total_scatter(narrow.reshape(seqs * group, -1)).reshape(-1, proj_width + rank)
-    narrow = placed(gathered(narrow), 0)
-
-    small = total_sum(jnp.concatenate([grad_a, scan_sums, stats], axis=0))
-    dtb, skip_sum = small[states], small[states + 1]
-    sum_one, sum_two = small[states + 9], small[states + 10]
+    owned = to_owner(wide[:high])
 
     grad_normed = dot(grad_inner_low, in_weight[:, :channels], ((1,), (1,))) + dot(
         grad_gate_low, in_weight[:, channels:], ((1,), (1,))
     )
-    gain_part = jnp.sum(grad_normed * normed, axis=0)
+    gain_part = jnp.sum(grad_normed * normed, axis=0).reshape(fold, width)
     scaled = grad_normed * norm_gain
     grad_tokens = cotangent + inv_scale * (
         scaled - normed * jnp.mean(scaled * normed, axis=1, keepdims=True)
     )
-    live_part = jnp.broadcast_to(live_rows.astype(F32), (channels - features,))
-    late = jnp.concatenate([conv_sums[: taps + 1], jnp.concatenate([gain_part, live_part])[None]], axis=0)
-    late = total_sum(late)
-    live_count = late[taps + 1, features]
-    dt_mean = sum_one / live_count
-    dt_spread = jnp.sqrt(sum_two / live_count - dt_mean * dt_mean + 1e-06)
-    grad_a_log = lax.dynamic_slice_in_dim(small, member * a_log.shape[0], a_log.shape[0], 0)
+
+    last = inner_grads(normed_all, inner_pieces, thin_pieces, gain_part, live_rows.astype(F32), seqs)
+    last, sums, _, owned = seq_scatter(*last, extra=SUM_ROWS, behind=owned)
+    wide_pieces = gathered(jnp.concatenate([owned, wide[high:]], axis=0))
+    *wide_pieces, last, sums = lax.optimization_barrier((*wide_pieces, last, sums))
+    last = gathered(jnp.concatenate([last, sums], axis=0))
+
+    (
+        grad_in_w, grad_out_w, grad_xproj, grad_dtproj, grad_conv, grad_bias, grad_dtb, grad_skip, dt_mean,
+        dt_spread, grad_a_log, grad_gain,
+    ) = assemble(
+        wide_pieces, last, features, channels, seqs, taps, states, proj_width, rank
+    )
     return (
         output,
         grad_tokens,
-        late[taps + 1, :features],
+        grad_gain.reshape(features),
         grad_in_w,
-        late[:taps],
-        late[taps],
-        narrow[:, :proj_width],
-        narrow[:, proj_width:],
-        dtb,
+        grad_conv,
+        grad_bias[0],
+        grad_xproj,
+        grad_dtproj,
+        grad_dtb[0],
         grad_a_log,
-        skip_sum,
+        grad_skip[0],
         grad_out_w,
-        dt_mean,
-        dt_spread,
+        dt_mean[0],
+        dt_spread[0],
     )
 
 

time: 509 us -> 417 us (0.82); the launches traced: 502 us -> 416 us
  local copies, waits for them, and re-layouts: 56.3 us -> 14 us
  Pallas kernels: 180 us -> 210 us
  matrix products: 55.6 us -> 29.3 us
  starting transfers between devices: 75.9 us -> 56.9 us
  other arithmetic: 26.6 us -> 16.8 us
  blocking collectives: 9.33 us -> 0 us
  waiting for transfers between devices: 81.7 us -> 73.2 us
    ppermute x21 -> x6, waiting for transfers between devices: 59.2 us -> 31.6 us  [seq_exchange(): return lax.ppermute(value, 'seq', [(i, i ^ distance) for i in range(count)])]
    pallas_call x2 -> x5, Pallas kernels: 108 us -> 134 us  [the longest x2 110 us: full_scan(): pl.pallas_call(functools.partial(scan_kernel, len(earlier)), grid_spec=pl...]
    dot_general x16 -> x4, matrix products: 40.3 us -> 14.2 us  [dot(): return lax.dot_general(a, b, (dims, ((), ())), preferred_element_type=F32)]
    ppermute x21, starting transfers between devices: 42.7 us -> 28 us  [swapped(): lax.ppermute(value, 'state', [(i, i ^ distance) for i in range(count)])]
    ppermute x21, waiting for transfers between devices: 22.4 us -> 36.1 us  [swapped(): lax.ppermute(value, 'state', [(i, i ^ distance) for i in range(count)])]
    concatenate x5 -> x1, local copies, waits for them, and re-layouts: 9.5 us -> 0.01 us  [body(): last = gathered(jnp.concatenate([last, sums], axis=0))]
    all_gather x1 -> x0, blocking collectives: 9.33 us -> none  [body(): a_full = lax.all_gather(a_log, 'state', axis=0, tiled=True)]
    dynamic_update_slice x16 -> x4, local copies, waits for them, and re-layouts: 6.24 us -> 0.07 us  [placed(): lax.dynamic_update_slice_in_dim(out, piece, start + (me ^ d) * size, axis)]
  transfers between devices with their start and end apart: 47 -> 32, of which waited for: 12 -> 13; matrix products, arithmetic and copies ran while one was open for 26% -> 11% of each run, Pallas kernels for 36% -> 45%
where the time goes in v3:
time: 417 us; the launch traced here: 416 us
  Pallas kernels  210 us (50%)
  waiting for transfers between devices  73.2 us (18%)
  starting transfers between devices  56.9 us (14%)
  matrix products  29.3 us (7%)
  other arithmetic  16.8 us (4%)
  between operations  15.6 us (4%)
  local copies, waits for them, and re-layouts  14 us (3%)
    pallas_call x2, Pallas kernels, full_scan(): pl.pallas_call(functools.partial(scan_kernel, len(earlier)), grid_spec=pl...  110 us
    pallas_call x1, Pallas kernels, local_ends(): pl.pallas_call(ends_kernel, grid=(channels // width,), in_specs=[pl.Block...  44 us
    ppermute x21, waiting for transfers between devices, swapped(): lax.ppermute(value, 'state', [(i, i ^ distance) for i in range(count)])  36.1 us
    ppermute x6, waiting for transfers between devices, seq_exchange(): return lax.ppermute(value, 'seq', [(i, i ^ distance) for i in range(count)])  31.6 us
    ppermute x21, starting transfers between devices, swapped(): lax.ppermute(value, 'state', [(i, i ^ distance) for i in range(count)])  28 us
    pallas_call x1, Pallas kernels, back(): pl.pallas_call(back_kernel, grid_spec=pltpu.PrefetchScalarGridSpec(num_sc...  23.3 us
    ppermute x6, starting transfers between devices, seq_exchange(): return lax.ppermute(value, 'seq', [(i, i ^ distance) for i in range(count)])  22.3 us
    dot_general x4, matrix products, dot(): return lax.dot_general(a, b, (dims, ((), ())), preferred_element_type=F32)  14.2 us
  transfers between devices with their start and end apart: 32, of which 13 were waited for; matrix products, arithmetic and copies ran while one was open for 11% of the time, Pallas kernels for 45%

profile of v3, /device:TPU:0, one launch (start us, length us, event | category | flops | bytes accessed | tf_op | source)
XLA Modules:
  0.0 416.0 jit_solution(14539250309757724736)
XLA Ops:
  8.0 2.4 fusion.15
  10.5 3.0 collective-permute-start.1
  15.7 4.9 %fusion.12.inner = bf16[512,2048]{1,0:T(8,128)(2,1)S(1)} fusion(bf16[512,1024]{1,0:T(8,128)(2,1)S(1)} %fusion.16, bf16[1024,4096]{1,0:T(8,128)(2,1)} %param.17), kind=kOutput, calls=%fused_computation.15 | convolution fusion | flops 2148532224 | bytes 7340032 | tf_op jit(solution)/shard_map/dot_general | solution.py:976
  22.0 4.0 collective-permute-start
  26.0 6.8 %fusion.2.gate = f32[512,2048]{1,0:T(8,128)} fusion(bf16[512,1024]{1,0:T(8,128)(2,1)S(1)} %fusion.16, bf16[1024,4096]{1,0:T(8,128)(2,1)} %param.17), kind=kOutput, calls=%fused_computation.2 | convolution fusion | flops 2147483648 | bytes 9437184 | tf_op jit(solution)/shard_map/dot_general | solution.py:978
  32.8 4.3 %fusion.50.grad_gated = f32[512,2048]{1,0:T(8,128)} fusion(bf16[512,1024]{1,0:T(8,128)(2,1)S(1)} %copy-done.4, bf16[2048,1024]{1,0:T(8,128)(2,1)S(1)} %copy-done.36), kind=kOutput, calls=%fused_computation.111 | convolution fusion | flops 2147483648 | bytes 9437184 | tf_op jit(solution)/shard_map/dot_general | solution.py:934
  40.1 8.5 %front.1 = (f32[512,2048]{1,0:T(8,128)}, f32[512,128]{1,0:T(8,128)}) custom-call(bf16[512,2048]{1,0:T(8,128)(2,1)} %copy-done.3, bf16[8,2048]{1,0:T(8,128)(2,1)} %copy-done.21, f32[4,2048]{1,0:T(4,128)} %conv_w.3, f32[1,2048]{1,0:T(1,128)} %bitcast.111, bf16[2048,128]{1,0:T(8,128)(2,1)} %pad.4.xproj), custom_call_target="tpu_custom_call" | custom-call | flops 8 | bytes 1024 | tf_op jit(solution)/shard_map/front/pallas_call | solution.py:681
  49.4 44.0 %ends.1 = (f32[512,2048]{1,0:T(8,128)}, f32[512,2048]{1,0:T(8,128)}, f32[512,2048]{1,0:T(8,128)}, f32[8,2048]{1,0:T(8,128)}, f32[16,2048]{1,0:T(8,128)}, /*index=5*/f32[16,2048]{1,0:T(8,128)}, f32[32,512]{1,0:T(8,128)}) custom-call(s32[1]{0:T(128)} %min.6.live, f32[512,128]{1,0:T(8,128)} %get-tuple-element.98.proj, bf16[2048,64]{1,0:T(8,128)(2,1)} %copy.43.dtproj, ...), custom_call_target="tpu_custom_call" | custom-call | flops 40 | bytes 1024 | tf_op jit(solution)/shard_map/ends/pallas_call | solution.py:705
  99.0 4.1 collective-permute-done.4
  103.1 3.3 collective-permute-done.5
  108.1 54.8 %scan.2 = (bf16[512,2048]{1,0:T(8,128)(2,1)}, bf16[512,2048]{1,0:T(8,128)(2,1)}, f32[512,2048]{1,0:T(8,128)}, f32[16,2048]{1,0:T(8,128)}, f32[8,2048]{1,0:T(8,12...) custom-call(s32[2]{0:T(128)} %get-tuple-element.243.order, ...), custom_call_target="tpu_custom_call" | custom-call | flops 50 | bytes 1024 | tf_op jit(solution)/shard_map/scan/pallas_call | solution.py:764
  166.3 54.8 %scan.3 = (bf16[512,2048]{1,0:T(8,128)(2,1)}, bf16[512,2048]{1,0:T(8,128)(2,1)}, f32[512,2048]{1,0:T(8,128)}, f32[16,2048]{1,0:T(8,128)}, f32[8,2048]{1,0:T(8,12...) custom-call(s32[2]{0:T(128)} %get-tuple-element.242.order, ...), custom_call_target="tpu_custom_call", output_to_operand_aliasing={{0}: (14, {}), {1}: (15, {}), {2}: (16, {}), {3}: (17, {}),... | custom-call | flops 50 | bytes 1024 | tf_op jit(solution)/shard_map/scan/pallas_call | solution.py:764
  226.5 5.3 %collective-permute-done.9.ahead = f32[8,2048]{1,0:T(8,128)S(1)} collective-permute-done((f32[8,2048]{1,0:T(8,128)S(1)}, f32[8,2048]{1,0:T(8,128)S(1)}, u32[]{:S(2)}, u32[]{:S(2)}) %collective-permute-start.9) | collective-permute-done | bytes 65568 | tf_op jit(solution)/shard_map/ppermute | solution.py:25
  233.1 23.3 %back.1 = (bf16[512,2048]{1,0:T(8,128)(2,1)}, bf16[4,12,64,128]{3,2,1,0:T(8,128)(2,1)}, bf16[576,512]{1,0:T(8,128)(2,1)}, bf16[576,512]{1,0:T(8,128)(2,1)}, bf16...) custom-call(s32[4]{0:T(128)} %pad_add_fusion.2.order, bf16[512,128]{1,0:T(8,128)(2,1)} %copy-done.13, ...), custom_call_target="tpu_custom_call" | custom-call | flops 18 | bytes 1024 | tf_op jit(solution)/shard_map/back/pallas_call | solution.py:807
  256.5 12.5 %wide.1 = (f32[1024,512]{1,0:T(8,128)}, f32[1024,512]{1,0:T(8,128)}) custom-call(s32[5]{0:T(128)} %stack.33.at, bf16[512,1024]{1,0:T(8,128)(2,1)} %get-tuple-element.134.refs_0_.refs_4_, bf16[512,1024]{1,0:T(8,128)(2,1)} %collective-permute-done.7.refs_1_.refs_5_, bf16[512,1024]{1,0:T(8,128)(2,1)} %collective-permute-done.8.refs_2_.refs_6_, ...), custom_call_target="tpu_custom_call" | custom-call | flops 10 | bytes 1024 | tf_op jit(solution)/shard_map/wide/pallas_call | solution.py:863
  269.1 4.4 %collective-permute-done.11 = f32[1024,512]{1,0:T(8,128)S(1)} collective-permute-done((f32[1024,512]{1,0:T(8,128)}, f32[1024,512]{1,0:T(8,128)S(1)}, u32[]{:S(2)}, u32[]{:S(2)}) %collective-permute-start.11) | collective-permute-done | bytes 2097184 | tf_op jit(solution)/shard_map/ppermute | solution.py:50
  277.4 4.7 %fusion = f32[512,1024]{1,0:T(8,128)S(1)} fusion(bf16[512,2048]{1,0:T(8,128)(2,1)S(1)} %copy-done.10, bf16[1024,4096]{1,0:T(8,128)(2,1)} %param.17), kind=kOutput, calls=%fused_computation | convolution fusion | flops 2147483648 | bytes 8388608 | tf_op jit(solution)/shard_map/dot_general | solution.py:934
  290.0 2.6 collective-permute-start.13
  292.7 4.0 fusion.20
  299.4 4.8 %collective-permute-done.13 = bf16[256,512]{1,0:T(8,128)(2,1)S(1)} collective-permute-done((bf16[256,512]{1,0:T(8,128)(2,1)S(1)}, bf16[256,512]{1,0:T(8,128)(2,1)S(1)}, u32[]{:S(2)}, u32[]{:S(2)}) %collective-permute-start.13) | collective-permute-done | bytes 262176 | tf_op jit(solution)/shard_map/ppermute | solution.py:50
  304.2 2.9 collective-permute-start.19
  307.2 13.9 %collective-permute-done.18.refs_10_ = bf16[12,64,128]{2,1,0:T(8,128)(2,1)S(1)} collective-permute-done((bf16[12,64,128]{2,1,0:T(8,128)(2,1)S(1)}, bf16[12,64,128]{2,1,0:T(8,128)(2,1)S(1)}, u32[]{:S(2)}, u32[]{:S(2)}) %collective-permute-start.18) | collective-permute-done | bytes 196640 | tf_op jit(solution)/shard_map/ppermute | solution.py:19
  321.8 8.1 %inner.1 = (f32[688,512]{1,0:T(8,128)}, f32[688,512]{1,0:T(8,128)}) custom-call(s32[5]{0:T(128)} %stack.33.at, bf16[2048,1024]{1,0:T(8,128)(2,1)} %all-gather.5.cloned.1.call-done.refs_12_.refs_13_.refs_14_.refs_15_.refs_0_.refs_1_.refs_2_.refs_3_, ...), custom_call_target="tpu_custom_call" | custom-call | flops 5 | bytes 1024 | tf_op jit(solution)/shard_map/inner/pallas_call | solution.py:895
  330.9 2.4 collective-permute-done.20
  335.2 17.9 %collective-permute-start.25 = (bf16[416,512]{1,0:T(8,128)(2,1)S(1)}, bf16[416,512]{1,0:T(8,128)(2,1)S(1)}, u32[]{:S(2)}, u32[]{:S(2)}) collective-permute-start(bf16[416,512]{1,0:T(8,128)(2,1)S(1)} %pad_maximum_fusion.2), channel_id=1, source_target_pairs={{0,8},{4,12},{8,0},{12,4},{16,24},{20,28},{24,16},{28,20},{1,9},{5... | collective-permute-start | bytes 1277960 | tf_op jit(solution)/shard_map/ppermute | solution.py:50
  353.3 3.4 collective-permute-start.23
  356.7 6.5 %collective-permute-done.25 = bf16[416,512]{1,0:T(8,128)(2,1)S(1)} collective-permute-done((bf16[416,512]{1,0:T(8,128)(2,1)S(1)}, bf16[416,512]{1,0:T(8,128)(2,1)S(1)}, u32[]{:S(2)}, u32[]{:S(2)}) %collective-permute-start.25) | collective-permute-done | bytes 426016 | tf_op jit(solution)/shard_map/ppermute | solution.py:50
  365.5 12.4 %collective-permute-done.26 = bf16[256,512]{1,0:T(8,128)(2,1)S(1)} collective-permute-done((bf16[256,512]{1,0:T(8,128)(2,1)S(1)}, bf16[256,512]{1,0:T(8,128)(2,1)S(1)}, u32[]{:S(2)}, u32[]{:S(2)}) %collective-permute-start.26) | collective-permute-done | bytes 262176 | tf_op jit(solution)/shard_map/ppermute | solution.py:50
  381.9 3.3 fusion.22
  385.2 5.9 %collective-permute-done.27.refs_5_ = f32[208,512]{1,0:T(8,128)S(1)} collective-permute-done((f32[208,512]{1,0:T(8,128)S(1)}, f32[208,512]{1,0:T(8,128)S(1)}, u32[]{:S(2)}, u32[]{:S(2)}) %collective-permute-start.27) | collective-permute-done | bytes 426016 | tf_op jit(solution)/shard_map/ppermute | solution.py:19
  391.1 8.5 %collective-permute-done.28.refs_6_ = f32[208,512]{1,0:T(8,128)S(1)} collective-permute-done((f32[208,512]{1,0:T(8,128)S(1)}, f32[208,512]{1,0:T(8,128)S(1)}, u32[]{:S(2)}, u32[]{:S(2)}) %collective-permute-start.28) | collective-permute-done | bytes 426016 | tf_op jit(solution)/shard_map/ppermute | solution.py:19
  400.5 4.2 %assemble.1 = (f32[128,4096]{1,0:T(8,128)}, f32[256,1024]{1,0:T(8,128)}, f32[256,96]{1,0:T(8,128)}, f32[256,64]{1,0:T(8,128)}, f32[4,2048]{1,0:T(4,128)}, /*inde...) custom-call(s32[5]{0:T(128)} %stack.33.at, ...), custom_call_target="tpu_custom_call" | custom-call | flops 4 | bytes 1024 | tf_op jit(solution)/shard_map/assemble/pallas_call | solution.py:921
  (191 shorter events, 54.2 us)
Async XLA Ops:
  7.2 249.3 %all-gather.3.cloned.1.call-start = ((), (), s32[]{:S(2)}) async-start(), calls=%async_computation | async-start | bytes 5242880 | tf_op jit(solution)/shard_map/all_gather | solution.py:971
  10.5 246.0 %all-gather.5.cloned.1.call-start = ((), (), s32[]{:S(2)}) async-start(), calls=%async_computation.1 | async-start | bytes 5242880 | tf_op jit(solution)/shard_map/all_gather | solution.py:1003
  10.5 28.9 %collective-permute-start.1 = (f32[4,2048]{1,0:T(4,128)S(1)}, f32[4,2048]{1,0:T(4,128)S(1)}, u32[]{:S(2)}, u32[]{:S(2)}) collective-permute-start(f32[4,2048]{1,0:T(4,128)S(1)} %copy-done.29), channel_id=1, source_target_pairs={{0,1},{1,0},{2,3},{3,2},{4,5},{5,4},{6,7},{7,6},{8,9},{9,8},{10,11... | collective-permute-start | bytes 98312 | tf_op jit(solution)/shard_map/ppermute | solution.py:19
  13.5 25.9 %collective-permute-start.2 = (f32[4,2048]{1,0:T(4,128)S(1)}, f32[4,2048]{1,0:T(4,128)S(1)}, u32[]{:S(2)}, u32[]{:S(2)}) collective-permute-start(f32[4,2048]{1,0:T(4,128)S(1)} %copy-done.29), channel_id=1, source_target_pairs={{0,2},{1,3},{2,0},{3,1},{4,6},{5,7},{6,4},{7,5},{8,10},{9,11},{10,... | collective-permute-start | bytes 98312 | tf_op jit(solution)/shard_map/ppermute | solution.py:19
  15.1 33.6 %collective-permute-start.3 = (f32[4,2048]{1,0:T(4,128)S(1)}, f32[4,2048]{1,0:T(4,128)S(1)}, u32[]{:S(2)}, u32[]{:S(2)}) collective-permute-start(f32[4,2048]{1,0:T(4,128)S(1)} %copy-done.29), channel_id=1, source_target_pairs={{0,3},{1,2},{2,1},{3,0},{4,7},{5,6},{6,5},{7,4},{8,11},{9,10},{10,... | collective-permute-start | bytes 98312 | tf_op jit(solution)/shard_map/ppermute | solution.py:19
  22.0 17.5 %collective-permute-start = (bf16[8,2048]{1,0:T(8,128)(2,1)S(1)}, bf16[8,2048]{1,0:T(8,128)(2,1)S(1)}, u32[]{:S(2)}, u32[]{:S(2)}) collective-permute-start(bf16[8,2048]{1,0:T(8,128)(2,1)S(1)} %get-tuple-element.212), channel_id=1, source_target_pairs={{0,1},{1,2},{2,3},{4,5},{5,6},{6,7},{8,9},{9,10},{10,11},{12,13},{... | collective-permute-start | bytes 98312 | tf_op jit(solution)/shard_map/ppermute | solution.py:25
  95.4 7.7 %collective-permute-start.4 = (f32[24,2048]{1,0:T(8,128)S(1)}, f32[24,2048]{1,0:T(8,128)S(1)}, u32[]{:S(2)}, u32[]{:S(2)}) collective-permute-start(f32[24,2048]{1,0:T(8,128)S(1)} %get-tuple-element.234), channel_id=1, source_target_pairs={{0,1},{1,0},{2,3},{3,2},{4,5},{5,4},{6,7},{7,6},{8,9},{9,8},{10,11... | collective-permute-start | bytes 589832 | tf_op jit(solution)/shard_map/ppermute | solution.py:19
  97.0 9.5 %collective-permute-start.5 = (f32[24,2048]{1,0:T(8,128)S(1)}, f32[24,2048]{1,0:T(8,128)S(1)}, u32[]{:S(2)}, u32[]{:S(2)}) collective-permute-start(f32[24,2048]{1,0:T(8,128)S(1)} %get-tuple-element.235), channel_id=1, source_target_pairs={{0,2},{1,3},{2,0},{3,1},{4,6},{5,7},{6,4},{7,5},{8,10},{9,11},{10,... | collective-permute-start | bytes 589832 | tf_op jit(solution)/shard_map/ppermute | solution.py:19
  97.1 9.3 %collective-permute-start.6 = (f32[24,2048]{1,0:T(8,128)S(1)}, f32[24,2048]{1,0:T(8,128)S(1)}, u32[]{:S(2)}, u32[]{:S(2)}) collective-permute-start(f32[24,2048]{1,0:T(8,128)S(1)} %get-tuple-element.236), channel_id=1, source_target_pairs={{0,3},{1,2},{2,1},{3,0},{4,7},{5,6},{6,5},{7,4},{8,11},{9,10},{10,... | collective-permute-start | bytes 589832 | tf_op jit(solution)/shard_map/ppermute | solution.py:19
  162.9 60.2 %collective-permute-start.7 = (bf16[512,1024]{1,0:T(8,128)(2,1)}, bf16[512,1024]{1,0:T(8,128)(2,1)}, u32[]{:S(2)}, u32[]{:S(2)}) collective-permute-start(bf16[512,1024]{1,0:T(8,128)(2,1)} %get-tuple-element.115), channel_id=1, source_target_pairs={{0,1},{1,0},{2,3},{3,2},{4,5},{5,4},{6,7},{7,6},{8,9},{9,8},{10,11... | collective-permute-start | bytes 3145736 | tf_op jit(solution)/shard_map/ppermute | solution.py:19
  163.7 59.4 %collective-permute-start.8 = (bf16[512,1024]{1,0:T(8,128)(2,1)}, bf16[512,1024]{1,0:T(8,128)(2,1)}, u32[]{:S(2)}, u32[]{:S(2)}) collective-permute-start(bf16[512,1024]{1,0:T(8,128)(2,1)} %get-tuple-element.116), channel_id=1, source_target_pairs={{0,2},{1,3},{2,0},{3,1},{4,6},{5,7},{6,4},{7,5},{8,10},{9,11},{10,... | collective-permute-start | bytes 3145736 | tf_op jit(solution)/shard_map/ppermute | solution.py:19
  225.0 6.9 %collective-permute-start.9 = (f32[8,2048]{1,0:T(8,128)S(1)}, f32[8,2048]{1,0:T(8,128)S(1)}, u32[]{:S(2)}, u32[]{:S(2)}) collective-permute-start(f32[8,2048]{1,0:T(8,128)S(1)} %add_multiply_fusion), channel_id=1, source_target_pairs={{1,0},{2,1},{3,2},{5,4},{6,5},{7,6},{9,8},{10,9},{11,10},{13,12},{... | collective-permute-start | bytes 196616 | tf_op jit(solution)/shard_map/ppermute | solution.py:25
  231.9 24.6 %collective-permute-start.10 = (bf16[512,1024]{1,0:T(8,128)(2,1)}, bf16[512,1024]{1,0:T(8,128)(2,1)}, u32[]{:S(2)}, u32[]{:S(2)}) collective-permute-start(bf16[512,1024]{1,0:T(8,128)(2,1)} %get-tuple-element.124), channel_id=1, source_target_pairs={{0,3},{1,2},{2,1},{3,0},{4,7},{5,6},{6,5},{7,4},{8,11},{9,10},{10,... | collective-permute-start | bytes 3145736 | tf_op jit(solution)/shard_map/ppermute | solution.py:19
  269.0 4.4 %collective-permute-start.11 = (f32[1024,512]{1,0:T(8,128)}, f32[1024,512]{1,0:T(8,128)S(1)}, u32[]{:S(2)}, u32[]{:S(2)}) collective-permute-start(f32[1024,512]{1,0:T(8,128)} %get-tuple-element.140), channel_id=1, source_target_pairs={{0,4},{4,0},{8,12},{12,8},{16,20},{20,16},{24,28},{28,24},{1,5},{5... | collective-permute-start | bytes 6291464 | tf_op jit(solution)/shard_map/ppermute | solution.py:50
  275.7 14.0 %collective-permute-start.12 = (bf16[512,512]{1,0:T(8,128)(2,1)S(1)}, bf16[512,512]{1,0:T(8,128)(2,1)S(1)}, u32[]{:S(2)}, u32[]{:S(2)}) collective-permute-start(bf16[512,512]{1,0:T(8,128)(2,1)S(1)} %bitcast.106), channel_id=1, source_target_pairs={{0,8},{4,12},{8,0},{12,4},{16,24},{20,28},{24,16},{28,20},{1,9},{5... | collective-permute-start | bytes 1572872 | tf_op jit(solution)/shard_map/ppermute | solution.py:50
  282.9 14.4 %collective-permute-start.17 = (bf16[12,64,128]{2,1,0:T(8,128)(2,1)S(1)}, bf16[12,64,128]{2,1,0:T(8,128)(2,1)S(1)}, u32[]{:S(2)}, u32[]{:S(2)}) collective-permute-start(bf16[12,64,128]{2,1,0:T(8,128)(2,1)S(1)} %get-tuple-element.222), channel_id=1, source_target_pairs={{0,1},{1,0},{2,3},{3,2},{4,5},{5,4},{6,7},{7,6},{8,9},{9,8},{10,11... | collective-permute-start | bytes 589832 | tf_op jit(solution)/shard_map/ppermute | solution.py:19
  285.0 36.1 %collective-permute-start.14 = (bf16[576,512]{1,0:T(8,128)(2,1)}, bf16[576,512]{1,0:T(8,128)(2,1)}, u32[]{:S(2)}, u32[]{:S(2)}) collective-permute-start(bf16[576,512]{1,0:T(8,128)(2,1)} %get-tuple-element.147), channel_id=1, source_target_pairs={{0,1},{1,0},{2,3},{3,2},{4,5},{5,4},{6,7},{7,6},{8,9},{9,8},{10,11... | collective-permute-start | bytes 1769480 | tf_op jit(solution)/shard_map/ppermute | solution.py:19
  285.0 36.1 %collective-permute-start.15 = (bf16[576,512]{1,0:T(8,128)(2,1)}, bf16[576,512]{1,0:T(8,128)(2,1)}, u32[]{:S(2)}, u32[]{:S(2)}) collective-permute-start(bf16[576,512]{1,0:T(8,128)(2,1)} %get-tuple-element.148), channel_id=1, source_target_pairs={{0,2},{1,3},{2,0},{3,1},{4,6},{5,7},{6,4},{7,5},{8,10},{9,11},{10,... | collective-permute-start | bytes 1769480 | tf_op jit(solution)/shard_map/ppermute | solution.py:19
  287.0 34.1 %collective-permute-start.16 = (bf16[576,512]{1,0:T(8,128)(2,1)}, bf16[576,512]{1,0:T(8,128)(2,1)}, u32[]{:S(2)}, u32[]{:S(2)}) collective-permute-start(bf16[576,512]{1,0:T(8,128)(2,1)} %get-tuple-element.149), channel_id=1, source_target_pairs={{0,3},{1,2},{2,1},{3,0},{4,7},{5,6},{6,5},{7,4},{8,11},{9,10},{10,... | collective-permute-start | bytes 1769480 | tf_op jit(solution)/shard_map/ppermute | solution.py:19
  290.0 14.2 %collective-permute-start.13 = (bf16[256,512]{1,0:T(8,128)(2,1)S(1)}, bf16[256,512]{1,0:T(8,128)(2,1)S(1)}, u32[]{:S(2)}, u32[]{:S(2)}) collective-permute-start(bf16[256,512]{1,0:T(8,128)(2,1)S(1)} %fusion.26), channel_id=1, source_target_pairs={{0,16},{4,20},{8,24},{12,28},{16,0},{20,4},{24,8},{28,12},{1,17},{... | collective-permute-start | bytes 786440 | tf_op jit(solution)/shard_map/ppermute | solution.py:50
  297.3 23.9 %collective-permute-start.18 = (bf16[12,64,128]{2,1,0:T(8,128)(2,1)S(1)}, bf16[12,64,128]{2,1,0:T(8,128)(2,1)S(1)}, u32[]{:S(2)}, u32[]{:S(2)}) collective-permute-start(bf16[12,64,128]{2,1,0:T(8,128)(2,1)S(1)} %get-tuple-element.221), channel_id=1, source_target_pairs={{0,2},{1,3},{2,0},{3,1},{4,6},{5,7},{6,4},{7,5},{8,10},{9,11},{10,... | collective-permute-start | bytes 589832 | tf_op jit(solution)/shard_map/ppermute | solution.py:19
  304.2 17.0 %collective-permute-start.19 = (bf16[12,64,128]{2,1,0:T(8,128)(2,1)S(1)}, bf16[12,64,128]{2,1,0:T(8,128)(2,1)}, u32[]{:S(2)}, u32[]{:S(2)}) collective-permute-start(bf16[12,64,128]{2,1,0:T(8,128)(2,1)S(1)} %get-tuple-element.220), channel_id=1, source_target_pairs={{0,3},{1,2},{2,1},{3,0},{4,7},{5,6},{6,5},{7,4},{8,11},{9,10},{10,... | collective-permute-start | bytes 589832 | tf_op jit(solution)/shard_map/ppermute | solution.py:19
  329.9 3.4 collective-permute-start.20
  330.0 5.0 %collective-permute-start.21 = (f32[128,512]{1,0:T(8,128)S(1)}, f32[128,512]{1,0:T(8,128)S(1)}, u32[]{:S(2)}, u32[]{:S(2)}) collective-permute-start(f32[128,512]{1,0:T(8,128)S(1)} %get-tuple-element.228), channel_id=1, source_target_pairs={{0,0},{1,8},{2,16},{3,24},{4,1},{5,9},{6,17},{7,25},{8,2},{9,10},{... | collective-permute-start | bytes 786440 | tf_op jit(solution)/shard_map/ppermute | solution.py:88
  335.2 28.0 %collective-permute-start.25 = (bf16[416,512]{1,0:T(8,128)(2,1)S(1)}, bf16[416,512]{1,0:T(8,128)(2,1)S(1)}, u32[]{:S(2)}, u32[]{:S(2)}) collective-permute-start(bf16[416,512]{1,0:T(8,128)(2,1)S(1)} %pad_maximum_fusion.2), channel_id=1, source_target_pairs={{0,8},{4,12},{8,0},{12,4},{16,24},{20,28},{24,16},{28,20},{1,9},{5... | collective-permute-start | bytes 1277960 | tf_op jit(solution)/shard_map/ppermute | solution.py:50
  353.2 24.8 %collective-permute-start.22 = (f32[256,512]{1,0:T(8,128)S(1)}, f32[256,512]{1,0:T(8,128)S(1)}, u32[]{:S(2)}, u32[]{:S(2)}) collective-permute-start(f32[256,512]{1,0:T(8,128)S(1)} %pad_maximum_fusion.1.refs_0_), channel_id=1, source_target_pairs={{0,1},{1,0},{2,3},{3,2},{4,5},{5,4},{6,7},{7,6},{8,9},{9,8},{10,11... | collective-permute-start | bytes 1572872 | tf_op jit(solution)/shard_map/ppermute | solution.py:19
  353.3 25.0 %collective-permute-start.23 = (f32[256,512]{1,0:T(8,128)S(1)}, f32[256,512]{1,0:T(8,128)S(1)}, u32[]{:S(2)}, u32[]{:S(2)}) collective-permute-start(f32[256,512]{1,0:T(8,128)S(1)} %pad_maximum_fusion.1.refs_0_), channel_id=1, source_target_pairs={{0,2},{1,3},{2,0},{3,1},{4,6},{5,7},{6,4},{7,5},{8,10},{9,11},{10,... | collective-permute-start | bytes 1572872 | tf_op jit(solution)/shard_map/ppermute | solution.py:19
  356.7 21.6 %collective-permute-start.24 = (f32[256,512]{1,0:T(8,128)S(1)}, f32[256,512]{1,0:T(8,128)S(1)}, u32[]{:S(2)}, u32[]{:S(2)}) collective-permute-start(f32[256,512]{1,0:T(8,128)S(1)} %pad_maximum_fusion.1.refs_0_), channel_id=1, source_target_pairs={{0,3},{1,2},{2,1},{3,0},{4,7},{5,6},{6,5},{7,4},{8,11},{9,10},{10,... | collective-permute-start | bytes 1572872 | tf_op jit(solution)/shard_map/ppermute | solution.py:19
  363.5 14.4 %collective-permute-start.26 = (bf16[256,512]{1,0:T(8,128)(2,1)S(1)}, bf16[256,512]{1,0:T(8,128)(2,1)S(1)}, u32[]{:S(2)}, u32[]{:S(2)}) collective-permute-start(bf16[256,512]{1,0:T(8,128)(2,1)S(1)} %pad_maximum_fusion.7), channel_id=1, source_target_pairs={{0,16},{4,20},{8,24},{12,28},{16,0},{20,4},{24,8},{28,12},{1,17},{... | collective-permute-start | bytes 786440 | tf_op jit(solution)/shard_map/ppermute | solution.py:50
  378.3 12.8 %collective-permute-start.27 = (f32[208,512]{1,0:T(8,128)S(1)}, f32[208,512]{1,0:T(8,128)S(1)}, u32[]{:S(2)}, u32[]{:S(2)}) collective-permute-start(f32[208,512]{1,0:T(8,128)S(1)} %constant_dynamic-update-slice_fusion.refs_4_), channel_id=1, source_target_pairs={{0,1},{1,0},{2,3},{3,2},{4,5},{5,4},{6,7},{7,6},{8,9},{9,8},{10,11... | collective-permute-start | bytes 1277960 | tf_op jit(solution)/shard_map/ppermute | solution.py:19
  380.1 19.6 %collective-permute-start.28 = (f32[208,512]{1,0:T(8,128)S(1)}, f32[208,512]{1,0:T(8,128)S(1)}, u32[]{:S(2)}, u32[]{:S(2)}) collective-permute-start(f32[208,512]{1,0:T(8,128)S(1)} %constant_dynamic-update-slice_fusion.refs_4_), channel_id=1, source_target_pairs={{0,2},{1,3},{2,0},{3,1},{4,6},{5,7},{6,4},{7,5},{8,10},{9,11},{10,... | collective-permute-start | bytes 1277960 | tf_op jit(solution)/shard_map/ppermute | solution.py:19
  380.3 20.2 %collective-permute-start.29 = (f32[208,512]{1,0:T(8,128)S(1)}, f32[208,512]{1,0:T(8,128)}, u32[]{:S(2)}, u32[]{:S(2)}) collective-permute-start(f32[208,512]{1,0:T(8,128)S(1)} %constant_dynamic-update-slice_fusion.refs_4_), channel_id=1, source_target_pairs={{0,3},{1,2},{2,1},{3,0},{4,7},{5,6},{6,5},{7,4},{8,11},{9,10},{10,... | collective-permute-start | bytes 1277960 | tf_op jit(solution)/shard_map/ppermute | solution.py:19
  (41 other events, 545.1 us)
Sparse Core Ops, SparseCore 0:
  10.6 55.5 all-gather.2
  107.6 53.0 all-gather.4

commit v4 on v3

--- a/solution.py
+++ b/solution.py
@@ -12,6 +12,10 @@
 LN2 = 0.6931471805599453
 F32 = jnp.float32
 BF16 = jnp.bfloat16
+ENDS_ROWS = 64
+SCAN_ROWS = 64
+BACK_ROWS = 64
+WIDE_STEP = 128
 
 
 def swapped(value, distance):
@@ -50,7 +54,7 @@
     return lax.ppermute(value, "seq", [(i, i ^ distance) for i in range(count)])
 
 
-def seq_scatter(mine, other, extra=0, hold=None, behind=None):
+def seq_scatter(mine, other, extra=0, hold=None, behind=None, late=None):
     seqs = lax.axis_size("seq")
     seq = lax.axis_index("seq")
     width = mine.shape[1]
@@ -74,11 +78,13 @@
         total = kept + got[: chips * high].astype(F32).reshape(kept.shape)
         if extra:
             sums = sums + one_word(got[chips * high :])
+        if late is not None and k == 1:
+            total, late = lax.optimization_barrier((total, late))
         k += 1
     total = total.reshape(high, width)
     if hold is not None:
         total, hold = lax.optimization_barrier((total, hold))
-    return total, sums, hold, behind
+    return total, sums, hold, behind if late is None else late
 
 
 def to_owner(value):
@@ -154,6 +160,10 @@
     return 1.0 / (1.0 + jnp.exp(-value))
 
 
+def rounded_grad(gate, grad_gated):
+    return (grad_gated * (gate * logistic(gate))).astype(BF16).astype(F32)
+
+
 def by_eight(value):
     total = value[0:8]
     for k in range(8, value.shape[0], 8):
@@ -185,24 +195,24 @@
     bias = conv_b[...]
 
     def chunk(i, unused):
-        at = pl.multiple_of(i * 32, 32)
-        pre = conv_window(ext[pl.ds(at, 40), :], weight, bias, 32)
+        at = pl.multiple_of(i * BACK_ROWS, BACK_ROWS)
+        pre = conv_window(ext[pl.ds(at, BACK_ROWS + 8), :], weight, bias, BACK_ROWS)
         mixed = pre * logistic(pre)
-        mixed_out[pl.ds(at, 32), :] = mixed
-        low[pl.ds(at, 32), :] = mixed.astype(BF16)
+        mixed_out[pl.ds(at, BACK_ROWS), :] = mixed
+        low[pl.ds(at, BACK_ROWS), :] = mixed.astype(BF16)
         return 0
 
-    lax.fori_loop(0, rows // 32, chunk, 0)
-    proj_out[...] += jnp.dot(low[...], xproj[...], preferred_element_type=F32)
+    lax.fori_loop(0, rows // BACK_ROWS, chunk, 0)
+    proj_out[...] += dot(low[...], xproj[...], ((1,), (1,)))
 
 
 def ends_kernel(
     live, proj, dtproj, dt_b, mixed, gate, grad_gated, rate,
-    step_out, gy_out, sig_out, stat_out, state_out, grad_out, cols_out, lanes, drive, rank_low,
+    step_out, stat_out, state_out, grad_out, cols_out, lanes, drive, rank_low, raised_all, gy_out,
 ):
     rows, width = mixed.shape
     states = rate.shape[0]
-    rank = dtproj.shape[1]
+    rank = dtproj.shape[0]
     reps = width // 128
 
     @pl.when(pl.program_id(0) == 0)
@@ -211,22 +221,18 @@
         rank_low[...] = proj[:, :rank].astype(BF16)
         fill_lanes(lanes, cols_out, rows)
 
-    bias = dt_b[...]
-    count = min(64, rows)
+    raised_all[...] = dt_b[...] + jnp.dot(rank_low[...], dtproj[...], preferred_element_type=F32)
+    count = ENDS_ROWS
     zero8 = jnp.zeros((8, width), F32)
 
     def prepare(i, sums):
         at = pl.ds(pl.multiple_of(i * count, count), count)
-        raised = bias + dot(rank_low[at, :], dtproj[...], ((1,), (1,)))
+        raised = raised_all[at, :]
         small = jnp.exp(-jnp.abs(raised))
         step = jnp.maximum(raised, 0.0) + jnp.log1p(small)
-        inverse = 1.0 / (1.0 + small)
         step_out[at, :] = step
-        sig_out[at, :] = jnp.where(raised >= 0.0, inverse, small * inverse)
         drive[at, :] = step * mixed[at, :]
-        value = gate[at, :]
-        grad_y = grad_gated[at, :] * (value * logistic(value))
-        gy_out[at, :] = grad_y.astype(BF16).astype(F32)
+        gy_out[at, :] = rounded_grad(gate[at, :], grad_gated[at, :])
         row = i * count + lax.broadcasted_iota(jnp.int32, (count, width), 0)
         seen = jnp.where(row < live[0], step, 0.0)
         return sums[0] + by_eight(step), sums[1] + by_eight(seen), sums[2] + by_eight(seen * step)
@@ -260,18 +266,18 @@
 
 
 def scan_kernel(
-    skipped, order, cols, proj, rate, step, mixed, grad_y, sig, gate, grad_gated, state_in, grad_in, skip, dtproj,
+    skipped, order, cols, proj, rate, step, mixed, gate, grad_gated, state_in, grad_in, skip, dtproj,
     *rest,
 ):
     rest = rest[skipped:]
     gated_out, gate_out, mix_out, rate_out, vec_out, dtproj_out, rank_out, bc_out = rest[:8]
-    sends = rest[8:-10]
+    sends = rest[8:-11]
     (
-        lanes, held, b_sum, c_sum, drive, y_sum, decay_sum, source_sum, raised_low, rank_low
-    ) = rest[-10:]
+        lanes, held, b_sum, c_sum, drive, y_sum, decay_sum, source_sum, raised_low, rank_low, grad_y
+    ) = rest[-11:]
     rows, width = step.shape
     states = rate.shape[0]
-    rank = dtproj.shape[1]
+    rank = dtproj.shape[0]
     half = states // 2
     reps = width // 128
     block = pl.program_id(0)
@@ -293,6 +299,7 @@
         parts = []
         row = pl.ds(pl.multiple_of(i * 8, 8), 8)
         drive[row, :] = step[row, :] * mixed[row, :]
+        grad_y[row, :] = rounded_grad(gate[row, :], grad_gated[row, :])
         for r in range(8):
             p = i * 8 + r
             factor = jnp.exp2(rates * spread(step, p, states))
@@ -348,7 +355,7 @@
     rate_out[...] = rate_sum * (rates * LN2)
 
     gain = skip[...]
-    count = min(32, rows)
+    count = SCAN_ROWS
     zero8 = jnp.zeros((8, width), F32)
 
     def finish(i, sums):
@@ -363,27 +370,27 @@
         grad_gate = (upstream * full_y * squash * (1.0 + value * (1.0 - squash))).astype(BF16)
         gated_out[at, :] = gated
         gate_out[at, :] = grad_gate
-        for d, send in enumerate(sends):
-
-            @pl.when(block == d)
-            def _(send=send):
-                send[at, 0:width] = gated
-                send[at, width : 2 * width] = grad_gate
-
         grad_full = upstream * act
         source = source_sum[at, :]
-        grad_raised = (LN2 * decay_sum[at, :] + mix * source) * sig[at, :]
-        raised = grad_raised.astype(BF16)
-        raised_low[at, :] = raised
-        mix_out[at, :] = step[at, :] * source + grad_full * gain
-        rank_out[at, :] += jnp.dot(raised, dtproj[...], preferred_element_type=F32)
+        width_step = step[at, :]
+        grad_raised = (LN2 * decay_sum[at, :] + mix * source) * (1.0 - jnp.exp(-width_step))
+        raised_low[at, :] = grad_raised.astype(BF16)
+        mix_out[at, :] = width_step * source + grad_full * gain
         return sums[0] + by_eight(grad_raised), sums[1] + by_eight(grad_full * mix)
 
     sums = lax.fori_loop(0, rows // count, finish, (zero8, zero8))
+    for d, send in enumerate(sends):
+
+        @pl.when(block == d)
+        def _(send=send):
+            send[:, 0:width] = gated_out[...]
+            send[:, width : 2 * width] = gate_out[...]
+
     vec_out[...] = zero8
     for k in range(2):
         vec_out[k : k + 1, :] = jnp.sum(sums[k], axis=0, keepdims=True)
     dtproj_out[...] = dot(raised_low[...], rank_low[...], ((0,), (0,)))
+    rank_out[...] += dot(raised_low[...], dtproj[...], ((1,), (1,)))
 
     @pl.when(block == pl.num_programs(0) - 1)
     def _():
@@ -410,38 +417,44 @@
 
 
 def back_kernel(
-    order, proj_grad, xproj, mix_grad, inner, before, ahead, conv_w, conv_b, rate_sums, scan_sums, step_sums,
-    dtproj_grad, inner_out, thin_out, *rest,
+    skipped, order, proj_grad, xproj, mix_grad, inner, before, ahead, conv_w, conv_b, rate_sums, scan_sums, step_sums,
+    dtproj_grad, *rest,
 ):
-    sends, (ext, pre_ext, low) = rest[:-3], rest[-3:]
+    thin_before = rest[1] if skipped else None
+    inner_out, thin_out, *rest = rest[skipped:]
+    sends, (ext, pre_ext, low, mixed_grad) = rest[:-4], rest[-4:]
     rows, width = mix_grad.shape
     taps = conv_w.shape[0]
     states = rate_sums.shape[0]
     block = pl.program_id(0)
+    if skipped:
+
+        @pl.when(block == 0)
+        def _():
+            thin_out[...] = thin_before[...]
+
     widen_rows(ext, before, inner)
     weight = conv_w[...]
     bias = conv_b[...]
     pre_ext[rows : rows + 8, :] = ahead[...]
+    mixed_grad[...] = mix_grad[...] + jnp.dot(proj_grad[...], xproj[...], preferred_element_type=F32)
     zero8 = jnp.zeros((8, width), F32)
 
     def chunk(i, sums):
-        at = pl.multiple_of(i * 32, 32)
-        window = ext[pl.ds(at, 40), :]
-        pre = conv_window(window, weight, bias, 32)
+        at = pl.multiple_of(i * BACK_ROWS, BACK_ROWS)
+        window = ext[pl.ds(at, BACK_ROWS + 8), :]
+        pre = conv_window(window, weight, bias, BACK_ROWS)
         squash = logistic(pre)
-        low[pl.ds(at, 32), :] = (pre * squash).astype(BF16)
-        grad_mixed = mix_grad[pl.ds(at, 32), :] + dot(
-            proj_grad[pl.ds(at, 32), :], xproj[...], ((1,), (1,))
-        )
-        grad_pre = grad_mixed * squash * (1.0 + pre * (1.0 - squash))
-        pre_ext[pl.ds(at, 32), :] = grad_pre
+        low[pl.ds(at, BACK_ROWS), :] = (pre * squash).astype(BF16)
+        grad_pre = mixed_grad[pl.ds(at, BACK_ROWS), :] * squash * (1.0 + pre * (1.0 - squash))
+        pre_ext[pl.ds(at, BACK_ROWS), :] = grad_pre
         added = [sums[taps] + by_eight(grad_pre)]
         for k in range(taps - 1, -1, -1):
             shift = taps - 1 - k
-            added.insert(0, sums[k] + by_eight(grad_pre * window[8 - shift : 40 - shift]))
+            added.insert(0, sums[k] + by_eight(grad_pre * window[8 - shift : 8 + BACK_ROWS - shift]))
         return tuple(added)
 
-    sums = lax.fori_loop(0, rows // 32, chunk, (zero8,) * (taps + 1))
+    sums = lax.fori_loop(0, rows // BACK_ROWS, chunk, (zero8,) * (taps + 1))
 
     summed = jnp.concatenate(
         [rate_sums[...], scan_sums[0:2, :], step_sums[1:3, :]]
@@ -458,7 +471,7 @@
     group, entries, thin, _ = thin_out.shape
     seqs = width // thin
     side = seqs // (entries - seqs)
-    me = order[group - 1]
+    me = order[len(sends)]
     for c in range(seqs):
         chunk_index = order[block] * seqs + c
         place = lax.rem(chunk_index, group) ^ me
@@ -473,26 +486,20 @@
             thin_out[t ^ me, seqs + at] = jnp.concatenate(parts, axis=1)
 
     def spread_back(i, unused):
-        at = pl.multiple_of(i * 32, 32)
-        window = pre_ext[pl.ds(at, 40), :]
-        total = weight[taps - 1 : taps] * window[0:32]
+        at = pl.multiple_of(i * BACK_ROWS, BACK_ROWS)
+        window = pre_ext[pl.ds(at, BACK_ROWS + 8), :]
+        total = weight[taps - 1 : taps] * window[0:BACK_ROWS]
         for s in range(1, taps):
-            total = total + weight[taps - 1 - s : taps - s] * window[s : s + 32]
-        rounded = total.astype(BF16)
-        inner_out[pl.ds(at, 32), :] = rounded
-        for d, send in enumerate(sends):
-
-            @pl.when(block == d)
-            def _(send=send):
-                send[pl.ds(at, 32), :] = rounded
-
+            total = total + weight[taps - 1 - s : taps - s] * window[s : s + BACK_ROWS]
+        inner_out[pl.ds(at, BACK_ROWS), :] = total.astype(BF16)
         return 0
 
-    lax.fori_loop(0, rows // 32, spread_back, 0)
+    lax.fori_loop(0, rows // BACK_ROWS, spread_back, 0)
     for d, send in enumerate(sends):
 
         @pl.when(block == d)
         def _(send=send):
+            send[0:rows, :] = inner_out[...]
             send[rows : rows + 64, :] = words
 
 
@@ -618,42 +625,46 @@
     mine = a_out.shape[0]
     states = mine * count
     rest = None
-    first = high + packed
     for d in range(count):
         them = at[d + 1]
-        piece = lasts[d]
         lanes = pl.ds(pl.multiple_of(them * width, 128), width)
-        in_out[:, lanes] = piece[0:high, :]
-        in_out[:, pl.ds(pl.multiple_of(channels + them * width, 128), width)] = wides[d][high : 2 * high, :]
+        half = (lasts[d].shape[0] - high) // 2
+        words = lasts[d][high : high + half, :].astype(F32) + lasts[d][high + half :, :].astype(F32)
+        piece = words[packed:]
+        in_out[:, lanes] = lasts[d][0:high, :].astype(F32)
+        in_out[:, pl.ds(pl.multiple_of(channels + them * width, 128), width)] = wides[d][
+            high : 2 * high, :
+        ].astype(F32)
         for f in range(fold):
             rows = pl.ds(pl.multiple_of(them * strip, 8), strip)
-            out_out[rows, f * width : (f + 1) * width] = wides[d][f * strip : (f + 1) * strip, :]
+            out_out[rows, f * width : (f + 1) * width] = wides[d][f * strip : (f + 1) * strip, :].astype(F32)
         if columns >= width:
             for f in range(columns // width):
                 rows = pl.ds(pl.multiple_of(them * thin, 8), thin)
-                narrow[rows, f * width : (f + 1) * width] = piece[high + f * thin : high + (f + 1) * thin, :]
+                narrow[rows, f * width : (f + 1) * width] = words[f * thin : (f + 1) * thin]
         else:
             for f in range(width // columns):
                 rows = pl.ds(pl.multiple_of(them * thin + f * packed, 8), packed)
-                narrow[rows, :] = piece[high : high + packed, f * columns : (f + 1) * columns]
+                narrow[rows, :] = words[0:packed, f * columns : (f + 1) * columns]
         for k in range(count):
 
             @pl.when(at[1] == k)
             def _(k=k, lanes=lanes, piece=piece):
-                a_out[:, lanes] = piece[first + k * mine : first + (k + 1) * mine, :]
-
-        after = first + states
-        dtb_out[:, lanes] = piece[after : after + 1, :]
-        skip_out[:, lanes] = piece[after + 1 : after + 2, :]
-        mean_out[:, lanes] = piece[after + 2 : after + 3, :]
-        spread_out[:, lanes] = piece[after + 3 : after + 4, :]
-        conv_out[:, lanes] = piece[after + 4 : after + 4 + taps, :]
-        bias_out[:, lanes] = piece[after + 4 + taps : after + 5 + taps, :]
-        tail = piece[first + 32 : first + 48, :]
+                a_out[:, lanes] = piece[k * mine : (k + 1) * mine]
+
+        dtb_out[:, lanes] = piece[states : states + 1]
+        skip_out[:, lanes] = piece[states + 1 : states + 2]
+        mean_out[:, lanes] = piece[states + 2 : states + 3]
+        spread_out[:, lanes] = piece[states + 3 : states + 4]
+        conv_out[:, lanes] = piece[states + 4 : states + 4 + taps]
+        bias_out[:, lanes] = piece[states + 4 + taps : states + 5 + taps]
+        tail = piece[32:48]
         rest = tail if rest is None else rest + tail
-    xproj_out[...] = narrow[:, 0 : xproj_out.shape[1]]
-    dtproj_out[...] = narrow[:, 128 : 128 + dtproj_out.shape[1]]
-    gain_out[...] = rest[0:fold]
+    turned = jnp.transpose(narrow[...])
+    xproj_out[...] = turned[0 : xproj_out.shape[0]]
+    dtproj_out[...] = turned[128 : 128 + dtproj_out.shape[0]]
+    for f in range(fold):
+        gain_out[:, f * width : (f + 1) * width] = rest[f : f + 1]
     live = rest[fold : fold + 1, 0:1]
     mean = mean_out[...] / live
     spread = spread_out[...] / live - mean * mean + 1e-06
@@ -683,10 +694,10 @@
         grid=(channels // width,),
         in_specs=[
             part(rows), part(8), part(conv_weight.shape[0]), part(1),
-            pl.BlockSpec((width, xproj.shape[1]), lambda q: (q, 0)),
+            part(xproj.shape[0]),
         ],
-        out_specs=[part(rows), whole((rows, xproj.shape[1]))],
-        out_shape=[struct(rows, channels), struct(rows, xproj.shape[1])],
+        out_specs=[part(rows), whole((rows, xproj.shape[0]))],
+        out_shape=[struct(rows, channels), struct(rows, xproj.shape[0])],
         scratch_shapes=[pltpu.VMEM((rows + 8, width), F32), pltpu.VMEM((rows, width), BF16)],
         compiler_params=LIMIT,
         cost_estimate=cost(8),
@@ -697,7 +708,7 @@
 def local_ends(live, proj, dtproj, dt_bias, mixed, gate, grad_gated, rate, width):
     rows, channels = mixed.shape
     states = rate.shape[0]
-    rank = dtproj.shape[1]
+    rank = dtproj.shape[0]
 
     def part(height):
         return pl.BlockSpec((height, width), lambda q: (0, q))
@@ -707,16 +718,17 @@
         grid=(channels // width,),
         in_specs=[
             pl.BlockSpec(memory_space=pltpu.SMEM), whole(proj.shape),
-            pl.BlockSpec((width, rank), lambda q: (q, 0)), part(1),
-            part(rows), part(rows), part(rows), part(states),
+            part(rank), part(1), part(rows), part(rows), part(rows), part(states),
         ],
-        out_specs=[part(rows)] * 3 + [part(8), part(states), part(states), whole((2 * states, rows))],
-        out_shape=[struct(rows, channels)] * 3
+        out_specs=[part(rows)] + [part(8), part(states), part(states), whole((2 * states, rows))],
+        out_shape=[struct(rows, channels)]
         + [struct(8, channels), struct(states, channels), struct(states, channels), struct(2 * states, rows)],
         scratch_shapes=[
             pltpu.VMEM((rows, 2 * states, 128), F32),
             pltpu.VMEM((rows, width), F32),
             pltpu.VMEM((rows, rank), BF16),
+            pltpu.VMEM((rows, width), F32),
+            pltpu.VMEM((rows, width), F32),
         ],
         compiler_params=LIMIT,
         cost_estimate=cost(40),
@@ -725,12 +737,11 @@
 
 
 def full_scan(
-    order, cols, proj, rate, step, mixed, grad_y, sig, gate, grad_gated, state_in, grad_in, skip, dtproj,
-    earlier,
+    order, cols, proj, rate, step, mixed, gate, grad_gated, state_in, grad_in, skip, dtproj, earlier,
 ):
     rows, channels = step.shape
     states = rate.shape[0]
-    rank = dtproj.shape[1]
+    rank = dtproj.shape[0]
     width = channels // lax.axis_size("state")
     blocks = order.shape[0]
 
@@ -741,7 +752,7 @@
     rows_f32 = part(rows)
     in_specs = [
         whole(cols.shape), whole(proj.shape), part(states), rows_f32, rows_f32, rows_f32, rows_f32,
-        rows_f32, rows_f32, part(states), part(states), part(1), tall,
+        part(states), part(states), part(1), part(rank),
     ]
     out_specs = [
         part(rows), part(rows), part(rows), part(states), part(8), tall, whole((rows, rank)),
@@ -753,7 +764,7 @@
         struct(8, channels), struct(channels, rank), struct(rows, rank), struct(2 * states, rows),
     ] + [struct(rows, 2 * width, dtype=BF16)] * blocks
     args = [
-        order, cols, proj, rate, step, mixed, grad_y, sig, gate, grad_gated, state_in, grad_in, skip, dtproj,
+        order, cols, proj, rate, step, mixed, gate, grad_gated, state_in, grad_in, skip, dtproj,
     ]
     aliases = {}
     for out, value in earlier:
@@ -776,6 +787,7 @@
                 block, block, block, block,
                 pltpu.VMEM((rows, width), BF16),
                 pltpu.VMEM((rows, rank), BF16),
+                block,
             ],
         ),
         out_shape=out_shape,
@@ -788,14 +800,15 @@
 
 def back(
     order, proj_grad, xproj, mix_grad, inner, before, ahead, conv_weight, conv_bias, rate_sums, scan_sums,
-    step_sums, dtproj_grad,
+    step_sums, dtproj_grad, earlier,
 ):
     rows, channels = mix_grad.shape
-    blocks = order.shape[0]
+    blocks = order.shape[0] - 1
     seqs = lax.axis_size("seq")
-    width = channels // blocks
+    group = lax.axis_size("state")
+    width = channels // group
     thin = width // seqs
-    side = min(2, seqs // blocks)
+    side = min(2, seqs // group)
     rank = dtproj_grad.shape[1]
 
     def part(height):
@@ -804,33 +817,42 @@
     def tall(columns):
         return pl.BlockSpec((width, columns), lambda q, order: (order[q], 0))
 
+    in_specs = [
+        whole(proj_grad.shape), part(xproj.shape[0]), part(rows), part(rows), part(8), part(8),
+        part(conv_weight.shape[0]), part(1), part(rate_sums.shape[0]), part(8), part(8), tall(rank),
+    ]
+    args = [
+        order, proj_grad, xproj, mix_grad, inner, before, ahead, conv_weight, conv_bias, rate_sums,
+        scan_sums, step_sums, dtproj_grad,
+    ]
+    aliases = {}
+    for out, value in earlier:
+        aliases[len(args)] = out
+        args.append(value)
+        in_specs.append(pl.BlockSpec(memory_space=pl.ANY) if out == 0 else whole(value.shape))
     return pl.pallas_call(
-        back_kernel,
+        functools.partial(back_kernel, len(earlier)),
         grid_spec=pltpu.PrefetchScalarGridSpec(
             num_scalar_prefetch=1,
             grid=(blocks,),
-            in_specs=[
-                whole(proj_grad.shape), tall(xproj.shape[1]), part(rows), part(rows), part(8), part(8),
-                part(conv_weight.shape[0]), part(1), part(rate_sums.shape[0]), part(8), part(8), tall(rank),
-            ],
-            out_specs=[part(rows), whole((blocks, seqs + seqs // side, thin, 128))]
+            in_specs=in_specs,
+            out_specs=[part(rows), whole((group, seqs + seqs // side, thin, 128))]
             + [whole((rows + 64, width))] * blocks,
             scratch_shapes=[
                 pltpu.VMEM((rows + 8, width), F32),
                 pltpu.VMEM((rows + 8, width), F32),
                 pltpu.VMEM((rows, width), BF16),
+                pltpu.VMEM((rows, width), F32),
             ],
         ),
         out_shape=[
-            struct(rows, channels, dtype=BF16), struct(blocks, seqs + seqs // side, thin, 128, dtype=BF16),
+            struct(rows, channels, dtype=BF16), struct(group, seqs + seqs // side, thin, 128, dtype=BF16),
         ] + [struct(rows + 64, width, dtype=BF16)] * blocks,
+        input_output_aliases=aliases,
         compiler_params=LIMIT,
         cost_estimate=cost(18),
         name="back",
-    )(
-        order, proj_grad, xproj, mix_grad, inner, before, ahead, conv_weight, conv_bias, rate_sums,
-        scan_sums, step_sums, dtproj_grad,
-    )
+    )(*args)
 
 
 def cost(micros):
@@ -847,33 +869,29 @@
     count = len(gates)
     rows = gates[0].shape[0]
     width = gates[0].shape[1] // 2
-    features = masked.shape[1]
-    steps = max(1, width // 256)
+    features = masked[0].shape[1]
+    steps = max(1, width // WIDE_STEP)
     high = features // seqs
     chips = seqs // 2
     fixed = pl.BlockSpec((rows, width), lambda i, at: (0, 1))
     part = pl.BlockSpec((rows, width // steps), lambda i, at: (0, i))
 
-    def wholly(d):
-        return pl.BlockSpec((rows, features), lambda i, at: (at[d + 1], 0))
-
-    def partly(d):
-        return pl.BlockSpec((rows, features // steps), lambda i, at: (at[d + 1], i))
-
+    wholly = pl.BlockSpec((rows, features), lambda i, at: (0, 0))
+    partly = pl.BlockSpec((rows, features // steps), lambda i, at: (0, i))
     return pl.pallas_call(
         functools.partial(wide_kernel, high),
         grid_spec=pltpu.PrefetchScalarGridSpec(
             num_scalar_prefetch=1,
             grid=(steps,),
             in_specs=[part] * count + [fixed] * count
-            + [wholly(d) for d in range(count)] + [partly(d) for d in range(count)],
+            + [wholly] * count + [partly] * count,
             out_specs=[whole((chips * 2 * high, width))] * 2,
         ),
         out_shape=[struct(chips * 2 * high, width)] * 2,
         compiler_params=LIMIT,
         cost_estimate=cost(10),
         name="wide",
-    )(places(), *gates, *gates, *([masked] * count), *([normed] * count))
+    )(places(), *gates, *gates, *masked, *normed)
 
 
 SUM_ROWS = 48
@@ -882,22 +900,19 @@
 def inner_grads(normed, inners, thins, gain, live, seqs):
     count = len(inners)
     width = inners[0].shape[1]
-    features = normed.shape[1]
-    rows = normed.shape[0] // count
-    steps = max(1, width // 256)
+    rows, features = normed[0].shape
+    steps = max(1, width // WIDE_STEP)
     chips = seqs // 2
     entry = features // seqs + thins[0].shape[1] * 256 // width
 
-    def partly(d):
-        return pl.BlockSpec((rows, features // steps), lambda i, at: (at[d + 1], i))
-
+    partly = pl.BlockSpec((rows, features // steps), lambda i, at: (0, i))
     shape = (chips * entry + SUM_ROWS, width)
     return pl.pallas_call(
         functools.partial(inner_kernel, seqs),
         grid_spec=pltpu.PrefetchScalarGridSpec(
             num_scalar_prefetch=1,
             grid=(steps,),
-            in_specs=[partly(d) for d in range(count)]
+            in_specs=[partly] * count
             + [whole(inners[0].shape)] * count + [whole(thins[0].shape)] * count
             + [whole(gain.shape), pl.BlockSpec(memory_space=pltpu.SMEM)],
             out_specs=[whole(shape)] * 2,
@@ -906,7 +921,7 @@
         compiler_params=LIMIT,
         cost_estimate=cost(5),
         name="inner",
-    )(places(), *([normed] * count), *inners, *thins, gain, live)
+    )(places(), *normed, *inners, *thins, gain, live)
 
 
 def assemble(wides, lasts, features, channels, seqs, taps, states, proj_width, rank):
@@ -914,9 +929,9 @@
     count = len(wides)
     rows = channels // seqs
     shapes = [
-        (features // seqs, 2 * channels), (rows, features), (rows, proj_width), (rows, rank), (taps, channels),
+        (features // seqs, 2 * channels), (rows, features), (proj_width, rows), (rank, rows), (taps, channels),
         (1, channels), (1, channels), (1, channels), (1, channels), (1, channels),
-        (states // count, channels), (features // width, width),
+        (states // count, channels), (1, features),
     ]
     return pl.pallas_call(
         assemble_kernel,
@@ -962,13 +977,12 @@
     live_rows = jnp.clip(lengths - member * rows, 0, rows)
     alive = (jnp.arange(rows, dtype=jnp.int32) < live_rows[0]).astype(F32)[:, None]
     conv_row = conv_bias[None]
-    xproj = jnp.pad(xproj_weight, ((0, 0), (0, 128 - proj_width)))
+    xproj = jnp.pad(xproj_weight.T, ((0, 128 - proj_width), (0, 0)))
 
     a_full = placed(gathered(a_log), 0)
     rate2 = -jnp.exp(a_full) * LOG2E
     cotangent = grad_out.astype(F32)
     masked_low = (cotangent * alive).astype(BF16)
-    masked_all = lax.all_gather(masked_low, "state", axis=0, tiled=True)
     inputs = tokens.astype(F32)
     inv_scale = lax.rsqrt(jnp.mean(inputs * inputs, axis=1, keepdims=True) + EPSILON)
     normed = inputs * inv_scale
@@ -978,9 +992,15 @@
     gate_in = jnp.dot(normed_low, in_weight[:, channels:], preferred_element_type=F32)
     grad_gated = dot(masked_low, out_weight, ((1,), (1,)))
     mixed, proj = front(inner, before, conv_weight, conv_row, xproj, width)
-    step, grad_y, sig, stats, state_end, grad_end, cols = local_ends(
-        live_rows, proj, dtproj_weight, dt_bias[None], mixed, gate_in, grad_gated, rate2, width
+
+    near = [d for d in range(1, group) if d & (d - 1) == 0]
+    normed_late, mixed = lax.optimization_barrier((normed_low, mixed))
+    normed_near = [swapped(normed_late, d) for d in near]
+    step, stats, state_end, grad_end, cols = local_ends(
+        live_rows, proj, dtproj_weight.T, dt_bias[None], mixed, gate_in, grad_gated, rate2, width
     )
+    *normed_near, state_end = lax.optimization_barrier((*normed_near, state_end))
+    normed_pieces = {0: normed_low, **dict(zip(near, normed_near))}
 
     sums_row = stats[0:8]
     pieces = [jnp.concatenate([state_end, sums_row], axis=0)]
@@ -999,14 +1019,17 @@
         passed = one[:states] + jnp.exp2(rate2 * one[states : states + 1]) * grad_in
         grad_in = jnp.where(k > member, passed, grad_in)
 
-    normed_late, state_in = lax.optimization_barrier((normed_low, state_in))
-    normed_all = lax.all_gather(normed_late, "state", axis=0, tiled=True)
+    masked_late, state_in = lax.optimization_barrier((masked_low, state_in))
+    masked_pieces = gathered(masked_late)
 
     first = list(range(1, group // 2 + 1))
     second = list(range(group // 2 + 1, group)) + [0]
-    call = (cols, proj, rate2, step, mixed, grad_y, sig, gate_in, grad_gated, state_in, grad_in)
-    call += (d_skip[None], dtproj_weight)
-    one = full_scan(jnp.stack([member ^ d for d in first]), *call, [])
+    call = (cols, proj, rate2, step, mixed, gate_in, grad_gated, state_in, grad_in)
+    call += (d_skip[None], dtproj_weight.T)
+    one = list(full_scan(jnp.stack([member ^ d for d in first]), *call, []))
+    *masked_pieces, normed_late, one[0] = lax.optimization_barrier((*masked_pieces, normed_low, one[0]))
+    normed_pieces.update({d: swapped(normed_late, d) for d in range(1, group) if d not in near})
+    normed_pieces = [normed_pieces[d] for d in range(group)]
     gates = {d: swapped(one[8 + q], d) for q, d in enumerate(first)}
     shared = [(k, one[k]) for k in (0, 1, 2, 3, 4, 5)]
     two = full_scan(jnp.stack([member ^ d for d in second]), *call, shared)
@@ -1022,32 +1045,36 @@
     window = jnp.concatenate([before, inner[:8]], axis=0).astype(F32)
     head_pre = conv_window(window, conv_weight, conv_row, 8)
     head_squash = jax.nn.sigmoid(head_pre)
-    head_mixed = mix_grad[:8] + dot(grad_proj[:8], xproj, ((1,), (1,)))
+    head_mixed = mix_grad[:8] + jnp.dot(grad_proj[:8], xproj, preferred_element_type=F32)
     head_grad = head_mixed * head_squash * (1.0 + head_pre * (1.0 - head_squash))
     ahead = shifted(head_grad, "state", -1)
     late_sends = [two[8 + q] for q in range(len(second))]
-    ahead, *late_sends = lax.optimization_barrier((ahead, *late_sends))
+    ahead, normed_pieces, *late_sends = lax.optimization_barrier((ahead, normed_pieces, *late_sends))
     gates.update({d: swapped(v, d) if d else v for d, v in zip(second, late_sends)})
-    order = jnp.stack([member ^ d for d in range(1, group)] + [member])
-    grad_inner_low, thin_sends, *inner_sends = back(
-        order, grad_proj, xproj, mix_grad, inner, before, ahead, conv_weight, conv_row, grad_a, scan_sums,
-        stats, grad_dtproj,
-    )
-    *last_gates, inner_sends = lax.optimization_barrier((*[gates[d] for d in second], inner_sends))
-    gates.update(dict(zip(second, last_gates)))
-    inner_pieces = [inner_sends[-1]] + [swapped(v, d + 1) for d, v in enumerate(inner_sends[:-1])]
+    call = (grad_proj, xproj, mix_grad, inner, before, ahead, conv_weight, conv_row, grad_a, scan_sums, stats)
+    call += (grad_dtproj,)
+    one = back(jnp.stack([member ^ d for d in first] + [member]), *call, [])
+    inner_pieces = {d: swapped(one[2 + q], d) for q, d in enumerate(first)}
+    two = back(jnp.stack([member ^ d for d in second] + [member]), *call, [(0, one[0]), (1, one[1])])
+    grad_inner_low, thin_sends = two[:2]
+    inner_pieces.update({d: swapped(two[2 + q], d) if d else two[2 + q] for q, d in enumerate(second)})
     thin_pieces = [thin_sends[0]] + [swapped(thin_sends[d], d) for d in range(1, group)]
+    arrived = [inner_pieces[d] for d in first]
+    gates, arrived, thin_sends = lax.optimization_barrier((gates, arrived, thin_sends))
+    inner_pieces.update(dict(zip(first, arrived)))
+    inner_pieces = [inner_pieces[d] for d in range(group)]
     fold = features // width
     high = features // seqs
     thin = width // seqs
     thin_rows = thin * 256 // width
 
-    wide = wide_grads([gates[d] for d in range(group)], masked_all, normed_all, seqs)
-    wide, _, (inner_pieces, thin_pieces), gated_late = seq_scatter(
-        *wide, hold=(inner_pieces, thin_pieces), behind=gated_low
+    wide = wide_grads([gates[d] for d in range(group)], masked_pieces, normed_pieces, seqs)
+    wide, _, (inner_pieces, thin_pieces), (gated_late, grad_gate_low) = seq_scatter(
+        *wide, hold=(inner_pieces, thin_pieces), late=(gated_low, grad_gate_low)
     )
     branch = jnp.dot(gated_late, out_weight, preferred_element_type=F32)
     output = (inputs + alive * branch).astype(BF16)
+    wide = wide.astype(BF16)
     owned = to_owner(wide[:high])
 
     grad_normed = dot(grad_inner_low, in_weight[:, :channels], ((1,), (1,))) + dot(
@@ -1059,11 +1086,12 @@
         scaled - normed * jnp.mean(scaled * normed, axis=1, keepdims=True)
     )
 
-    last = inner_grads(normed_all, inner_pieces, thin_pieces, gain_part, live_rows.astype(F32), seqs)
-    last, sums, _, owned = seq_scatter(*last, extra=SUM_ROWS, behind=owned)
+    last = inner_grads(normed_pieces, inner_pieces, thin_pieces, gain_part, live_rows.astype(F32), seqs)
+    last, sums, _, owned = seq_scatter(*last, extra=SUM_ROWS, late=owned)
     wide_pieces = gathered(jnp.concatenate([owned, wide[high:]], axis=0))
     *wide_pieces, last, sums = lax.optimization_barrier((*wide_pieces, last, sums))
-    last = gathered(jnp.concatenate([last, sums], axis=0))
+    words = two_words(jnp.concatenate([last[high:], sums], axis=0))
+    last = gathered(jnp.concatenate([last[:high].astype(BF16), words], axis=0))
 
     (
         grad_in_w, grad_out_w, grad_xproj, grad_dtproj, grad_conv, grad_bias, grad_dtb, grad_skip, dt_mean,
@@ -1074,12 +1102,12 @@
     return (
         output,
         grad_tokens,
-        grad_gain.reshape(features),
+        grad_gain[0],
         grad_in_w,
         grad_conv,
         grad_bias[0],
-        grad_xproj,
-        grad_dtproj,
+        grad_xproj.T,
+        grad_dtproj.T,
         grad_dtb[0],
         grad_a_log,
         grad_skip[0],

time: 417 us -> 372 us (0.89)
  Pallas kernels: 210 us -> 195 us
  between operations: 15.6 us -> 2.31 us
  starting transfers between devices: 56.9 us -> 45.9 us
  waiting for transfers between devices: 73.2 us -> 64.8 us
  local copies, waits for them, and re-layouts: 14 us -> 8.74 us
    ppermute x6, starting transfers between devices: 22.3 us -> 6.01 us  [seq_exchange(): return lax.ppermute(value, 'seq', [(i, i ^ distance) for i in range(count)])]
    ppermute x21 -> x27, waiting for transfers between devices: 36.1 us -> 22 us  [swapped(): lax.ppermute(value, 'state', [(i, i ^ distance) for i in range(count)])]
    pallas_call x2, Pallas kernels: 110 us -> 103 us  [full_scan(): pl.pallas_call(functools.partial(scan_kernel, len(earlier)), grid_spec=pl...]
    ppermute x21 -> x27, starting transfers between devices: 28 us -> 34.1 us  [swapped(): lax.ppermute(value, 'state', [(i, i ^ distance) for i in range(count)])]
    pallas_call x1, Pallas kernels: 44 us -> 38 us  [local_ends(): pl.pallas_call(ends_kernel, grid=(channels // width,), in_specs=[pl.Block...]
    ppermute x6, waiting for transfers between devices: 31.6 us -> 37.2 us  [seq_exchange(): return lax.ppermute(value, 'seq', [(i, i ^ distance) for i in range(count)])]
    unnamed x88 -> x68, local copies, waits for them, and re-layouts: 9.36 us -> 5.13 us
    dot_general x4 -> x3, matrix products: 14.2 us -> 17.7 us  [dot(): return lax.dot_general(a, b, (dims, ((), ())), preferred_element_type=F32)]
  transfers between devices with their start and end apart: 32 -> 36, of which waited for: 13 -> 13; matrix products, arithmetic and copies ran while one was open for 11% -> 13% of each run, Pallas kernels for 45% -> 46%
where the time goes in v4:
time: 372 us; the launch traced here: 368 us
  Pallas kernels  195 us (52%)
  waiting for transfers between devices  64.8 us (17%)
  starting transfers between devices  45.9 us (12%)
  matrix products  31.4 us (8%)
  other arithmetic  19.3 us (5%)
  local copies, waits for them, and re-layouts  8.74 us (2%)
    pallas_call x2, Pallas kernels, full_scan(): pl.pallas_call(functools.partial(scan_kernel, len(earlier)), grid_spec=pl...  103 us
    pallas_call x1, Pallas kernels, local_ends(): pl.pallas_call(ends_kernel, grid=(channels // width,), in_specs=[pl.Block...  38 us
    ppermute x6, waiting for transfers between devices, seq_exchange(): return lax.ppermute(value, 'seq', [(i, i ^ distance) for i in range(count)])  37.2 us
    ppermute x27, starting transfers between devices, swapped(): lax.ppermute(value, 'state', [(i, i ^ distance) for i in range(count)])  34.1 us
    ppermute x27, waiting for transfers between devices, swapped(): lax.ppermute(value, 'state', [(i, i ^ distance) for i in range(count)])  22 us
    pallas_call x2, Pallas kernels, back(): pl.pallas_call(functools.partial(back_kernel, len(earlier)), grid_spec=pl...  21.7 us
    dot_general x3, matrix products, dot(): return lax.dot_general(a, b, (dims, ((), ())), preferred_element_type=F32)  17.7 us
    pallas_call x1, Pallas kernels, wide_grads(): pl.pallas_call(functools.partial(wide_kernel, high), grid_spec=pltpu.Pref...  12.7 us
  transfers between devices with their start and end apart: 36, of which 13 were waited for; matrix products, arithmetic and copies ran while one was open for 13% of the time, Pallas kernels for 46%

profile of v4, /device:TPU:0, one launch (start us, length us, event | category | flops | bytes accessed | tf_op | source)
XLA Modules:
  0.0 367.8 jit_solution(7851137940868946308)
XLA Ops:
  0.6 3.0 collective-permute-start.1
  8.4 4.9 %fusion.12.inner = bf16[512,2048]{1,0:T(8,128)(2,1)S(1)} fusion(bf16[512,1024]{1,0:T(8,128)(2,1)S(1)} %fusion.16.refs_12_.refs_0_, bf16[1024,4096]{1,0:T(8,128)(2,1)} %param.17), kind=kOutput, calls=%fused_computation.15 | convolution fusion | flops 2148532224 | bytes 7340032 | tf_op jit(solution)/shard_map/dot_general | solution.py:990
  14.7 3.8 %collective-permute-start = (bf16[8,2048]{1,0:T(8,128)(2,1)S(1)}, bf16[8,2048]{1,0:T(8,128)(2,1)S(1)}, u32[]{:S(2)}, u32[]{:S(2)}) collective-permute-start(bf16[8,2048]{1,0:T(8,128)(2,1)S(1)} %get-tuple-element.216), channel_id=1, source_target_pairs={{0,1},{1,2},{2,3},{4,5},{5,6},{6,7},{8,9},{9,10},{10,11},{12,13},{... | collective-permute-start | bytes 98312 | tf_op jit(solution)/shard_map/ppermute | solution.py:29
  18.6 4.4 %fusion.2.gate = f32[512,2048]{1,0:T(8,128)} fusion(bf16[512,1024]{1,0:T(8,128)(2,1)S(1)} %fusion.16.refs_12_.refs_0_, bf16[1024,4096]{1,0:T(8,128)(2,1)S(1)} %bitcast.133), kind=kOutput, calls=%fused_computation.2 | convolution fusion | flops 2147483648 | bytes 9437184 | tf_op jit(solution)/shard_map/dot_general | solution.py:992
  24.8 7.0 %fusion.51.grad_gated = f32[512,2048]{1,0:T(8,128)} fusion(bf16[512,1024]{1,0:T(8,128)(2,1)} %fusion.15.refs_8_, bf16[2048,1024]{1,0:T(8,128)(2,1)} %param.25), kind=kOutput, calls=%fused_computation.116 | convolution fusion | flops 2147483648 | bytes 9437184 | tf_op jit(solution)/shard_map/dot_general | solution.py:949
  33.4 7.7 %front.1 = (f32[512,2048]{1,0:T(8,128)}, f32[512,128]{1,0:T(8,128)}) custom-call(bf16[512,2048]{1,0:T(8,128)(2,1)} %copy-done, bf16[8,2048]{1,0:T(8,128)(2,1)} %copy-done.17, f32[4,2048]{1,0:T(4,128)} %conv_w.5, f32[1,2048]{1,0:T(1,128)} %bitcast.118, bf16[128,2048]{1,0:T(8,128)(2,1)} %pad.4.xproj), custom_call_target="tpu_custom_call" | custom-call | flops 8 | bytes 1024 | tf_op jit(solution)/shard_map/front/pallas_call | solution.py:692
  43.4 38.0 %ends.1 = (f32[512,2048]{1,0:T(8,128)}, f32[8,2048]{1,0:T(8,128)}, f32[16,2048]{1,0:T(8,128)}, f32[16,2048]{1,0:T(8,128)}, f32[32,512]{1,0:T(8,128)}) custom-call(s32[1]{0:T(128)} %min.6.live, f32[512,128]{1,0:T(8,128)} %get-tuple-element.114.proj, bf16[64,2048]{1,0:T(8,128)(2,1)} %bitcast.106, f32[1,2048]{1,0:T(1,128)} %bitcast.131, ...), custom_call_target="tpu_custom_call" | custom-call | flops 40 | bytes 1024 | tf_op jit(solution)/shard_map/ends/pallas_call | solution.py:716
  87.1 4.2 %collective-permute-done.6 = f32[24,2048]{1,0:T(8,128)S(1)} collective-permute-done((f32[24,2048]{1,0:T(8,128)S(1)}, f32[24,2048]{1,0:T(8,128)S(1)}, u32[]{:S(2)}, u32[]{:S(2)}) %collective-permute-start.6) | collective-permute-done | bytes 196640 | tf_op jit(solution)/shard_map/ppermute | solution.py:23
  91.3 3.2 collective-permute-done.7
  99.5 51.4 %scan.2 = (bf16[512,2048]{1,0:T(8,128)(2,1)}, bf16[512,2048]{1,0:T(8,128)(2,1)}, f32[512,2048]{1,0:T(8,128)}, f32[16,2048]{1,0:T(8,128)}, f32[8,2048]{1,0:T(8,12...) custom-call(s32[2]{0:T(128)} %get-tuple-element.249.order, ...), custom_call_target="tpu_custom_call" | custom-call | flops 50 | bytes 1024 | tf_op jit(solution)/shard_map/scan/pallas_call | solution.py:775
  154.8 51.5 %scan.3 = (bf16[512,2048]{1,0:T(8,128)(2,1)}, bf16[512,2048]{1,0:T(8,128)(2,1)}, f32[512,2048]{1,0:T(8,128)}, f32[16,2048]{1,0:T(8,128)}, f32[8,2048]{1,0:T(8,12...) custom-call(s32[2]{0:T(128)} %get-tuple-element.248.order, ...), custom_call_target="tpu_custom_call", output_to_operand_aliasing={{0}: (12, {}), {1}: (13, {}), {2}: (14, {}), {3}: (15, {}),... | custom-call | flops 50 | bytes 1024 | tf_op jit(solution)/shard_map/scan/pallas_call | solution.py:775
  210.7 5.6 %collective-permute-done.14.ahead = f32[8,2048]{1,0:T(8,128)S(1)} collective-permute-done((f32[8,2048]{1,0:T(8,128)S(1)}, f32[8,2048]{1,0:T(8,128)S(1)}, u32[]{:S(2)}, u32[]{:S(2)}) %collective-permute-start.14) | collective-permute-done | bytes 65568 | tf_op jit(solution)/shard_map/ppermute | solution.py:29
  217.0 10.8 %back.2 = (bf16[512,2048]{1,0:T(8,128)(2,1)}, bf16[4,12,64,128]{3,2,1,0:T(8,128)(2,1)}, bf16[576,512]{1,0:T(8,128)(2,1)}, bf16[576,512]{1,0:T(8,128)(2,1)}) custom-call(s32[3]{0:T(128)} %get-tuple-element.250.order, bf16[512,128]{1,0:T(8,128)(2,1)} %copy-done.12, bf16[128,2048]{1,0:T(8,128)(2,1)} %pad.4.xproj, f32[512,2048]{1,0:T(8,128)} %get-tuple-element.133.mix_grad, ...), custom_call_target="tpu_custom_call" | custom-call | flops 18 | bytes 1024 | tf_op jit(solution)/shard_map/back/pallas_call | solution.py:833
  227.8 2.6 collective-permute-start.17
  231.9 10.9 %back.3 = (bf16[512,2048]{1,0:T(8,128)(2,1)}, bf16[4,12,64,128]{3,2,1,0:T(8,128)(2,1)}, bf16[576,512]{1,0:T(8,128)(2,1)}, bf16[576,512]{1,0:T(8,128)(2,1)}) custom-call(s32[3]{0:T(128)} %get-tuple-element.251.order, bf16[512,128]{1,0:T(8,128)(2,1)} %copy-done.12, bf16[128,2048]{1,0:T(8,128)(2,1)} %pad.4.xproj, ...), custom_call_target="tpu_custom_call", output_to_operand_aliasing={{0}: (13, {}), {1}: (14, {})} | custom-call | flops 18 | bytes 1024 | tf_op jit(solution)/shard_map/back/pallas_call | solution.py:833
  242.8 6.6 %collective-permute-done.17.refs_5_ = bf16[576,512]{1,0:T(8,128)(2,1)S(1)} collective-permute-done((bf16[576,512]{1,0:T(8,128)(2,1)}, bf16[576,512]{1,0:T(8,128)(2,1)S(1)}, u32[]{:S(2)}, u32[]{:S(2)}) %collective-permute-start.17) | collective-permute-done | bytes 589856 | tf_op jit(solution)/shard_map/ppermute | solution.py:23
  249.4 12.7 %wide.1 = (f32[1024,512]{1,0:T(8,128)}, f32[1024,512]{1,0:T(8,128)}) custom-call(s32[5]{0:T(128)} %stack.35.at, bf16[512,1024]{1,0:T(8,128)(2,1)} %get-tuple-element.159.refs_0_.refs_4_, bf16[512,1024]{1,0:T(8,128)(2,1)} %collective-permute-done.12.refs_1_.refs_5_, bf16[512,1024]{1,0:T(8,128)(2,1)} %collective-permute-done.13.refs_2_.refs_6_, ...), custom_call_target="tpu_custom_call" | custom-call | flops 10 | bytes 1024 | tf_op jit(solution)/shard_map/wide/pallas_call | solution.py:881
  262.2 4.4 %collective-permute-done.19 = f32[1024,512]{1,0:T(8,128)S(1)} collective-permute-done((f32[1024,512]{1,0:T(8,128)}, f32[1024,512]{1,0:T(8,128)S(1)}, u32[]{:S(2)}, u32[]{:S(2)}) %collective-permute-start.19) | collective-permute-done | bytes 2097184 | tf_op jit(solution)/shard_map/ppermute | solution.py:54
  267.9 2.8 add.186
  278.5 6.4 %collective-permute-done.20 = bf16[512,512]{1,0:T(8,128)(2,1)} collective-permute-done((bf16[512,512]{1,0:T(8,128)(2,1)S(1)}, bf16[512,512]{1,0:T(8,128)(2,1)}, u32[]{:S(2)}, u32[]{:S(2)}) %collective-permute-start.20) | collective-permute-done | bytes 524320 | tf_op jit(solution)/shard_map/ppermute | solution.py:54
  286.2 2.6 collective-permute-start.21
  288.8 4.5 %fusion = f32[512,1024]{1,0:T(8,128)S(1)} fusion(bf16[512,2048]{1,0:T(8,128)(2,1)S(1)} %copy-done.11, bf16[1024,4096]{1,0:T(8,128)(2,1)} %param.17), kind=kOutput, calls=%fused_computation | convolution fusion | flops 2147483648 | bytes 8388608 | tf_op jit(solution)/shard_map/dot_general | solution.py:949
  293.4 6.2 %fusion.20 = (f32[1024]{0:T(1024)S(1)}, f32[512]{0:T(512)S(1)}, f32[512,1024]{1,0:T(8,128)}) fusion(bf16[512,1024]{1,0:T(8,128)(2,1)S(1)} %copy-done.2, f32[512]{0:T(512)S(1)} %add_rsqrt_fusion, f32[1024]{0:T(1024)S(1)} %copy-done.30, f32[512,1024]{1,0:T(8,128)S(1)} %fusion, bf16[512,2048]{1,0:T(8,128)(2,1)S(1)} %copy-done.7, bf16[1024,4096]{1,0:T(8,128)(2,1)} %param.17), kind=kOutput, calls=%fused_computation.23 | convolution fusion | flops 2151676416 | bytes 11546624 | tf_op jit(solution)/shard_map/dot_general | solution.py:949
  300.4 8.6 %inner.1 = (f32[688,512]{1,0:T(8,128)}, f32[688,512]{1,0:T(8,128)}) custom-call(s32[5]{0:T(128)} %stack.35.at, bf16[512,1024]{1,0:T(8,128)(2,1)} %copy-done.1, bf16[512,1024]{1,0:T(8,128)(2,1)} %collective-permute-done.4.refs_13_.refs_1_, bf16[512,1024]{1,0:T(8,128)(2,1)} %collective-permute-done.5.refs_14_.refs_2_, ...), custom_call_target="tpu_custom_call" | custom-call | flops 5 | bytes 1024 | tf_op jit(solution)/shard_map/inner/pallas_call | solution.py:910
  309.1 3.4 collective-permute-done.26
  316.3 3.3 fusion.22
  320.4 15.1 %collective-permute-done.27 = bf16[416,512]{1,0:T(8,128)(2,1)S(1)} collective-permute-done((bf16[416,512]{1,0:T(8,128)(2,1)S(1)}, bf16[416,512]{1,0:T(8,128)(2,1)S(1)}, u32[]{:S(2)}, u32[]{:S(2)}) %collective-permute-start.27) | collective-permute-done | bytes 426016 | tf_op jit(solution)/shard_map/ppermute | solution.py:54
  336.0 4.2 %collective-permute-start.30 = (bf16[256,512]{1,0:T(8,128)(2,1)S(1)}, bf16[256,512]{1,0:T(8,128)(2,1)S(1)}, u32[]{:S(2)}, u32[]{:S(2)}) collective-permute-start(bf16[256,512]{1,0:T(8,128)(2,1)S(1)} %pad_maximum_fusion.7.refs_0_), channel_id=1, source_target_pairs={{0,2},{1,3},{2,0},{3,1},{4,6},{5,7},{6,4},{7,5},{8,10},{9,11},{10,... | collective-permute-start | bytes 786440 | tf_op jit(solution)/shard_map/ppermute | solution.py:23
  340.9 7.9 %collective-permute-done.32 = bf16[256,512]{1,0:T(8,128)(2,1)S(1)} collective-permute-done((bf16[256,512]{1,0:T(8,128)(2,1)S(1)}, bf16[256,512]{1,0:T(8,128)(2,1)S(1)}, u32[]{:S(2)}, u32[]{:S(2)}) %collective-permute-start.32) | collective-permute-done | bytes 262176 | tf_op jit(solution)/shard_map/ppermute | solution.py:54
  356.1 2.2 collective-permute-done.33.refs_5_
  358.3 4.8 %collective-permute-done.34.refs_6_ = bf16[288,512]{1,0:T(8,128)(2,1)S(1)} collective-permute-done((bf16[288,512]{1,0:T(8,128)(2,1)S(1)}, bf16[288,512]{1,0:T(8,128)(2,1)S(1)}, u32[]{:S(2)}, u32[]{:S(2)}) %collective-permute-start.34) | collective-permute-done | bytes 294944 | tf_op jit(solution)/shard_map/ppermute | solution.py:23
  363.9 3.7 assemble.1
  (181 shorter events, 57.0 us)
Async XLA Ops:
  0.6 42.0 %collective-permute-start.1 = (f32[4,2048]{1,0:T(4,128)}, f32[4,2048]{1,0:T(4,128)S(1)}, u32[]{:S(2)}, u32[]{:S(2)}) collective-permute-start(f32[4,2048]{1,0:T(4,128)} %param.23), channel_id=1, source_target_pairs={{0,1},{1,0},{2,3},{3,2},{4,5},{5,4},{6,7},{7,6},{8,9},{9,8},{10,11... | collective-permute-start | bytes 98312 | tf_op jit(solution)/shard_map/ppermute | solution.py:23
  3.6 39.0 %collective-permute-start.2 = (f32[4,2048]{1,0:T(4,128)}, f32[4,2048]{1,0:T(4,128)S(1)}, u32[]{:S(2)}, u32[]{:S(2)}) collective-permute-start(f32[4,2048]{1,0:T(4,128)} %param.23), channel_id=1, source_target_pairs={{0,2},{1,3},{2,0},{3,1},{4,6},{5,7},{6,4},{7,5},{8,10},{9,11},{10,... | collective-permute-start | bytes 98312 | tf_op jit(solution)/shard_map/ppermute | solution.py:23
  5.2 37.6 %collective-permute-start.3 = (f32[4,2048]{1,0:T(4,128)}, f32[4,2048]{1,0:T(4,128)S(1)}, u32[]{:S(2)}, u32[]{:S(2)}) collective-permute-start(f32[4,2048]{1,0:T(4,128)} %param.23), channel_id=1, source_target_pairs={{0,3},{1,2},{2,1},{3,0},{4,7},{5,6},{6,5},{7,4},{8,11},{9,10},{10,... | collective-permute-start | bytes 98312 | tf_op jit(solution)/shard_map/ppermute | solution.py:23
  14.7 18.0 %collective-permute-start = (bf16[8,2048]{1,0:T(8,128)(2,1)S(1)}, bf16[8,2048]{1,0:T(8,128)(2,1)S(1)}, u32[]{:S(2)}, u32[]{:S(2)}) collective-permute-start(bf16[8,2048]{1,0:T(8,128)(2,1)S(1)} %get-tuple-element.216), channel_id=1, source_target_pairs={{0,1},{1,2},{2,3},{4,5},{5,6},{6,7},{8,9},{9,10},{10,11},{12,13},{... | collective-permute-start | bytes 98312 | tf_op jit(solution)/shard_map/ppermute | solution.py:29
  41.1 40.4 %collective-permute-start.4 = (bf16[512,1024]{1,0:T(8,128)(2,1)}, bf16[512,1024]{1,0:T(8,128)(2,1)}, u32[]{:S(2)}, u32[]{:S(2)}) collective-permute-start(bf16[512,1024]{1,0:T(8,128)(2,1)} %copy-done.1), channel_id=1, source_target_pairs={{0,1},{1,0},{2,3},{3,2},{4,5},{5,4},{6,7},{7,6},{8,9},{9,8},{10,11... | collective-permute-start | bytes 3145736 | tf_op jit(solution)/shard_map/ppermute | solution.py:23
  42.6 38.9 %collective-permute-start.5 = (bf16[512,1024]{1,0:T(8,128)(2,1)}, bf16[512,1024]{1,0:T(8,128)(2,1)}, u32[]{:S(2)}, u32[]{:S(2)}) collective-permute-start(bf16[512,1024]{1,0:T(8,128)(2,1)} %copy-done.1), channel_id=1, source_target_pairs={{0,2},{1,3},{2,0},{3,1},{4,6},{5,7},{6,4},{7,5},{8,10},{9,11},{10,... | collective-permute-start | bytes 3145736 | tf_op jit(solution)/shard_map/ppermute | solution.py:23
  83.5 7.8 %collective-permute-start.6 = (f32[24,2048]{1,0:T(8,128)S(1)}, f32[24,2048]{1,0:T(8,128)S(1)}, u32[]{:S(2)}, u32[]{:S(2)}) collective-permute-start(f32[24,2048]{1,0:T(8,128)S(1)} %get-tuple-element.240), channel_id=1, source_target_pairs={{0,1},{1,0},{2,3},{3,2},{4,5},{5,4},{6,7},{7,6},{8,9},{9,8},{10,11... | collective-permute-start | bytes 589832 | tf_op jit(solution)/shard_map/ppermute | solution.py:23
  85.5 8.9 %collective-permute-start.7 = (f32[24,2048]{1,0:T(8,128)S(1)}, f32[24,2048]{1,0:T(8,128)S(1)}, u32[]{:S(2)}, u32[]{:S(2)}) collective-permute-start(f32[24,2048]{1,0:T(8,128)S(1)} %get-tuple-element.241), channel_id=1, source_target_pairs={{0,2},{1,3},{2,0},{3,1},{4,6},{5,7},{6,4},{7,5},{8,10},{9,11},{10,... | collective-permute-start | bytes 589832 | tf_op jit(solution)/shard_map/ppermute | solution.py:23
  86.0 8.4 %collective-permute-start.8 = (f32[24,2048]{1,0:T(8,128)S(1)}, f32[24,2048]{1,0:T(8,128)S(1)}, u32[]{:S(2)}, u32[]{:S(2)}) collective-permute-start(f32[24,2048]{1,0:T(8,128)S(1)} %get-tuple-element.242), channel_id=1, source_target_pairs={{0,3},{1,2},{2,1},{3,0},{4,7},{5,6},{6,5},{7,4},{8,11},{9,10},{10,... | collective-permute-start | bytes 589832 | tf_op jit(solution)/shard_map/ppermute | solution.py:23
  95.4 57.7 %collective-permute-start.10 = (bf16[512,1024]{1,0:T(8,128)(2,1)}, bf16[512,1024]{1,0:T(8,128)(2,1)}, u32[]{:S(2)}, u32[]{:S(2)}) collective-permute-start(bf16[512,1024]{1,0:T(8,128)(2,1)} %fusion.15.refs_8_), channel_id=1, source_target_pairs={{0,2},{1,3},{2,0},{3,1},{4,6},{5,7},{6,4},{7,5},{8,10},{9,11},{10,... | collective-permute-start | bytes 3145736 | tf_op jit(solution)/shard_map/ppermute | solution.py:23
  96.4 56.7 %collective-permute-start.11 = (bf16[512,1024]{1,0:T(8,128)(2,1)}, bf16[512,1024]{1,0:T(8,128)(2,1)}, u32[]{:S(2)}, u32[]{:S(2)}) collective-permute-start(bf16[512,1024]{1,0:T(8,128)(2,1)} %fusion.15.refs_8_), channel_id=1, source_target_pairs={{0,3},{1,2},{2,1},{3,0},{4,7},{5,6},{6,5},{7,4},{8,11},{9,10},{10,... | collective-permute-start | bytes 3145736 | tf_op jit(solution)/shard_map/ppermute | solution.py:23
  97.5 55.6 %collective-permute-start.9 = (bf16[512,1024]{1,0:T(8,128)(2,1)}, bf16[512,1024]{1,0:T(8,128)(2,1)}, u32[]{:S(2)}, u32[]{:S(2)}) collective-permute-start(bf16[512,1024]{1,0:T(8,128)(2,1)} %fusion.15.refs_8_), channel_id=1, source_target_pairs={{0,1},{1,0},{2,3},{3,2},{4,5},{5,4},{6,7},{7,6},{8,9},{9,8},{10,11... | collective-permute-start | bytes 3145736 | tf_op jit(solution)/shard_map/ppermute | solution.py:23
  150.9 56.3 %collective-permute-start.12 = (bf16[512,1024]{1,0:T(8,128)(2,1)}, bf16[512,1024]{1,0:T(8,128)(2,1)}, u32[]{:S(2)}, u32[]{:S(2)}) collective-permute-start(bf16[512,1024]{1,0:T(8,128)(2,1)} %get-tuple-element.134), channel_id=1, source_target_pairs={{0,1},{1,0},{2,3},{3,2},{4,5},{5,4},{6,7},{7,6},{8,9},{9,8},{10,11... | collective-permute-start | bytes 3145736 | tf_op jit(solution)/shard_map/ppermute | solution.py:23
  151.6 55.6 %collective-permute-start.13 = (bf16[512,1024]{1,0:T(8,128)(2,1)}, bf16[512,1024]{1,0:T(8,128)(2,1)}, u32[]{:S(2)}, u32[]{:S(2)}) collective-permute-start(bf16[512,1024]{1,0:T(8,128)(2,1)} %get-tuple-element.135), channel_id=1, source_target_pairs={{0,2},{1,3},{2,0},{3,1},{4,6},{5,7},{6,4},{7,5},{8,10},{9,11},{10,... | collective-permute-start | bytes 3145736 | tf_op jit(solution)/shard_map/ppermute | solution.py:23
  153.1 63.2 %collective-permute-start.15 = (bf16[512,1024]{1,0:T(8,128)(2,1)}, bf16[512,1024]{1,0:T(8,128)(2,1)}, u32[]{:S(2)}, u32[]{:S(2)}) collective-permute-start(bf16[512,1024]{1,0:T(8,128)(2,1)} %copy-done.1), channel_id=1, source_target_pairs={{0,3},{1,2},{2,1},{3,0},{4,7},{5,6},{6,5},{7,4},{8,11},{9,10},{10,... | collective-permute-start | bytes 3145736 | tf_op jit(solution)/shard_map/ppermute | solution.py:23
  216.3 33.1 %collective-permute-start.16 = (bf16[512,1024]{1,0:T(8,128)(2,1)}, bf16[512,1024]{1,0:T(8,128)(2,1)}, u32[]{:S(2)}, u32[]{:S(2)}) collective-permute-start(bf16[512,1024]{1,0:T(8,128)(2,1)} %get-tuple-element.149), channel_id=1, source_target_pairs={{0,3},{1,2},{2,1},{3,0},{4,7},{5,6},{6,5},{7,4},{8,11},{9,10},{10,... | collective-permute-start | bytes 3145736 | tf_op jit(solution)/shard_map/ppermute | solution.py:23
  227.8 21.7 %collective-permute-start.17 = (bf16[576,512]{1,0:T(8,128)(2,1)}, bf16[576,512]{1,0:T(8,128)(2,1)S(1)}, u32[]{:S(2)}, u32[]{:S(2)}) collective-permute-start(bf16[576,512]{1,0:T(8,128)(2,1)} %get-tuple-element.154), channel_id=1, source_target_pairs={{0,1},{1,0},{2,3},{3,2},{4,5},{5,4},{6,7},{7,6},{8,9},{9,8},{10,11... | collective-permute-start | bytes 1769480 | tf_op jit(solution)/shard_map/ppermute | solution.py:23
  230.4 19.1 %collective-permute-start.18 = (bf16[576,512]{1,0:T(8,128)(2,1)}, bf16[576,512]{1,0:T(8,128)(2,1)}, u32[]{:S(2)}, u32[]{:S(2)}) collective-permute-start(bf16[576,512]{1,0:T(8,128)(2,1)} %get-tuple-element.155), channel_id=1, source_target_pairs={{0,2},{1,3},{2,0},{3,1},{4,6},{5,7},{6,4},{7,5},{8,10},{9,11},{10,... | collective-permute-start | bytes 1769480 | tf_op jit(solution)/shard_map/ppermute | solution.py:23
  270.7 14.1 %collective-permute-start.20 = (bf16[512,512]{1,0:T(8,128)(2,1)S(1)}, bf16[512,512]{1,0:T(8,128)(2,1)}, u32[]{:S(2)}, u32[]{:S(2)}) collective-permute-start(bf16[512,512]{1,0:T(8,128)(2,1)S(1)} %bitcast.112), channel_id=1, source_target_pairs={{0,8},{4,12},{8,0},{12,4},{16,24},{20,28},{24,16},{28,20},{1,9},{5... | collective-permute-start | bytes 1572872 | tf_op jit(solution)/shard_map/ppermute | solution.py:54
  273.3 27.1 %collective-permute-start.23 = (bf16[12,64,128]{2,1,0:T(8,128)(2,1)}, bf16[12,64,128]{2,1,0:T(8,128)(2,1)}, u32[]{:S(2)}, u32[]{:S(2)}) collective-permute-start(bf16[12,64,128]{2,1,0:T(8,128)(2,1)} %get-tuple-element.226), channel_id=1, source_target_pairs={{0,1},{1,0},{2,3},{3,2},{4,5},{5,4},{6,7},{7,6},{8,9},{9,8},{10,11... | collective-permute-start | bytes 589832 | tf_op jit(solution)/shard_map/ppermute | solution.py:23
  275.0 25.4 %collective-permute-start.24 = (bf16[12,64,128]{2,1,0:T(8,128)(2,1)}, bf16[12,64,128]{2,1,0:T(8,128)(2,1)}, u32[]{:S(2)}, u32[]{:S(2)}) collective-permute-start(bf16[12,64,128]{2,1,0:T(8,128)(2,1)} %get-tuple-element.225), channel_id=1, source_target_pairs={{0,2},{1,3},{2,0},{3,1},{4,6},{5,7},{6,4},{7,5},{8,10},{9,11},{10,... | collective-permute-start | bytes 589832 | tf_op jit(solution)/shard_map/ppermute | solution.py:23
  275.5 24.9 %collective-permute-start.25 = (bf16[12,64,128]{2,1,0:T(8,128)(2,1)}, bf16[12,64,128]{2,1,0:T(8,128)(2,1)}, u32[]{:S(2)}, u32[]{:S(2)}) collective-permute-start(bf16[12,64,128]{2,1,0:T(8,128)(2,1)} %get-tuple-element.224), channel_id=1, source_target_pairs={{0,3},{1,2},{2,1},{3,0},{4,7},{5,6},{6,5},{7,4},{8,11},{9,10},{10,... | collective-permute-start | bytes 589832 | tf_op jit(solution)/shard_map/ppermute | solution.py:23
  276.8 23.6 %collective-permute-start.22 = (bf16[576,512]{1,0:T(8,128)(2,1)}, bf16[576,512]{1,0:T(8,128)(2,1)}, u32[]{:S(2)}, u32[]{:S(2)}) collective-permute-start(bf16[576,512]{1,0:T(8,128)(2,1)} %get-tuple-element.182), channel_id=1, source_target_pairs={{0,3},{1,2},{2,1},{3,0},{4,7},{5,6},{6,5},{7,4},{8,11},{9,10},{10,... | collective-permute-start | bytes 1769480 | tf_op jit(solution)/shard_map/ppermute | solution.py:23
  286.2 14.1 %collective-permute-start.21 = (bf16[256,512]{1,0:T(8,128)(2,1)S(1)}, bf16[256,512]{1,0:T(8,128)(2,1)S(1)}, u32[]{:S(2)}, u32[]{:S(2)}) collective-permute-start(bf16[256,512]{1,0:T(8,128)(2,1)S(1)} %fusion.26), channel_id=1, source_target_pairs={{0,16},{4,20},{8,24},{12,28},{16,0},{20,4},{24,8},{28,12},{1,17},{... | collective-permute-start | bytes 786440 | tf_op jit(solution)/shard_map/ppermute | solution.py:54
  314.5 21.0 %collective-permute-start.27 = (bf16[416,512]{1,0:T(8,128)(2,1)S(1)}, bf16[416,512]{1,0:T(8,128)(2,1)S(1)}, u32[]{:S(2)}, u32[]{:S(2)}) collective-permute-start(bf16[416,512]{1,0:T(8,128)(2,1)S(1)} %pad_maximum_fusion.1), channel_id=1, source_target_pairs={{0,8},{4,12},{8,0},{12,4},{16,24},{20,28},{24,16},{28,20},{1,9},{5... | collective-permute-start | bytes 1277960 | tf_op jit(solution)/shard_map/ppermute | solution.py:54
  319.7 16.0 %collective-permute-start.28 = (bf16[128,512]{1,0:T(8,128)(2,1)S(1)}, bf16[128,512]{1,0:T(8,128)(2,1)S(1)}, u32[]{:S(2)}, u32[]{:S(2)}) collective-permute-start(bf16[128,512]{1,0:T(8,128)(2,1)S(1)} %get-tuple-element.232), channel_id=1, source_target_pairs={{0,0},{1,8},{2,16},{3,24},{4,1},{5,9},{6,17},{7,25},{8,2},{9,10},{... | collective-permute-start | bytes 393224 | tf_op jit(solution)/shard_map/ppermute | solution.py:94
  335.8 13.0 %collective-permute-start.32 = (bf16[256,512]{1,0:T(8,128)(2,1)S(1)}, bf16[256,512]{1,0:T(8,128)(2,1)S(1)}, u32[]{:S(2)}, u32[]{:S(2)}) collective-permute-start(bf16[256,512]{1,0:T(8,128)(2,1)S(1)} %pad_maximum_fusion.8), channel_id=1, source_target_pairs={{0,16},{4,20},{8,24},{12,28},{16,0},{20,4},{24,8},{28,12},{1,17},{... | collective-permute-start | bytes 786440 | tf_op jit(solution)/shard_map/ppermute | solution.py:54
  335.9 12.9 %collective-permute-start.29 = (bf16[256,512]{1,0:T(8,128)(2,1)S(1)}, bf16[256,512]{1,0:T(8,128)(2,1)S(1)}, u32[]{:S(2)}, u32[]{:S(2)}) collective-permute-start(bf16[256,512]{1,0:T(8,128)(2,1)S(1)} %pad_maximum_fusion.7.refs_0_), channel_id=1, source_target_pairs={{0,1},{1,0},{2,3},{3,2},{4,5},{5,4},{6,7},{7,6},{8,9},{9,8},{10,11... | collective-permute-start | bytes 786440 | tf_op jit(solution)/shard_map/ppermute | solution.py:23
  336.0 13.8 %collective-permute-start.30 = (bf16[256,512]{1,0:T(8,128)(2,1)S(1)}, bf16[256,512]{1,0:T(8,128)(2,1)S(1)}, u32[]{:S(2)}, u32[]{:S(2)}) collective-permute-start(bf16[256,512]{1,0:T(8,128)(2,1)S(1)} %pad_maximum_fusion.7.refs_0_), channel_id=1, source_target_pairs={{0,2},{1,3},{2,0},{3,1},{4,6},{5,7},{6,4},{7,5},{8,10},{9,11},{10,... | collective-permute-start | bytes 786440 | tf_op jit(solution)/shard_map/ppermute | solution.py:23
  340.2 9.6 %collective-permute-start.31 = (bf16[256,512]{1,0:T(8,128)(2,1)S(1)}, bf16[256,512]{1,0:T(8,128)(2,1)S(1)}, u32[]{:S(2)}, u32[]{:S(2)}) collective-permute-start(bf16[256,512]{1,0:T(8,128)(2,1)S(1)} %pad_maximum_fusion.7.refs_0_), channel_id=1, source_target_pairs={{0,3},{1,2},{2,1},{3,0},{4,7},{5,6},{6,5},{7,4},{8,11},{9,10},{10,... | collective-permute-start | bytes 786440 | tf_op jit(solution)/shard_map/ppermute | solution.py:23
  351.4 11.8 %collective-permute-start.34 = (bf16[288,512]{1,0:T(8,128)(2,1)S(1)}, bf16[288,512]{1,0:T(8,128)(2,1)S(1)}, u32[]{:S(2)}, u32[]{:S(2)}) collective-permute-start(bf16[288,512]{1,0:T(8,128)(2,1)S(1)} %pad_maximum_fusion.6.refs_4_), channel_id=1, source_target_pairs={{0,2},{1,3},{2,0},{3,1},{4,6},{5,7},{6,4},{7,5},{8,10},{9,11},{10,... | collective-permute-start | bytes 884744 | tf_op jit(solution)/shard_map/ppermute | solution.py:23
  353.2 10.8 %collective-permute-start.35 = (bf16[288,512]{1,0:T(8,128)(2,1)S(1)}, bf16[288,512]{1,0:T(8,128)(2,1)}, u32[]{:S(2)}, u32[]{:S(2)}) collective-permute-start(bf16[288,512]{1,0:T(8,128)(2,1)S(1)} %pad_maximum_fusion.6.refs_4_), channel_id=1, source_target_pairs={{0,3},{1,2},{2,1},{3,0},{4,7},{5,6},{6,5},{7,4},{8,11},{9,10},{10,... | collective-permute-start | bytes 884744 | tf_op jit(solution)/shard_map/ppermute | solution.py:23
  (38 other events, 489.7 us)

commit v5 on v4

--- a/solution.py
+++ b/solution.py
@@ -90,7 +90,13 @@
 def to_owner(value):
     seqs = lax.axis_size("seq")
     states = lax.axis_size("state")
-    pairs = [(s * states + t, t * seqs + s) for s in range(seqs) for t in range(states)]
+    there = [(s * states + t, s * states + (t ^ (s % states))) for s in range(seqs) for t in range(states)]
+    value = lax.ppermute(value, ("seq", "state"), there)
+    pairs = [
+        (s * states + (t ^ (s % states)), (t * seqs + s) // states * states + (t ^ (s % states)))
+        for s in range(seqs)
+        for t in range(states)
+    ]
     return lax.ppermute(value, ("seq", "state"), pairs)
 
 
@@ -107,7 +113,7 @@
 
 
 def fill_lanes(out_ref, cols_ref, rows):
-    groups = 8
+    groups = min(16, rows // 8)
     states = cols_ref.shape[0]
     lanes = min(128, rows)
 
@@ -208,12 +214,13 @@
 
 def ends_kernel(
     live, proj, dtproj, dt_b, mixed, gate, grad_gated, rate,
-    step_out, stat_out, state_out, grad_out, cols_out, lanes, drive, rank_low, raised_all, gy_out,
+    step_out, stat_out, state_out, grad_out, cols_out, *rest,
 ):
     rows, width = mixed.shape
     states = rate.shape[0]
     rank = dtproj.shape[0]
     reps = width // 128
+    messages, (lanes, drive, rank_low, raised_all, gy_out) = rest[:-5], rest[-5:]
 
     @pl.when(pl.program_id(0) == 0)
     def _():
@@ -263,6 +270,9 @@
     state, grad = lax.fori_loop(0, groups, body, (zero, zero))
     state_out[...] = state
     grad_out[...] = grad
+    for d, message in enumerate(messages):
+        message[0:states, :] = jnp.where(live[1] < (live[1] ^ (d + 1)), state, grad)
+        message[states : states + 8, :] = stat_out[...]
 
 
 def scan_kernel(
@@ -636,7 +646,7 @@
             high : 2 * high, :
         ].astype(F32)
         for f in range(fold):
-            rows = pl.ds(pl.multiple_of(them * strip, 8), strip)
+            rows = pl.ds(pl.multiple_of(at[1 + count + d] * strip, 8), strip)
             out_out[rows, f * width : (f + 1) * width] = wides[d][f * strip : (f + 1) * strip, :].astype(F32)
         if columns >= width:
             for f in range(columns // width):
@@ -709,6 +719,7 @@
     rows, channels = mixed.shape
     states = rate.shape[0]
     rank = dtproj.shape[0]
+    group = channels // width
 
     def part(height):
         return pl.BlockSpec((height, width), lambda q: (0, q))
@@ -720,9 +731,11 @@
             pl.BlockSpec(memory_space=pltpu.SMEM), whole(proj.shape),
             part(rank), part(1), part(rows), part(rows), part(rows), part(states),
         ],
-        out_specs=[part(rows)] + [part(8), part(states), part(states), whole((2 * states, rows))],
+        out_specs=[part(rows)] + [part(8), part(states), part(states), whole((2 * states, rows))]
+        + [part(states + 8)] * (group - 1),
         out_shape=[struct(rows, channels)]
-        + [struct(8, channels), struct(states, channels), struct(states, channels), struct(2 * states, rows)],
+        + [struct(8, channels), struct(states, channels), struct(states, channels), struct(2 * states, rows)]
+        + [struct(states + 8, channels)] * (group - 1),
         scratch_shapes=[
             pltpu.VMEM((rows, 2 * states, 128), F32),
             pltpu.VMEM((rows, width), F32),
@@ -862,7 +875,10 @@
 def places():
     me = lax.axis_index("state")
     core = lax.axis_index("seq") % 2
-    return jnp.stack([core] + [me ^ d for d in range(lax.axis_size("state"))]).astype(jnp.int32)
+    group = lax.axis_size("state")
+    base = lax.axis_index("seq") * group // lax.axis_size("seq")
+    order = [me ^ d for d in range(group)]
+    return jnp.stack([core] + order + [base ^ k for k in order]).astype(jnp.int32)
 
 
 def wide_grads(gates, masked, normed, seqs):
@@ -996,17 +1012,14 @@
     near = [d for d in range(1, group) if d & (d - 1) == 0]
     normed_late, mixed = lax.optimization_barrier((normed_low, mixed))
     normed_near = [swapped(normed_late, d) for d in near]
-    step, stats, state_end, grad_end, cols = local_ends(
-        live_rows, proj, dtproj_weight.T, dt_bias[None], mixed, gate_in, grad_gated, rate2, width
+    step, stats, state_end, grad_end, cols, *offers = local_ends(
+        jnp.stack([live_rows[0], member]), proj, dtproj_weight.T, dt_bias[None], mixed, gate_in, grad_gated, rate2, width
     )
-    *normed_near, state_end = lax.optimization_barrier((*normed_near, state_end))
+    *normed_near, offers = lax.optimization_barrier((*normed_near, offers))
     normed_pieces = {0: normed_low, **dict(zip(near, normed_near))}
 
-    sums_row = stats[0:8]
-    pieces = [jnp.concatenate([state_end, sums_row], axis=0)]
-    for d in range(1, group):
-        chosen = jnp.where(member < (member ^ d), state_end, grad_end)
-        pieces.append(swapped(jnp.concatenate([chosen, sums_row], axis=0), d))
+    pieces = [jnp.concatenate([state_end, stats], axis=0)]
+    pieces += [swapped(offer, d + 1) for d, offer in enumerate(offers)]
     pieces = jnp.stack(pieces)
     state_in = jnp.zeros((states, channels), F32)
     grad_in = jnp.zeros((states, channels), F32)
@@ -1035,7 +1048,9 @@
     two = full_scan(jnp.stack([member ^ d for d in second]), *call, shared)
     gated_low, grad_gate_low, mix_grad, grad_a, scan_sums, grad_dtproj = two[:6]
     first_gates = [gates[d] for d in first]
-    *first_gates, grad_rank = lax.optimization_barrier((*first_gates, one[6] + two[6]))
+    normed_pieces, *first_gates, grad_rank = lax.optimization_barrier(
+        (normed_pieces, *first_gates, one[6] + two[6])
+    )
     gates.update(dict(zip(first, first_gates)))
     grad_bc = (one[7] + two[7]).T
 
@@ -1049,7 +1064,7 @@
     head_grad = head_mixed * head_squash * (1.0 + head_pre * (1.0 - head_squash))
     ahead = shifted(head_grad, "state", -1)
     late_sends = [two[8 + q] for q in range(len(second))]
-    ahead, normed_pieces, *late_sends = lax.optimization_barrier((ahead, normed_pieces, *late_sends))
+    ahead, *late_sends = lax.optimization_barrier((ahead, *late_sends))
     gates.update({d: swapped(v, d) if d else v for d, v in zip(second, late_sends)})
     call = (grad_proj, xproj, mix_grad, inner, before, ahead, conv_weight, conv_row, grad_a, scan_sums, stats)
     call += (grad_dtproj,)

time: 372 us -> 365 us (0.981)
  waiting for transfers between devices: 64.8 us -> 59.7 us
    ppermute x6, waiting for transfers between devices: 37.2 us -> 28.4 us  [seq_exchange(): return lax.ppermute(value, 'seq', [(i, i ^ distance) for i in range(count)])]
  transfers between devices with their start and end apart: 36 -> 37, of which waited for: 13 -> 14; matrix products, arithmetic and copies ran while one was open for 13% -> 13% of each run, Pallas kernels for 46% -> 47%
where the time goes in v5:
time: 365 us; the launch traced here: 364 us
  Pallas kernels  195 us (53%)
  waiting for transfers between devices  59.7 us (16%)
  starting transfers between devices  49.5 us (14%)
  matrix products  31.4 us (9%)
  other arithmetic  18.9 us (5%)
  local copies, waits for them, and re-layouts  7.79 us (2%)
    pallas_call x2, Pallas kernels, full_scan(): pl.pallas_call(functools.partial(scan_kernel, len(earlier)), grid_spec=pl...  102 us
    pallas_call x1, Pallas kernels, local_ends(): pl.pallas_call(ends_kernel, grid=(channels // width,), in_specs=[pl.Block...  37.9 us
    ppermute x27, starting transfers between devices, swapped(): lax.ppermute(value, 'state', [(i, i ^ distance) for i in range(count)])  34.1 us
    ppermute x6, waiting for transfers between devices, seq_exchange(): return lax.ppermute(value, 'seq', [(i, i ^ distance) for i in range(count)])  28.4 us
    ppermute x27, waiting for transfers between devices, swapped(): lax.ppermute(value, 'state', [(i, i ^ distance) for i in range(count)])  25.7 us
    pallas_call x2, Pallas kernels, back(): pl.pallas_call(functools.partial(back_kernel, len(earlier)), grid_spec=pl...  21.8 us
    dot_general x3, matrix products, dot(): return lax.dot_general(a, b, (dims, ((), ())), preferred_element_type=F32)  17.7 us
    pallas_call x1, Pallas kernels, wide_grads(): pl.pallas_call(functools.partial(wide_kernel, high), grid_spec=pltpu.Pref...  12.7 us
  transfers between devices with their start and end apart: 37, of which 14 were waited for; matrix products, arithmetic and copies ran while one was open for 13% of the time, Pallas kernels for 47%

profile of v5, /device:TPU:0, one launch (start us, length us, event | category | flops | bytes accessed | tf_op | source)
XLA Modules:
  0.0 364.2 jit_solution(13215703592724447184)
XLA Ops:
  0.6 3.0 collective-permute-start.1
  8.4 4.9 %fusion.12.inner = bf16[512,2048]{1,0:T(8,128)(2,1)S(1)} fusion(bf16[512,1024]{1,0:T(8,128)(2,1)S(1)} %fusion.16.refs_12_.refs_0_, bf16[1024,4096]{1,0:T(8,128)(2,1)} %param.17), kind=kOutput, calls=%fused_computation.15 | convolution fusion | flops 2148532224 | bytes 7340032 | tf_op jit(solution)/shard_map/dot_general | solution.py:1006
  14.7 3.8 %collective-permute-start = (bf16[8,2048]{1,0:T(8,128)(2,1)S(1)}, bf16[8,2048]{1,0:T(8,128)(2,1)S(1)}, u32[]{:S(2)}, u32[]{:S(2)}) collective-permute-start(bf16[8,2048]{1,0:T(8,128)(2,1)S(1)} %get-tuple-element.224), channel_id=1, source_target_pairs={{0,1},{1,2},{2,3},{4,5},{5,6},{6,7},{8,9},{9,10},{10,11},{12,13},{... | collective-permute-start | bytes 98312 | tf_op jit(solution)/shard_map/ppermute | solution.py:29
  18.6 4.3 %fusion.2.gate = f32[512,2048]{1,0:T(8,128)} fusion(bf16[512,1024]{1,0:T(8,128)(2,1)S(1)} %fusion.16.refs_12_.refs_0_, bf16[1024,4096]{1,0:T(8,128)(2,1)S(1)} %bitcast.137), kind=kOutput, calls=%fused_computation.2 | convolution fusion | flops 2147483648 | bytes 9437184 | tf_op jit(solution)/shard_map/dot_general | solution.py:1008
  24.9 7.0 %fusion.50.grad_gated = f32[512,2048]{1,0:T(8,128)} fusion(bf16[512,1024]{1,0:T(8,128)(2,1)} %fusion.15.refs_8_, bf16[2048,1024]{1,0:T(8,128)(2,1)} %param.25), kind=kOutput, calls=%fused_computation.110 | convolution fusion | flops 2147483648 | bytes 9437184 | tf_op jit(solution)/shard_map/dot_general | solution.py:965
  33.9 7.7 %front.1 = (f32[512,2048]{1,0:T(8,128)}, f32[512,128]{1,0:T(8,128)}) custom-call(bf16[512,2048]{1,0:T(8,128)(2,1)} %copy-done, bf16[8,2048]{1,0:T(8,128)(2,1)} %copy-done.17, f32[4,2048]{1,0:T(4,128)} %conv_w.5, f32[1,2048]{1,0:T(1,128)} %bitcast.122, bf16[128,2048]{1,0:T(8,128)(2,1)} %pad.4.xproj), custom_call_target="tpu_custom_call" | custom-call | flops 8 | bytes 1024 | tf_op jit(solution)/shard_map/front/pallas_call | solution.py:702
  44.0 37.9 %ends.1 = (f32[512,2048]{1,0:T(8,128)}, f32[8,2048]{1,0:T(8,128)}, f32[16,2048]{1,0:T(8,128)}, f32[16,2048]{1,0:T(8,128)}, f32[32,512]{1,0:T(8,128)}, /*index=5*...) custom-call(s32[2]{0:T(128)} %get-tuple-element.250.live, f32[512,128]{1,0:T(8,128)} %get-tuple-element.118.proj, ...), custom_call_target="tpu_custom_call" | custom-call | flops 40 | bytes 1024 | tf_op jit(solution)/shard_map/ends/pallas_call | solution.py:727
  86.4 3.5 collective-permute-done.6
  90.0 3.1 collective-permute-done.7
  98.1 51.1 %scan.2 = (bf16[512,2048]{1,0:T(8,128)(2,1)}, bf16[512,2048]{1,0:T(8,128)(2,1)}, f32[512,2048]{1,0:T(8,128)}, f32[16,2048]{1,0:T(8,128)}, f32[8,2048]{1,0:T(8,12...) custom-call(s32[2]{0:T(128)} %pad_add_fusion.2.order, ...), custom_call_target="tpu_custom_call" | custom-call | flops 50 | bytes 1024 | tf_op jit(solution)/shard_map/scan/pallas_call | solution.py:788
  153.0 51.1 %scan.3 = (bf16[512,2048]{1,0:T(8,128)(2,1)}, bf16[512,2048]{1,0:T(8,128)(2,1)}, f32[512,2048]{1,0:T(8,128)}, f32[16,2048]{1,0:T(8,128)}, f32[8,2048]{1,0:T(8,12...) custom-call(s32[2]{0:T(128)} %get-tuple-element.249.order, ...), custom_call_target="tpu_custom_call", output_to_operand_aliasing={{0}: (12, {}), {1}: (13, {}), {2}: (14, {}), {3}: (15, {}),... | custom-call | flops 50 | bytes 1024 | tf_op jit(solution)/shard_map/scan/pallas_call | solution.py:788
  208.6 5.6 %collective-permute-done.15.ahead = f32[8,2048]{1,0:T(8,128)S(1)} collective-permute-done((f32[8,2048]{1,0:T(8,128)S(1)}, f32[8,2048]{1,0:T(8,128)S(1)}, u32[]{:S(2)}, u32[]{:S(2)}) %collective-permute-start.15) | collective-permute-done | bytes 65568 | tf_op jit(solution)/shard_map/ppermute | solution.py:29
  214.9 10.9 %back.2 = (bf16[512,2048]{1,0:T(8,128)(2,1)}, bf16[4,12,64,128]{3,2,1,0:T(8,128)(2,1)}, bf16[576,512]{1,0:T(8,128)(2,1)}, bf16[576,512]{1,0:T(8,128)(2,1)}) custom-call(s32[3]{0:T(128)} %get-tuple-element.251.order, bf16[512,128]{1,0:T(8,128)(2,1)} %copy-done.12, bf16[128,2048]{1,0:T(8,128)(2,1)} %pad.4.xproj, f32[512,2048]{1,0:T(8,128)} %get-tuple-element.141.mix_grad, ...), custom_call_target="tpu_custom_call" | custom-call | flops 18 | bytes 1024 | tf_op jit(solution)/shard_map/back/pallas_call | solution.py:846
  225.7 2.5 collective-permute-start.17
  229.9 10.9 %back.3 = (bf16[512,2048]{1,0:T(8,128)(2,1)}, bf16[4,12,64,128]{3,2,1,0:T(8,128)(2,1)}, bf16[576,512]{1,0:T(8,128)(2,1)}, bf16[576,512]{1,0:T(8,128)(2,1)}) custom-call(s32[3]{0:T(128)} %get-tuple-element.252.order, bf16[512,128]{1,0:T(8,128)(2,1)} %copy-done.12, bf16[128,2048]{1,0:T(8,128)(2,1)} %pad.4.xproj, ...), custom_call_target="tpu_custom_call", output_to_operand_aliasing={{0}: (13, {}), {1}: (14, {})} | custom-call | flops 18 | bytes 1024 | tf_op jit(solution)/shard_map/back/pallas_call | solution.py:846
  240.8 6.5 %collective-permute-done.17.refs_5_ = bf16[576,512]{1,0:T(8,128)(2,1)S(1)} collective-permute-done((bf16[576,512]{1,0:T(8,128)(2,1)}, bf16[576,512]{1,0:T(8,128)(2,1)S(1)}, u32[]{:S(2)}, u32[]{:S(2)}) %collective-permute-start.17) | collective-permute-done | bytes 589856 | tf_op jit(solution)/shard_map/ppermute | solution.py:23
  247.3 12.7 %wide.1 = (f32[1024,512]{1,0:T(8,128)}, f32[1024,512]{1,0:T(8,128)}) custom-call(s32[9]{0:T(128)} %stack.49.at, bf16[512,1024]{1,0:T(8,128)(2,1)} %get-tuple-element.167.refs_0_.refs_4_, bf16[512,1024]{1,0:T(8,128)(2,1)} %collective-permute-done.13.refs_1_.refs_5_, bf16[512,1024]{1,0:T(8,128)(2,1)} %collective-permute-done.14.refs_2_.refs_6_, ...), custom_call_target="tpu_custom_call" | custom-call | flops 10 | bytes 1024 | tf_op jit(solution)/shard_map/wide/pallas_call | solution.py:897
  260.1 4.4 %collective-permute-done.19 = f32[1024,512]{1,0:T(8,128)S(1)} collective-permute-done((f32[1024,512]{1,0:T(8,128)}, f32[1024,512]{1,0:T(8,128)S(1)}, u32[]{:S(2)}, u32[]{:S(2)}) %collective-permute-start.19) | collective-permute-done | bytes 2097184 | tf_op jit(solution)/shard_map/ppermute | solution.py:54
  265.8 2.8 add.187
  276.4 6.4 %collective-permute-done.20 = bf16[512,512]{1,0:T(8,128)(2,1)} collective-permute-done((bf16[512,512]{1,0:T(8,128)(2,1)S(1)}, bf16[512,512]{1,0:T(8,128)(2,1)}, u32[]{:S(2)}, u32[]{:S(2)}) %collective-permute-start.20) | collective-permute-done | bytes 524320 | tf_op jit(solution)/shard_map/ppermute | solution.py:54
  284.1 2.6 collective-permute-start.21
  286.7 4.5 %fusion = f32[512,1024]{1,0:T(8,128)S(1)} fusion(bf16[512,2048]{1,0:T(8,128)(2,1)S(1)} %copy-done.11, bf16[1024,4096]{1,0:T(8,128)(2,1)} %param.17), kind=kOutput, calls=%fused_computation | convolution fusion | flops 2147483648 | bytes 8388608 | tf_op jit(solution)/shard_map/dot_general | solution.py:965
  291.3 6.2 %fusion.20 = (f32[1024]{0:T(1024)S(1)}, f32[512]{0:T(512)S(1)}, f32[512,1024]{1,0:T(8,128)}) fusion(bf16[512,1024]{1,0:T(8,128)(2,1)S(1)} %copy-done.2, f32[512]{0:T(512)S(1)} %add_rsqrt_fusion, f32[1024]{0:T(1024)S(1)} %copy-done.30, f32[512,1024]{1,0:T(8,128)S(1)} %fusion, bf16[512,2048]{1,0:T(8,128)(2,1)S(1)} %copy-done.7, bf16[1024,4096]{1,0:T(8,128)(2,1)} %param.17), kind=kOutput, calls=%fused_computation.23 | convolution fusion | flops 2151676416 | bytes 11546624 | tf_op jit(solution)/shard_map/dot_general | solution.py:965
  298.3 8.7 %inner.1 = (f32[688,512]{1,0:T(8,128)}, f32[688,512]{1,0:T(8,128)}) custom-call(s32[9]{0:T(128)} %stack.49.at, bf16[512,1024]{1,0:T(8,128)(2,1)} %copy-done.1, bf16[512,1024]{1,0:T(8,128)(2,1)} %collective-permute-done.4.refs_13_.refs_1_, bf16[512,1024]{1,0:T(8,128)(2,1)} %collective-permute-done.5.refs_14_.refs_2_, ...), custom_call_target="tpu_custom_call" | custom-call | flops 5 | bytes 1024 | tf_op jit(solution)/shard_map/inner/pallas_call | solution.py:926
  308.0 2.4 collective-permute-done.26
  314.4 3.3 fusion.22
  318.4 7.3 %collective-permute-done.27 = bf16[416,512]{1,0:T(8,128)(2,1)S(1)} collective-permute-done((bf16[416,512]{1,0:T(8,128)(2,1)S(1)}, bf16[416,512]{1,0:T(8,128)(2,1)S(1)}, u32[]{:S(2)}, u32[]{:S(2)}) %collective-permute-start.27) | collective-permute-done | bytes 426016 | tf_op jit(solution)/shard_map/ppermute | solution.py:54
  329.7 2.4 collective-permute-start.31
  333.4 7.9 %collective-permute-done.33 = bf16[256,512]{1,0:T(8,128)(2,1)S(1)} collective-permute-done((bf16[256,512]{1,0:T(8,128)(2,1)S(1)}, bf16[256,512]{1,0:T(8,128)(2,1)S(1)}, u32[]{:S(2)}, u32[]{:S(2)}) %collective-permute-start.33) | collective-permute-done | bytes 262176 | tf_op jit(solution)/shard_map/ppermute | solution.py:54
  349.9 4.5 %collective-permute-done.34.refs_5_ = bf16[288,512]{1,0:T(8,128)(2,1)S(1)} collective-permute-done((bf16[288,512]{1,0:T(8,128)(2,1)S(1)}, bf16[288,512]{1,0:T(8,128)(2,1)S(1)}, u32[]{:S(2)}, u32[]{:S(2)}) %collective-permute-start.34) | collective-permute-done | bytes 294944 | tf_op jit(solution)/shard_map/ppermute | solution.py:23
  354.4 4.4 %collective-permute-done.35.refs_6_ = bf16[288,512]{1,0:T(8,128)(2,1)S(1)} collective-permute-done((bf16[288,512]{1,0:T(8,128)(2,1)S(1)}, bf16[288,512]{1,0:T(8,128)(2,1)S(1)}, u32[]{:S(2)}, u32[]{:S(2)}) %collective-permute-start.35) | collective-permute-done | bytes 294944 | tf_op jit(solution)/shard_map/ppermute | solution.py:23
  360.3 3.7 %assemble.1 = (f32[128,4096]{1,0:T(8,128)}, f32[256,1024]{1,0:T(8,128)}, f32[96,256]{1,0:T(8,128)}, f32[64,256]{1,0:T(8,128)}, f32[4,2048]{1,0:T(4,128)}, /*inde...) custom-call(s32[9]{0:T(128)} %stack.49.at, ...), custom_call_target="tpu_custom_call" | custom-call | flops 4 | bytes 1024 | tf_op jit(solution)/shard_map/assemble/pallas_call | solution.py:952
  (183 shorter events, 63.8 us)
Async XLA Ops:
  0.6 42.6 %collective-permute-start.1 = (f32[4,2048]{1,0:T(4,128)}, f32[4,2048]{1,0:T(4,128)S(1)}, u32[]{:S(2)}, u32[]{:S(2)}) collective-permute-start(f32[4,2048]{1,0:T(4,128)} %param.23), channel_id=1, source_target_pairs={{0,1},{1,0},{2,3},{3,2},{4,5},{5,4},{6,7},{7,6},{8,9},{9,8},{10,11... | collective-permute-start | bytes 98312 | tf_op jit(solution)/shard_map/ppermute | solution.py:23
  3.6 39.6 %collective-permute-start.2 = (f32[4,2048]{1,0:T(4,128)}, f32[4,2048]{1,0:T(4,128)S(1)}, u32[]{:S(2)}, u32[]{:S(2)}) collective-permute-start(f32[4,2048]{1,0:T(4,128)} %param.23), channel_id=1, source_target_pairs={{0,2},{1,3},{2,0},{3,1},{4,6},{5,7},{6,4},{7,5},{8,10},{9,11},{10,... | collective-permute-start | bytes 98312 | tf_op jit(solution)/shard_map/ppermute | solution.py:23
  5.2 38.1 %collective-permute-start.3 = (f32[4,2048]{1,0:T(4,128)}, f32[4,2048]{1,0:T(4,128)S(1)}, u32[]{:S(2)}, u32[]{:S(2)}) collective-permute-start(f32[4,2048]{1,0:T(4,128)} %param.23), channel_id=1, source_target_pairs={{0,3},{1,2},{2,1},{3,0},{4,7},{5,6},{6,5},{7,4},{8,11},{9,10},{10,... | collective-permute-start | bytes 98312 | tf_op jit(solution)/shard_map/ppermute | solution.py:23
  14.7 18.6 %collective-permute-start = (bf16[8,2048]{1,0:T(8,128)(2,1)S(1)}, bf16[8,2048]{1,0:T(8,128)(2,1)S(1)}, u32[]{:S(2)}, u32[]{:S(2)}) collective-permute-start(bf16[8,2048]{1,0:T(8,128)(2,1)S(1)} %get-tuple-element.224), channel_id=1, source_target_pairs={{0,1},{1,2},{2,3},{4,5},{5,6},{6,7},{8,9},{9,10},{10,11},{12,13},{... | collective-permute-start | bytes 98312 | tf_op jit(solution)/shard_map/ppermute | solution.py:29
  41.6 40.3 %collective-permute-start.4 = (bf16[512,1024]{1,0:T(8,128)(2,1)}, bf16[512,1024]{1,0:T(8,128)(2,1)}, u32[]{:S(2)}, u32[]{:S(2)}) collective-permute-start(bf16[512,1024]{1,0:T(8,128)(2,1)} %copy-done.1), channel_id=1, source_target_pairs={{0,1},{1,0},{2,3},{3,2},{4,5},{5,4},{6,7},{7,6},{8,9},{9,8},{10,11... | collective-permute-start | bytes 3145736 | tf_op jit(solution)/shard_map/ppermute | solution.py:23
  43.1 38.8 %collective-permute-start.5 = (bf16[512,1024]{1,0:T(8,128)(2,1)}, bf16[512,1024]{1,0:T(8,128)(2,1)}, u32[]{:S(2)}, u32[]{:S(2)}) collective-permute-start(bf16[512,1024]{1,0:T(8,128)(2,1)} %copy-done.1), channel_id=1, source_target_pairs={{0,2},{1,3},{2,0},{3,1},{4,6},{5,7},{6,4},{7,5},{8,10},{9,11},{10,... | collective-permute-start | bytes 3145736 | tf_op jit(solution)/shard_map/ppermute | solution.py:23
  83.9 9.1 %collective-permute-start.7 = (f32[24,2048]{1,0:T(8,128)}, f32[24,2048]{1,0:T(8,128)S(1)}, u32[]{:S(2)}, u32[]{:S(2)}) collective-permute-start(f32[24,2048]{1,0:T(8,128)} %get-tuple-element.130), channel_id=1, source_target_pairs={{0,2},{1,3},{2,0},{3,1},{4,6},{5,7},{6,4},{7,5},{8,10},{9,11},{10,... | collective-permute-start | bytes 589832 | tf_op jit(solution)/shard_map/ppermute | solution.py:23
  84.4 8.6 %collective-permute-start.8 = (f32[24,2048]{1,0:T(8,128)}, f32[24,2048]{1,0:T(8,128)S(1)}, u32[]{:S(2)}, u32[]{:S(2)}) collective-permute-start(f32[24,2048]{1,0:T(8,128)} %get-tuple-element.131), channel_id=1, source_target_pairs={{0,3},{1,2},{2,1},{3,0},{4,7},{5,6},{6,5},{7,4},{8,11},{9,10},{10,... | collective-permute-start | bytes 589832 | tf_op jit(solution)/shard_map/ppermute | solution.py:23
  94.0 57.3 %collective-permute-start.10 = (bf16[512,1024]{1,0:T(8,128)(2,1)}, bf16[512,1024]{1,0:T(8,128)(2,1)}, u32[]{:S(2)}, u32[]{:S(2)}) collective-permute-start(bf16[512,1024]{1,0:T(8,128)(2,1)} %fusion.15.refs_8_), channel_id=1, source_target_pairs={{0,2},{1,3},{2,0},{3,1},{4,6},{5,7},{6,4},{7,5},{8,10},{9,11},{10,... | collective-permute-start | bytes 3145736 | tf_op jit(solution)/shard_map/ppermute | solution.py:23
  95.1 56.2 %collective-permute-start.11 = (bf16[512,1024]{1,0:T(8,128)(2,1)}, bf16[512,1024]{1,0:T(8,128)(2,1)}, u32[]{:S(2)}, u32[]{:S(2)}) collective-permute-start(bf16[512,1024]{1,0:T(8,128)(2,1)} %fusion.15.refs_8_), channel_id=1, source_target_pairs={{0,3},{1,2},{2,1},{3,0},{4,7},{5,6},{6,5},{7,4},{8,11},{9,10},{10,... | collective-permute-start | bytes 3145736 | tf_op jit(solution)/shard_map/ppermute | solution.py:23
  96.1 55.2 %collective-permute-start.9 = (bf16[512,1024]{1,0:T(8,128)(2,1)}, bf16[512,1024]{1,0:T(8,128)(2,1)}, u32[]{:S(2)}, u32[]{:S(2)}) collective-permute-start(bf16[512,1024]{1,0:T(8,128)(2,1)} %fusion.15.refs_8_), channel_id=1, source_target_pairs={{0,1},{1,0},{2,3},{3,2},{4,5},{5,4},{6,7},{7,6},{8,9},{9,8},{10,11... | collective-permute-start | bytes 3145736 | tf_op jit(solution)/shard_map/ppermute | solution.py:23
  149.2 56.9 %collective-permute-start.13 = (bf16[512,1024]{1,0:T(8,128)(2,1)}, bf16[512,1024]{1,0:T(8,128)(2,1)}, u32[]{:S(2)}, u32[]{:S(2)}) collective-permute-start(bf16[512,1024]{1,0:T(8,128)(2,1)} %get-tuple-element.145), channel_id=1, source_target_pairs={{0,1},{1,0},{2,3},{3,2},{4,5},{5,4},{6,7},{7,6},{8,9},{9,8},{10,11... | collective-permute-start | bytes 3145736 | tf_op jit(solution)/shard_map/ppermute | solution.py:23
  149.9 56.2 %collective-permute-start.14 = (bf16[512,1024]{1,0:T(8,128)(2,1)}, bf16[512,1024]{1,0:T(8,128)(2,1)}, u32[]{:S(2)}, u32[]{:S(2)}) collective-permute-start(bf16[512,1024]{1,0:T(8,128)(2,1)} %get-tuple-element.146), channel_id=1, source_target_pairs={{0,2},{1,3},{2,0},{3,1},{4,6},{5,7},{6,4},{7,5},{8,10},{9,11},{10,... | collective-permute-start | bytes 3145736 | tf_op jit(solution)/shard_map/ppermute | solution.py:23
  151.3 54.8 %collective-permute-start.12 = (bf16[512,1024]{1,0:T(8,128)(2,1)}, bf16[512,1024]{1,0:T(8,128)(2,1)}, u32[]{:S(2)}, u32[]{:S(2)}) collective-permute-start(bf16[512,1024]{1,0:T(8,128)(2,1)} %copy-done.1), channel_id=1, source_target_pairs={{0,3},{1,2},{2,1},{3,0},{4,7},{5,6},{6,5},{7,4},{8,11},{9,10},{10,... | collective-permute-start | bytes 3145736 | tf_op jit(solution)/shard_map/ppermute | solution.py:23
  214.3 33.1 %collective-permute-start.16 = (bf16[512,1024]{1,0:T(8,128)(2,1)}, bf16[512,1024]{1,0:T(8,128)(2,1)}, u32[]{:S(2)}, u32[]{:S(2)}) collective-permute-start(bf16[512,1024]{1,0:T(8,128)(2,1)} %get-tuple-element.157), channel_id=1, source_target_pairs={{0,3},{1,2},{2,1},{3,0},{4,7},{5,6},{6,5},{7,4},{8,11},{9,10},{10,... | collective-permute-start | bytes 3145736 | tf_op jit(solution)/shard_map/ppermute | solution.py:23
  225.7 21.6 %collective-permute-start.17 = (bf16[576,512]{1,0:T(8,128)(2,1)}, bf16[576,512]{1,0:T(8,128)(2,1)S(1)}, u32[]{:S(2)}, u32[]{:S(2)}) collective-permute-start(bf16[576,512]{1,0:T(8,128)(2,1)} %get-tuple-element.162), channel_id=1, source_target_pairs={{0,1},{1,0},{2,3},{3,2},{4,5},{5,4},{6,7},{7,6},{8,9},{9,8},{10,11... | collective-permute-start | bytes 1769480 | tf_op jit(solution)/shard_map/ppermute | solution.py:23
  228.2 19.1 %collective-permute-start.18 = (bf16[576,512]{1,0:T(8,128)(2,1)}, bf16[576,512]{1,0:T(8,128)(2,1)}, u32[]{:S(2)}, u32[]{:S(2)}) collective-permute-start(bf16[576,512]{1,0:T(8,128)(2,1)} %get-tuple-element.163), channel_id=1, source_target_pairs={{0,2},{1,3},{2,0},{3,1},{4,6},{5,7},{6,4},{7,5},{8,10},{9,11},{10,... | collective-permute-start | bytes 1769480 | tf_op jit(solution)/shard_map/ppermute | solution.py:23
  268.7 14.1 %collective-permute-start.20 = (bf16[512,512]{1,0:T(8,128)(2,1)S(1)}, bf16[512,512]{1,0:T(8,128)(2,1)}, u32[]{:S(2)}, u32[]{:S(2)}) collective-permute-start(bf16[512,512]{1,0:T(8,128)(2,1)S(1)} %bitcast.116), channel_id=1, source_target_pairs={{0,8},{4,12},{8,0},{12,4},{16,24},{20,28},{24,16},{28,20},{1,9},{5... | collective-permute-start | bytes 1572872 | tf_op jit(solution)/shard_map/ppermute | solution.py:54
  271.2 27.1 %collective-permute-start.23 = (bf16[12,64,128]{2,1,0:T(8,128)(2,1)}, bf16[12,64,128]{2,1,0:T(8,128)(2,1)}, u32[]{:S(2)}, u32[]{:S(2)}) collective-permute-start(bf16[12,64,128]{2,1,0:T(8,128)(2,1)} %get-tuple-element.234), channel_id=1, source_target_pairs={{0,1},{1,0},{2,3},{3,2},{4,5},{5,4},{6,7},{7,6},{8,9},{9,8},{10,11... | collective-permute-start | bytes 589832 | tf_op jit(solution)/shard_map/ppermute | solution.py:23
  272.9 25.3 %collective-permute-start.24 = (bf16[12,64,128]{2,1,0:T(8,128)(2,1)}, bf16[12,64,128]{2,1,0:T(8,128)(2,1)}, u32[]{:S(2)}, u32[]{:S(2)}) collective-permute-start(bf16[12,64,128]{2,1,0:T(8,128)(2,1)} %get-tuple-element.233), channel_id=1, source_target_pairs={{0,2},{1,3},{2,0},{3,1},{4,6},{5,7},{6,4},{7,5},{8,10},{9,11},{10,... | collective-permute-start | bytes 589832 | tf_op jit(solution)/shard_map/ppermute | solution.py:23
  273.5 24.8 %collective-permute-start.25 = (bf16[12,64,128]{2,1,0:T(8,128)(2,1)}, bf16[12,64,128]{2,1,0:T(8,128)(2,1)}, u32[]{:S(2)}, u32[]{:S(2)}) collective-permute-start(bf16[12,64,128]{2,1,0:T(8,128)(2,1)} %get-tuple-element.232), channel_id=1, source_target_pairs={{0,3},{1,2},{2,1},{3,0},{4,7},{5,6},{6,5},{7,4},{8,11},{9,10},{10,... | collective-permute-start | bytes 589832 | tf_op jit(solution)/shard_map/ppermute | solution.py:23
  274.7 23.6 %collective-permute-start.22 = (bf16[576,512]{1,0:T(8,128)(2,1)}, bf16[576,512]{1,0:T(8,128)(2,1)}, u32[]{:S(2)}, u32[]{:S(2)}) collective-permute-start(bf16[576,512]{1,0:T(8,128)(2,1)} %get-tuple-element.190), channel_id=1, source_target_pairs={{0,3},{1,2},{2,1},{3,0},{4,7},{5,6},{6,5},{7,4},{8,11},{9,10},{10,... | collective-permute-start | bytes 1769480 | tf_op jit(solution)/shard_map/ppermute | solution.py:23
  284.1 14.1 %collective-permute-start.21 = (bf16[256,512]{1,0:T(8,128)(2,1)S(1)}, bf16[256,512]{1,0:T(8,128)(2,1)S(1)}, u32[]{:S(2)}, u32[]{:S(2)}) collective-permute-start(bf16[256,512]{1,0:T(8,128)(2,1)S(1)} %fusion.26), channel_id=1, source_target_pairs={{0,16},{4,20},{8,24},{12,28},{16,0},{20,4},{24,8},{28,12},{1,17},{... | collective-permute-start | bytes 786440 | tf_op jit(solution)/shard_map/ppermute | solution.py:54
  307.0 10.7 %collective-permute-start.28 = (bf16[128,512]{1,0:T(8,128)(2,1)S(1)}, bf16[128,512]{1,0:T(8,128)(2,1)S(1)}, u32[]{:S(2)}, u32[]{:S(2)}) collective-permute-start(bf16[128,512]{1,0:T(8,128)(2,1)S(1)} %get-tuple-element.240), channel_id=1, source_target_pairs={{0,0},{1,1},{2,2},{3,3},{4,5},{5,4},{6,7},{7,6},{8,10},{9,11},{10,... | collective-permute-start | bytes 393224 | tf_op jit(solution)/shard_map/ppermute | solution.py:94
  312.4 13.3 %collective-permute-start.27 = (bf16[416,512]{1,0:T(8,128)(2,1)S(1)}, bf16[416,512]{1,0:T(8,128)(2,1)S(1)}, u32[]{:S(2)}, u32[]{:S(2)}) collective-permute-start(bf16[416,512]{1,0:T(8,128)(2,1)S(1)} %pad_maximum_fusion.1), channel_id=1, source_target_pairs={{0,8},{4,12},{8,0},{12,4},{16,24},{20,28},{24,16},{28,20},{1,9},{5... | collective-permute-start | bytes 1277960 | tf_op jit(solution)/shard_map/ppermute | solution.py:54
  326.0 15.3 %collective-permute-start.33 = (bf16[256,512]{1,0:T(8,128)(2,1)S(1)}, bf16[256,512]{1,0:T(8,128)(2,1)S(1)}, u32[]{:S(2)}, u32[]{:S(2)}) collective-permute-start(bf16[256,512]{1,0:T(8,128)(2,1)S(1)} %pad_maximum_fusion.4), channel_id=1, source_target_pairs={{0,16},{4,20},{8,24},{12,28},{16,0},{20,4},{24,8},{28,12},{1,17},{... | collective-permute-start | bytes 786440 | tf_op jit(solution)/shard_map/ppermute | solution.py:54
  328.4 13.0 %collective-permute-start.30 = (bf16[256,512]{1,0:T(8,128)(2,1)S(1)}, bf16[256,512]{1,0:T(8,128)(2,1)S(1)}, u32[]{:S(2)}, u32[]{:S(2)}) collective-permute-start(bf16[256,512]{1,0:T(8,128)(2,1)S(1)} %pad_maximum_fusion.3.refs_0_), channel_id=1, source_target_pairs={{0,1},{1,0},{2,3},{3,2},{4,5},{5,4},{6,7},{7,6},{8,9},{9,8},{10,11... | collective-permute-start | bytes 786440 | tf_op jit(solution)/shard_map/ppermute | solution.py:23
  329.7 12.7 %collective-permute-start.31 = (bf16[256,512]{1,0:T(8,128)(2,1)S(1)}, bf16[256,512]{1,0:T(8,128)(2,1)S(1)}, u32[]{:S(2)}, u32[]{:S(2)}) collective-permute-start(bf16[256,512]{1,0:T(8,128)(2,1)S(1)} %pad_maximum_fusion.3.refs_0_), channel_id=1, source_target_pairs={{0,2},{1,3},{2,0},{3,1},{4,6},{5,7},{6,4},{7,5},{8,10},{9,11},{10,... | collective-permute-start | bytes 786440 | tf_op jit(solution)/shard_map/ppermute | solution.py:23
  332.0 12.2 %collective-permute-start.32 = (bf16[256,512]{1,0:T(8,128)(2,1)S(1)}, bf16[256,512]{1,0:T(8,128)(2,1)S(1)}, u32[]{:S(2)}, u32[]{:S(2)}) collective-permute-start(bf16[256,512]{1,0:T(8,128)(2,1)S(1)} %pad_maximum_fusion.3.refs_0_), channel_id=1, source_target_pairs={{0,3},{1,2},{2,1},{3,0},{4,7},{5,6},{6,5},{7,4},{8,11},{9,10},{10,... | collective-permute-start | bytes 786440 | tf_op jit(solution)/shard_map/ppermute | solution.py:23
  344.4 10.0 %collective-permute-start.34 = (bf16[288,512]{1,0:T(8,128)(2,1)S(1)}, bf16[288,512]{1,0:T(8,128)(2,1)S(1)}, u32[]{:S(2)}, u32[]{:S(2)}) collective-permute-start(bf16[288,512]{1,0:T(8,128)(2,1)S(1)} %pad_maximum_fusion.2.refs_4_), channel_id=1, source_target_pairs={{0,1},{1,0},{2,3},{3,2},{4,5},{5,4},{6,7},{7,6},{8,9},{9,8},{10,11... | collective-permute-start | bytes 884744 | tf_op jit(solution)/shard_map/ppermute | solution.py:23
  345.7 13.1 %collective-permute-start.35 = (bf16[288,512]{1,0:T(8,128)(2,1)S(1)}, bf16[288,512]{1,0:T(8,128)(2,1)S(1)}, u32[]{:S(2)}, u32[]{:S(2)}) collective-permute-start(bf16[288,512]{1,0:T(8,128)(2,1)S(1)} %pad_maximum_fusion.2.refs_4_), channel_id=1, source_target_pairs={{0,2},{1,3},{2,0},{3,1},{4,6},{5,7},{6,4},{7,5},{8,10},{9,11},{10,... | collective-permute-start | bytes 884744 | tf_op jit(solution)/shard_map/ppermute | solution.py:23
  347.4 12.8 %collective-permute-start.36 = (bf16[288,512]{1,0:T(8,128)(2,1)S(1)}, bf16[288,512]{1,0:T(8,128)(2,1)}, u32[]{:S(2)}, u32[]{:S(2)}) collective-permute-start(bf16[288,512]{1,0:T(8,128)(2,1)S(1)} %pad_maximum_fusion.2.refs_4_), channel_id=1, source_target_pairs={{0,3},{1,2},{2,1},{3,0},{4,7},{5,6},{6,5},{7,4},{8,11},{9,10},{10,... | collective-permute-start | bytes 884744 | tf_op jit(solution)/shard_map/ppermute | solution.py:23
  (39 other events, 507.2 us)

commit v6 on v5

--- a/solution.py
+++ b/solution.py
@@ -189,13 +189,17 @@
     lax.fori_loop(0, rows // 32, move, 0)
 
 
-def front_kernel(inner, before, conv_w, conv_b, xproj, mixed_out, proj_out, ext, low):
+def front_kernel(
+    normed, halo, in_w, conv_w, conv_b, xproj, mixed_out, proj_out, inner, before, ext, low
+):
     rows = inner.shape[0]
 
     @pl.when(pl.program_id(0) == 0)
     def _():
         proj_out[...] = jnp.zeros_like(proj_out)
 
+    inner[...] = jnp.dot(normed[...], in_w[...], preferred_element_type=F32).astype(BF16)
+    before[...] = jnp.dot(halo[...], in_w[...], preferred_element_type=F32).astype(BF16)
     widen_rows(ext, before, inner)
     weight = conv_w[...]
     bias = conv_b[...]
@@ -213,8 +217,8 @@
 
 
 def ends_kernel(
-    live, proj, dtproj, dt_b, mixed, gate, grad_gated, rate,
-    step_out, stat_out, state_out, grad_out, cols_out, *rest,
+    live, proj, dtproj, dt_b, mixed, normed, gate_w, masked, out_w, rate,
+    step_out, gate, grad_gated, stat_out, state_out, grad_out, cols_out, *rest,
 ):
     rows, width = mixed.shape
     states = rate.shape[0]
@@ -228,6 +232,8 @@
         rank_low[...] = proj[:, :rank].astype(BF16)
         fill_lanes(lanes, cols_out, rows)
 
+    gate[...] = jnp.dot(normed[...], gate_w[...], preferred_element_type=F32)
+    grad_gated[...] = dot(masked[...], out_w[...], ((1,), (1,)))
     raised_all[...] = dt_b[...] + jnp.dot(rank_low[...], dtproj[...], preferred_element_type=F32)
     count = ENDS_ROWS
     zero8 = jnp.zeros((8, width), F32)
@@ -279,9 +285,10 @@
     skipped, order, cols, proj, rate, step, mixed, gate, grad_gated, state_in, grad_in, skip, dtproj,
     *rest,
 ):
+    rank_before, bc_before = rest[skipped - 2 : skipped] if skipped else (None, None)
     rest = rest[skipped:]
-    gated_out, gate_out, mix_out, rate_out, vec_out, dtproj_out, rank_out, bc_out = rest[:8]
-    sends = rest[8:-11]
+    gated_out, gate_out, mix_out, rate_out, vec_out, dtproj_out, rank_out, bc_out, proj_grad = rest[:9]
+    sends = rest[9:-11]
     (
         lanes, held, b_sum, c_sum, drive, y_sum, decay_sum, source_sum, raised_low, rank_low, grad_y
     ) = rest[-11:]
@@ -298,7 +305,7 @@
         rank_low[...] = proj[:, :rank].astype(BF16)
         b_sum[...] = jnp.zeros_like(b_sum)
         c_sum[...] = jnp.zeros_like(c_sum)
-        rank_out[...] = jnp.zeros_like(rank_out)
+        rank_out[...] = rank_before[...] if skipped else jnp.zeros_like(rank_out)
 
     rates = rate[...]
     groups = rows // 8
@@ -424,6 +431,12 @@
             return 0
 
         lax.fori_loop(0, rows // 128, tile, 0)
+        if skipped:
+            bc_out[...] += bc_before[...]
+        turned = jnp.transpose(bc_out[...])
+        proj_grad[...] = jnp.concatenate(
+            [rank_out[...], turned, jnp.zeros((rows, 128 - rank - 2 * states), F32)], axis=1
+        ).astype(BF16)
 
 
 def back_kernel(
@@ -693,8 +706,9 @@
 LIMIT = pltpu.CompilerParams(vmem_limit_bytes=63 << 20)
 
 
-def front(inner, before, conv_weight, conv_bias, xproj, width):
-    rows, channels = inner.shape
+def front(normed, halo, in_weight, conv_weight, conv_bias, xproj, width):
+    rows, features = normed.shape
+    channels = in_weight.shape[1] // 2
 
     def part(height):
         return pl.BlockSpec((height, width), lambda q: (0, q))
@@ -703,20 +717,24 @@
         front_kernel,
         grid=(channels // width,),
         in_specs=[
-            part(rows), part(8), part(conv_weight.shape[0]), part(1),
+            whole(normed.shape), whole(halo.shape), part(features), part(conv_weight.shape[0]), part(1),
             part(xproj.shape[0]),
         ],
-        out_specs=[part(rows), whole((rows, xproj.shape[0]))],
-        out_shape=[struct(rows, channels), struct(rows, xproj.shape[0])],
+        out_specs=[part(rows), whole((rows, xproj.shape[0])), part(rows), part(8)],
+        out_shape=[
+            struct(rows, channels), struct(rows, xproj.shape[0]), struct(rows, channels, dtype=BF16),
+            struct(8, channels, dtype=BF16),
+        ],
         scratch_shapes=[pltpu.VMEM((rows + 8, width), F32), pltpu.VMEM((rows, width), BF16)],
         compiler_params=LIMIT,
         cost_estimate=cost(8),
         name="front",
-    )(inner, before, conv_weight, conv_bias, xproj)
-
-
-def local_ends(live, proj, dtproj, dt_bias, mixed, gate, grad_gated, rate, width):
+    )(normed, halo, in_weight, conv_weight, conv_bias, xproj)
+
+
+def local_ends(live, proj, dtproj, dt_bias, mixed, normed, in_weight, masked, out_weight, rate, width):
     rows, channels = mixed.shape
+    features = normed.shape[1]
     states = rate.shape[0]
     rank = dtproj.shape[0]
     group = channels // width
@@ -729,11 +747,13 @@
         grid=(channels // width,),
         in_specs=[
             pl.BlockSpec(memory_space=pltpu.SMEM), whole(proj.shape),
-            part(rank), part(1), part(rows), part(rows), part(rows), part(states),
+            part(rank), part(1), part(rows), whole(normed.shape),
+            pl.BlockSpec((features, width), lambda q: (0, q + group)), whole(masked.shape),
+            pl.BlockSpec((width, features), lambda q: (q, 0)), part(states),
         ],
-        out_specs=[part(rows)] + [part(8), part(states), part(states), whole((2 * states, rows))]
+        out_specs=[part(rows)] * 3 + [part(8), part(states), part(states), whole((2 * states, rows))]
         + [part(states + 8)] * (group - 1),
-        out_shape=[struct(rows, channels)]
+        out_shape=[struct(rows, channels)] * 3
         + [struct(8, channels), struct(states, channels), struct(states, channels), struct(2 * states, rows)]
         + [struct(states + 8, channels)] * (group - 1),
         scratch_shapes=[
@@ -746,7 +766,7 @@
         compiler_params=LIMIT,
         cost_estimate=cost(40),
         name="ends",
-    )(live, proj, dtproj, dt_bias, mixed, gate, grad_gated, rate)
+    )(live, proj, dtproj, dt_bias, mixed, normed, in_weight, masked, out_weight, rate)
 
 
 def full_scan(
@@ -769,12 +789,13 @@
     ]
     out_specs = [
         part(rows), part(rows), part(rows), part(states), part(8), tall, whole((rows, rank)),
-        whole((2 * states, rows)),
+        whole((2 * states, rows)), whole((rows, 128)),
     ] + [whole((rows, 2 * width))] * blocks
     out_shape = [
         struct(rows, channels, dtype=BF16), struct(rows, channels, dtype=BF16),
         struct(rows, channels), struct(states, channels),
         struct(8, channels), struct(channels, rank), struct(rows, rank), struct(2 * states, rows),
+        struct(rows, 128, dtype=BF16),
     ] + [struct(rows, 2 * width, dtype=BF16)] * blocks
     args = [
         order, cols, proj, rate, step, mixed, gate, grad_gated, state_in, grad_in, skip, dtproj,
@@ -783,7 +804,7 @@
     for out, value in earlier:
         aliases[len(args)] = out
         args.append(value)
-        in_specs.append(pl.BlockSpec(memory_space=pl.ANY))
+        in_specs.append(pl.BlockSpec(memory_space=pl.ANY) if out < 6 else whole(value.shape))
     block = pltpu.VMEM((rows, width), F32)
     return pl.pallas_call(
         functools.partial(scan_kernel, len(earlier)),
@@ -1003,17 +1024,15 @@
     inv_scale = lax.rsqrt(jnp.mean(inputs * inputs, axis=1, keepdims=True) + EPSILON)
     normed = inputs * inv_scale
     normed_low = (normed * norm_gain).astype(BF16)
-    inner = jnp.dot(normed_low, in_weight[:, :channels], preferred_element_type=F32).astype(BF16)
-    before = shifted(inner[rows - 8 :], "state", 1)
-    gate_in = jnp.dot(normed_low, in_weight[:, channels:], preferred_element_type=F32)
-    grad_gated = dot(masked_low, out_weight, ((1,), (1,)))
-    mixed, proj = front(inner, before, conv_weight, conv_row, xproj, width)
+    halo = shifted(normed_low[rows - 8 :], "state", 1)
+    mixed, proj, inner, before = front(normed_low, halo, in_weight, conv_weight, conv_row, xproj, width)
 
     near = [d for d in range(1, group) if d & (d - 1) == 0]
     normed_late, mixed = lax.optimization_barrier((normed_low, mixed))
     normed_near = [swapped(normed_late, d) for d in near]
-    step, stats, state_end, grad_end, cols, *offers = local_ends(
-        jnp.stack([live_rows[0], member]), proj, dtproj_weight.T, dt_bias[None], mixed, gate_in, grad_gated, rate2, width
+    step, gate_in, grad_gated, stats, state_end, grad_end, cols, *offers = local_ends(
+        jnp.stack([live_rows[0], member]), proj, dtproj_weight.T, dt_bias[None], mixed, normed_low, in_weight,
+        masked_low, out_weight, rate2, width,
     )
     *normed_near, offers = lax.optimization_barrier((*normed_near, offers))
     normed_pieces = {0: normed_low, **dict(zip(near, normed_near))}
@@ -1043,27 +1062,21 @@
     *masked_pieces, normed_late, one[0] = lax.optimization_barrier((*masked_pieces, normed_low, one[0]))
     normed_pieces.update({d: swapped(normed_late, d) for d in range(1, group) if d not in near})
     normed_pieces = [normed_pieces[d] for d in range(group)]
-    gates = {d: swapped(one[8 + q], d) for q, d in enumerate(first)}
-    shared = [(k, one[k]) for k in (0, 1, 2, 3, 4, 5)]
+    gates = {d: swapped(one[9 + q], d) for q, d in enumerate(first)}
+    shared = [(k, one[k]) for k in range(8)]
     two = full_scan(jnp.stack([member ^ d for d in second]), *call, shared)
     gated_low, grad_gate_low, mix_grad, grad_a, scan_sums, grad_dtproj = two[:6]
     first_gates = [gates[d] for d in first]
-    normed_pieces, *first_gates, grad_rank = lax.optimization_barrier(
-        (normed_pieces, *first_gates, one[6] + two[6])
-    )
+    normed_pieces, *first_gates, grad_proj = lax.optimization_barrier((normed_pieces, *first_gates, two[8]))
     gates.update(dict(zip(first, first_gates)))
-    grad_bc = (one[7] + two[7]).T
-
-    grad_proj = jnp.concatenate(
-        [grad_rank, grad_bc, jnp.zeros((rows, 128 - proj_width), F32)], axis=1
-    ).astype(BF16)
+
     window = jnp.concatenate([before, inner[:8]], axis=0).astype(F32)
     head_pre = conv_window(window, conv_weight, conv_row, 8)
     head_squash = jax.nn.sigmoid(head_pre)
     head_mixed = mix_grad[:8] + jnp.dot(grad_proj[:8], xproj, preferred_element_type=F32)
     head_grad = head_mixed * head_squash * (1.0 + head_pre * (1.0 - head_squash))
     ahead = shifted(head_grad, "state", -1)
-    late_sends = [two[8 + q] for q in range(len(second))]
+    late_sends = [two[9 + q] for q in range(len(second))]
     ahead, *late_sends = lax.optimization_barrier((ahead, *late_sends))
     gates.update({d: swapped(v, d) if d else v for d, v in zip(second, late_sends)})
     call = (grad_proj, xproj, mix_grad, inner, before, ahead, conv_weight, conv_row, grad_a, scan_sums, stats)

time: 365 us -> 356 us (0.975)
  matrix products: 31.4 us -> 13.5 us
  Pallas kernels: 195 us -> 204 us
    dot_general x2 -> x0, matrix products: 9.28 us -> none  [the longest x1 4.94 us: body(): jnp.dot(normed_low, in_weight[:, :channels], preferred_element_type=F32)]
    dot_general x3 -> x2, matrix products: 17.7 us -> 9.15 us  [dot(): return lax.dot_general(a, b, (dims, ((), ())), preferred_element_type=F32)]
    pallas_call x1, Pallas kernels: 37.9 us -> 43.9 us  [local_ends(): pl.pallas_call(ends_kernel, grid=(channels // width,), in_specs=[pl.Block...]
    pallas_call x1, Pallas kernels: 7.72 us -> 11.7 us  [front(): pl.pallas_call(front_kernel, grid=(channels // width,), in_specs=[whole(n...]
  transfers between devices with their start and end apart: 37 -> 37, of which waited for: 14 -> 15; matrix products, arithmetic and copies ran while one was open for 13% -> 8% of each run, Pallas kernels for 47% -> 51%
where the time goes in v6:
time: 356 us; the launch traced here: 355 us
  Pallas kernels  204 us (57%)
  waiting for transfers between devices  60.3 us (17%)
  starting transfers between devices  49.1 us (14%)
  other arithmetic  16.8 us (5%)
  matrix products  13.5 us (4%)
  local copies, waits for them, and re-layouts  8.81 us (2%)
    pallas_call x2, Pallas kernels, full_scan(): pl.pallas_call(functools.partial(scan_kernel, len(earlier)), grid_spec=pl...  103 us
    pallas_call x1, Pallas kernels, local_ends(): pl.pallas_call(ends_kernel, grid=(channels // width,), in_specs=[pl.Block...  43.9 us
    ppermute x27, starting transfers between devices, swapped(): lax.ppermute(value, 'state', [(i, i ^ distance) for i in range(count)])  33.5 us
    ppermute x6, waiting for transfers between devices, seq_exchange(): return lax.ppermute(value, 'seq', [(i, i ^ distance) for i in range(count)])  30.2 us
    ppermute x27, waiting for transfers between devices, swapped(): lax.ppermute(value, 'state', [(i, i ^ distance) for i in range(count)])  24.7 us
    pallas_call x2, Pallas kernels, back(): pl.pallas_call(functools.partial(back_kernel, len(earlier)), grid_spec=pl...  21.5 us
    pallas_call x1, Pallas kernels, wide_grads(): pl.pallas_call(functools.partial(wide_kernel, high), grid_spec=pltpu.Pref...  12.6 us
    pallas_call x1, Pallas kernels, front(): pl.pallas_call(front_kernel, grid=(channels // width,), in_specs=[whole(n...  11.7 us
  transfers between devices with their start and end apart: 37, of which 15 were waited for; matrix products, arithmetic and copies ran while one was open for 8% of the time, Pallas kernels for 51%

profile of v6, /device:TPU:0, one launch (start us, length us, event | category | flops | bytes accessed | tf_op | source)
XLA Modules:
  0.0 355.2 jit_solution(16511990912619900949)
XLA Ops:
  0.7 3.0 collective-permute-start.1
  9.3 3.8 %collective-permute-start = (bf16[8,1024]{1,0:T(8,128)(2,1)S(1)}, bf16[8,1024]{1,0:T(8,128)(2,1)S(1)}, u32[]{:S(2)}, u32[]{:S(2)}) collective-permute-start(bf16[8,1024]{1,0:T(8,128)(2,1)S(1)} %slice.183), channel_id=1, source_target_pairs={{0,1},{1,2},{2,3},{4,5},{5,6},{6,7},{8,9},{9,10},{10,11},{12,13},{... | collective-permute-start | bytes 49160 | tf_op jit(solution)/shard_map/ppermute | solution.py:29
  17.1 11.7 %front.1 = (f32[512,2048]{1,0:T(8,128)}, f32[512,128]{1,0:T(8,128)}, bf16[512,2048]{1,0:T(8,128)(2,1)}, bf16[8,2048]{1,0:T(8,128)(2,1)}) custom-call(bf16[512,1024]{1,0:T(8,128)(2,1)} %copy-done, bf16[8,1024]{1,0:T(8,128)(2,1)} %copy-done.26, bf16[1024,4096]{1,0:T(8,128)(2,1)} %gate_w.1, f32[4,2048]{1,0:T(4,128)} %conv_w.5, f32[1,2048]{1,0:T(1,128)} %bitcast.116, ...), custom_call_target="tpu_custom_call" | custom-call | flops 8 | bytes 1024 | tf_op jit(solution)/shard_map/front/pallas_call | solution.py:716
  31.5 43.9 %ends.1 = (f32[512,2048]{1,0:T(8,128)}, f32[512,2048]{1,0:T(8,128)}, f32[512,2048]{1,0:T(8,128)}, f32[8,2048]{1,0:T(8,128)}, f32[16,2048]{1,0:T(8,128)}, /*index...) custom-call(s32[2]{0:T(128)} %get-tuple-element.254.live, ...), custom_call_target="tpu_custom_call" | custom-call | flops 40 | bytes 1024 | tf_op jit(solution)/shard_map/ends/pallas_call | solution.py:745
  79.9 3.3 collective-permute-done.6
  83.2 3.0 collective-permute-done.7
  91.3 51.3 %scan.2 = (bf16[512,2048]{1,0:T(8,128)(2,1)}, bf16[512,2048]{1,0:T(8,128)(2,1)}, f32[512,2048]{1,0:T(8,128)}, f32[16,2048]{1,0:T(8,128)}, f32[8,2048]{1,0:T(8,12...) custom-call(s32[2]{0:T(128)} %pad_add_fusion.2.order, ...), custom_call_target="tpu_custom_call" | custom-call | flops 50 | bytes 1024 | tf_op jit(solution)/shard_map/scan/pallas_call | solution.py:809
  147.1 51.3 %scan.3 = (bf16[512,2048]{1,0:T(8,128)(2,1)}, bf16[512,2048]{1,0:T(8,128)(2,1)}, f32[512,2048]{1,0:T(8,128)}, f32[16,2048]{1,0:T(8,128)}, f32[8,2048]{1,0:T(8,12...) custom-call(s32[2]{0:T(128)} %get-tuple-element.253.order, ...), custom_call_target="tpu_custom_call", output_to_operand_aliasing={{0}: (12, {}), {1}: (13, {}), {2}: (14, {}), {3}: (15, {}),... | custom-call | flops 50 | bytes 1024 | tf_op jit(solution)/shard_map/scan/pallas_call | solution.py:809
  200.9 5.4 %collective-permute-done.15.ahead = f32[8,2048]{1,0:T(8,128)S(1)} collective-permute-done((f32[8,2048]{1,0:T(8,128)S(1)}, f32[8,2048]{1,0:T(8,128)S(1)}, u32[]{:S(2)}, u32[]{:S(2)}) %collective-permute-start.15) | collective-permute-done | bytes 65568 | tf_op jit(solution)/shard_map/ppermute | solution.py:29
  207.0 10.7 %back.2 = (bf16[512,2048]{1,0:T(8,128)(2,1)}, bf16[4,12,64,128]{3,2,1,0:T(8,128)(2,1)}, bf16[576,512]{1,0:T(8,128)(2,1)}, bf16[576,512]{1,0:T(8,128)(2,1)}) custom-call(s32[3]{0:T(128)} %get-tuple-element.255.order, bf16[512,128]{1,0:T(8,128)(2,1)} %get-tuple-element.155.proj_grad, bf16[128,2048]{1,0:T(8,128)(2,1)} %pad.4.xproj, ...), custom_call_target="tpu_custom_call" | custom-call | flops 18 | bytes 1024 | tf_op jit(solution)/shard_map/back/pallas_call | solution.py:867
  217.6 2.3 collective-permute-start.17
  221.7 10.9 %back.3 = (bf16[512,2048]{1,0:T(8,128)(2,1)}, bf16[4,12,64,128]{3,2,1,0:T(8,128)(2,1)}, bf16[576,512]{1,0:T(8,128)(2,1)}, bf16[576,512]{1,0:T(8,128)(2,1)}) custom-call(s32[3]{0:T(128)} %get-tuple-element.256.order, bf16[512,128]{1,0:T(8,128)(2,1)} %get-tuple-element.155.proj_grad, ...), custom_call_target="tpu_custom_call", output_to_operand_aliasing={{0}: (13, {}), {1}: (14, {})} | custom-call | flops 18 | bytes 1024 | tf_op jit(solution)/shard_map/back/pallas_call | solution.py:867
  232.6 6.3 %collective-permute-done.17.refs_5_ = bf16[576,512]{1,0:T(8,128)(2,1)S(1)} collective-permute-done((bf16[576,512]{1,0:T(8,128)(2,1)}, bf16[576,512]{1,0:T(8,128)(2,1)S(1)}, u32[]{:S(2)}, u32[]{:S(2)}) %collective-permute-start.17) | collective-permute-done | bytes 589856 | tf_op jit(solution)/shard_map/ppermute | solution.py:23
  239.0 12.6 %wide.1 = (f32[1024,512]{1,0:T(8,128)}, f32[1024,512]{1,0:T(8,128)}) custom-call(s32[9]{0:T(128)} %stack.49.at, bf16[512,1024]{1,0:T(8,128)(2,1)} %get-tuple-element.173.refs_0_.refs_4_, bf16[512,1024]{1,0:T(8,128)(2,1)} %collective-permute-done.13.refs_1_.refs_5_, bf16[512,1024]{1,0:T(8,128)(2,1)} %collective-permute-done.14.refs_2_.refs_6_, ...), custom_call_target="tpu_custom_call" | custom-call | flops 10 | bytes 1024 | tf_op jit(solution)/shard_map/wide/pallas_call | solution.py:918
  251.7 4.4 %collective-permute-done.19 = f32[1024,512]{1,0:T(8,128)S(1)} collective-permute-done((f32[1024,512]{1,0:T(8,128)}, f32[1024,512]{1,0:T(8,128)S(1)}, u32[]{:S(2)}, u32[]{:S(2)}) %collective-permute-start.19) | collective-permute-done | bytes 2097184 | tf_op jit(solution)/shard_map/ppermute | solution.py:54
  257.4 2.8 add.179
  262.8 2.1 collective-permute-start.23
  266.4 2.0 collective-permute-start.22
  268.4 6.0 %collective-permute-done.20 = bf16[512,512]{1,0:T(8,128)(2,1)} collective-permute-done((bf16[512,512]{1,0:T(8,128)(2,1)S(1)}, bf16[512,512]{1,0:T(8,128)(2,1)}, u32[]{:S(2)}, u32[]{:S(2)}) %collective-permute-start.20) | collective-permute-done | bytes 524320 | tf_op jit(solution)/shard_map/ppermute | solution.py:54
  275.8 2.7 collective-permute-start.21
  278.4 5.1 %fusion = f32[512,1024]{1,0:T(8,128)S(1)} fusion(bf16[512,2048]{1,0:T(8,128)(2,1)S(1)} %copy-done.9, bf16[1024,4096]{1,0:T(8,128)(2,1)} %gate_w.1), kind=kOutput, calls=%fused_computation | convolution fusion | flops 2147483648 | bytes 8388608 | tf_op jit(solution)/shard_map/dot_general | solution.py:986
  283.6 4.0 %fusion.13 = (f32[1024]{0:T(1024)S(1)}, f32[512]{0:T(512)S(1)}, f32[512,1024]{1,0:T(8,128)}) fusion(bf16[512,1024]{1,0:T(8,128)(2,1)S(1)} %copy-done.1, f32[512]{0:T(512)S(1)} %add_rsqrt_fusion, f32[1024]{0:T(1024)S(1)} %copy-done.27, f32[512,1024]{1,0:T(8,128)S(1)} %fusion, bf16[512,2048]{1,0:T(8,128)(2,1)S(1)} %copy-done.7, ...), kind=kOutput, calls=%fused_computation.18 | convolution fusion | flops 2151676416 | bytes 11546624 | tf_op jit(solution)/shard_map/dot_general | solution.py:986
  290.0 8.6 %inner.1 = (f32[688,512]{1,0:T(8,128)}, f32[688,512]{1,0:T(8,128)}) custom-call(s32[9]{0:T(128)} %stack.49.at, bf16[512,1024]{1,0:T(8,128)(2,1)} %copy-done, bf16[512,1024]{1,0:T(8,128)(2,1)} %collective-permute-done.4.refs_13_.refs_1_, bf16[512,1024]{1,0:T(8,128)(2,1)} %collective-permute-done.5.refs_14_.refs_2_, ...), custom_call_target="tpu_custom_call" | custom-call | flops 5 | bytes 1024 | tf_op jit(solution)/shard_map/inner/pallas_call | solution.py:947
  299.5 2.5 collective-permute-done.26
  305.8 3.3 fusion.15
  309.8 6.8 %collective-permute-done.27 = bf16[416,512]{1,0:T(8,128)(2,1)S(1)} collective-permute-done((bf16[416,512]{1,0:T(8,128)(2,1)S(1)}, bf16[416,512]{1,0:T(8,128)(2,1)S(1)}, u32[]{:S(2)}, u32[]{:S(2)}) %collective-permute-start.27) | collective-permute-done | bytes 426016 | tf_op jit(solution)/shard_map/ppermute | solution.py:54
  316.9 3.3 collective-permute-start.33
  324.0 8.9 %collective-permute-done.33 = bf16[256,512]{1,0:T(8,128)(2,1)S(1)} collective-permute-done((bf16[256,512]{1,0:T(8,128)(2,1)S(1)}, bf16[256,512]{1,0:T(8,128)(2,1)S(1)}, u32[]{:S(2)}, u32[]{:S(2)}) %collective-permute-start.33) | collective-permute-done | bytes 262176 | tf_op jit(solution)/shard_map/ppermute | solution.py:54
  339.6 1.9 convert_add_fusion.1
  341.5 4.5 %collective-permute-done.34.refs_5_ = bf16[288,512]{1,0:T(8,128)(2,1)S(1)} collective-permute-done((bf16[288,512]{1,0:T(8,128)(2,1)S(1)}, bf16[288,512]{1,0:T(8,128)(2,1)S(1)}, u32[]{:S(2)}, u32[]{:S(2)}) %collective-permute-start.34) | collective-permute-done | bytes 294944 | tf_op jit(solution)/shard_map/ppermute | solution.py:23
  346.0 4.6 %collective-permute-done.35.refs_6_ = bf16[288,512]{1,0:T(8,128)(2,1)S(1)} collective-permute-done((bf16[288,512]{1,0:T(8,128)(2,1)S(1)}, bf16[288,512]{1,0:T(8,128)(2,1)S(1)}, u32[]{:S(2)}, u32[]{:S(2)}) %collective-permute-start.35) | collective-permute-done | bytes 294944 | tf_op jit(solution)/shard_map/ppermute | solution.py:23
  351.3 3.7 %assemble.1 = (f32[128,4096]{1,0:T(8,128)}, f32[256,1024]{1,0:T(8,128)}, f32[96,256]{1,0:T(8,128)}, f32[64,256]{1,0:T(8,128)}, f32[4,2048]{1,0:T(4,128)}, /*inde...) custom-call(s32[9]{0:T(128)} %stack.49.at, ...), custom_call_target="tpu_custom_call" | custom-call | flops 4 | bytes 1024 | tf_op jit(solution)/shard_map/assemble/pallas_call | solution.py:973
  (167 shorter events, 56.3 us)
Async XLA Ops:
  0.7 30.1 %collective-permute-start.1 = (f32[4,2048]{1,0:T(4,128)}, f32[4,2048]{1,0:T(4,128)S(1)}, u32[]{:S(2)}, u32[]{:S(2)}) collective-permute-start(f32[4,2048]{1,0:T(4,128)} %param.23), channel_id=1, source_target_pairs={{0,1},{1,0},{2,3},{3,2},{4,5},{5,4},{6,7},{7,6},{8,9},{9,8},{10,11... | collective-permute-start | bytes 98312 | tf_op jit(solution)/shard_map/ppermute | solution.py:23
  3.7 27.1 %collective-permute-start.2 = (f32[4,2048]{1,0:T(4,128)}, f32[4,2048]{1,0:T(4,128)S(1)}, u32[]{:S(2)}, u32[]{:S(2)}) collective-permute-start(f32[4,2048]{1,0:T(4,128)} %param.23), channel_id=1, source_target_pairs={{0,2},{1,3},{2,0},{3,1},{4,6},{5,7},{6,4},{7,5},{8,10},{9,11},{10,... | collective-permute-start | bytes 98312 | tf_op jit(solution)/shard_map/ppermute | solution.py:23
  5.2 25.6 %collective-permute-start.3 = (f32[4,2048]{1,0:T(4,128)}, f32[4,2048]{1,0:T(4,128)S(1)}, u32[]{:S(2)}, u32[]{:S(2)}) collective-permute-start(f32[4,2048]{1,0:T(4,128)} %param.23), channel_id=1, source_target_pairs={{0,3},{1,2},{2,1},{3,0},{4,7},{5,6},{6,5},{7,4},{8,11},{9,10},{10,... | collective-permute-start | bytes 98312 | tf_op jit(solution)/shard_map/ppermute | solution.py:23
  28.8 46.6 %collective-permute-start.4 = (bf16[512,1024]{1,0:T(8,128)(2,1)}, bf16[512,1024]{1,0:T(8,128)(2,1)}, u32[]{:S(2)}, u32[]{:S(2)}) collective-permute-start(bf16[512,1024]{1,0:T(8,128)(2,1)} %copy-done), channel_id=1, source_target_pairs={{0,1},{1,0},{2,3},{3,2},{4,5},{5,4},{6,7},{7,6},{8,9},{9,8},{10,11... | collective-permute-start | bytes 3145736 | tf_op jit(solution)/shard_map/ppermute | solution.py:23
  30.4 45.0 %collective-permute-start.5 = (bf16[512,1024]{1,0:T(8,128)(2,1)}, bf16[512,1024]{1,0:T(8,128)(2,1)}, u32[]{:S(2)}, u32[]{:S(2)}) collective-permute-start(bf16[512,1024]{1,0:T(8,128)(2,1)} %copy-done), channel_id=1, source_target_pairs={{0,2},{1,3},{2,0},{3,1},{4,6},{5,7},{6,4},{7,5},{8,10},{9,11},{10,... | collective-permute-start | bytes 3145736 | tf_op jit(solution)/shard_map/ppermute | solution.py:23
  75.4 7.8 %collective-permute-start.6 = (f32[24,2048]{1,0:T(8,128)}, f32[24,2048]{1,0:T(8,128)S(1)}, u32[]{:S(2)}, u32[]{:S(2)}) collective-permute-start(f32[24,2048]{1,0:T(8,128)} %get-tuple-element.134), channel_id=1, source_target_pairs={{0,1},{1,0},{2,3},{3,2},{4,5},{5,4},{6,7},{7,6},{8,9},{9,8},{10,11... | collective-permute-start | bytes 589832 | tf_op jit(solution)/shard_map/ppermute | solution.py:23
  77.1 9.1 %collective-permute-start.7 = (f32[24,2048]{1,0:T(8,128)}, f32[24,2048]{1,0:T(8,128)S(1)}, u32[]{:S(2)}, u32[]{:S(2)}) collective-permute-start(f32[24,2048]{1,0:T(8,128)} %get-tuple-element.135), channel_id=1, source_target_pairs={{0,2},{1,3},{2,0},{3,1},{4,6},{5,7},{6,4},{7,5},{8,10},{9,11},{10,... | collective-permute-start | bytes 589832 | tf_op jit(solution)/shard_map/ppermute | solution.py:23
  77.6 8.6 %collective-permute-start.8 = (f32[24,2048]{1,0:T(8,128)}, f32[24,2048]{1,0:T(8,128)S(1)}, u32[]{:S(2)}, u32[]{:S(2)}) collective-permute-start(f32[24,2048]{1,0:T(8,128)} %get-tuple-element.136), channel_id=1, source_target_pairs={{0,3},{1,2},{2,1},{3,0},{4,7},{5,6},{6,5},{7,4},{8,11},{9,10},{10,... | collective-permute-start | bytes 589832 | tf_op jit(solution)/shard_map/ppermute | solution.py:23
  87.2 57.4 %collective-permute-start.10 = (bf16[512,1024]{1,0:T(8,128)(2,1)}, bf16[512,1024]{1,0:T(8,128)(2,1)}, u32[]{:S(2)}, u32[]{:S(2)}) collective-permute-start(bf16[512,1024]{1,0:T(8,128)(2,1)} %fusion.8.masked.refs_8_), channel_id=1, source_target_pairs={{0,2},{1,3},{2,0},{3,1},{4,6},{5,7},{6,4},{7,5},{8,10},{9,11},{10,... | collective-permute-start | bytes 3145736 | tf_op jit(solution)/shard_map/ppermute | solution.py:23
  88.1 56.5 %collective-permute-start.11 = (bf16[512,1024]{1,0:T(8,128)(2,1)}, bf16[512,1024]{1,0:T(8,128)(2,1)}, u32[]{:S(2)}, u32[]{:S(2)}) collective-permute-start(bf16[512,1024]{1,0:T(8,128)(2,1)} %fusion.8.masked.refs_8_), channel_id=1, source_target_pairs={{0,3},{1,2},{2,1},{3,0},{4,7},{5,6},{6,5},{7,4},{8,11},{9,10},{10,... | collective-permute-start | bytes 3145736 | tf_op jit(solution)/shard_map/ppermute | solution.py:23
  89.5 55.2 %collective-permute-start.9 = (bf16[512,1024]{1,0:T(8,128)(2,1)}, bf16[512,1024]{1,0:T(8,128)(2,1)}, u32[]{:S(2)}, u32[]{:S(2)}) collective-permute-start(bf16[512,1024]{1,0:T(8,128)(2,1)} %fusion.8.masked.refs_8_), channel_id=1, source_target_pairs={{0,1},{1,0},{2,3},{3,2},{4,5},{5,4},{6,7},{7,6},{8,9},{9,8},{10,11... | collective-permute-start | bytes 3145736 | tf_op jit(solution)/shard_map/ppermute | solution.py:23
  142.6 55.7 %collective-permute-start.13 = (bf16[512,1024]{1,0:T(8,128)(2,1)}, bf16[512,1024]{1,0:T(8,128)(2,1)}, u32[]{:S(2)}, u32[]{:S(2)}) collective-permute-start(bf16[512,1024]{1,0:T(8,128)(2,1)} %get-tuple-element.152), channel_id=1, source_target_pairs={{0,1},{1,0},{2,3},{3,2},{4,5},{5,4},{6,7},{7,6},{8,9},{9,8},{10,11... | collective-permute-start | bytes 3145736 | tf_op jit(solution)/shard_map/ppermute | solution.py:23
  143.4 54.9 %collective-permute-start.14 = (bf16[512,1024]{1,0:T(8,128)(2,1)}, bf16[512,1024]{1,0:T(8,128)(2,1)}, u32[]{:S(2)}, u32[]{:S(2)}) collective-permute-start(bf16[512,1024]{1,0:T(8,128)(2,1)} %get-tuple-element.153), channel_id=1, source_target_pairs={{0,2},{1,3},{2,0},{3,1},{4,6},{5,7},{6,4},{7,5},{8,10},{9,11},{10,... | collective-permute-start | bytes 3145736 | tf_op jit(solution)/shard_map/ppermute | solution.py:23
  144.7 53.7 %collective-permute-start.12 = (bf16[512,1024]{1,0:T(8,128)(2,1)}, bf16[512,1024]{1,0:T(8,128)(2,1)}, u32[]{:S(2)}, u32[]{:S(2)}) collective-permute-start(bf16[512,1024]{1,0:T(8,128)(2,1)} %copy-done), channel_id=1, source_target_pairs={{0,3},{1,2},{2,1},{3,0},{4,7},{5,6},{6,5},{7,4},{8,11},{9,10},{10,... | collective-permute-start | bytes 3145736 | tf_op jit(solution)/shard_map/ppermute | solution.py:23
  206.3 32.6 %collective-permute-start.16 = (bf16[512,1024]{1,0:T(8,128)(2,1)}, bf16[512,1024]{1,0:T(8,128)(2,1)}, u32[]{:S(2)}, u32[]{:S(2)}) collective-permute-start(bf16[512,1024]{1,0:T(8,128)(2,1)} %get-tuple-element.163), channel_id=1, source_target_pairs={{0,3},{1,2},{2,1},{3,0},{4,7},{5,6},{6,5},{7,4},{8,11},{9,10},{10,... | collective-permute-start | bytes 3145736 | tf_op jit(solution)/shard_map/ppermute | solution.py:23
  217.6 21.2 %collective-permute-start.17 = (bf16[576,512]{1,0:T(8,128)(2,1)}, bf16[576,512]{1,0:T(8,128)(2,1)S(1)}, u32[]{:S(2)}, u32[]{:S(2)}) collective-permute-start(bf16[576,512]{1,0:T(8,128)(2,1)} %get-tuple-element.168), channel_id=1, source_target_pairs={{0,1},{1,0},{2,3},{3,2},{4,5},{5,4},{6,7},{7,6},{8,9},{9,8},{10,11... | collective-permute-start | bytes 1769480 | tf_op jit(solution)/shard_map/ppermute | solution.py:23
  220.0 19.0 %collective-permute-start.18 = (bf16[576,512]{1,0:T(8,128)(2,1)}, bf16[576,512]{1,0:T(8,128)(2,1)}, u32[]{:S(2)}, u32[]{:S(2)}) collective-permute-start(bf16[576,512]{1,0:T(8,128)(2,1)} %get-tuple-element.169), channel_id=1, source_target_pairs={{0,2},{1,3},{2,0},{3,1},{4,6},{5,7},{6,4},{7,5},{8,10},{9,11},{10,... | collective-permute-start | bytes 1769480 | tf_op jit(solution)/shard_map/ppermute | solution.py:23
  260.3 14.1 %collective-permute-start.20 = (bf16[512,512]{1,0:T(8,128)(2,1)S(1)}, bf16[512,512]{1,0:T(8,128)(2,1)}, u32[]{:S(2)}, u32[]{:S(2)}) collective-permute-start(bf16[512,512]{1,0:T(8,128)(2,1)S(1)} %bitcast.110), channel_id=1, source_target_pairs={{0,8},{4,12},{8,0},{12,4},{16,24},{20,28},{24,16},{28,20},{1,9},{5... | collective-permute-start | bytes 1572872 | tf_op jit(solution)/shard_map/ppermute | solution.py:54
  262.8 27.1 %collective-permute-start.23 = (bf16[12,64,128]{2,1,0:T(8,128)(2,1)}, bf16[12,64,128]{2,1,0:T(8,128)(2,1)}, u32[]{:S(2)}, u32[]{:S(2)}) collective-permute-start(bf16[12,64,128]{2,1,0:T(8,128)(2,1)} %get-tuple-element.238), channel_id=1, source_target_pairs={{0,1},{1,0},{2,3},{3,2},{4,5},{5,4},{6,7},{7,6},{8,9},{9,8},{10,11... | collective-permute-start | bytes 589832 | tf_op jit(solution)/shard_map/ppermute | solution.py:23
  265.0 25.0 %collective-permute-start.24 = (bf16[12,64,128]{2,1,0:T(8,128)(2,1)}, bf16[12,64,128]{2,1,0:T(8,128)(2,1)}, u32[]{:S(2)}, u32[]{:S(2)}) collective-permute-start(bf16[12,64,128]{2,1,0:T(8,128)(2,1)} %get-tuple-element.237), channel_id=1, source_target_pairs={{0,2},{1,3},{2,0},{3,1},{4,6},{5,7},{6,4},{7,5},{8,10},{9,11},{10,... | collective-permute-start | bytes 589832 | tf_op jit(solution)/shard_map/ppermute | solution.py:23
  265.5 24.5 %collective-permute-start.25 = (bf16[12,64,128]{2,1,0:T(8,128)(2,1)}, bf16[12,64,128]{2,1,0:T(8,128)(2,1)}, u32[]{:S(2)}, u32[]{:S(2)}) collective-permute-start(bf16[12,64,128]{2,1,0:T(8,128)(2,1)} %get-tuple-element.236), channel_id=1, source_target_pairs={{0,3},{1,2},{2,1},{3,0},{4,7},{5,6},{6,5},{7,4},{8,11},{9,10},{10,... | collective-permute-start | bytes 589832 | tf_op jit(solution)/shard_map/ppermute | solution.py:23
  266.4 23.5 %collective-permute-start.22 = (bf16[576,512]{1,0:T(8,128)(2,1)}, bf16[576,512]{1,0:T(8,128)(2,1)}, u32[]{:S(2)}, u32[]{:S(2)}) collective-permute-start(bf16[576,512]{1,0:T(8,128)(2,1)} %get-tuple-element.196), channel_id=1, source_target_pairs={{0,3},{1,2},{2,1},{3,0},{4,7},{5,6},{6,5},{7,4},{8,11},{9,10},{10,... | collective-permute-start | bytes 1769480 | tf_op jit(solution)/shard_map/ppermute | solution.py:23
  275.8 14.1 %collective-permute-start.21 = (bf16[256,512]{1,0:T(8,128)(2,1)S(1)}, bf16[256,512]{1,0:T(8,128)(2,1)S(1)}, u32[]{:S(2)}, u32[]{:S(2)}) collective-permute-start(bf16[256,512]{1,0:T(8,128)(2,1)S(1)} %fusion.19), channel_id=1, source_target_pairs={{0,16},{4,20},{8,24},{12,28},{16,0},{20,4},{24,8},{28,12},{1,17},{... | collective-permute-start | bytes 786440 | tf_op jit(solution)/shard_map/ppermute | solution.py:54
  298.6 10.6 %collective-permute-start.28 = (bf16[128,512]{1,0:T(8,128)(2,1)S(1)}, bf16[128,512]{1,0:T(8,128)(2,1)S(1)}, u32[]{:S(2)}, u32[]{:S(2)}) collective-permute-start(bf16[128,512]{1,0:T(8,128)(2,1)S(1)} %get-tuple-element.244), channel_id=1, source_target_pairs={{0,0},{1,1},{2,2},{3,3},{4,5},{5,4},{6,7},{7,6},{8,10},{9,11},{10,... | collective-permute-start | bytes 393224 | tf_op jit(solution)/shard_map/ppermute | solution.py:94
  304.0 12.7 %collective-permute-start.27 = (bf16[416,512]{1,0:T(8,128)(2,1)S(1)}, bf16[416,512]{1,0:T(8,128)(2,1)S(1)}, u32[]{:S(2)}, u32[]{:S(2)}) collective-permute-start(bf16[416,512]{1,0:T(8,128)(2,1)S(1)} %pad_maximum_fusion.1), channel_id=1, source_target_pairs={{0,8},{4,12},{8,0},{12,4},{16,24},{20,28},{24,16},{28,20},{1,9},{5... | collective-permute-start | bytes 1277960 | tf_op jit(solution)/shard_map/ppermute | solution.py:54
  316.9 16.0 %collective-permute-start.33 = (bf16[256,512]{1,0:T(8,128)(2,1)S(1)}, bf16[256,512]{1,0:T(8,128)(2,1)S(1)}, u32[]{:S(2)}, u32[]{:S(2)}) collective-permute-start(bf16[256,512]{1,0:T(8,128)(2,1)S(1)} %pad_maximum_fusion.4), channel_id=1, source_target_pairs={{0,16},{4,20},{8,24},{12,28},{16,0},{20,4},{24,8},{28,12},{1,17},{... | collective-permute-start | bytes 786440 | tf_op jit(solution)/shard_map/ppermute | solution.py:54
  320.2 12.8 %collective-permute-start.30 = (bf16[256,512]{1,0:T(8,128)(2,1)S(1)}, bf16[256,512]{1,0:T(8,128)(2,1)S(1)}, u32[]{:S(2)}, u32[]{:S(2)}) collective-permute-start(bf16[256,512]{1,0:T(8,128)(2,1)S(1)} %pad_maximum_fusion.3.refs_0_), channel_id=1, source_target_pairs={{0,1},{1,0},{2,3},{3,2},{4,5},{5,4},{6,7},{7,6},{8,9},{9,8},{10,11... | collective-permute-start | bytes 786440 | tf_op jit(solution)/shard_map/ppermute | solution.py:23
  321.5 12.5 %collective-permute-start.31 = (bf16[256,512]{1,0:T(8,128)(2,1)S(1)}, bf16[256,512]{1,0:T(8,128)(2,1)S(1)}, u32[]{:S(2)}, u32[]{:S(2)}) collective-permute-start(bf16[256,512]{1,0:T(8,128)(2,1)S(1)} %pad_maximum_fusion.3.refs_0_), channel_id=1, source_target_pairs={{0,2},{1,3},{2,0},{3,1},{4,6},{5,7},{6,4},{7,5},{8,10},{9,11},{10,... | collective-permute-start | bytes 786440 | tf_op jit(solution)/shard_map/ppermute | solution.py:23
  323.3 12.6 %collective-permute-start.32 = (bf16[256,512]{1,0:T(8,128)(2,1)S(1)}, bf16[256,512]{1,0:T(8,128)(2,1)S(1)}, u32[]{:S(2)}, u32[]{:S(2)}) collective-permute-start(bf16[256,512]{1,0:T(8,128)(2,1)S(1)} %pad_maximum_fusion.3.refs_0_), channel_id=1, source_target_pairs={{0,3},{1,2},{2,1},{3,0},{4,7},{5,6},{6,5},{7,4},{8,11},{9,10},{10,... | collective-permute-start | bytes 786440 | tf_op jit(solution)/shard_map/ppermute | solution.py:23
  336.0 10.0 %collective-permute-start.34 = (bf16[288,512]{1,0:T(8,128)(2,1)S(1)}, bf16[288,512]{1,0:T(8,128)(2,1)S(1)}, u32[]{:S(2)}, u32[]{:S(2)}) collective-permute-start(bf16[288,512]{1,0:T(8,128)(2,1)S(1)} %pad_maximum_fusion.2.refs_4_), channel_id=1, source_target_pairs={{0,1},{1,0},{2,3},{3,2},{4,5},{5,4},{6,7},{7,6},{8,9},{9,8},{10,11... | collective-permute-start | bytes 884744 | tf_op jit(solution)/shard_map/ppermute | solution.py:23
  336.6 14.0 %collective-permute-start.35 = (bf16[288,512]{1,0:T(8,128)(2,1)S(1)}, bf16[288,512]{1,0:T(8,128)(2,1)S(1)}, u32[]{:S(2)}, u32[]{:S(2)}) collective-permute-start(bf16[288,512]{1,0:T(8,128)(2,1)S(1)} %pad_maximum_fusion.2.refs_4_), channel_id=1, source_target_pairs={{0,2},{1,3},{2,0},{3,1},{4,6},{5,7},{6,4},{7,5},{8,10},{9,11},{10,... | collective-permute-start | bytes 884744 | tf_op jit(solution)/shard_map/ppermute | solution.py:23
  338.4 13.0 %collective-permute-start.36 = (bf16[288,512]{1,0:T(8,128)(2,1)S(1)}, bf16[288,512]{1,0:T(8,128)(2,1)}, u32[]{:S(2)}, u32[]{:S(2)}) collective-permute-start(bf16[288,512]{1,0:T(8,128)(2,1)S(1)} %pad_maximum_fusion.2.refs_4_), channel_id=1, source_target_pairs={{0,3},{1,2},{2,1},{3,0},{4,7},{5,6},{6,5},{7,4},{8,11},{9,10},{10,... | collective-permute-start | bytes 884744 | tf_op jit(solution)/shard_map/ppermute | solution.py:23
  (35 other events, 410.1 us)

commit v7 on v6

--- a/solution.py
+++ b/solution.py
@@ -15,7 +15,7 @@
 ENDS_ROWS = 64
 SCAN_ROWS = 64
 BACK_ROWS = 64
-WIDE_STEP = 128
+WIDE_STEP = 256
 
 
 def swapped(value, distance):
@@ -563,7 +563,11 @@
     put_chunks(targets, total, at[0], step, 2 * high, high, high, 1)
 
 
-def inner_kernel(total_chunks, at, *refs):
+def sum_rows(used, gains):
+    return -(-(used + gains + 1) // 16) * 16
+
+
+def inner_kernel(total_chunks, used, at, *refs):
     count = (len(refs) - 4) // 3
     normed, inners, thins = (refs[k * count : (k + 1) * count] for k in range(3))
     gain, live = refs[3 * count : 3 * count + 2]
@@ -576,7 +580,7 @@
     seqs = total_chunks
     side = seqs // (entries - seqs)
     chips = seqs // 2
-    extra = 48 if gain.shape[0] <= 8 else 0
+    extra = sum_rows(used, gain.shape[0])
     entry = (targets[0].shape[0] - extra) // chips
     packed = thin * columns // width
     high = entry - packed
@@ -624,7 +628,12 @@
             value = words[0:32].astype(F32) + words[32:64].astype(F32)
             sums = value if sums is None else sums + value
         tail = jnp.concatenate(
-            [sums, gain[...], jnp.full((extra - 32 - gain.shape[0], width), live[0], F32)], axis=0
+            [
+                sums[0:used],
+                gain[...],
+                jnp.full((extra - used - gain.shape[0], width), live[0], F32),
+            ],
+            axis=0,
         )
         for target in targets:
             target[chips * entry : chips * entry + extra, :] = tail
@@ -681,7 +690,7 @@
         spread_out[:, lanes] = piece[states + 3 : states + 4]
         conv_out[:, lanes] = piece[states + 4 : states + 4 + taps]
         bias_out[:, lanes] = piece[states + 4 + taps : states + 5 + taps]
-        tail = piece[32:48]
+        tail = piece[states + 5 + taps : states + 6 + taps + fold]
         rest = tail if rest is None else rest + tail
     turned = jnp.transpose(narrow[...])
     xproj_out[...] = turned[0 : xproj_out.shape[0]]
@@ -931,10 +940,7 @@
     )(places(), *gates, *gates, *masked, *normed)
 
 
-SUM_ROWS = 48
-
-
-def inner_grads(normed, inners, thins, gain, live, seqs):
+def inner_grads(normed, inners, thins, gain, live, seqs, used):
     count = len(inners)
     width = inners[0].shape[1]
     rows, features = normed[0].shape
@@ -943,9 +949,9 @@
     entry = features // seqs + thins[0].shape[1] * 256 // width
 
     partly = pl.BlockSpec((rows, features // steps), lambda i, at: (0, i))
-    shape = (chips * entry + SUM_ROWS, width)
+    shape = (chips * entry + sum_rows(used, gain.shape[0]), width)
     return pl.pallas_call(
-        functools.partial(inner_kernel, seqs),
+        functools.partial(inner_kernel, seqs, used),
         grid_spec=pltpu.PrefetchScalarGridSpec(
             num_scalar_prefetch=1,
             grid=(steps,),
@@ -1095,6 +1101,7 @@
     high = features // seqs
     thin = width // seqs
     thin_rows = thin * 256 // width
+    used = states + 5 + taps
 
     wide = wide_grads([gates[d] for d in range(group)], masked_pieces, normed_pieces, seqs)
     wide, _, (inner_pieces, thin_pieces), (gated_late, grad_gate_low) = seq_scatter(
@@ -1114,8 +1121,8 @@
         scaled - normed * jnp.mean(scaled * normed, axis=1, keepdims=True)
     )
 
-    last = inner_grads(normed_pieces, inner_pieces, thin_pieces, gain_part, live_rows.astype(F32), seqs)
-    last, sums, _, owned = seq_scatter(*last, extra=SUM_ROWS, late=owned)
+    last = inner_grads(normed_pieces, inner_pieces, thin_pieces, gain_part, live_rows.astype(F32), seqs, used)
+    last, sums, _, owned = seq_scatter(*last, extra=sum_rows(used, fold), late=owned)
     wide_pieces = gathered(jnp.concatenate([owned, wide[high:]], axis=0))
     *wide_pieces, last, sums = lax.optimization_barrier((*wide_pieces, last, sums))
     words = two_words(jnp.concatenate([last[high:], sums], axis=0))

time: 356 us -> 353 us (level)
  no operation moved by 1% of the time
where the time goes in v7:
time: 353 us
  Pallas kernels  204 us (58%)
  waiting for transfers between devices  58.8 us (17%)
  starting transfers between devices  49 us (14%)
  other arithmetic  16.8 us (5%)
  matrix products  13.5 us (4%)
  local copies, waits for them, and re-layouts  8.81 us (2%)
    pallas_call x2, Pallas kernels, full_scan(): pl.pallas_call(functools.partial(scan_kernel, len(earlier)), grid_spec=pl...  103 us
    pallas_call x1, Pallas kernels, local_ends(): pl.pallas_call(ends_kernel, grid=(channels // width,), in_specs=[pl.Block...  43.9 us
    ppermute x27, starting transfers between devices, swapped(): lax.ppermute(value, 'state', [(i, i ^ distance) for i in range(count)])  33.3 us
    ppermute x6, waiting for transfers between devices, seq_exchange(): return lax.ppermute(value, 'seq', [(i, i ^ distance) for i in range(count)])  27.8 us
    ppermute x27, waiting for transfers between devices, swapped(): lax.ppermute(value, 'state', [(i, i ^ distance) for i in range(count)])  25.4 us
    pallas_call x2, Pallas kernels, back(): pl.pallas_call(functools.partial(back_kernel, len(earlier)), grid_spec=pl...  21.7 us
    pallas_call x1, Pallas kernels, wide_grads(): pl.pallas_call(functools.partial(wide_kernel, high), grid_spec=pltpu.Pref...  12.3 us
    pallas_call x1, Pallas kernels, front(): pl.pallas_call(front_kernel, grid=(channels // width,), in_specs=[whole(n...  11.7 us
  transfers between devices with their start and end apart: 37, of which 15 were waited for; matrix products, arithmetic and copies ran while one was open for 8% of the time, Pallas kernels for 51%

profile of v7, /device:TPU:0, one launch (start us, length us, event | category | flops | bytes accessed | tf_op | source)
XLA Modules:
  0.0 352.8 jit_solution(9477684361135309385)
XLA Ops:
  0.7 3.0 collective-permute-start.1
  9.3 3.8 %collective-permute-start = (bf16[8,1024]{1,0:T(8,128)(2,1)S(1)}, bf16[8,1024]{1,0:T(8,128)(2,1)S(1)}, u32[]{:S(2)}, u32[]{:S(2)}) collective-permute-start(bf16[8,1024]{1,0:T(8,128)(2,1)S(1)} %slice.183), channel_id=1, source_target_pairs={{0,1},{1,2},{2,3},{4,5},{5,6},{6,7},{8,9},{9,10},{10,11},{12,13},{... | collective-permute-start | bytes 49160 | tf_op jit(solution)/shard_map/ppermute | solution.py:29
  17.1 11.7 %front.1 = (f32[512,2048]{1,0:T(8,128)}, f32[512,128]{1,0:T(8,128)}, bf16[512,2048]{1,0:T(8,128)(2,1)}, bf16[8,2048]{1,0:T(8,128)(2,1)}) custom-call(bf16[512,1024]{1,0:T(8,128)(2,1)} %copy-done, bf16[8,1024]{1,0:T(8,128)(2,1)} %copy-done.26, bf16[1024,4096]{1,0:T(8,128)(2,1)} %gate_w.1, f32[4,2048]{1,0:T(4,128)} %conv_w.5, f32[1,2048]{1,0:T(1,128)} %bitcast.116, ...), custom_call_target="tpu_custom_call" | custom-call | flops 8 | bytes 1024 | tf_op jit(solution)/shard_map/front/pallas_call | solution.py:725
  31.5 43.9 %ends.1 = (f32[512,2048]{1,0:T(8,128)}, f32[512,2048]{1,0:T(8,128)}, f32[512,2048]{1,0:T(8,128)}, f32[8,2048]{1,0:T(8,128)}, f32[16,2048]{1,0:T(8,128)}, /*index...) custom-call(s32[2]{0:T(128)} %get-tuple-element.254.live, ...), custom_call_target="tpu_custom_call" | custom-call | flops 40 | bytes 1024 | tf_op jit(solution)/shard_map/ends/pallas_call | solution.py:754
  79.9 3.3 collective-permute-done.6
  83.2 3.0 collective-permute-done.7
  91.3 51.3 %scan.2 = (bf16[512,2048]{1,0:T(8,128)(2,1)}, bf16[512,2048]{1,0:T(8,128)(2,1)}, f32[512,2048]{1,0:T(8,128)}, f32[16,2048]{1,0:T(8,128)}, f32[8,2048]{1,0:T(8,12...) custom-call(s32[2]{0:T(128)} %pad_add_fusion.2.order, ...), custom_call_target="tpu_custom_call" | custom-call | flops 50 | bytes 1024 | tf_op jit(solution)/shard_map/scan/pallas_call | solution.py:818
  147.1 51.3 %scan.3 = (bf16[512,2048]{1,0:T(8,128)(2,1)}, bf16[512,2048]{1,0:T(8,128)(2,1)}, f32[512,2048]{1,0:T(8,128)}, f32[16,2048]{1,0:T(8,128)}, f32[8,2048]{1,0:T(8,12...) custom-call(s32[2]{0:T(128)} %get-tuple-element.253.order, ...), custom_call_target="tpu_custom_call", output_to_operand_aliasing={{0}: (12, {}), {1}: (13, {}), {2}: (14, {}), {3}: (15, {}),... | custom-call | flops 50 | bytes 1024 | tf_op jit(solution)/shard_map/scan/pallas_call | solution.py:818
  200.7 5.6 %collective-permute-done.15.ahead = f32[8,2048]{1,0:T(8,128)S(1)} collective-permute-done((f32[8,2048]{1,0:T(8,128)S(1)}, f32[8,2048]{1,0:T(8,128)S(1)}, u32[]{:S(2)}, u32[]{:S(2)}) %collective-permute-start.15) | collective-permute-done | bytes 65568 | tf_op jit(solution)/shard_map/ppermute | solution.py:29
  207.0 10.8 %back.2 = (bf16[512,2048]{1,0:T(8,128)(2,1)}, bf16[4,12,64,128]{3,2,1,0:T(8,128)(2,1)}, bf16[576,512]{1,0:T(8,128)(2,1)}, bf16[576,512]{1,0:T(8,128)(2,1)}) custom-call(s32[3]{0:T(128)} %get-tuple-element.255.order, bf16[512,128]{1,0:T(8,128)(2,1)} %get-tuple-element.155.proj_grad, bf16[128,2048]{1,0:T(8,128)(2,1)} %pad.4.xproj, ...), custom_call_target="tpu_custom_call" | custom-call | flops 18 | bytes 1024 | tf_op jit(solution)/shard_map/back/pallas_call | solution.py:876
  217.8 2.3 collective-permute-start.17
  221.9 10.9 %back.3 = (bf16[512,2048]{1,0:T(8,128)(2,1)}, bf16[4,12,64,128]{3,2,1,0:T(8,128)(2,1)}, bf16[576,512]{1,0:T(8,128)(2,1)}, bf16[576,512]{1,0:T(8,128)(2,1)}) custom-call(s32[3]{0:T(128)} %get-tuple-element.256.order, bf16[512,128]{1,0:T(8,128)(2,1)} %get-tuple-element.155.proj_grad, ...), custom_call_target="tpu_custom_call", output_to_operand_aliasing={{0}: (13, {}), {1}: (14, {})} | custom-call | flops 18 | bytes 1024 | tf_op jit(solution)/shard_map/back/pallas_call | solution.py:876
  232.8 6.1 %collective-permute-done.17.refs_5_ = bf16[576,512]{1,0:T(8,128)(2,1)S(1)} collective-permute-done((bf16[576,512]{1,0:T(8,128)(2,1)}, bf16[576,512]{1,0:T(8,128)(2,1)S(1)}, u32[]{:S(2)}, u32[]{:S(2)}) %collective-permute-start.17) | collective-permute-done | bytes 589856 | tf_op jit(solution)/shard_map/ppermute | solution.py:23
  239.0 12.3 %wide.1 = (f32[1024,512]{1,0:T(8,128)}, f32[1024,512]{1,0:T(8,128)}) custom-call(s32[9]{0:T(128)} %stack.49.at, bf16[512,1024]{1,0:T(8,128)(2,1)} %get-tuple-element.173.refs_0_.refs_4_, bf16[512,1024]{1,0:T(8,128)(2,1)} %collective-permute-done.13.refs_1_.refs_5_, bf16[512,1024]{1,0:T(8,128)(2,1)} %collective-permute-done.14.refs_2_.refs_6_, ...), custom_call_target="tpu_custom_call" | custom-call | flops 10 | bytes 1024 | tf_op jit(solution)/shard_map/wide/pallas_call | solution.py:927
  251.4 4.4 %collective-permute-done.19 = f32[1024,512]{1,0:T(8,128)S(1)} collective-permute-done((f32[1024,512]{1,0:T(8,128)}, f32[1024,512]{1,0:T(8,128)S(1)}, u32[]{:S(2)}, u32[]{:S(2)}) %collective-permute-start.19) | collective-permute-done | bytes 2097184 | tf_op jit(solution)/shard_map/ppermute | solution.py:54
  257.1 2.8 add.179
  262.5 2.2 collective-permute-start.23
  266.1 2.0 collective-permute-start.22
  268.1 6.0 %collective-permute-done.20 = bf16[512,512]{1,0:T(8,128)(2,1)} collective-permute-done((bf16[512,512]{1,0:T(8,128)(2,1)S(1)}, bf16[512,512]{1,0:T(8,128)(2,1)}, u32[]{:S(2)}, u32[]{:S(2)}) %collective-permute-start.20) | collective-permute-done | bytes 524320 | tf_op jit(solution)/shard_map/ppermute | solution.py:54
  275.4 2.7 collective-permute-start.21
  278.1 5.1 %fusion = f32[512,1024]{1,0:T(8,128)S(1)} fusion(bf16[512,2048]{1,0:T(8,128)(2,1)S(1)} %copy-done.9, bf16[1024,4096]{1,0:T(8,128)(2,1)} %gate_w.1), kind=kOutput, calls=%fused_computation | convolution fusion | flops 2147483648 | bytes 8388608 | tf_op jit(solution)/shard_map/dot_general | solution.py:992
  283.3 4.0 %fusion.13 = (f32[1024]{0:T(1024)S(1)}, f32[512]{0:T(512)S(1)}, f32[512,1024]{1,0:T(8,128)}) fusion(bf16[512,1024]{1,0:T(8,128)(2,1)S(1)} %copy-done.1, f32[512]{0:T(512)S(1)} %add_rsqrt_fusion, f32[1024]{0:T(1024)S(1)} %copy-done.27, f32[512,1024]{1,0:T(8,128)S(1)} %fusion, bf16[512,2048]{1,0:T(8,128)(2,1)S(1)} %copy-done.7, ...), kind=kOutput, calls=%fused_computation.18 | convolution fusion | flops 2151676416 | bytes 11546624 | tf_op jit(solution)/shard_map/dot_general | solution.py:992
  289.6 8.1 %inner.1 = (f32[672,512]{1,0:T(8,128)}, f32[672,512]{1,0:T(8,128)}) custom-call(s32[9]{0:T(128)} %stack.49.at, bf16[512,1024]{1,0:T(8,128)(2,1)} %copy-done, bf16[512,1024]{1,0:T(8,128)(2,1)} %collective-permute-done.4.refs_13_.refs_1_, bf16[512,1024]{1,0:T(8,128)(2,1)} %collective-permute-done.5.refs_14_.refs_2_, ...), custom_call_target="tpu_custom_call" | custom-call | flops 5 | bytes 1024 | tf_op jit(solution)/shard_map/inner/pallas_call | solution.py:953
  298.6 2.4 collective-permute-done.26
  304.9 3.3 fusion.15
  308.9 5.9 %collective-permute-done.27 = bf16[384,512]{1,0:T(8,128)(2,1)S(1)} collective-permute-done((bf16[384,512]{1,0:T(8,128)(2,1)S(1)}, bf16[384,512]{1,0:T(8,128)(2,1)S(1)}, u32[]{:S(2)}, u32[]{:S(2)}) %collective-permute-start.27) | collective-permute-done | bytes 393248 | tf_op jit(solution)/shard_map/ppermute | solution.py:54
  315.1 3.6 %collective-permute-start.33 = (bf16[224,512]{1,0:T(8,128)(2,1)S(1)}, bf16[224,512]{1,0:T(8,128)(2,1)S(1)}, u32[]{:S(2)}, u32[]{:S(2)}) collective-permute-start(bf16[224,512]{1,0:T(8,128)(2,1)S(1)} %pad_maximum_fusion.4), channel_id=1, source_target_pairs={{0,16},{4,20},{8,24},{12,28},{16,0},{20,4},{24,8},{28,12},{1,17},{... | collective-permute-start | bytes 688136 | tf_op jit(solution)/shard_map/ppermute | solution.py:54
  322.3 7.5 %collective-permute-done.33 = bf16[224,512]{1,0:T(8,128)(2,1)S(1)} collective-permute-done((bf16[224,512]{1,0:T(8,128)(2,1)S(1)}, bf16[224,512]{1,0:T(8,128)(2,1)S(1)}, u32[]{:S(2)}, u32[]{:S(2)}) %collective-permute-start.33) | collective-permute-done | bytes 229408 | tf_op jit(solution)/shard_map/ppermute | solution.py:54
  329.9 2.5 collective-permute-done.31.refs_2_
  339.9 3.8 %collective-permute-done.34.refs_5_ = bf16[256,512]{1,0:T(8,128)(2,1)S(1)} collective-permute-done((bf16[256,512]{1,0:T(8,128)(2,1)S(1)}, bf16[256,512]{1,0:T(8,128)(2,1)S(1)}, u32[]{:S(2)}, u32[]{:S(2)}) %collective-permute-start.34) | collective-permute-done | bytes 262176 | tf_op jit(solution)/shard_map/ppermute | solution.py:23
  343.7 4.6 %collective-permute-done.35.refs_6_ = bf16[256,512]{1,0:T(8,128)(2,1)S(1)} collective-permute-done((bf16[256,512]{1,0:T(8,128)(2,1)S(1)}, bf16[256,512]{1,0:T(8,128)(2,1)S(1)}, u32[]{:S(2)}, u32[]{:S(2)}) %collective-permute-start.35) | collective-permute-done | bytes 262176 | tf_op jit(solution)/shard_map/ppermute | solution.py:23
  349.0 3.6 %assemble.1 = (f32[128,4096]{1,0:T(8,128)}, f32[256,1024]{1,0:T(8,128)}, f32[96,256]{1,0:T(8,128)}, f32[64,256]{1,0:T(8,128)}, f32[4,2048]{1,0:T(4,128)}, /*inde...) custom-call(s32[9]{0:T(128)} %stack.49.at, ...), custom_call_target="tpu_custom_call" | custom-call | flops 4 | bytes 1024 | tf_op jit(solution)/shard_map/assemble/pallas_call | solution.py:979
  (167 shorter events, 56.9 us)
Async XLA Ops:
  0.7 30.1 %collective-permute-start.1 = (f32[4,2048]{1,0:T(4,128)}, f32[4,2048]{1,0:T(4,128)S(1)}, u32[]{:S(2)}, u32[]{:S(2)}) collective-permute-start(f32[4,2048]{1,0:T(4,128)} %param.23), channel_id=1, source_target_pairs={{0,1},{1,0},{2,3},{3,2},{4,5},{5,4},{6,7},{7,6},{8,9},{9,8},{10,11... | collective-permute-start | bytes 98312 | tf_op jit(solution)/shard_map/ppermute | solution.py:23
  3.7 27.1 %collective-permute-start.2 = (f32[4,2048]{1,0:T(4,128)}, f32[4,2048]{1,0:T(4,128)S(1)}, u32[]{:S(2)}, u32[]{:S(2)}) collective-permute-start(f32[4,2048]{1,0:T(4,128)} %param.23), channel_id=1, source_target_pairs={{0,2},{1,3},{2,0},{3,1},{4,6},{5,7},{6,4},{7,5},{8,10},{9,11},{10,... | collective-permute-start | bytes 98312 | tf_op jit(solution)/shard_map/ppermute | solution.py:23
  5.2 25.6 %collective-permute-start.3 = (f32[4,2048]{1,0:T(4,128)}, f32[4,2048]{1,0:T(4,128)S(1)}, u32[]{:S(2)}, u32[]{:S(2)}) collective-permute-start(f32[4,2048]{1,0:T(4,128)} %param.23), channel_id=1, source_target_pairs={{0,3},{1,2},{2,1},{3,0},{4,7},{5,6},{6,5},{7,4},{8,11},{9,10},{10,... | collective-permute-start | bytes 98312 | tf_op jit(solution)/shard_map/ppermute | solution.py:23
  28.8 46.6 %collective-permute-start.4 = (bf16[512,1024]{1,0:T(8,128)(2,1)}, bf16[512,1024]{1,0:T(8,128)(2,1)}, u32[]{:S(2)}, u32[]{:S(2)}) collective-permute-start(bf16[512,1024]{1,0:T(8,128)(2,1)} %copy-done), channel_id=1, source_target_pairs={{0,1},{1,0},{2,3},{3,2},{4,5},{5,4},{6,7},{7,6},{8,9},{9,8},{10,11... | collective-permute-start | bytes 3145736 | tf_op jit(solution)/shard_map/ppermute | solution.py:23
  30.4 45.0 %collective-permute-start.5 = (bf16[512,1024]{1,0:T(8,128)(2,1)}, bf16[512,1024]{1,0:T(8,128)(2,1)}, u32[]{:S(2)}, u32[]{:S(2)}) collective-permute-start(bf16[512,1024]{1,0:T(8,128)(2,1)} %copy-done), channel_id=1, source_target_pairs={{0,2},{1,3},{2,0},{3,1},{4,6},{5,7},{6,4},{7,5},{8,10},{9,11},{10,... | collective-permute-start | bytes 3145736 | tf_op jit(solution)/shard_map/ppermute | solution.py:23
  75.4 7.8 %collective-permute-start.6 = (f32[24,2048]{1,0:T(8,128)}, f32[24,2048]{1,0:T(8,128)S(1)}, u32[]{:S(2)}, u32[]{:S(2)}) collective-permute-start(f32[24,2048]{1,0:T(8,128)} %get-tuple-element.134), channel_id=1, source_target_pairs={{0,1},{1,0},{2,3},{3,2},{4,5},{5,4},{6,7},{7,6},{8,9},{9,8},{10,11... | collective-permute-start | bytes 589832 | tf_op jit(solution)/shard_map/ppermute | solution.py:23
  77.1 9.1 %collective-permute-start.7 = (f32[24,2048]{1,0:T(8,128)}, f32[24,2048]{1,0:T(8,128)S(1)}, u32[]{:S(2)}, u32[]{:S(2)}) collective-permute-start(f32[24,2048]{1,0:T(8,128)} %get-tuple-element.135), channel_id=1, source_target_pairs={{0,2},{1,3},{2,0},{3,1},{4,6},{5,7},{6,4},{7,5},{8,10},{9,11},{10,... | collective-permute-start | bytes 589832 | tf_op jit(solution)/shard_map/ppermute | solution.py:23
  77.6 8.6 %collective-permute-start.8 = (f32[24,2048]{1,0:T(8,128)}, f32[24,2048]{1,0:T(8,128)S(1)}, u32[]{:S(2)}, u32[]{:S(2)}) collective-permute-start(f32[24,2048]{1,0:T(8,128)} %get-tuple-element.136), channel_id=1, source_target_pairs={{0,3},{1,2},{2,1},{3,0},{4,7},{5,6},{6,5},{7,4},{8,11},{9,10},{10,... | collective-permute-start | bytes 589832 | tf_op jit(solution)/shard_map/ppermute | solution.py:23
  87.2 57.4 %collective-permute-start.10 = (bf16[512,1024]{1,0:T(8,128)(2,1)}, bf16[512,1024]{1,0:T(8,128)(2,1)}, u32[]{:S(2)}, u32[]{:S(2)}) collective-permute-start(bf16[512,1024]{1,0:T(8,128)(2,1)} %fusion.8.masked.refs_8_), channel_id=1, source_target_pairs={{0,2},{1,3},{2,0},{3,1},{4,6},{5,7},{6,4},{7,5},{8,10},{9,11},{10,... | collective-permute-start | bytes 3145736 | tf_op jit(solution)/shard_map/ppermute | solution.py:23
  88.1 56.5 %collective-permute-start.11 = (bf16[512,1024]{1,0:T(8,128)(2,1)}, bf16[512,1024]{1,0:T(8,128)(2,1)}, u32[]{:S(2)}, u32[]{:S(2)}) collective-permute-start(bf16[512,1024]{1,0:T(8,128)(2,1)} %fusion.8.masked.refs_8_), channel_id=1, source_target_pairs={{0,3},{1,2},{2,1},{3,0},{4,7},{5,6},{6,5},{7,4},{8,11},{9,10},{10,... | collective-permute-start | bytes 3145736 | tf_op jit(solution)/shard_map/ppermute | solution.py:23
  89.5 55.2 %collective-permute-start.9 = (bf16[512,1024]{1,0:T(8,128)(2,1)}, bf16[512,1024]{1,0:T(8,128)(2,1)}, u32[]{:S(2)}, u32[]{:S(2)}) collective-permute-start(bf16[512,1024]{1,0:T(8,128)(2,1)} %fusion.8.masked.refs_8_), channel_id=1, source_target_pairs={{0,1},{1,0},{2,3},{3,2},{4,5},{5,4},{6,7},{7,6},{8,9},{9,8},{10,11... | collective-permute-start | bytes 3145736 | tf_op jit(solution)/shard_map/ppermute | solution.py:23
  142.6 55.7 %collective-permute-start.13 = (bf16[512,1024]{1,0:T(8,128)(2,1)}, bf16[512,1024]{1,0:T(8,128)(2,1)}, u32[]{:S(2)}, u32[]{:S(2)}) collective-permute-start(bf16[512,1024]{1,0:T(8,128)(2,1)} %get-tuple-element.152), channel_id=1, source_target_pairs={{0,1},{1,0},{2,3},{3,2},{4,5},{5,4},{6,7},{7,6},{8,9},{9,8},{10,11... | collective-permute-start | bytes 3145736 | tf_op jit(solution)/shard_map/ppermute | solution.py:23
  143.4 54.9 %collective-permute-start.14 = (bf16[512,1024]{1,0:T(8,128)(2,1)}, bf16[512,1024]{1,0:T(8,128)(2,1)}, u32[]{:S(2)}, u32[]{:S(2)}) collective-permute-start(bf16[512,1024]{1,0:T(8,128)(2,1)} %get-tuple-element.153), channel_id=1, source_target_pairs={{0,2},{1,3},{2,0},{3,1},{4,6},{5,7},{6,4},{7,5},{8,10},{9,11},{10,... | collective-permute-start | bytes 3145736 | tf_op jit(solution)/shard_map/ppermute | solution.py:23
  144.7 53.7 %collective-permute-start.12 = (bf16[512,1024]{1,0:T(8,128)(2,1)}, bf16[512,1024]{1,0:T(8,128)(2,1)}, u32[]{:S(2)}, u32[]{:S(2)}) collective-permute-start(bf16[512,1024]{1,0:T(8,128)(2,1)} %copy-done), channel_id=1, source_target_pairs={{0,3},{1,2},{2,1},{3,0},{4,7},{5,6},{6,5},{7,4},{8,11},{9,10},{10,... | collective-permute-start | bytes 3145736 | tf_op jit(solution)/shard_map/ppermute | solution.py:23
  206.3 32.6 %collective-permute-start.16 = (bf16[512,1024]{1,0:T(8,128)(2,1)}, bf16[512,1024]{1,0:T(8,128)(2,1)}, u32[]{:S(2)}, u32[]{:S(2)}) collective-permute-start(bf16[512,1024]{1,0:T(8,128)(2,1)} %get-tuple-element.163), channel_id=1, source_target_pairs={{0,3},{1,2},{2,1},{3,0},{4,7},{5,6},{6,5},{7,4},{8,11},{9,10},{10,... | collective-permute-start | bytes 3145736 | tf_op jit(solution)/shard_map/ppermute | solution.py:23
  217.8 21.0 %collective-permute-start.17 = (bf16[576,512]{1,0:T(8,128)(2,1)}, bf16[576,512]{1,0:T(8,128)(2,1)S(1)}, u32[]{:S(2)}, u32[]{:S(2)}) collective-permute-start(bf16[576,512]{1,0:T(8,128)(2,1)} %get-tuple-element.168), channel_id=1, source_target_pairs={{0,1},{1,0},{2,3},{3,2},{4,5},{5,4},{6,7},{7,6},{8,9},{9,8},{10,11... | collective-permute-start | bytes 1769480 | tf_op jit(solution)/shard_map/ppermute | solution.py:23
  220.1 18.8 %collective-permute-start.18 = (bf16[576,512]{1,0:T(8,128)(2,1)}, bf16[576,512]{1,0:T(8,128)(2,1)}, u32[]{:S(2)}, u32[]{:S(2)}) collective-permute-start(bf16[576,512]{1,0:T(8,128)(2,1)} %get-tuple-element.169), channel_id=1, source_target_pairs={{0,2},{1,3},{2,0},{3,1},{4,6},{5,7},{6,4},{7,5},{8,10},{9,11},{10,... | collective-permute-start | bytes 1769480 | tf_op jit(solution)/shard_map/ppermute | solution.py:23
  259.9 14.1 %collective-permute-start.20 = (bf16[512,512]{1,0:T(8,128)(2,1)S(1)}, bf16[512,512]{1,0:T(8,128)(2,1)}, u32[]{:S(2)}, u32[]{:S(2)}) collective-permute-start(bf16[512,512]{1,0:T(8,128)(2,1)S(1)} %bitcast.110), channel_id=1, source_target_pairs={{0,8},{4,12},{8,0},{12,4},{16,24},{20,28},{24,16},{28,20},{1,9},{5... | collective-permute-start | bytes 1572872 | tf_op jit(solution)/shard_map/ppermute | solution.py:54
  262.5 27.1 %collective-permute-start.23 = (bf16[12,64,128]{2,1,0:T(8,128)(2,1)}, bf16[12,64,128]{2,1,0:T(8,128)(2,1)}, u32[]{:S(2)}, u32[]{:S(2)}) collective-permute-start(bf16[12,64,128]{2,1,0:T(8,128)(2,1)} %get-tuple-element.238), channel_id=1, source_target_pairs={{0,1},{1,0},{2,3},{3,2},{4,5},{5,4},{6,7},{7,6},{8,9},{9,8},{10,11... | collective-permute-start | bytes 589832 | tf_op jit(solution)/shard_map/ppermute | solution.py:23
  264.7 24.9 %collective-permute-start.24 = (bf16[12,64,128]{2,1,0:T(8,128)(2,1)}, bf16[12,64,128]{2,1,0:T(8,128)(2,1)}, u32[]{:S(2)}, u32[]{:S(2)}) collective-permute-start(bf16[12,64,128]{2,1,0:T(8,128)(2,1)} %get-tuple-element.237), channel_id=1, source_target_pairs={{0,2},{1,3},{2,0},{3,1},{4,6},{5,7},{6,4},{7,5},{8,10},{9,11},{10,... | collective-permute-start | bytes 589832 | tf_op jit(solution)/shard_map/ppermute | solution.py:23
  265.2 24.4 %collective-permute-start.25 = (bf16[12,64,128]{2,1,0:T(8,128)(2,1)}, bf16[12,64,128]{2,1,0:T(8,128)(2,1)}, u32[]{:S(2)}, u32[]{:S(2)}) collective-permute-start(bf16[12,64,128]{2,1,0:T(8,128)(2,1)} %get-tuple-element.236), channel_id=1, source_target_pairs={{0,3},{1,2},{2,1},{3,0},{4,7},{5,6},{6,5},{7,4},{8,11},{9,10},{10,... | collective-permute-start | bytes 589832 | tf_op jit(solution)/shard_map/ppermute | solution.py:23
  266.1 23.5 %collective-permute-start.22 = (bf16[576,512]{1,0:T(8,128)(2,1)}, bf16[576,512]{1,0:T(8,128)(2,1)}, u32[]{:S(2)}, u32[]{:S(2)}) collective-permute-start(bf16[576,512]{1,0:T(8,128)(2,1)} %get-tuple-element.196), channel_id=1, source_target_pairs={{0,3},{1,2},{2,1},{3,0},{4,7},{5,6},{6,5},{7,4},{8,11},{9,10},{10,... | collective-permute-start | bytes 1769480 | tf_op jit(solution)/shard_map/ppermute | solution.py:23
  275.4 14.1 %collective-permute-start.21 = (bf16[256,512]{1,0:T(8,128)(2,1)S(1)}, bf16[256,512]{1,0:T(8,128)(2,1)S(1)}, u32[]{:S(2)}, u32[]{:S(2)}) collective-permute-start(bf16[256,512]{1,0:T(8,128)(2,1)S(1)} %fusion.19), channel_id=1, source_target_pairs={{0,16},{4,20},{8,24},{12,28},{16,0},{20,4},{24,8},{28,12},{1,17},{... | collective-permute-start | bytes 786440 | tf_op jit(solution)/shard_map/ppermute | solution.py:54
  297.7 10.5 %collective-permute-start.28 = (bf16[128,512]{1,0:T(8,128)(2,1)S(1)}, bf16[128,512]{1,0:T(8,128)(2,1)S(1)}, u32[]{:S(2)}, u32[]{:S(2)}) collective-permute-start(bf16[128,512]{1,0:T(8,128)(2,1)S(1)} %get-tuple-element.244), channel_id=1, source_target_pairs={{0,0},{1,1},{2,2},{3,3},{4,5},{5,4},{6,7},{7,6},{8,10},{9,11},{10,... | collective-permute-start | bytes 393224 | tf_op jit(solution)/shard_map/ppermute | solution.py:94
  303.1 11.8 %collective-permute-start.27 = (bf16[384,512]{1,0:T(8,128)(2,1)S(1)}, bf16[384,512]{1,0:T(8,128)(2,1)S(1)}, u32[]{:S(2)}, u32[]{:S(2)}) collective-permute-start(bf16[384,512]{1,0:T(8,128)(2,1)S(1)} %pad_maximum_fusion.1), channel_id=1, source_target_pairs={{0,8},{4,12},{8,0},{12,4},{16,24},{20,28},{24,16},{28,20},{1,9},{5... | collective-permute-start | bytes 1179656 | tf_op jit(solution)/shard_map/ppermute | solution.py:54
  315.1 14.7 %collective-permute-start.33 = (bf16[224,512]{1,0:T(8,128)(2,1)S(1)}, bf16[224,512]{1,0:T(8,128)(2,1)S(1)}, u32[]{:S(2)}, u32[]{:S(2)}) collective-permute-start(bf16[224,512]{1,0:T(8,128)(2,1)S(1)} %pad_maximum_fusion.4), channel_id=1, source_target_pairs={{0,16},{4,20},{8,24},{12,28},{16,0},{20,4},{24,8},{28,12},{1,17},{... | collective-permute-start | bytes 688136 | tf_op jit(solution)/shard_map/ppermute | solution.py:54
  318.7 11.2 %collective-permute-start.30 = (bf16[256,512]{1,0:T(8,128)(2,1)S(1)}, bf16[256,512]{1,0:T(8,128)(2,1)S(1)}, u32[]{:S(2)}, u32[]{:S(2)}) collective-permute-start(bf16[256,512]{1,0:T(8,128)(2,1)S(1)} %pad_maximum_fusion.2.refs_0_), channel_id=1, source_target_pairs={{0,1},{1,0},{2,3},{3,2},{4,5},{5,4},{6,7},{7,6},{8,9},{9,8},{10,11... | collective-permute-start | bytes 786440 | tf_op jit(solution)/shard_map/ppermute | solution.py:23
  319.7 12.8 %collective-permute-start.31 = (bf16[256,512]{1,0:T(8,128)(2,1)S(1)}, bf16[256,512]{1,0:T(8,128)(2,1)S(1)}, u32[]{:S(2)}, u32[]{:S(2)}) collective-permute-start(bf16[256,512]{1,0:T(8,128)(2,1)S(1)} %pad_maximum_fusion.2.refs_0_), channel_id=1, source_target_pairs={{0,2},{1,3},{2,0},{3,1},{4,6},{5,7},{6,4},{7,5},{8,10},{9,11},{10,... | collective-permute-start | bytes 786440 | tf_op jit(solution)/shard_map/ppermute | solution.py:23
  321.0 13.3 %collective-permute-start.32 = (bf16[256,512]{1,0:T(8,128)(2,1)S(1)}, bf16[256,512]{1,0:T(8,128)(2,1)S(1)}, u32[]{:S(2)}, u32[]{:S(2)}) collective-permute-start(bf16[256,512]{1,0:T(8,128)(2,1)S(1)} %pad_maximum_fusion.2.refs_0_), channel_id=1, source_target_pairs={{0,3},{1,2},{2,1},{3,0},{4,7},{5,6},{6,5},{7,4},{8,11},{9,10},{10,... | collective-permute-start | bytes 786440 | tf_op jit(solution)/shard_map/ppermute | solution.py:23
  334.4 9.3 %collective-permute-start.34 = (bf16[256,512]{1,0:T(8,128)(2,1)S(1)}, bf16[256,512]{1,0:T(8,128)(2,1)S(1)}, u32[]{:S(2)}, u32[]{:S(2)}) collective-permute-start(bf16[256,512]{1,0:T(8,128)(2,1)S(1)} %pad_maximum_fusion.3.refs_4_), channel_id=1, source_target_pairs={{0,1},{1,0},{2,3},{3,2},{4,5},{5,4},{6,7},{7,6},{8,9},{9,8},{10,11... | collective-permute-start | bytes 786440 | tf_op jit(solution)/shard_map/ppermute | solution.py:23
  335.6 12.7 %collective-permute-start.35 = (bf16[256,512]{1,0:T(8,128)(2,1)S(1)}, bf16[256,512]{1,0:T(8,128)(2,1)S(1)}, u32[]{:S(2)}, u32[]{:S(2)}) collective-permute-start(bf16[256,512]{1,0:T(8,128)(2,1)S(1)} %pad_maximum_fusion.3.refs_4_), channel_id=1, source_target_pairs={{0,2},{1,3},{2,0},{3,1},{4,6},{5,7},{6,4},{7,5},{8,10},{9,11},{10,... | collective-permute-start | bytes 786440 | tf_op jit(solution)/shard_map/ppermute | solution.py:23
  337.4 11.7 %collective-permute-start.36 = (bf16[256,512]{1,0:T(8,128)(2,1)S(1)}, bf16[256,512]{1,0:T(8,128)(2,1)}, u32[]{:S(2)}, u32[]{:S(2)}) collective-permute-start(bf16[256,512]{1,0:T(8,128)(2,1)S(1)} %pad_maximum_fusion.3.refs_4_), channel_id=1, source_target_pairs={{0,3},{1,2},{2,1},{3,0},{4,7},{5,6},{6,5},{7,4},{8,11},{9,10},{10,... | collective-permute-start | bytes 786440 | tf_op jit(solution)/shard_map/ppermute | solution.py:23
  (35 other events, 404.3 us)

commit v8 on v7

--- a/solution.py
+++ b/solution.py
@@ -12,9 +12,9 @@
 LN2 = 0.6931471805599453
 F32 = jnp.float32
 BF16 = jnp.bfloat16
-ENDS_ROWS = 64
+ENDS_ROWS = 128
 SCAN_ROWS = 64
-BACK_ROWS = 64
+BACK_ROWS = 128
 WIDE_STEP = 256
 
 
@@ -416,15 +416,15 @@
         def tile(j, unused):
             def gather(i, carry):
                 b_tile, c_tile = carry
-                for r in range(16):
-                    p = j * 128 + i * 16 + r
-                    here = lane == i * 16 + r
+                for r in range(64):
+                    p = j * 128 + i * 64 + r
+                    here = lane == i * 64 + r
                     b_tile = jnp.where(here, jnp.sum(b_sum[p], axis=1, keepdims=True), b_tile)
                     c_tile = jnp.where(here, jnp.sum(c_sum[p], axis=1, keepdims=True), c_tile)
                 return b_tile, c_tile
 
             zero_tile = jnp.zeros((states, 128), F32)
-            b_tile, c_tile = lax.fori_loop(0, 8, gather, (zero_tile, zero_tile))
+            b_tile, c_tile = lax.fori_loop(0, 2, gather, (zero_tile, zero_tile))
             at = pl.ds(pl.multiple_of(j * 128, 128), 128)
             bc_out[0:states, at] = b_tile
             bc_out[states : 2 * states, at] = c_tile

time: 353 us -> 349 us (0.989)
  Pallas kernels: 204 us -> 199 us
    pallas_call x2, Pallas kernels: 103 us -> 99 us  [full_scan(): pl.pallas_call(functools.partial(scan_kernel, len(earlier)), grid_spec=pl...]
  transfers between devices with their start and end apart: 37 -> 37, of which waited for: 15 -> 16; matrix products, arithmetic and copies ran while one was open for 8% -> 8% of each run, Pallas kernels for 51% -> 50%
where the time goes in v8:
time: 349 us; the launch traced here: 348 us
  Pallas kernels  199 us (57%)
  waiting for transfers between devices  59.4 us (17%)
  starting transfers between devices  48.5 us (14%)
  other arithmetic  16.8 us (5%)
  matrix products  13.5 us (4%)
  local copies, waits for them, and re-layouts  9.03 us (3%)
    pallas_call x2, Pallas kernels, full_scan(): pl.pallas_call(functools.partial(scan_kernel, len(earlier)), grid_spec=pl...  99 us
    pallas_call x1, Pallas kernels, local_ends(): pl.pallas_call(ends_kernel, grid=(channels // width,), in_specs=[pl.Block...  43.7 us
    ppermute x27, starting transfers between devices, swapped(): lax.ppermute(value, 'state', [(i, i ^ distance) for i in range(count)])  33.5 us
    ppermute x6, waiting for transfers between devices, seq_exchange(): return lax.ppermute(value, 'seq', [(i, i ^ distance) for i in range(count)])  28.1 us
    ppermute x27, waiting for transfers between devices, swapped(): lax.ppermute(value, 'state', [(i, i ^ distance) for i in range(count)])  25.8 us
    pallas_call x2, Pallas kernels, back(): pl.pallas_call(functools.partial(back_kernel, len(earlier)), grid_spec=pl...  21 us
    pallas_call x1, Pallas kernels, wide_grads(): pl.pallas_call(functools.partial(wide_kernel, high), grid_spec=pltpu.Pref...  12.3 us
    pallas_call x1, Pallas kernels, front(): pl.pallas_call(front_kernel, grid=(channels // width,), in_specs=[whole(n...  11.2 us
  transfers between devices with their start and end apart: 37, of which 16 were waited for; matrix products, arithmetic and copies ran while one was open for 8% of the time, Pallas kernels for 50%

profile of v8, /device:TPU:0, one launch (start us, length us, event | category | flops | bytes accessed | tf_op | source)
XLA Modules:
  0.0 348.3 jit_solution(14250301475682334884)
XLA Ops:
  0.7 3.0 collective-permute-start.1
  9.3 3.8 %collective-permute-start = (bf16[8,1024]{1,0:T(8,128)(2,1)S(1)}, bf16[8,1024]{1,0:T(8,128)(2,1)S(1)}, u32[]{:S(2)}, u32[]{:S(2)}) collective-permute-start(bf16[8,1024]{1,0:T(8,128)(2,1)S(1)} %slice.183), channel_id=1, source_target_pairs={{0,1},{1,2},{2,3},{4,5},{5,6},{6,7},{8,9},{9,10},{10,11},{12,13},{... | collective-permute-start | bytes 49160 | tf_op jit(solution)/shard_map/ppermute | solution.py:29
  17.1 11.2 %front.1 = (f32[512,2048]{1,0:T(8,128)}, f32[512,128]{1,0:T(8,128)}, bf16[512,2048]{1,0:T(8,128)(2,1)}, bf16[8,2048]{1,0:T(8,128)(2,1)}) custom-call(bf16[512,1024]{1,0:T(8,128)(2,1)} %copy-done, bf16[8,1024]{1,0:T(8,128)(2,1)} %copy-done.26, bf16[1024,4096]{1,0:T(8,128)(2,1)} %gate_w.1, f32[4,2048]{1,0:T(4,128)} %conv_w.5, f32[1,2048]{1,0:T(1,128)} %bitcast.116, ...), custom_call_target="tpu_custom_call" | custom-call | flops 8 | bytes 1024 | tf_op jit(solution)/shard_map/front/pallas_call | solution.py:725
  31.1 43.7 %ends.1 = (f32[512,2048]{1,0:T(8,128)}, f32[512,2048]{1,0:T(8,128)}, f32[512,2048]{1,0:T(8,128)}, f32[8,2048]{1,0:T(8,128)}, f32[16,2048]{1,0:T(8,128)}, /*index...) custom-call(s32[2]{0:T(128)} %get-tuple-element.254.live, ...), custom_call_target="tpu_custom_call" | custom-call | flops 40 | bytes 1024 | tf_op jit(solution)/shard_map/ends/pallas_call | solution.py:754
  79.3 3.3 collective-permute-done.6
  82.6 3.0 collective-permute-done.7
  90.7 49.5 %scan.2 = (bf16[512,2048]{1,0:T(8,128)(2,1)}, bf16[512,2048]{1,0:T(8,128)(2,1)}, f32[512,2048]{1,0:T(8,128)}, f32[16,2048]{1,0:T(8,128)}, f32[8,2048]{1,0:T(8,12...) custom-call(s32[2]{0:T(128)} %pad_add_fusion.2.order, ...), custom_call_target="tpu_custom_call" | custom-call | flops 50 | bytes 1024 | tf_op jit(solution)/shard_map/scan/pallas_call | solution.py:818
  144.7 49.5 %scan.3 = (bf16[512,2048]{1,0:T(8,128)(2,1)}, bf16[512,2048]{1,0:T(8,128)(2,1)}, f32[512,2048]{1,0:T(8,128)}, f32[16,2048]{1,0:T(8,128)}, f32[8,2048]{1,0:T(8,12...) custom-call(s32[2]{0:T(128)} %get-tuple-element.253.order, ...), custom_call_target="tpu_custom_call", output_to_operand_aliasing={{0}: (12, {}), {1}: (13, {}), {2}: (14, {}), {3}: (15, {}),... | custom-call | flops 50 | bytes 1024 | tf_op jit(solution)/shard_map/scan/pallas_call | solution.py:818
  196.7 5.4 %collective-permute-done.15.ahead = f32[8,2048]{1,0:T(8,128)S(1)} collective-permute-done((f32[8,2048]{1,0:T(8,128)S(1)}, f32[8,2048]{1,0:T(8,128)S(1)}, u32[]{:S(2)}, u32[]{:S(2)}) %collective-permute-start.15) | collective-permute-done | bytes 65568 | tf_op jit(solution)/shard_map/ppermute | solution.py:29
  202.7 10.4 %back.2 = (bf16[512,2048]{1,0:T(8,128)(2,1)}, bf16[4,12,64,128]{3,2,1,0:T(8,128)(2,1)}, bf16[576,512]{1,0:T(8,128)(2,1)}, bf16[576,512]{1,0:T(8,128)(2,1)}) custom-call(s32[3]{0:T(128)} %get-tuple-element.255.order, bf16[512,128]{1,0:T(8,128)(2,1)} %get-tuple-element.155.proj_grad, bf16[128,2048]{1,0:T(8,128)(2,1)} %pad.4.xproj, ...), custom_call_target="tpu_custom_call" | custom-call | flops 18 | bytes 1024 | tf_op jit(solution)/shard_map/back/pallas_call | solution.py:876
  213.1 2.3 collective-permute-start.17
  217.2 10.6 %back.3 = (bf16[512,2048]{1,0:T(8,128)(2,1)}, bf16[4,12,64,128]{3,2,1,0:T(8,128)(2,1)}, bf16[576,512]{1,0:T(8,128)(2,1)}, bf16[576,512]{1,0:T(8,128)(2,1)}) custom-call(s32[3]{0:T(128)} %get-tuple-element.256.order, bf16[512,128]{1,0:T(8,128)(2,1)} %get-tuple-element.155.proj_grad, ...), custom_call_target="tpu_custom_call", output_to_operand_aliasing={{0}: (13, {}), {1}: (14, {})} | custom-call | flops 18 | bytes 1024 | tf_op jit(solution)/shard_map/back/pallas_call | solution.py:876
  227.8 6.8 %collective-permute-done.17.refs_5_ = bf16[576,512]{1,0:T(8,128)(2,1)S(1)} collective-permute-done((bf16[576,512]{1,0:T(8,128)(2,1)}, bf16[576,512]{1,0:T(8,128)(2,1)S(1)}, u32[]{:S(2)}, u32[]{:S(2)}) %collective-permute-start.17) | collective-permute-done | bytes 589856 | tf_op jit(solution)/shard_map/ppermute | solution.py:23
  234.8 12.3 %wide.1 = (f32[1024,512]{1,0:T(8,128)}, f32[1024,512]{1,0:T(8,128)}) custom-call(s32[9]{0:T(128)} %stack.49.at, bf16[512,1024]{1,0:T(8,128)(2,1)} %get-tuple-element.173.refs_0_.refs_4_, bf16[512,1024]{1,0:T(8,128)(2,1)} %collective-permute-done.13.refs_1_.refs_5_, bf16[512,1024]{1,0:T(8,128)(2,1)} %collective-permute-done.14.refs_2_.refs_6_, ...), custom_call_target="tpu_custom_call" | custom-call | flops 10 | bytes 1024 | tf_op jit(solution)/shard_map/wide/pallas_call | solution.py:927
  247.2 4.4 %collective-permute-done.19 = f32[1024,512]{1,0:T(8,128)S(1)} collective-permute-done((f32[1024,512]{1,0:T(8,128)}, f32[1024,512]{1,0:T(8,128)S(1)}, u32[]{:S(2)}, u32[]{:S(2)}) %collective-permute-start.19) | collective-permute-done | bytes 2097184 | tf_op jit(solution)/shard_map/ppermute | solution.py:54
  252.9 2.8 add.179
  258.3 2.2 collective-permute-start.23
  261.9 2.0 collective-permute-start.22
  263.9 6.0 %collective-permute-done.20 = bf16[512,512]{1,0:T(8,128)(2,1)} collective-permute-done((bf16[512,512]{1,0:T(8,128)(2,1)S(1)}, bf16[512,512]{1,0:T(8,128)(2,1)}, u32[]{:S(2)}, u32[]{:S(2)}) %collective-permute-start.20) | collective-permute-done | bytes 524320 | tf_op jit(solution)/shard_map/ppermute | solution.py:54
  271.2 2.7 collective-permute-start.21
  273.9 5.1 %fusion = f32[512,1024]{1,0:T(8,128)S(1)} fusion(bf16[512,2048]{1,0:T(8,128)(2,1)S(1)} %copy-done.9, bf16[1024,4096]{1,0:T(8,128)(2,1)} %gate_w.1), kind=kOutput, calls=%fused_computation | convolution fusion | flops 2147483648 | bytes 8388608 | tf_op jit(solution)/shard_map/dot_general | solution.py:992
  279.1 4.0 %fusion.13 = (f32[1024]{0:T(1024)S(1)}, f32[512]{0:T(512)S(1)}, f32[512,1024]{1,0:T(8,128)}) fusion(bf16[512,1024]{1,0:T(8,128)(2,1)S(1)} %copy-done.1, f32[512]{0:T(512)S(1)} %add_rsqrt_fusion, f32[1024]{0:T(1024)S(1)} %copy-done.27, f32[512,1024]{1,0:T(8,128)S(1)} %fusion, bf16[512,2048]{1,0:T(8,128)(2,1)S(1)} %copy-done.7, ...), kind=kOutput, calls=%fused_computation.18 | convolution fusion | flops 2151676416 | bytes 11546624 | tf_op jit(solution)/shard_map/dot_general | solution.py:992
  285.4 8.3 %inner.1 = (f32[672,512]{1,0:T(8,128)}, f32[672,512]{1,0:T(8,128)}) custom-call(s32[9]{0:T(128)} %stack.49.at, bf16[512,1024]{1,0:T(8,128)(2,1)} %copy-done, bf16[512,1024]{1,0:T(8,128)(2,1)} %collective-permute-done.4.refs_13_.refs_1_, bf16[512,1024]{1,0:T(8,128)(2,1)} %collective-permute-done.5.refs_14_.refs_2_, ...), custom_call_target="tpu_custom_call" | custom-call | flops 5 | bytes 1024 | tf_op jit(solution)/shard_map/inner/pallas_call | solution.py:953
  294.4 2.6 collective-permute-done.26
  300.9 3.3 fusion.15
  304.9 6.1 %collective-permute-done.27 = bf16[384,512]{1,0:T(8,128)(2,1)S(1)} collective-permute-done((bf16[384,512]{1,0:T(8,128)(2,1)S(1)}, bf16[384,512]{1,0:T(8,128)(2,1)S(1)}, u32[]{:S(2)}, u32[]{:S(2)}) %collective-permute-start.27) | collective-permute-done | bytes 393248 | tf_op jit(solution)/shard_map/ppermute | solution.py:54
  311.3 3.1 collective-permute-start.33
  318.2 7.4 %collective-permute-done.33 = bf16[224,512]{1,0:T(8,128)(2,1)S(1)} collective-permute-done((bf16[224,512]{1,0:T(8,128)(2,1)S(1)}, bf16[224,512]{1,0:T(8,128)(2,1)S(1)}, u32[]{:S(2)}, u32[]{:S(2)}) %collective-permute-start.33) | collective-permute-done | bytes 229408 | tf_op jit(solution)/shard_map/ppermute | solution.py:54
  325.7 2.7 collective-permute-done.31.refs_2_
  335.9 3.8 %collective-permute-done.34.refs_5_ = bf16[256,512]{1,0:T(8,128)(2,1)S(1)} collective-permute-done((bf16[256,512]{1,0:T(8,128)(2,1)S(1)}, bf16[256,512]{1,0:T(8,128)(2,1)S(1)}, u32[]{:S(2)}, u32[]{:S(2)}) %collective-permute-start.34) | collective-permute-done | bytes 262176 | tf_op jit(solution)/shard_map/ppermute | solution.py:23
  339.7 3.9 %collective-permute-done.35.refs_6_ = bf16[256,512]{1,0:T(8,128)(2,1)S(1)} collective-permute-done((bf16[256,512]{1,0:T(8,128)(2,1)S(1)}, bf16[256,512]{1,0:T(8,128)(2,1)S(1)}, u32[]{:S(2)}, u32[]{:S(2)}) %collective-permute-start.35) | collective-permute-done | bytes 262176 | tf_op jit(solution)/shard_map/ppermute | solution.py:23
  344.5 3.6 %assemble.1 = (f32[128,4096]{1,0:T(8,128)}, f32[256,1024]{1,0:T(8,128)}, f32[96,256]{1,0:T(8,128)}, f32[64,256]{1,0:T(8,128)}, f32[4,2048]{1,0:T(4,128)}, /*inde...) custom-call(s32[9]{0:T(128)} %stack.49.at, ...), custom_call_target="tpu_custom_call" | custom-call | flops 4 | bytes 1024 | tf_op jit(solution)/shard_map/assemble/pallas_call | solution.py:979
  (167 shorter events, 57.2 us)
Async XLA Ops:
  0.7 29.6 %collective-permute-start.1 = (f32[4,2048]{1,0:T(4,128)}, f32[4,2048]{1,0:T(4,128)S(1)}, u32[]{:S(2)}, u32[]{:S(2)}) collective-permute-start(f32[4,2048]{1,0:T(4,128)} %param.23), channel_id=1, source_target_pairs={{0,1},{1,0},{2,3},{3,2},{4,5},{5,4},{6,7},{7,6},{8,9},{9,8},{10,11... | collective-permute-start | bytes 98312 | tf_op jit(solution)/shard_map/ppermute | solution.py:23
  3.7 26.7 %collective-permute-start.2 = (f32[4,2048]{1,0:T(4,128)}, f32[4,2048]{1,0:T(4,128)S(1)}, u32[]{:S(2)}, u32[]{:S(2)}) collective-permute-start(f32[4,2048]{1,0:T(4,128)} %param.23), channel_id=1, source_target_pairs={{0,2},{1,3},{2,0},{3,1},{4,6},{5,7},{6,4},{7,5},{8,10},{9,11},{10,... | collective-permute-start | bytes 98312 | tf_op jit(solution)/shard_map/ppermute | solution.py:23
  5.2 25.2 %collective-permute-start.3 = (f32[4,2048]{1,0:T(4,128)}, f32[4,2048]{1,0:T(4,128)S(1)}, u32[]{:S(2)}, u32[]{:S(2)}) collective-permute-start(f32[4,2048]{1,0:T(4,128)} %param.23), channel_id=1, source_target_pairs={{0,3},{1,2},{2,1},{3,0},{4,7},{5,6},{6,5},{7,4},{8,11},{9,10},{10,... | collective-permute-start | bytes 98312 | tf_op jit(solution)/shard_map/ppermute | solution.py:23
  28.4 46.4 %collective-permute-start.4 = (bf16[512,1024]{1,0:T(8,128)(2,1)}, bf16[512,1024]{1,0:T(8,128)(2,1)}, u32[]{:S(2)}, u32[]{:S(2)}) collective-permute-start(bf16[512,1024]{1,0:T(8,128)(2,1)} %copy-done), channel_id=1, source_target_pairs={{0,1},{1,0},{2,3},{3,2},{4,5},{5,4},{6,7},{7,6},{8,9},{9,8},{10,11... | collective-permute-start | bytes 3145736 | tf_op jit(solution)/shard_map/ppermute | solution.py:23
  29.9 44.8 %collective-permute-start.5 = (bf16[512,1024]{1,0:T(8,128)(2,1)}, bf16[512,1024]{1,0:T(8,128)(2,1)}, u32[]{:S(2)}, u32[]{:S(2)}) collective-permute-start(bf16[512,1024]{1,0:T(8,128)(2,1)} %copy-done), channel_id=1, source_target_pairs={{0,2},{1,3},{2,0},{3,1},{4,6},{5,7},{6,4},{7,5},{8,10},{9,11},{10,... | collective-permute-start | bytes 3145736 | tf_op jit(solution)/shard_map/ppermute | solution.py:23
  74.8 7.8 %collective-permute-start.6 = (f32[24,2048]{1,0:T(8,128)}, f32[24,2048]{1,0:T(8,128)S(1)}, u32[]{:S(2)}, u32[]{:S(2)}) collective-permute-start(f32[24,2048]{1,0:T(8,128)} %get-tuple-element.134), channel_id=1, source_target_pairs={{0,1},{1,0},{2,3},{3,2},{4,5},{5,4},{6,7},{7,6},{8,9},{9,8},{10,11... | collective-permute-start | bytes 589832 | tf_op jit(solution)/shard_map/ppermute | solution.py:23
  76.5 9.1 %collective-permute-start.7 = (f32[24,2048]{1,0:T(8,128)}, f32[24,2048]{1,0:T(8,128)S(1)}, u32[]{:S(2)}, u32[]{:S(2)}) collective-permute-start(f32[24,2048]{1,0:T(8,128)} %get-tuple-element.135), channel_id=1, source_target_pairs={{0,2},{1,3},{2,0},{3,1},{4,6},{5,7},{6,4},{7,5},{8,10},{9,11},{10,... | collective-permute-start | bytes 589832 | tf_op jit(solution)/shard_map/ppermute | solution.py:23
  77.0 8.6 %collective-permute-start.8 = (f32[24,2048]{1,0:T(8,128)}, f32[24,2048]{1,0:T(8,128)S(1)}, u32[]{:S(2)}, u32[]{:S(2)}) collective-permute-start(f32[24,2048]{1,0:T(8,128)} %get-tuple-element.136), channel_id=1, source_target_pairs={{0,3},{1,2},{2,1},{3,0},{4,7},{5,6},{6,5},{7,4},{8,11},{9,10},{10,... | collective-permute-start | bytes 589832 | tf_op jit(solution)/shard_map/ppermute | solution.py:23
  86.6 55.6 %collective-permute-start.10 = (bf16[512,1024]{1,0:T(8,128)(2,1)}, bf16[512,1024]{1,0:T(8,128)(2,1)}, u32[]{:S(2)}, u32[]{:S(2)}) collective-permute-start(bf16[512,1024]{1,0:T(8,128)(2,1)} %fusion.8.masked.refs_8_), channel_id=1, source_target_pairs={{0,2},{1,3},{2,0},{3,1},{4,6},{5,7},{6,4},{7,5},{8,10},{9,11},{10,... | collective-permute-start | bytes 3145736 | tf_op jit(solution)/shard_map/ppermute | solution.py:23
  87.5 54.7 %collective-permute-start.11 = (bf16[512,1024]{1,0:T(8,128)(2,1)}, bf16[512,1024]{1,0:T(8,128)(2,1)}, u32[]{:S(2)}, u32[]{:S(2)}) collective-permute-start(bf16[512,1024]{1,0:T(8,128)(2,1)} %fusion.8.masked.refs_8_), channel_id=1, source_target_pairs={{0,3},{1,2},{2,1},{3,0},{4,7},{5,6},{6,5},{7,4},{8,11},{9,10},{10,... | collective-permute-start | bytes 3145736 | tf_op jit(solution)/shard_map/ppermute | solution.py:23
  88.8 53.4 %collective-permute-start.9 = (bf16[512,1024]{1,0:T(8,128)(2,1)}, bf16[512,1024]{1,0:T(8,128)(2,1)}, u32[]{:S(2)}, u32[]{:S(2)}) collective-permute-start(bf16[512,1024]{1,0:T(8,128)(2,1)} %fusion.8.masked.refs_8_), channel_id=1, source_target_pairs={{0,1},{1,0},{2,3},{3,2},{4,5},{5,4},{6,7},{7,6},{8,9},{9,8},{10,11... | collective-permute-start | bytes 3145736 | tf_op jit(solution)/shard_map/ppermute | solution.py:23
  140.2 53.9 %collective-permute-start.13 = (bf16[512,1024]{1,0:T(8,128)(2,1)}, bf16[512,1024]{1,0:T(8,128)(2,1)}, u32[]{:S(2)}, u32[]{:S(2)}) collective-permute-start(bf16[512,1024]{1,0:T(8,128)(2,1)} %get-tuple-element.152), channel_id=1, source_target_pairs={{0,1},{1,0},{2,3},{3,2},{4,5},{5,4},{6,7},{7,6},{8,9},{9,8},{10,11... | collective-permute-start | bytes 3145736 | tf_op jit(solution)/shard_map/ppermute | solution.py:23
  141.0 53.1 %collective-permute-start.14 = (bf16[512,1024]{1,0:T(8,128)(2,1)}, bf16[512,1024]{1,0:T(8,128)(2,1)}, u32[]{:S(2)}, u32[]{:S(2)}) collective-permute-start(bf16[512,1024]{1,0:T(8,128)(2,1)} %get-tuple-element.153), channel_id=1, source_target_pairs={{0,2},{1,3},{2,0},{3,1},{4,6},{5,7},{6,4},{7,5},{8,10},{9,11},{10,... | collective-permute-start | bytes 3145736 | tf_op jit(solution)/shard_map/ppermute | solution.py:23
  142.3 51.9 %collective-permute-start.12 = (bf16[512,1024]{1,0:T(8,128)(2,1)}, bf16[512,1024]{1,0:T(8,128)(2,1)}, u32[]{:S(2)}, u32[]{:S(2)}) collective-permute-start(bf16[512,1024]{1,0:T(8,128)(2,1)} %copy-done), channel_id=1, source_target_pairs={{0,3},{1,2},{2,1},{3,0},{4,7},{5,6},{6,5},{7,4},{8,11},{9,10},{10,... | collective-permute-start | bytes 3145736 | tf_op jit(solution)/shard_map/ppermute | solution.py:23
  202.1 32.6 %collective-permute-start.16 = (bf16[512,1024]{1,0:T(8,128)(2,1)}, bf16[512,1024]{1,0:T(8,128)(2,1)}, u32[]{:S(2)}, u32[]{:S(2)}) collective-permute-start(bf16[512,1024]{1,0:T(8,128)(2,1)} %get-tuple-element.163), channel_id=1, source_target_pairs={{0,3},{1,2},{2,1},{3,0},{4,7},{5,6},{6,5},{7,4},{8,11},{9,10},{10,... | collective-permute-start | bytes 3145736 | tf_op jit(solution)/shard_map/ppermute | solution.py:23
  213.1 21.5 %collective-permute-start.17 = (bf16[576,512]{1,0:T(8,128)(2,1)}, bf16[576,512]{1,0:T(8,128)(2,1)S(1)}, u32[]{:S(2)}, u32[]{:S(2)}) collective-permute-start(bf16[576,512]{1,0:T(8,128)(2,1)} %get-tuple-element.168), channel_id=1, source_target_pairs={{0,1},{1,0},{2,3},{3,2},{4,5},{5,4},{6,7},{7,6},{8,9},{9,8},{10,11... | collective-permute-start | bytes 1769480 | tf_op jit(solution)/shard_map/ppermute | solution.py:23
  215.5 19.3 %collective-permute-start.18 = (bf16[576,512]{1,0:T(8,128)(2,1)}, bf16[576,512]{1,0:T(8,128)(2,1)}, u32[]{:S(2)}, u32[]{:S(2)}) collective-permute-start(bf16[576,512]{1,0:T(8,128)(2,1)} %get-tuple-element.169), channel_id=1, source_target_pairs={{0,2},{1,3},{2,0},{3,1},{4,6},{5,7},{6,4},{7,5},{8,10},{9,11},{10,... | collective-permute-start | bytes 1769480 | tf_op jit(solution)/shard_map/ppermute | solution.py:23
  255.8 14.1 %collective-permute-start.20 = (bf16[512,512]{1,0:T(8,128)(2,1)S(1)}, bf16[512,512]{1,0:T(8,128)(2,1)}, u32[]{:S(2)}, u32[]{:S(2)}) collective-permute-start(bf16[512,512]{1,0:T(8,128)(2,1)S(1)} %bitcast.110), channel_id=1, source_target_pairs={{0,8},{4,12},{8,0},{12,4},{16,24},{20,28},{24,16},{28,20},{1,9},{5... | collective-permute-start | bytes 1572872 | tf_op jit(solution)/shard_map/ppermute | solution.py:54
  258.3 27.1 %collective-permute-start.23 = (bf16[12,64,128]{2,1,0:T(8,128)(2,1)}, bf16[12,64,128]{2,1,0:T(8,128)(2,1)}, u32[]{:S(2)}, u32[]{:S(2)}) collective-permute-start(bf16[12,64,128]{2,1,0:T(8,128)(2,1)} %get-tuple-element.238), channel_id=1, source_target_pairs={{0,1},{1,0},{2,3},{3,2},{4,5},{5,4},{6,7},{7,6},{8,9},{9,8},{10,11... | collective-permute-start | bytes 589832 | tf_op jit(solution)/shard_map/ppermute | solution.py:23
  260.5 24.9 %collective-permute-start.24 = (bf16[12,64,128]{2,1,0:T(8,128)(2,1)}, bf16[12,64,128]{2,1,0:T(8,128)(2,1)}, u32[]{:S(2)}, u32[]{:S(2)}) collective-permute-start(bf16[12,64,128]{2,1,0:T(8,128)(2,1)} %get-tuple-element.237), channel_id=1, source_target_pairs={{0,2},{1,3},{2,0},{3,1},{4,6},{5,7},{6,4},{7,5},{8,10},{9,11},{10,... | collective-permute-start | bytes 589832 | tf_op jit(solution)/shard_map/ppermute | solution.py:23
  261.0 24.4 %collective-permute-start.25 = (bf16[12,64,128]{2,1,0:T(8,128)(2,1)}, bf16[12,64,128]{2,1,0:T(8,128)(2,1)}, u32[]{:S(2)}, u32[]{:S(2)}) collective-permute-start(bf16[12,64,128]{2,1,0:T(8,128)(2,1)} %get-tuple-element.236), channel_id=1, source_target_pairs={{0,3},{1,2},{2,1},{3,0},{4,7},{5,6},{6,5},{7,4},{8,11},{9,10},{10,... | collective-permute-start | bytes 589832 | tf_op jit(solution)/shard_map/ppermute | solution.py:23
  261.9 23.5 %collective-permute-start.22 = (bf16[576,512]{1,0:T(8,128)(2,1)}, bf16[576,512]{1,0:T(8,128)(2,1)}, u32[]{:S(2)}, u32[]{:S(2)}) collective-permute-start(bf16[576,512]{1,0:T(8,128)(2,1)} %get-tuple-element.196), channel_id=1, source_target_pairs={{0,3},{1,2},{2,1},{3,0},{4,7},{5,6},{6,5},{7,4},{8,11},{9,10},{10,... | collective-permute-start | bytes 1769480 | tf_op jit(solution)/shard_map/ppermute | solution.py:23
  271.2 14.1 %collective-permute-start.21 = (bf16[256,512]{1,0:T(8,128)(2,1)S(1)}, bf16[256,512]{1,0:T(8,128)(2,1)S(1)}, u32[]{:S(2)}, u32[]{:S(2)}) collective-permute-start(bf16[256,512]{1,0:T(8,128)(2,1)S(1)} %fusion.19), channel_id=1, source_target_pairs={{0,16},{4,20},{8,24},{12,28},{16,0},{20,4},{24,8},{28,12},{1,17},{... | collective-permute-start | bytes 786440 | tf_op jit(solution)/shard_map/ppermute | solution.py:54
  293.8 10.5 %collective-permute-start.28 = (bf16[128,512]{1,0:T(8,128)(2,1)S(1)}, bf16[128,512]{1,0:T(8,128)(2,1)S(1)}, u32[]{:S(2)}, u32[]{:S(2)}) collective-permute-start(bf16[128,512]{1,0:T(8,128)(2,1)S(1)} %get-tuple-element.244), channel_id=1, source_target_pairs={{0,0},{1,1},{2,2},{3,3},{4,5},{5,4},{6,7},{7,6},{8,10},{9,11},{10,... | collective-permute-start | bytes 393224 | tf_op jit(solution)/shard_map/ppermute | solution.py:94
  299.1 12.0 %collective-permute-start.27 = (bf16[384,512]{1,0:T(8,128)(2,1)S(1)}, bf16[384,512]{1,0:T(8,128)(2,1)S(1)}, u32[]{:S(2)}, u32[]{:S(2)}) collective-permute-start(bf16[384,512]{1,0:T(8,128)(2,1)S(1)} %pad_maximum_fusion.1), channel_id=1, source_target_pairs={{0,8},{4,12},{8,0},{12,4},{16,24},{20,28},{24,16},{28,20},{1,9},{5... | collective-permute-start | bytes 1179656 | tf_op jit(solution)/shard_map/ppermute | solution.py:54
  311.3 14.3 %collective-permute-start.33 = (bf16[224,512]{1,0:T(8,128)(2,1)S(1)}, bf16[224,512]{1,0:T(8,128)(2,1)S(1)}, u32[]{:S(2)}, u32[]{:S(2)}) collective-permute-start(bf16[224,512]{1,0:T(8,128)(2,1)S(1)} %pad_maximum_fusion.4), channel_id=1, source_target_pairs={{0,16},{4,20},{8,24},{12,28},{16,0},{20,4},{24,8},{28,12},{1,17},{... | collective-permute-start | bytes 688136 | tf_op jit(solution)/shard_map/ppermute | solution.py:54
  314.5 11.2 %collective-permute-start.30 = (bf16[256,512]{1,0:T(8,128)(2,1)S(1)}, bf16[256,512]{1,0:T(8,128)(2,1)S(1)}, u32[]{:S(2)}, u32[]{:S(2)}) collective-permute-start(bf16[256,512]{1,0:T(8,128)(2,1)S(1)} %pad_maximum_fusion.2.refs_0_), channel_id=1, source_target_pairs={{0,1},{1,0},{2,3},{3,2},{4,5},{5,4},{6,7},{7,6},{8,9},{9,8},{10,11... | collective-permute-start | bytes 786440 | tf_op jit(solution)/shard_map/ppermute | solution.py:23
  315.7 12.7 %collective-permute-start.31 = (bf16[256,512]{1,0:T(8,128)(2,1)S(1)}, bf16[256,512]{1,0:T(8,128)(2,1)S(1)}, u32[]{:S(2)}, u32[]{:S(2)}) collective-permute-start(bf16[256,512]{1,0:T(8,128)(2,1)S(1)} %pad_maximum_fusion.2.refs_0_), channel_id=1, source_target_pairs={{0,2},{1,3},{2,0},{3,1},{4,6},{5,7},{6,4},{7,5},{8,10},{9,11},{10,... | collective-permute-start | bytes 786440 | tf_op jit(solution)/shard_map/ppermute | solution.py:23
  316.8 13.4 %collective-permute-start.32 = (bf16[256,512]{1,0:T(8,128)(2,1)S(1)}, bf16[256,512]{1,0:T(8,128)(2,1)S(1)}, u32[]{:S(2)}, u32[]{:S(2)}) collective-permute-start(bf16[256,512]{1,0:T(8,128)(2,1)S(1)} %pad_maximum_fusion.2.refs_0_), channel_id=1, source_target_pairs={{0,3},{1,2},{2,1},{3,0},{4,7},{5,6},{6,5},{7,4},{8,11},{9,10},{10,... | collective-permute-start | bytes 786440 | tf_op jit(solution)/shard_map/ppermute | solution.py:23
  330.4 9.3 %collective-permute-start.34 = (bf16[256,512]{1,0:T(8,128)(2,1)S(1)}, bf16[256,512]{1,0:T(8,128)(2,1)S(1)}, u32[]{:S(2)}, u32[]{:S(2)}) collective-permute-start(bf16[256,512]{1,0:T(8,128)(2,1)S(1)} %pad_maximum_fusion.3.refs_4_), channel_id=1, source_target_pairs={{0,1},{1,0},{2,3},{3,2},{4,5},{5,4},{6,7},{7,6},{8,9},{9,8},{10,11... | collective-permute-start | bytes 786440 | tf_op jit(solution)/shard_map/ppermute | solution.py:23
  331.6 11.9 %collective-permute-start.35 = (bf16[256,512]{1,0:T(8,128)(2,1)S(1)}, bf16[256,512]{1,0:T(8,128)(2,1)S(1)}, u32[]{:S(2)}, u32[]{:S(2)}) collective-permute-start(bf16[256,512]{1,0:T(8,128)(2,1)S(1)} %pad_maximum_fusion.3.refs_4_), channel_id=1, source_target_pairs={{0,2},{1,3},{2,0},{3,1},{4,6},{5,7},{6,4},{7,5},{8,10},{9,11},{10,... | collective-permute-start | bytes 786440 | tf_op jit(solution)/shard_map/ppermute | solution.py:23
  333.4 11.1 %collective-permute-start.36 = (bf16[256,512]{1,0:T(8,128)(2,1)S(1)}, bf16[256,512]{1,0:T(8,128)(2,1)}, u32[]{:S(2)}, u32[]{:S(2)}) collective-permute-start(bf16[256,512]{1,0:T(8,128)(2,1)S(1)} %pad_maximum_fusion.3.refs_4_), channel_id=1, source_target_pairs={{0,3},{1,2},{2,1},{3,0},{4,7},{5,6},{6,5},{7,4},{8,11},{9,10},{10,... | collective-permute-start | bytes 786440 | tf_op jit(solution)/shard_map/ppermute | solution.py:23
  (35 other events, 398.2 us)

commit v9 on v8

--- a/solution.py
+++ b/solution.py
@@ -113,7 +113,7 @@
 
 
 def fill_lanes(out_ref, cols_ref, rows):
-    groups = min(16, rows // 8)
+    groups = min(32, rows // 8)
     states = cols_ref.shape[0]
     lanes = min(128, rows)
 
@@ -329,7 +329,7 @@
         y_sum[row, :] = sums_to_rows(parts, sublane)
         return state
 
-    lax.fori_loop(0, groups, forward, state_in[...])
+    lax.fori_loop(0, groups, forward, state_in[...], unroll=2)
 
     def over_tiles(value):
         total = value[:, 0:128]

time: 349 us -> 348 us (level)
  no operation moved by 1% of the time
where the time goes in v9:
time: 348 us; the launch traced here: 347 us
  Pallas kernels  198 us (57%)
  waiting for transfers between devices  59.5 us (17%)
  starting transfers between devices  48.3 us (14%)
  other arithmetic  16.8 us (5%)
  matrix products  13.5 us (4%)
  local copies, waits for them, and re-layouts  9.04 us (3%)
    pallas_call x2, Pallas kernels, full_scan(): pl.pallas_call(functools.partial(scan_kernel, len(earlier)), grid_spec=pl...  98.1 us
    pallas_call x1, Pallas kernels, local_ends(): pl.pallas_call(ends_kernel, grid=(channels // width,), in_specs=[pl.Block...  43.5 us
    ppermute x27, starting transfers between devices, swapped(): lax.ppermute(value, 'state', [(i, i ^ distance) for i in range(count)])  33.5 us
    ppermute x6, waiting for transfers between devices, seq_exchange(): return lax.ppermute(value, 'seq', [(i, i ^ distance) for i in range(count)])  28.1 us
    ppermute x27, waiting for transfers between devices, swapped(): lax.ppermute(value, 'state', [(i, i ^ distance) for i in range(count)])  25.8 us
    pallas_call x2, Pallas kernels, back(): pl.pallas_call(functools.partial(back_kernel, len(earlier)), grid_spec=pl...  21 us
    pallas_call x1, Pallas kernels, wide_grads(): pl.pallas_call(functools.partial(wide_kernel, high), grid_spec=pltpu.Pref...  12.3 us
    pallas_call x1, Pallas kernels, front(): pl.pallas_call(front_kernel, grid=(channels // width,), in_specs=[whole(n...  11.2 us
  transfers between devices with their start and end apart: 37, of which 16 were waited for; matrix products, arithmetic and copies ran while one was open for 8% of the time, Pallas kernels for 50%

profile of v9, /device:TPU:0, one launch (start us, length us, event | category | flops | bytes accessed | tf_op | source)
XLA Modules:
  0.0 347.3 jit_solution(1723237141422218705)
XLA Ops:
  0.7 3.0 collective-permute-start.1
  9.3 3.8 %collective-permute-start = (bf16[8,1024]{1,0:T(8,128)(2,1)S(1)}, bf16[8,1024]{1,0:T(8,128)(2,1)S(1)}, u32[]{:S(2)}, u32[]{:S(2)}) collective-permute-start(bf16[8,1024]{1,0:T(8,128)(2,1)S(1)} %slice.183), channel_id=1, source_target_pairs={{0,1},{1,2},{2,3},{4,5},{5,6},{6,7},{8,9},{9,10},{10,11},{12,13},{... | collective-permute-start | bytes 49160 | tf_op jit(solution)/shard_map/ppermute | solution.py:29
  17.1 11.2 %front.1 = (f32[512,2048]{1,0:T(8,128)}, f32[512,128]{1,0:T(8,128)}, bf16[512,2048]{1,0:T(8,128)(2,1)}, bf16[8,2048]{1,0:T(8,128)(2,1)}) custom-call(bf16[512,1024]{1,0:T(8,128)(2,1)} %copy-done, bf16[8,1024]{1,0:T(8,128)(2,1)} %copy-done.26, bf16[1024,4096]{1,0:T(8,128)(2,1)} %gate_w.1, f32[4,2048]{1,0:T(4,128)} %conv_w.5, f32[1,2048]{1,0:T(1,128)} %bitcast.116, ...), custom_call_target="tpu_custom_call" | custom-call | flops 8 | bytes 1024 | tf_op jit(solution)/shard_map/front/pallas_call | solution.py:725
  31.1 43.5 %ends.1 = (f32[512,2048]{1,0:T(8,128)}, f32[512,2048]{1,0:T(8,128)}, f32[512,2048]{1,0:T(8,128)}, f32[8,2048]{1,0:T(8,128)}, f32[16,2048]{1,0:T(8,128)}, /*index...) custom-call(s32[2]{0:T(128)} %get-tuple-element.254.live, ...), custom_call_target="tpu_custom_call" | custom-call | flops 40 | bytes 1024 | tf_op jit(solution)/shard_map/ends/pallas_call | solution.py:754
  79.2 3.3 collective-permute-done.6
  82.5 3.0 collective-permute-done.7
  90.6 49.0 %scan.2 = (bf16[512,2048]{1,0:T(8,128)(2,1)}, bf16[512,2048]{1,0:T(8,128)(2,1)}, f32[512,2048]{1,0:T(8,128)}, f32[16,2048]{1,0:T(8,128)}, f32[8,2048]{1,0:T(8,12...) custom-call(s32[2]{0:T(128)} %pad_add_fusion.2.order, ...), custom_call_target="tpu_custom_call" | custom-call | flops 50 | bytes 1024 | tf_op jit(solution)/shard_map/scan/pallas_call | solution.py:818
  144.0 49.1 %scan.3 = (bf16[512,2048]{1,0:T(8,128)(2,1)}, bf16[512,2048]{1,0:T(8,128)(2,1)}, f32[512,2048]{1,0:T(8,128)}, f32[16,2048]{1,0:T(8,128)}, f32[8,2048]{1,0:T(8,12...) custom-call(s32[2]{0:T(128)} %get-tuple-element.253.order, ...), custom_call_target="tpu_custom_call", output_to_operand_aliasing={{0}: (12, {}), {1}: (13, {}), {2}: (14, {}), {3}: (15, {}),... | custom-call | flops 50 | bytes 1024 | tf_op jit(solution)/shard_map/scan/pallas_call | solution.py:818
  195.5 5.6 %collective-permute-done.15.ahead = f32[8,2048]{1,0:T(8,128)S(1)} collective-permute-done((f32[8,2048]{1,0:T(8,128)S(1)}, f32[8,2048]{1,0:T(8,128)S(1)}, u32[]{:S(2)}, u32[]{:S(2)}) %collective-permute-start.15) | collective-permute-done | bytes 65568 | tf_op jit(solution)/shard_map/ppermute | solution.py:29
  201.8 10.4 %back.2 = (bf16[512,2048]{1,0:T(8,128)(2,1)}, bf16[4,12,64,128]{3,2,1,0:T(8,128)(2,1)}, bf16[576,512]{1,0:T(8,128)(2,1)}, bf16[576,512]{1,0:T(8,128)(2,1)}) custom-call(s32[3]{0:T(128)} %get-tuple-element.255.order, bf16[512,128]{1,0:T(8,128)(2,1)} %get-tuple-element.155.proj_grad, bf16[128,2048]{1,0:T(8,128)(2,1)} %pad.4.xproj, ...), custom_call_target="tpu_custom_call" | custom-call | flops 18 | bytes 1024 | tf_op jit(solution)/shard_map/back/pallas_call | solution.py:876
  212.2 2.3 collective-permute-start.17
  216.2 10.6 %back.3 = (bf16[512,2048]{1,0:T(8,128)(2,1)}, bf16[4,12,64,128]{3,2,1,0:T(8,128)(2,1)}, bf16[576,512]{1,0:T(8,128)(2,1)}, bf16[576,512]{1,0:T(8,128)(2,1)}) custom-call(s32[3]{0:T(128)} %get-tuple-element.256.order, bf16[512,128]{1,0:T(8,128)(2,1)} %get-tuple-element.155.proj_grad, ...), custom_call_target="tpu_custom_call", output_to_operand_aliasing={{0}: (13, {}), {1}: (14, {})} | custom-call | flops 18 | bytes 1024 | tf_op jit(solution)/shard_map/back/pallas_call | solution.py:876
  226.8 6.8 %collective-permute-done.17.refs_5_ = bf16[576,512]{1,0:T(8,128)(2,1)S(1)} collective-permute-done((bf16[576,512]{1,0:T(8,128)(2,1)}, bf16[576,512]{1,0:T(8,128)(2,1)S(1)}, u32[]{:S(2)}, u32[]{:S(2)}) %collective-permute-start.17) | collective-permute-done | bytes 589856 | tf_op jit(solution)/shard_map/ppermute | solution.py:23
  233.8 12.3 %wide.1 = (f32[1024,512]{1,0:T(8,128)}, f32[1024,512]{1,0:T(8,128)}) custom-call(s32[9]{0:T(128)} %stack.49.at, bf16[512,1024]{1,0:T(8,128)(2,1)} %get-tuple-element.173.refs_0_.refs_4_, bf16[512,1024]{1,0:T(8,128)(2,1)} %collective-permute-done.13.refs_1_.refs_5_, bf16[512,1024]{1,0:T(8,128)(2,1)} %collective-permute-done.14.refs_2_.refs_6_, ...), custom_call_target="tpu_custom_call" | custom-call | flops 10 | bytes 1024 | tf_op jit(solution)/shard_map/wide/pallas_call | solution.py:927
  246.2 4.4 %collective-permute-done.19 = f32[1024,512]{1,0:T(8,128)S(1)} collective-permute-done((f32[1024,512]{1,0:T(8,128)}, f32[1024,512]{1,0:T(8,128)S(1)}, u32[]{:S(2)}, u32[]{:S(2)}) %collective-permute-start.19) | collective-permute-done | bytes 2097184 | tf_op jit(solution)/shard_map/ppermute | solution.py:54
  251.9 2.8 add.179
  257.3 2.2 collective-permute-start.23
  261.0 2.0 collective-permute-start.22
  262.9 6.0 %collective-permute-done.20 = bf16[512,512]{1,0:T(8,128)(2,1)} collective-permute-done((bf16[512,512]{1,0:T(8,128)(2,1)S(1)}, bf16[512,512]{1,0:T(8,128)(2,1)}, u32[]{:S(2)}, u32[]{:S(2)}) %collective-permute-start.20) | collective-permute-done | bytes 524320 | tf_op jit(solution)/shard_map/ppermute | solution.py:54
  270.2 2.7 collective-permute-start.21
  272.9 5.1 %fusion = f32[512,1024]{1,0:T(8,128)S(1)} fusion(bf16[512,2048]{1,0:T(8,128)(2,1)S(1)} %copy-done.9, bf16[1024,4096]{1,0:T(8,128)(2,1)} %gate_w.1), kind=kOutput, calls=%fused_computation | convolution fusion | flops 2147483648 | bytes 8388608 | tf_op jit(solution)/shard_map/dot_general | solution.py:992
  278.1 4.0 %fusion.13 = (f32[1024]{0:T(1024)S(1)}, f32[512]{0:T(512)S(1)}, f32[512,1024]{1,0:T(8,128)}) fusion(bf16[512,1024]{1,0:T(8,128)(2,1)S(1)} %copy-done.1, f32[512]{0:T(512)S(1)} %add_rsqrt_fusion, f32[1024]{0:T(1024)S(1)} %copy-done.27, f32[512,1024]{1,0:T(8,128)S(1)} %fusion, bf16[512,2048]{1,0:T(8,128)(2,1)S(1)} %copy-done.7, ...), kind=kOutput, calls=%fused_computation.18 | convolution fusion | flops 2151676416 | bytes 11546624 | tf_op jit(solution)/shard_map/dot_general | solution.py:992
  284.4 8.3 %inner.1 = (f32[672,512]{1,0:T(8,128)}, f32[672,512]{1,0:T(8,128)}) custom-call(s32[9]{0:T(128)} %stack.49.at, bf16[512,1024]{1,0:T(8,128)(2,1)} %copy-done, bf16[512,1024]{1,0:T(8,128)(2,1)} %collective-permute-done.4.refs_13_.refs_1_, bf16[512,1024]{1,0:T(8,128)(2,1)} %collective-permute-done.5.refs_14_.refs_2_, ...), custom_call_target="tpu_custom_call" | custom-call | flops 5 | bytes 1024 | tf_op jit(solution)/shard_map/inner/pallas_call | solution.py:953
  293.4 2.6 collective-permute-done.26
  300.0 3.3 fusion.15
  304.0 6.1 %collective-permute-done.27 = bf16[384,512]{1,0:T(8,128)(2,1)S(1)} collective-permute-done((bf16[384,512]{1,0:T(8,128)(2,1)S(1)}, bf16[384,512]{1,0:T(8,128)(2,1)S(1)}, u32[]{:S(2)}, u32[]{:S(2)}) %collective-permute-start.27) | collective-permute-done | bytes 393248 | tf_op jit(solution)/shard_map/ppermute | solution.py:54
  310.3 3.1 collective-permute-start.33
  317.2 7.4 %collective-permute-done.33 = bf16[224,512]{1,0:T(8,128)(2,1)S(1)} collective-permute-done((bf16[224,512]{1,0:T(8,128)(2,1)S(1)}, bf16[224,512]{1,0:T(8,128)(2,1)S(1)}, u32[]{:S(2)}, u32[]{:S(2)}) %collective-permute-start.33) | collective-permute-done | bytes 229408 | tf_op jit(solution)/shard_map/ppermute | solution.py:54
  324.7 2.7 collective-permute-done.31.refs_2_
  334.9 3.8 %collective-permute-done.34.refs_5_ = bf16[256,512]{1,0:T(8,128)(2,1)S(1)} collective-permute-done((bf16[256,512]{1,0:T(8,128)(2,1)S(1)}, bf16[256,512]{1,0:T(8,128)(2,1)S(1)}, u32[]{:S(2)}, u32[]{:S(2)}) %collective-permute-start.34) | collective-permute-done | bytes 262176 | tf_op jit(solution)/shard_map/ppermute | solution.py:23
  338.7 3.9 %collective-permute-done.35.refs_6_ = bf16[256,512]{1,0:T(8,128)(2,1)S(1)} collective-permute-done((bf16[256,512]{1,0:T(8,128)(2,1)S(1)}, bf16[256,512]{1,0:T(8,128)(2,1)S(1)}, u32[]{:S(2)}, u32[]{:S(2)}) %collective-permute-start.35) | collective-permute-done | bytes 262176 | tf_op jit(solution)/shard_map/ppermute | solution.py:23
  343.5 3.6 %assemble.1 = (f32[128,4096]{1,0:T(8,128)}, f32[256,1024]{1,0:T(8,128)}, f32[96,256]{1,0:T(8,128)}, f32[64,256]{1,0:T(8,128)}, f32[4,2048]{1,0:T(4,128)}, /*inde...) custom-call(s32[9]{0:T(128)} %stack.49.at, ...), custom_call_target="tpu_custom_call" | custom-call | flops 4 | bytes 1024 | tf_op jit(solution)/shard_map/assemble/pallas_call | solution.py:979
  (167 shorter events, 57.0 us)
Async XLA Ops:
  0.7 29.6 %collective-permute-start.1 = (f32[4,2048]{1,0:T(4,128)}, f32[4,2048]{1,0:T(4,128)S(1)}, u32[]{:S(2)}, u32[]{:S(2)}) collective-permute-start(f32[4,2048]{1,0:T(4,128)} %param.23), channel_id=1, source_target_pairs={{0,1},{1,0},{2,3},{3,2},{4,5},{5,4},{6,7},{7,6},{8,9},{9,8},{10,11... | collective-permute-start | bytes 98312 | tf_op jit(solution)/shard_map/ppermute | solution.py:23
  3.7 26.7 %collective-permute-start.2 = (f32[4,2048]{1,0:T(4,128)}, f32[4,2048]{1,0:T(4,128)S(1)}, u32[]{:S(2)}, u32[]{:S(2)}) collective-permute-start(f32[4,2048]{1,0:T(4,128)} %param.23), channel_id=1, source_target_pairs={{0,2},{1,3},{2,0},{3,1},{4,6},{5,7},{6,4},{7,5},{8,10},{9,11},{10,... | collective-permute-start | bytes 98312 | tf_op jit(solution)/shard_map/ppermute | solution.py:23
  5.2 25.2 %collective-permute-start.3 = (f32[4,2048]{1,0:T(4,128)}, f32[4,2048]{1,0:T(4,128)S(1)}, u32[]{:S(2)}, u32[]{:S(2)}) collective-permute-start(f32[4,2048]{1,0:T(4,128)} %param.23), channel_id=1, source_target_pairs={{0,3},{1,2},{2,1},{3,0},{4,7},{5,6},{6,5},{7,4},{8,11},{9,10},{10,... | collective-permute-start | bytes 98312 | tf_op jit(solution)/shard_map/ppermute | solution.py:23
  28.4 46.2 %collective-permute-start.4 = (bf16[512,1024]{1,0:T(8,128)(2,1)}, bf16[512,1024]{1,0:T(8,128)(2,1)}, u32[]{:S(2)}, u32[]{:S(2)}) collective-permute-start(bf16[512,1024]{1,0:T(8,128)(2,1)} %copy-done), channel_id=1, source_target_pairs={{0,1},{1,0},{2,3},{3,2},{4,5},{5,4},{6,7},{7,6},{8,9},{9,8},{10,11... | collective-permute-start | bytes 3145736 | tf_op jit(solution)/shard_map/ppermute | solution.py:23
  29.9 44.7 %collective-permute-start.5 = (bf16[512,1024]{1,0:T(8,128)(2,1)}, bf16[512,1024]{1,0:T(8,128)(2,1)}, u32[]{:S(2)}, u32[]{:S(2)}) collective-permute-start(bf16[512,1024]{1,0:T(8,128)(2,1)} %copy-done), channel_id=1, source_target_pairs={{0,2},{1,3},{2,0},{3,1},{4,6},{5,7},{6,4},{7,5},{8,10},{9,11},{10,... | collective-permute-start | bytes 3145736 | tf_op jit(solution)/shard_map/ppermute | solution.py:23
  74.7 7.8 %collective-permute-start.6 = (f32[24,2048]{1,0:T(8,128)}, f32[24,2048]{1,0:T(8,128)S(1)}, u32[]{:S(2)}, u32[]{:S(2)}) collective-permute-start(f32[24,2048]{1,0:T(8,128)} %get-tuple-element.134), channel_id=1, source_target_pairs={{0,1},{1,0},{2,3},{3,2},{4,5},{5,4},{6,7},{7,6},{8,9},{9,8},{10,11... | collective-permute-start | bytes 589832 | tf_op jit(solution)/shard_map/ppermute | solution.py:23
  76.4 9.1 %collective-permute-start.7 = (f32[24,2048]{1,0:T(8,128)}, f32[24,2048]{1,0:T(8,128)S(1)}, u32[]{:S(2)}, u32[]{:S(2)}) collective-permute-start(f32[24,2048]{1,0:T(8,128)} %get-tuple-element.135), channel_id=1, source_target_pairs={{0,2},{1,3},{2,0},{3,1},{4,6},{5,7},{6,4},{7,5},{8,10},{9,11},{10,... | collective-permute-start | bytes 589832 | tf_op jit(solution)/shard_map/ppermute | solution.py:23
  76.9 8.6 %collective-permute-start.8 = (f32[24,2048]{1,0:T(8,128)}, f32[24,2048]{1,0:T(8,128)S(1)}, u32[]{:S(2)}, u32[]{:S(2)}) collective-permute-start(f32[24,2048]{1,0:T(8,128)} %get-tuple-element.136), channel_id=1, source_target_pairs={{0,3},{1,2},{2,1},{3,0},{4,7},{5,6},{6,5},{7,4},{8,11},{9,10},{10,... | collective-permute-start | bytes 589832 | tf_op jit(solution)/shard_map/ppermute | solution.py:23
  86.5 55.1 %collective-permute-start.10 = (bf16[512,1024]{1,0:T(8,128)(2,1)}, bf16[512,1024]{1,0:T(8,128)(2,1)}, u32[]{:S(2)}, u32[]{:S(2)}) collective-permute-start(bf16[512,1024]{1,0:T(8,128)(2,1)} %fusion.8.masked.refs_8_), channel_id=1, source_target_pairs={{0,2},{1,3},{2,0},{3,1},{4,6},{5,7},{6,4},{7,5},{8,10},{9,11},{10,... | collective-permute-start | bytes 3145736 | tf_op jit(solution)/shard_map/ppermute | solution.py:23
  87.4 54.2 %collective-permute-start.11 = (bf16[512,1024]{1,0:T(8,128)(2,1)}, bf16[512,1024]{1,0:T(8,128)(2,1)}, u32[]{:S(2)}, u32[]{:S(2)}) collective-permute-start(bf16[512,1024]{1,0:T(8,128)(2,1)} %fusion.8.masked.refs_8_), channel_id=1, source_target_pairs={{0,3},{1,2},{2,1},{3,0},{4,7},{5,6},{6,5},{7,4},{8,11},{9,10},{10,... | collective-permute-start | bytes 3145736 | tf_op jit(solution)/shard_map/ppermute | solution.py:23
  88.7 52.9 %collective-permute-start.9 = (bf16[512,1024]{1,0:T(8,128)(2,1)}, bf16[512,1024]{1,0:T(8,128)(2,1)}, u32[]{:S(2)}, u32[]{:S(2)}) collective-permute-start(bf16[512,1024]{1,0:T(8,128)(2,1)} %fusion.8.masked.refs_8_), channel_id=1, source_target_pairs={{0,1},{1,0},{2,3},{3,2},{4,5},{5,4},{6,7},{7,6},{8,9},{9,8},{10,11... | collective-permute-start | bytes 3145736 | tf_op jit(solution)/shard_map/ppermute | solution.py:23
  139.6 53.6 %collective-permute-start.13 = (bf16[512,1024]{1,0:T(8,128)(2,1)}, bf16[512,1024]{1,0:T(8,128)(2,1)}, u32[]{:S(2)}, u32[]{:S(2)}) collective-permute-start(bf16[512,1024]{1,0:T(8,128)(2,1)} %get-tuple-element.152), channel_id=1, source_target_pairs={{0,1},{1,0},{2,3},{3,2},{4,5},{5,4},{6,7},{7,6},{8,9},{9,8},{10,11... | collective-permute-start | bytes 3145736 | tf_op jit(solution)/shard_map/ppermute | solution.py:23
  140.4 52.8 %collective-permute-start.14 = (bf16[512,1024]{1,0:T(8,128)(2,1)}, bf16[512,1024]{1,0:T(8,128)(2,1)}, u32[]{:S(2)}, u32[]{:S(2)}) collective-permute-start(bf16[512,1024]{1,0:T(8,128)(2,1)} %get-tuple-element.153), channel_id=1, source_target_pairs={{0,2},{1,3},{2,0},{3,1},{4,6},{5,7},{6,4},{7,5},{8,10},{9,11},{10,... | collective-permute-start | bytes 3145736 | tf_op jit(solution)/shard_map/ppermute | solution.py:23
  141.6 51.5 %collective-permute-start.12 = (bf16[512,1024]{1,0:T(8,128)(2,1)}, bf16[512,1024]{1,0:T(8,128)(2,1)}, u32[]{:S(2)}, u32[]{:S(2)}) collective-permute-start(bf16[512,1024]{1,0:T(8,128)(2,1)} %copy-done), channel_id=1, source_target_pairs={{0,3},{1,2},{2,1},{3,0},{4,7},{5,6},{6,5},{7,4},{8,11},{9,10},{10,... | collective-permute-start | bytes 3145736 | tf_op jit(solution)/shard_map/ppermute | solution.py:23
  201.1 32.6 %collective-permute-start.16 = (bf16[512,1024]{1,0:T(8,128)(2,1)}, bf16[512,1024]{1,0:T(8,128)(2,1)}, u32[]{:S(2)}, u32[]{:S(2)}) collective-permute-start(bf16[512,1024]{1,0:T(8,128)(2,1)} %get-tuple-element.163), channel_id=1, source_target_pairs={{0,3},{1,2},{2,1},{3,0},{4,7},{5,6},{6,5},{7,4},{8,11},{9,10},{10,... | collective-permute-start | bytes 3145736 | tf_op jit(solution)/shard_map/ppermute | solution.py:23
  212.2 21.5 %collective-permute-start.17 = (bf16[576,512]{1,0:T(8,128)(2,1)}, bf16[576,512]{1,0:T(8,128)(2,1)S(1)}, u32[]{:S(2)}, u32[]{:S(2)}) collective-permute-start(bf16[576,512]{1,0:T(8,128)(2,1)} %get-tuple-element.168), channel_id=1, source_target_pairs={{0,1},{1,0},{2,3},{3,2},{4,5},{5,4},{6,7},{7,6},{8,9},{9,8},{10,11... | collective-permute-start | bytes 1769480 | tf_op jit(solution)/shard_map/ppermute | solution.py:23
  214.5 19.3 %collective-permute-start.18 = (bf16[576,512]{1,0:T(8,128)(2,1)}, bf16[576,512]{1,0:T(8,128)(2,1)}, u32[]{:S(2)}, u32[]{:S(2)}) collective-permute-start(bf16[576,512]{1,0:T(8,128)(2,1)} %get-tuple-element.169), channel_id=1, source_target_pairs={{0,2},{1,3},{2,0},{3,1},{4,6},{5,7},{6,4},{7,5},{8,10},{9,11},{10,... | collective-permute-start | bytes 1769480 | tf_op jit(solution)/shard_map/ppermute | solution.py:23
  254.8 14.1 %collective-permute-start.20 = (bf16[512,512]{1,0:T(8,128)(2,1)S(1)}, bf16[512,512]{1,0:T(8,128)(2,1)}, u32[]{:S(2)}, u32[]{:S(2)}) collective-permute-start(bf16[512,512]{1,0:T(8,128)(2,1)S(1)} %bitcast.110), channel_id=1, source_target_pairs={{0,8},{4,12},{8,0},{12,4},{16,24},{20,28},{24,16},{28,20},{1,9},{5... | collective-permute-start | bytes 1572872 | tf_op jit(solution)/shard_map/ppermute | solution.py:54
  257.3 27.1 %collective-permute-start.23 = (bf16[12,64,128]{2,1,0:T(8,128)(2,1)}, bf16[12,64,128]{2,1,0:T(8,128)(2,1)}, u32[]{:S(2)}, u32[]{:S(2)}) collective-permute-start(bf16[12,64,128]{2,1,0:T(8,128)(2,1)} %get-tuple-element.238), channel_id=1, source_target_pairs={{0,1},{1,0},{2,3},{3,2},{4,5},{5,4},{6,7},{7,6},{8,9},{9,8},{10,11... | collective-permute-start | bytes 589832 | tf_op jit(solution)/shard_map/ppermute | solution.py:23
  259.5 24.9 %collective-permute-start.24 = (bf16[12,64,128]{2,1,0:T(8,128)(2,1)}, bf16[12,64,128]{2,1,0:T(8,128)(2,1)}, u32[]{:S(2)}, u32[]{:S(2)}) collective-permute-start(bf16[12,64,128]{2,1,0:T(8,128)(2,1)} %get-tuple-element.237), channel_id=1, source_target_pairs={{0,2},{1,3},{2,0},{3,1},{4,6},{5,7},{6,4},{7,5},{8,10},{9,11},{10,... | collective-permute-start | bytes 589832 | tf_op jit(solution)/shard_map/ppermute | solution.py:23
  260.0 24.4 %collective-permute-start.25 = (bf16[12,64,128]{2,1,0:T(8,128)(2,1)}, bf16[12,64,128]{2,1,0:T(8,128)(2,1)}, u32[]{:S(2)}, u32[]{:S(2)}) collective-permute-start(bf16[12,64,128]{2,1,0:T(8,128)(2,1)} %get-tuple-element.236), channel_id=1, source_target_pairs={{0,3},{1,2},{2,1},{3,0},{4,7},{5,6},{6,5},{7,4},{8,11},{9,10},{10,... | collective-permute-start | bytes 589832 | tf_op jit(solution)/shard_map/ppermute | solution.py:23
  261.0 23.5 %collective-permute-start.22 = (bf16[576,512]{1,0:T(8,128)(2,1)}, bf16[576,512]{1,0:T(8,128)(2,1)}, u32[]{:S(2)}, u32[]{:S(2)}) collective-permute-start(bf16[576,512]{1,0:T(8,128)(2,1)} %get-tuple-element.196), channel_id=1, source_target_pairs={{0,3},{1,2},{2,1},{3,0},{4,7},{5,6},{6,5},{7,4},{8,11},{9,10},{10,... | collective-permute-start | bytes 1769480 | tf_op jit(solution)/shard_map/ppermute | solution.py:23
  270.2 14.1 %collective-permute-start.21 = (bf16[256,512]{1,0:T(8,128)(2,1)S(1)}, bf16[256,512]{1,0:T(8,128)(2,1)S(1)}, u32[]{:S(2)}, u32[]{:S(2)}) collective-permute-start(bf16[256,512]{1,0:T(8,128)(2,1)S(1)} %fusion.19), channel_id=1, source_target_pairs={{0,16},{4,20},{8,24},{12,28},{16,0},{20,4},{24,8},{28,12},{1,17},{... | collective-permute-start | bytes 786440 | tf_op jit(solution)/shard_map/ppermute | solution.py:54
  292.8 10.5 %collective-permute-start.28 = (bf16[128,512]{1,0:T(8,128)(2,1)S(1)}, bf16[128,512]{1,0:T(8,128)(2,1)S(1)}, u32[]{:S(2)}, u32[]{:S(2)}) collective-permute-start(bf16[128,512]{1,0:T(8,128)(2,1)S(1)} %get-tuple-element.244), channel_id=1, source_target_pairs={{0,0},{1,1},{2,2},{3,3},{4,5},{5,4},{6,7},{7,6},{8,10},{9,11},{10,... | collective-permute-start | bytes 393224 | tf_op jit(solution)/shard_map/ppermute | solution.py:94
  298.1 12.0 %collective-permute-start.27 = (bf16[384,512]{1,0:T(8,128)(2,1)S(1)}, bf16[384,512]{1,0:T(8,128)(2,1)S(1)}, u32[]{:S(2)}, u32[]{:S(2)}) collective-permute-start(bf16[384,512]{1,0:T(8,128)(2,1)S(1)} %pad_maximum_fusion.1), channel_id=1, source_target_pairs={{0,8},{4,12},{8,0},{12,4},{16,24},{20,28},{24,16},{28,20},{1,9},{5... | collective-permute-start | bytes 1179656 | tf_op jit(solution)/shard_map/ppermute | solution.py:54
  310.3 14.3 %collective-permute-start.33 = (bf16[224,512]{1,0:T(8,128)(2,1)S(1)}, bf16[224,512]{1,0:T(8,128)(2,1)S(1)}, u32[]{:S(2)}, u32[]{:S(2)}) collective-permute-start(bf16[224,512]{1,0:T(8,128)(2,1)S(1)} %pad_maximum_fusion.4), channel_id=1, source_target_pairs={{0,16},{4,20},{8,24},{12,28},{16,0},{20,4},{24,8},{28,12},{1,17},{... | collective-permute-start | bytes 688136 | tf_op jit(solution)/shard_map/ppermute | solution.py:54
  313.5 11.2 %collective-permute-start.30 = (bf16[256,512]{1,0:T(8,128)(2,1)S(1)}, bf16[256,512]{1,0:T(8,128)(2,1)S(1)}, u32[]{:S(2)}, u32[]{:S(2)}) collective-permute-start(bf16[256,512]{1,0:T(8,128)(2,1)S(1)} %pad_maximum_fusion.2.refs_0_), channel_id=1, source_target_pairs={{0,1},{1,0},{2,3},{3,2},{4,5},{5,4},{6,7},{7,6},{8,9},{9,8},{10,11... | collective-permute-start | bytes 786440 | tf_op jit(solution)/shard_map/ppermute | solution.py:23
  314.7 12.7 %collective-permute-start.31 = (bf16[256,512]{1,0:T(8,128)(2,1)S(1)}, bf16[256,512]{1,0:T(8,128)(2,1)S(1)}, u32[]{:S(2)}, u32[]{:S(2)}) collective-permute-start(bf16[256,512]{1,0:T(8,128)(2,1)S(1)} %pad_maximum_fusion.2.refs_0_), channel_id=1, source_target_pairs={{0,2},{1,3},{2,0},{3,1},{4,6},{5,7},{6,4},{7,5},{8,10},{9,11},{10,... | collective-permute-start | bytes 786440 | tf_op jit(solution)/shard_map/ppermute | solution.py:23
  315.8 13.4 %collective-permute-start.32 = (bf16[256,512]{1,0:T(8,128)(2,1)S(1)}, bf16[256,512]{1,0:T(8,128)(2,1)S(1)}, u32[]{:S(2)}, u32[]{:S(2)}) collective-permute-start(bf16[256,512]{1,0:T(8,128)(2,1)S(1)} %pad_maximum_fusion.2.refs_0_), channel_id=1, source_target_pairs={{0,3},{1,2},{2,1},{3,0},{4,7},{5,6},{6,5},{7,4},{8,11},{9,10},{10,... | collective-permute-start | bytes 786440 | tf_op jit(solution)/shard_map/ppermute | solution.py:23
  329.4 9.3 %collective-permute-start.34 = (bf16[256,512]{1,0:T(8,128)(2,1)S(1)}, bf16[256,512]{1,0:T(8,128)(2,1)S(1)}, u32[]{:S(2)}, u32[]{:S(2)}) collective-permute-start(bf16[256,512]{1,0:T(8,128)(2,1)S(1)} %pad_maximum_fusion.3.refs_4_), channel_id=1, source_target_pairs={{0,1},{1,0},{2,3},{3,2},{4,5},{5,4},{6,7},{7,6},{8,9},{9,8},{10,11... | collective-permute-start | bytes 786440 | tf_op jit(solution)/shard_map/ppermute | solution.py:23
  330.6 11.9 %collective-permute-start.35 = (bf16[256,512]{1,0:T(8,128)(2,1)S(1)}, bf16[256,512]{1,0:T(8,128)(2,1)S(1)}, u32[]{:S(2)}, u32[]{:S(2)}) collective-permute-start(bf16[256,512]{1,0:T(8,128)(2,1)S(1)} %pad_maximum_fusion.3.refs_4_), channel_id=1, source_target_pairs={{0,2},{1,3},{2,0},{3,1},{4,6},{5,7},{6,4},{7,5},{8,10},{9,11},{10,... | collective-permute-start | bytes 786440 | tf_op jit(solution)/shard_map/ppermute | solution.py:23
  332.4 11.1 %collective-permute-start.36 = (bf16[256,512]{1,0:T(8,128)(2,1)S(1)}, bf16[256,512]{1,0:T(8,128)(2,1)}, u32[]{:S(2)}, u32[]{:S(2)}) collective-permute-start(bf16[256,512]{1,0:T(8,128)(2,1)S(1)} %pad_maximum_fusion.3.refs_4_), channel_id=1, source_target_pairs={{0,3},{1,2},{2,1},{3,0},{4,7},{5,6},{6,5},{7,4},{8,11},{9,10},{10,... | collective-permute-start | bytes 786440 | tf_op jit(solution)/shard_map/ppermute | solution.py:23
  (35 other events, 396.8 us)
